TPU v7x, 32 devices: a whole 2x2x4 slice. The times are simulated.
32 devices in a mesh: dp: 8 (over y, x, core), ka: 4 (over z).
Axes of the slice: x: 2, y: 2, z: 4, core: 2. Of those that a mesh axis runs over, the one named last changes fastest.
Arguments:
- feats: bfloat16 [16384, 256], P('dp'), may hold values from -6 to 6
- coords: float32 [3, 16384], P(None, 'dp'), may hold values from 0 to 1
- cell_ids: int32 [8, 2048], P('dp'), may hold values from 0 to 7, never falling along the last dimension, each value on 1 to 1024 neighbouring positions
- recip: float32 [8, 8, 9], P('dp'), may hold values from 0.05 to 0.35
- kvec: int32 [3, 512], P(None, 'ka'), may hold values from -4 to 4
- w_in: bfloat16 [256, 256], replicated, may hold values from -0.375 to 0.375
- w_out: bfloat16 [256, 256], replicated, may hold values from -0.375 to 0.375
- kfilt: float32 [512, 256], P('ka'), may hold values from -3 to 3
- spread: float32 [256], replicated, may hold values from 0.02 to 0.5
- cotan: bfloat16 [16384, 256], P('dp'), may hold values from -6 to 6
Outputs:
- mixed: bfloat16 [16384, 256], P('dp')
- feat_grad: bfloat16 [16384, 256], P('dp')
- grad_w_in: float32 [256, 256], replicated
- grad_w_out: float32 [256, 256], replicated
- grad_kfilt: float32 [512, 256], P('ka')
Inputs may be any that keep to these rules, and one draw needn't show every extreme that they name: `cell_ids`: within each row, cell numbers never fall; each of the 8 cells holds 1 to 1024 atoms, and one holds exactly 1024.
All inputs are finite; a program needn't handle non-finite values.
Results may differ from a plain program's by a relative error of at most 0.0056.
The roundings to bfloat16 on the way count: a program that leaves them out, or rounds other values in their place, can miss the bound.
Values may be sent and summed in bfloat16 or wider, within the bound.
No kernel may reach another device: no remote copies, remote signals or barrier semaphores. Data moves between devices by JAX's collectives and lax.ppermute only.
A program may use at most 64 MiB of HBM per device.

v0:
```python
import functools

import jax
import jax.numpy as jnp
from jax import lax
from jax.experimental import pallas as pl
from jax.experimental.pallas import tpu as pltpu
from jax.sharding import PartitionSpec as P

F32 = jnp.float32
BF16 = jnp.bfloat16
LANES = 128
COS_TERMS = (
    0.9999999890590228,
    -19.73920449945383,
    64.93911745989081,
    -85.45013953079767,
    60.167630950263465,
    -25.967599245923743,
    6.52865815775625,
)
SIN_TERMS = (
    6.283184916495428,
    -41.34158923268831,
    81.59994332977429,
    -76.61447253115396,
    41.34288235413569,
    -12.471243534350362,
)
ROUNDER = 12582912.0


def mm(lhs, rhs, lhs_dim=1, rhs_dim=0):
    return lax.dot_general(
        lhs, rhs, (((lhs_dim,), (rhs_dim,)), ((), ())), preferred_element_type=F32
    )


def horner(terms, square):
    value = terms[-1] * square + terms[-2]
    for term in terms[-3::-1]:
        value = value * square + term
    return value


def partner(me, step, count):
    if count & (count - 1) == 0:
        return me ^ step
    return lax.rem(me + step, count)


def routes(step, count):
    if count & (count - 1) == 0:
        return [(i, i ^ step) for i in range(count)]
    return [(i, (i + step) % count) for i in range(count)]


def tile_of(size, most):
    tile = most
    while size % tile:
        tile //= 2
    return tile


def block_kernel(n_ka, n_dp, *refs):
    bounds, me_ref, feats_hbm, cotan_hbm, coords, ids, recip, spread = refs[:8]
    kvecs = refs[8 : 8 + n_ka]
    kfilts = refs[8 + n_ka : 8 + 2 * n_ka]
    w_in, w_out = refs[8 + 2 * n_ka : 10 + 2 * n_ka]
    mixed_hbm, fgrad_hbm, pieces, own_piece = refs[10 + 2 * n_ka : 14 + 2 * n_ka]
    (
        feats, cotan, kcols, krows, kfilt_t, spread_col, waves, proj_t, mess_t, mgrad_t,
        total, factors, filter_grad, raw_in_t, raw_out, mixed, fgrad, weights, sems,
    ) = refs[14 + 2 * n_ka :]
    atoms, chan = feats.shape
    own = kvecs[0].shape[1]
    k_all = own * n_ka
    cells = recip.shape[0]
    tile = tile_of(atoms, 256)
    tiles = atoms // tile

    feats_in = pltpu.make_async_copy(feats_hbm, feats, sems.at[0])
    feats_in.start()
    cotan_in = pltpu.make_async_copy(cotan_hbm, cotan, sems.at[1])
    cotan_in.start()

    for j in range(n_ka):
        rows = kvecs[j][...].astype(F32)
        rows = jnp.concatenate([rows, jnp.zeros((5, own), F32)], axis=0)
        krows[:, j * own : (j + 1) * own] = rows
        kcols[j * own : (j + 1) * own, :] = rows.T
        kfilt_t[:, j * own : (j + 1) * own] = kfilts[j][...].T
    spread_col[...] = jnp.broadcast_to(spread[...], (8, chan)).T

    wide = tile_of(atoms, 1024)

    def phase_rows(i, carry):
        row = pl.multiple_of(i * 16, 16)
        kv = kcols[pl.ds(row, 16), :]
        for start in range(0, atoms, wide):
            frac = coords[:, start : start + wide]
            turns = kv[:, 0:1] * frac[0:1, :] + kv[:, 1:2] * frac[1:2, :]
            turns = turns + kv[:, 2:3] * frac[2:3, :]
            turns = turns - ((turns + ROUNDER) - ROUNDER)
            square = turns * turns
            waves[pl.ds(row, 16), start : start + wide] = horner(COS_TERMS, square).astype(BF16)
            waves[pl.ds(pl.multiple_of(k_all + row, 16), 16), start : start + wide] = (
                horner(SIN_TERMS, square) * turns
            ).astype(BF16)
        return carry

    lax.fori_loop(0, k_all // 16, phase_rows, 0)

    feats_in.wait()

    def project(t, carry):
        at = pl.ds(pl.multiple_of(t * tile, tile), tile)
        proj_t[:, at] = mm(w_in[...], feats[at, :], 0, 1).astype(BF16)
        return carry

    lax.fori_loop(0, tiles, project, 0)

    lattice = krows[...]

    def shape_of(cell):
        squared = jnp.zeros((1, k_all), F32)
        line = recip[pl.ds(cell, 1), :]
        for r in range(3):
            part = line[:, 3 * r : 3 * r + 1] * lattice[0:1, :]
            part = part + line[:, 3 * r + 1 : 3 * r + 2] * lattice[1:2, :]
            part = part + line[:, 3 * r + 2 : 3 * r + 3] * lattice[2:3, :]
            squared = squared + part * part
        return jnp.exp(-squared * spread_col[:, 0:1])

    def span(cell):
        first = bounds[1, cell]
        count = bounds[0, cell]
        return lax.div(first, tile), lax.div(first + count + (tile - 1), tile), count

    def gather(cell, source):
        low, high, count = span(cell)
        total[...] = jnp.zeros_like(total)

        def step(t, carry):
            at = pl.ds(pl.multiple_of(t * tile, tile), tile)
            member = (ids[:, at] == cell).astype(F32).astype(BF16)
            total[...] += mm(source[:, at] * member, waves[:, at], 1, 1)
            return carry

        lax.fori_loop(low, high, step, 0)
        return low, high, 1.0 / jnp.full((1, 1), count, jnp.int32).astype(F32)

    def spread_back(cell, low, high):
        def step(t, carry):
            at = pl.ds(pl.multiple_of(t * tile, tile), tile)
            member = ids[:, at] == cell
            value = mm(weights[...], waves[:, at])
            mess_t[:, at] = jnp.where(member, value, mess_t[:, at])
            return carry

        lax.fori_loop(low, high, step, 0)

    def forward_cell(cell, carry):
        low, high, scale = gather(cell, proj_t)
        filt = kfilt_t[...] * shape_of(cell)
        real, imag = total[:, :k_all], total[:, k_all:]
        factors[cell] = total[...]
        weights[:, :k_all] = (filt * real * scale).astype(BF16)
        weights[:, k_all:] = (filt * imag * scale).astype(BF16)
        spread_back(cell, low, high)
        return carry

    lax.fori_loop(0, cells, forward_cell, 0)

    cotan_in.wait()
    raw_out[...] = jnp.zeros_like(raw_out)

    def middle(t, carry):
        at = pl.ds(pl.multiple_of(t * tile, tile), tile)
        message = mess_t[:, at]
        sigma = jax.nn.sigmoid(message)
        activated = (message * sigma).astype(BF16)
        cot = cotan[at, :]
        act_grad = mm(w_out[...], cot, 1, 1)
        mgrad_t[:, at] = (act_grad * (sigma * (1.0 + message * (1.0 - sigma)))).astype(BF16)
        raw_out[...] += mm(activated, cot)
        mixed[at, :] = (feats[at, :].astype(F32) + mm(activated.T, w_out[...])).astype(BF16)
        return carry

    lax.fori_loop(0, tiles, middle, 0)
    mixed_out = pltpu.make_async_copy(mixed, mixed_hbm, sems.at[2])
    mixed_out.start()

    filter_grad[...] = jnp.zeros_like(filter_grad)

    def backward_cell(cell, carry):
        low, high, scale = gather(cell, mgrad_t)
        shape = shape_of(cell)
        filt = kfilt_t[...] * shape
        real = total[:, :k_all] * scale
        imag = total[:, k_all:] * scale
        weights[:, :k_all] = (filt * real).astype(BF16)
        weights[:, k_all:] = (filt * imag).astype(BF16)
        filter_grad[...] += shape * (
            factors[cell, :, :k_all] * real + factors[cell, :, k_all:] * imag
        )
        spread_back(cell, low, high)
        return carry

    lax.fori_loop(0, cells, backward_cell, 0)

    raw_in_t[...] = jnp.zeros_like(raw_in_t)

    def last(t, carry):
        at = pl.ds(pl.multiple_of(t * tile, tile), tile)
        update = mess_t[:, at].astype(BF16)
        raw_in_t[...] += mm(update, feats[at, :])
        fgrad[at, :] = (cotan[at, :].astype(F32) + mm(update.T, w_in[...], 1, 1)).astype(BF16)
        return carry

    lax.fori_loop(0, tiles, last, 0)
    fgrad_out = pltpu.make_async_copy(fgrad, fgrad_hbm, sems.at[3])
    fgrad_out.start()

    me = me_ref[0]
    rows = chan // n_dp
    for s in range(n_dp):
        at = pl.ds(pl.multiple_of(partner(me, s, n_dp) * rows, rows), rows)
        dest = own_piece if s == 0 else pieces.at[s - 1]
        dest[:, :chan] = raw_in_t[at, :].astype(dest.dtype)
        dest[:, chan : 2 * chan] = raw_out[at, :].astype(dest.dtype)
        dest[:, 2 * chan :] = filter_grad[at, :].astype(dest.dtype)
    mixed_out.wait()
    fgrad_out.wait()


def block_call(n_ka, n_dp, bounds, me, feats, cotan, coords, ids, recip, spread, kvecs, kfilts, w_in, w_out):
    atoms, chan = feats.shape
    own = kvecs[0].shape[1]
    k_all = own * n_ka
    cells = recip.shape[0]
    rows = chan // n_dp
    width = 2 * chan + k_all
    vmem = pl.BlockSpec(memory_space=pltpu.VMEM)
    smem = pl.BlockSpec(memory_space=pltpu.SMEM)
    hbm = pl.BlockSpec(memory_space=pl.ANY)
    return pl.pallas_call(
        functools.partial(block_kernel, n_ka, n_dp),
        out_shape=(
            jax.ShapeDtypeStruct((atoms, chan), BF16),
            jax.ShapeDtypeStruct((atoms, chan), BF16),
            jax.ShapeDtypeStruct((n_dp - 1, rows, width), BF16),
            jax.ShapeDtypeStruct((rows, width), F32),
        ),
        in_specs=[smem, smem, hbm, hbm] + [vmem] * (6 + 2 * n_ka),
        out_specs=(hbm, hbm, vmem, vmem),
        scratch_shapes=[
            pltpu.VMEM((atoms, chan), BF16),
            pltpu.VMEM((atoms, chan), BF16),
            pltpu.VMEM((k_all, 8), F32),
            pltpu.VMEM((8, k_all), F32),
            pltpu.VMEM((chan, k_all), F32),
            pltpu.VMEM((chan, 8), F32),
            pltpu.VMEM((2 * k_all, atoms), BF16),
            pltpu.VMEM((chan, atoms), BF16),
            pltpu.VMEM((chan, atoms), F32),
            pltpu.VMEM((chan, atoms), BF16),
            pltpu.VMEM((chan, 2 * k_all), F32),
            pltpu.VMEM((cells, chan, 2 * k_all), F32),
            pltpu.VMEM((chan, k_all), F32),
            pltpu.VMEM((chan, chan), F32),
            pltpu.VMEM((chan, chan), F32),
            pltpu.VMEM((atoms, chan), BF16),
            pltpu.VMEM((atoms, chan), BF16),
            pltpu.VMEM((chan, 2 * k_all), BF16),
            pltpu.SemaphoreType.DMA((4,)),
        ],
        name="block",
    )(bounds, me, feats, cotan, coords, ids, recip, spread, *kvecs, *kfilts, w_in, w_out)


def sum_kernel(chan, own, piece, *refs):
    parts, out = refs[:-1], refs[-1]
    value = piece[...]
    for part in parts:
        value = value + part[...].astype(F32)
    weight_part = value[:, : 2 * chan]
    filter_part = value[:, 2 * chan :]
    out[:, : 2 * chan + own] = value[:, : 2 * chan + own]
    weight_squares = jnp.sum(weight_part * weight_part, axis=1, keepdims=True)
    filter_squares = jnp.sum(filter_part * filter_part, axis=1, keepdims=True)
    lane = lax.broadcasted_iota(jnp.int32, (value.shape[0], LANES), 1)
    out[:, 2 * chan + own :] = jnp.where(lane < LANES // 2, weight_squares, filter_squares)


def final_kernel(chan, own, n_ka, n_dp, me_ref, *refs):
    parts = refs[:n_dp]
    g_in, g_out, g_filt, raw_in_t, filt_t = refs[n_dp:]
    me = me_ref[0]
    rows = chan // n_dp
    squares = parts[0][:, 2 * chan + own :]
    for part in parts[1:]:
        squares = squares + part[:, 2 * chan + own :]
    squares = jnp.sum(squares, axis=0, keepdims=True)
    weight_scale = lax.rsqrt(squares[:, 0:1] / (2 * chan * chan) + 1e-06)
    filter_scale = lax.rsqrt(
        squares[:, LANES // 2 : LANES // 2 + 1] / (own * n_ka * chan) + 1e-06
    )
    for s in range(n_dp):
        at = pl.ds(pl.multiple_of(partner(me, s, n_dp) * rows, rows), rows)
        raw_in_t[at, :] = parts[s][:, :chan] * weight_scale
        g_out[at, :] = parts[s][:, chan : 2 * chan] * weight_scale
        filt_t[at, :] = parts[s][:, 2 * chan : 2 * chan + own] * filter_scale
    g_in[...] = raw_in_t[...].T
    g_filt[...] = filt_t[...].T


def body(feats, coords, cell_ids, recip, kvec, w_in, w_out, kfilt, spread, cotan):
    n_ka = lax.axis_size("ka")
    n_dp = lax.axis_size("dp")
    chan = feats.shape[1]
    own = kvec.shape[1]
    kvecs = [kvec] + [lax.ppermute(kvec, "ka", routes(s, n_ka)) for s in range(1, n_ka)]
    kfilts = [kfilt] + [lax.ppermute(kfilt, "ka", routes(s, n_ka)) for s in range(1, n_ka)]
    me = lax.axis_index("dp").astype(jnp.int32).reshape(1)
    numbers = jnp.arange(recip.shape[1], dtype=jnp.int32)[:, None]
    bounds = jnp.stack(
        [
            jnp.sum((cell_ids == numbers).astype(jnp.int32), axis=1),
            jnp.sum((cell_ids < numbers).astype(jnp.int32), axis=1),
        ]
    )
    mixed, feat_grad, pieces, piece = block_call(
        n_ka, n_dp, bounds, me, feats, cotan, coords, cell_ids, recip[0], spread[None], kvecs,
        kfilts, w_in, w_out,
    )
    parts = [lax.ppermute(pieces[s - 1], "dp", routes(s, n_dp)) for s in range(1, n_dp)]
    rows = piece.shape[0]
    summed = pl.pallas_call(
        functools.partial(sum_kernel, chan, own),
        out_shape=jax.ShapeDtypeStruct((rows, 2 * chan + own + LANES), F32),
        name="sum",
    )(piece, *parts)
    shares = [summed] + [lax.ppermute(summed, "dp", routes(s, n_dp)) for s in range(1, n_dp)]
    vmem = pl.BlockSpec(memory_space=pltpu.VMEM)
    grads = pl.pallas_call(
        functools.partial(final_kernel, chan, own, n_ka, n_dp),
        out_shape=(
            jax.ShapeDtypeStruct((chan, chan), F32),
            jax.ShapeDtypeStruct((chan, chan), F32),
            jax.ShapeDtypeStruct((own, chan), F32),
        ),
        in_specs=[pl.BlockSpec(memory_space=pltpu.SMEM)] + [vmem] * n_dp,
        scratch_shapes=[pltpu.VMEM((chan, chan), F32), pltpu.VMEM((chan, own), F32)],
        name="final",
    )(me, *shares)
    return (mixed, feat_grad, *grads)


def solution(mesh):
    placed = (
        P("dp", None),
        P(None, "dp"),
        P("dp", None),
        P("dp", None, None),
        P(None, "ka"),
        P(),
        P(),
        P("ka", None),
        P(),
        P("dp", None),
    )
    return jax.shard_map(
        body,
        mesh=mesh,
        in_specs=placed,
        out_specs=(P("dp", None), P("dp", None), P(), P(), P("ka", None)),
        check_vma=False,
    )
```

profile of v0, /device:TPU:0, one launch (start us, length us, event | category | flops | bytes accessed | tf_op | source)
XLA Modules:
  0.0 90.5 jit_solution(11156776740253004559)
XLA Ops:
  0.6 4.1 %collective-permute-start.1 = (s32[3,128]{1,0:T(4,128)}, s32[3,128]{1,0:T(4,128)S(1)}, u32[]{:S(2)}, u32[]{:S(2)}) collective-permute-start(s32[3,128]{1,0:T(4,128)} %refs_8_.1), channel_id=1, source_target_pairs={{0,2},{1,3},{2,0},{3,1},{4,6},{5,7},{6,4},{7,5},{8,10},{9,11},{10,... | collective-permute-start | bytes 4616 | tf_op jit(solution)/shard_map/ppermute | solution.py:323
  4.8 1.6 %collective-permute-start = (s32[3,128]{1,0:T(4,128)}, s32[3,128]{1,0:T(4,128)S(1)}, u32[]{:S(2)}, u32[]{:S(2)}) collective-permute-start(s32[3,128]{1,0:T(4,128)} %refs_8_.1), channel_id=1, source_target_pairs={{0,1},{1,0},{2,3},{3,2},{4,5},{5,4},{6,7},{7,6},{8,9},{9,8},{10,11... | collective-permute-start | bytes 4616 | tf_op jit(solution)/shard_map/ppermute | solution.py:323
  6.3 0.3 collective-permute-start.4
  6.7 0.2 collective-permute-start.3
  6.9 3.9 %collective-permute-start.5 = (f32[128,256]{1,0:T(8,128)}, f32[128,256]{1,0:T(8,128)S(1)}, u32[]{:S(2)}, u32[]{:S(2)}) collective-permute-start(f32[128,256]{1,0:T(8,128)} %refs_12_.1), channel_id=1, source_target_pairs={{0,3},{1,2},{2,1},{3,0},{4,7},{5,6},{6,5},{7,4},{8,11},{9,10},{10,... | collective-permute-start | bytes 393224 | tf_op jit(solution)/shard_map/ppermute | solution.py:324
  10.7 0.9 convert_reduce_fusion.1
  11.6 0.0 collective-permute-done.1.refs_10_
  11.6 0.0 copy-done.17
  11.6 0.0 copy-start.18
  11.6 0.1 collective-permute-start.2
  11.7 0.5 copy-done.18
  12.2 0.6 pad_add_fusion.refs_0_
  12.8 0.0 collective-permute-done.refs_9_
  12.8 4.9 %collective-permute-done.2.refs_11_ = s32[3,128]{1,0:T(4,128)S(1)} collective-permute-done((s32[3,128]{1,0:T(4,128)S(1)}, s32[3,128]{1,0:T(4,128)S(1)}, u32[]{:S(2)}, u32[]{:S(2)}) %collective-permute-start.2) | collective-permute-done | bytes 1568 | tf_op jit(solution)/shard_map/ppermute | solution.py:323
  17.7 0.3 collective-permute-done.4.refs_14_
  18.0 0.0 collective-permute-done.3.refs_13_
  18.0 0.0 collective-permute-done.5.refs_15_
  18.0 0.0 copy-start.2
  18.1 0.2 copy-done.20
  18.3 0.4 copy-done
  18.7 0.0 copy-done.1
  18.7 0.0 copy-done.2
  18.8 41.8 %block.1 = (bf16[2048,256]{1,0:T(8,128)(2,1)}, bf16[2048,256]{1,0:T(8,128)(2,1)}, bf16[7,32,1024]{2,1,0:T(8,128)(2,1)}, f32[32,1024]{1,0:T(8,128)}) custom-call(s32[2,8]{1,0:T(2,128)} %pad_add_fusion.refs_0_, s32[1]{0:T(128)} %bitcast.3.refs_1_.me_ref, bf16[2048,256]{1,0:T(8,128)(2,1)} %refs_2_.1, bf16[2048,256]{1,0:T(8,128)(2,1)} %refs_3_.1, ...), custom_call_target="tpu_custom_call" | custom-call | tf_op jit(solution)/shard_map/block/pallas_call | solution.py:247
  60.6 1.1 %slice_bitcast_fusion = (bf16[32,1024]{1,0:T(8,128)(2,1)S(1)}, bf16[32,1024]{1,0:T(8,128)(2,1)S(1)}, bf16[32,1024]{1,0:T(8,128)(2,1)S(1)}, bf16[32,1024]{1,0:T(8...) fusion(bf16[7,32,1024]{2,1,0:T(8,128)(2,1)} %get-tuple-element.15), kind=kLoop, calls=%fused_computation | loop fusion | bytes 917504 | tf_op jit(solution)/shard_map/squeeze | solution.py:337
  61.6 0.1 collective-permute-start.12
  61.7 2.5 %collective-permute-start.11 = (bf16[32,1024]{1,0:T(8,128)(2,1)S(1)}, bf16[32,1024]{1,0:T(8,128)(2,1)S(1)}, u32[]{:S(2)}, u32[]{:S(2)}) collective-permute-start(bf16[32,1024]{1,0:T(8,128)(2,1)S(1)} %get-tuple-element.22), channel_id=1, source_target_pairs={{0,24},{4,28},{8,16},{12,20},{16,8},{20,12},{24,0},{28,4},{1,25},{... | collective-permute-start | bytes 196616 | tf_op jit(solution)/shard_map/ppermute | solution.py:337
  64.2 1.4 %collective-permute-start.10 = (bf16[32,1024]{1,0:T(8,128)(2,1)S(1)}, bf16[32,1024]{1,0:T(8,128)(2,1)S(1)}, u32[]{:S(2)}, u32[]{:S(2)}) collective-permute-start(bf16[32,1024]{1,0:T(8,128)(2,1)S(1)} %get-tuple-element.23), channel_id=1, source_target_pairs={{0,20},{4,16},{8,28},{12,24},{16,4},{20,0},{24,12},{28,8},{1,21},{... | collective-permute-start | bytes 196616 | tf_op jit(solution)/shard_map/ppermute | solution.py:337
  65.6 0.5 collective-permute-start.9
  66.1 0.7 collective-permute-start.8
  66.7 0.2 collective-permute-done.12.refs_6_
  66.9 0.7 collective-permute-start.7
  67.7 0.1 collective-permute-done.11.refs_5_
  67.8 0.6 collective-permute-start.6
  68.3 1.4 %collective-permute-done.10.refs_4_ = bf16[32,1024]{1,0:T(8,128)(2,1)S(1)} collective-permute-done((bf16[32,1024]{1,0:T(8,128)(2,1)S(1)}, bf16[32,1024]{1,0:T(8,128)(2,1)S(1)}, u32[]{:S(2)}, u32[]{:S(2)}) %collective-permute-start.10) | collective-permute-done | bytes 65568 | tf_op jit(solution)/shard_map/ppermute | solution.py:337
  69.8 1.4 %collective-permute-done.9.refs_3_ = bf16[32,1024]{1,0:T(8,128)(2,1)S(1)} collective-permute-done((bf16[32,1024]{1,0:T(8,128)(2,1)S(1)}, bf16[32,1024]{1,0:T(8,128)(2,1)S(1)}, u32[]{:S(2)}, u32[]{:S(2)}) %collective-permute-start.9) | collective-permute-done | bytes 65568 | tf_op jit(solution)/shard_map/ppermute | solution.py:337
  71.2 0.0 collective-permute-done.8.refs_2_
  71.2 0.7 collective-permute-done.7.refs_1_
  71.9 0.0 collective-permute-done.6.refs_0_
  71.9 0.0 copy-done.11
  71.9 0.0 copy-done.12
  71.9 0.0 copy-done.13
  71.9 0.0 copy-done.14
  71.9 0.6 copy-done.15
  72.5 0.0 copy-done.16
  72.5 1.9 %sum.1.refs_0_ = f32[32,768]{1,0:T(8,128)} custom-call(f32[32,1024]{1,0:T(8,128)} %get-tuple-element.14.piece, bf16[32,1024]{1,0:T(8,128)(2,1)} %copy-done.16, bf16[32,1024]{1,0:T(8,128)(2,1)} %copy-done.15, bf16[32,1024]{1,0:T(8,128)(2,1)} %copy-done.14, bf16[32,1024]{1,0:T(8,128)(2,1)} %copy-done.13, bf16[32,1024]{1,0:T(8,128)(2,1)} %copy-done.12, ...), custom_call_target="tpu_custom_call" | custom-call | tf_op jit(solution)/shard_map/sum/pallas_call | solution.py:339
  74.4 1.2 %collective-permute-start.19 = (f32[32,768]{1,0:T(8,128)}, f32[32,768]{1,0:T(8,128)S(1)}, u32[]{:S(2)}, u32[]{:S(2)}) collective-permute-start(f32[32,768]{1,0:T(8,128)} %sum.1.refs_0_), channel_id=1, source_target_pairs={{0,28},{4,24},{8,20},{12,16},{16,12},{20,8},{24,4},{28,0},{1,29},{... | collective-permute-start | bytes 294920 | tf_op jit(solution)/shard_map/ppermute | solution.py:344
  75.6 1.3 %collective-permute-start.18 = (f32[32,768]{1,0:T(8,128)}, f32[32,768]{1,0:T(8,128)S(1)}, u32[]{:S(2)}, u32[]{:S(2)}) collective-permute-start(f32[32,768]{1,0:T(8,128)} %sum.1.refs_0_), channel_id=1, source_target_pairs={{0,24},{4,28},{8,16},{12,20},{16,8},{20,12},{24,0},{28,4},{1,25},{... | collective-permute-start | bytes 294920 | tf_op jit(solution)/shard_map/ppermute | solution.py:344
  76.9 1.3 %collective-permute-start.17 = (f32[32,768]{1,0:T(8,128)}, f32[32,768]{1,0:T(8,128)S(1)}, u32[]{:S(2)}, u32[]{:S(2)}) collective-permute-start(f32[32,768]{1,0:T(8,128)} %sum.1.refs_0_), channel_id=1, source_target_pairs={{0,20},{4,16},{8,28},{12,24},{16,4},{20,0},{24,12},{28,8},{1,21},{... | collective-permute-start | bytes 294920 | tf_op jit(solution)/shard_map/ppermute | solution.py:344
  78.3 0.5 collective-permute-start.16
  78.8 0.4 collective-permute-start.15
  79.2 1.3 %collective-permute-done.19.refs_7_ = f32[32,768]{1,0:T(8,128)S(1)} collective-permute-done((f32[32,768]{1,0:T(8,128)}, f32[32,768]{1,0:T(8,128)S(1)}, u32[]{:S(2)}, u32[]{:S(2)}) %collective-permute-start.19) | collective-permute-done | bytes 98336 | tf_op jit(solution)/shard_map/ppermute | solution.py:344
  80.5 1.1 %collective-permute-start.14 = (f32[32,768]{1,0:T(8,128)}, f32[32,768]{1,0:T(8,128)S(1)}, u32[]{:S(2)}, u32[]{:S(2)}) collective-permute-start(f32[32,768]{1,0:T(8,128)} %sum.1.refs_0_), channel_id=1, source_target_pairs={{0,8},{4,12},{8,0},{12,4},{16,24},{20,28},{24,16},{28,20},{1,9},{5... | collective-permute-start | bytes 294920 | tf_op jit(solution)/shard_map/ppermute | solution.py:344
  81.6 1.2 %collective-permute-done.18.refs_6_ = f32[32,768]{1,0:T(8,128)S(1)} collective-permute-done((f32[32,768]{1,0:T(8,128)}, f32[32,768]{1,0:T(8,128)S(1)}, u32[]{:S(2)}, u32[]{:S(2)}) %collective-permute-start.18) | collective-permute-done | bytes 98336 | tf_op jit(solution)/shard_map/ppermute | solution.py:344
  82.8 0.0 collective-permute-start.13
  82.8 2.0 %collective-permute-done.17.refs_5_ = f32[32,768]{1,0:T(8,128)S(1)} collective-permute-done((f32[32,768]{1,0:T(8,128)}, f32[32,768]{1,0:T(8,128)S(1)}, u32[]{:S(2)}, u32[]{:S(2)}) %collective-permute-start.17) | collective-permute-done | bytes 98336 | tf_op jit(solution)/shard_map/ppermute | solution.py:344
  84.8 2.1 %collective-permute-done.16.refs_4_ = f32[32,768]{1,0:T(8,128)S(1)} collective-permute-done((f32[32,768]{1,0:T(8,128)}, f32[32,768]{1,0:T(8,128)S(1)}, u32[]{:S(2)}, u32[]{:S(2)}) %collective-permute-start.16) | collective-permute-done | bytes 98336 | tf_op jit(solution)/shard_map/ppermute | solution.py:344
  86.9 0.0 collective-permute-done.15.refs_3_
  87.0 0.1 collective-permute-done.14.refs_2_
  87.0 0.0 collective-permute-done.13.refs_1_
  87.0 0.5 copy-done.6
  87.6 0.0 copy-done.7
  87.6 0.0 copy-done.8
  87.7 0.6 copy-done.9
  88.3 2.2 %final.1 = (f32[256,256]{1,0:T(8,128)}, f32[256,256]{1,0:T(8,128)}, f32[128,256]{1,0:T(8,128)}) custom-call(s32[1]{0:T(128)} %bitcast.3.refs_1_.me_ref, f32[32,768]{1,0:T(8,128)} %sum.1.refs_0_, f32[32,768]{1,0:T(8,128)} %copy-done.9, f32[32,768]{1,0:T(8,128)} %copy-done.8, f32[32,768]{1,0:T(8,128)} %copy-done.7, f32[32,768]{1,0:T(8,128)} %copy-done.6, ...), custom_call_target="tpu_custom_call" | custom-call | tf_op jit(solution)/shard_map/final/pallas_call | solution.py:346
  (24 shorter events, 0.0 us)
Async XLA Ops:
  0.6 11.0 %collective-permute-start.1 = (s32[3,128]{1,0:T(4,128)}, s32[3,128]{1,0:T(4,128)S(1)}, u32[]{:S(2)}, u32[]{:S(2)}) collective-permute-start(s32[3,128]{1,0:T(4,128)} %refs_8_.1), channel_id=1, source_target_pairs={{0,2},{1,3},{2,0},{3,1},{4,6},{5,7},{6,4},{7,5},{8,10},{9,11},{10,... | collective-permute-start | bytes 4616 | tf_op jit(solution)/shard_map/ppermute | solution.py:323
  4.8 8.1 %collective-permute-start = (s32[3,128]{1,0:T(4,128)}, s32[3,128]{1,0:T(4,128)S(1)}, u32[]{:S(2)}, u32[]{:S(2)}) collective-permute-start(s32[3,128]{1,0:T(4,128)} %refs_8_.1), channel_id=1, source_target_pairs={{0,1},{1,0},{2,3},{3,2},{4,5},{5,4},{6,7},{7,6},{8,9},{9,8},{10,11... | collective-permute-start | bytes 4616 | tf_op jit(solution)/shard_map/ppermute | solution.py:323
  6.3 11.7 %collective-permute-start.4 = (f32[128,256]{1,0:T(8,128)}, f32[128,256]{1,0:T(8,128)S(1)}, u32[]{:S(2)}, u32[]{:S(2)}) collective-permute-start(f32[128,256]{1,0:T(8,128)} %refs_12_.1), channel_id=1, source_target_pairs={{0,2},{1,3},{2,0},{3,1},{4,6},{5,7},{6,4},{7,5},{8,10},{9,11},{10,... | collective-permute-start | bytes 393224 | tf_op jit(solution)/shard_map/ppermute | solution.py:324
  6.7 11.3 %collective-permute-start.3 = (f32[128,256]{1,0:T(8,128)}, f32[128,256]{1,0:T(8,128)S(1)}, u32[]{:S(2)}, u32[]{:S(2)}) collective-permute-start(f32[128,256]{1,0:T(8,128)} %refs_12_.1), channel_id=1, source_target_pairs={{0,1},{1,0},{2,3},{3,2},{4,5},{5,4},{6,7},{7,6},{8,9},{9,8},{10,11... | collective-permute-start | bytes 393224 | tf_op jit(solution)/shard_map/ppermute | solution.py:324
  6.9 11.2 %collective-permute-start.5 = (f32[128,256]{1,0:T(8,128)}, f32[128,256]{1,0:T(8,128)S(1)}, u32[]{:S(2)}, u32[]{:S(2)}) collective-permute-start(f32[128,256]{1,0:T(8,128)} %refs_12_.1), channel_id=1, source_target_pairs={{0,3},{1,2},{2,1},{3,0},{4,7},{5,6},{6,5},{7,4},{8,11},{9,10},{10,... | collective-permute-start | bytes 393224 | tf_op jit(solution)/shard_map/ppermute | solution.py:324
  10.7 0.9 copy-start.17
  11.6 0.6 copy-start.18
  11.6 6.0 %collective-permute-start.2 = (s32[3,128]{1,0:T(4,128)S(1)}, s32[3,128]{1,0:T(4,128)S(1)}, u32[]{:S(2)}, u32[]{:S(2)}) collective-permute-start(s32[3,128]{1,0:T(4,128)S(1)} %copy-done.17), channel_id=1, source_target_pairs={{0,3},{1,2},{2,1},{3,0},{4,7},{5,6},{6,5},{7,4},{8,11},{9,10},{10,... | collective-permute-start | bytes 4616 | tf_op jit(solution)/shard_map/ppermute | solution.py:323
  12.8 5.2 %copy-start.19 = (s32[3,128]{1,0:T(4,128)}, s32[3,128]{1,0:T(4,128)S(1)}, u32[]{:S(2)}) copy-start(s32[3,128]{1,0:T(4,128)S(1)} %collective-permute-done.refs_9_) | copy-start | bytes 4612
  17.7 0.6 copy-start.20
  18.0 0.7 copy-start
  18.0 0.7 copy-start.1
  18.0 0.7 copy-start.2
  61.6 5.3 %collective-permute-start.12 = (bf16[32,1024]{1,0:T(8,128)(2,1)S(1)}, bf16[32,1024]{1,0:T(8,128)(2,1)S(1)}, u32[]{:S(2)}, u32[]{:S(2)}) collective-permute-start(bf16[32,1024]{1,0:T(8,128)(2,1)S(1)} %get-tuple-element.21), channel_id=1, source_target_pairs={{0,28},{4,24},{8,20},{12,16},{16,12},{20,8},{24,4},{28,0},{1,29},{... | collective-permute-start | bytes 196616 | tf_op jit(solution)/shard_map/ppermute | solution.py:337
  61.7 6.0 %collective-permute-start.11 = (bf16[32,1024]{1,0:T(8,128)(2,1)S(1)}, bf16[32,1024]{1,0:T(8,128)(2,1)S(1)}, u32[]{:S(2)}, u32[]{:S(2)}) collective-permute-start(bf16[32,1024]{1,0:T(8,128)(2,1)S(1)} %get-tuple-element.22), channel_id=1, source_target_pairs={{0,24},{4,28},{8,16},{12,20},{16,8},{20,12},{24,0},{28,4},{1,25},{... | collective-permute-start | bytes 196616 | tf_op jit(solution)/shard_map/ppermute | solution.py:337
  64.2 5.6 %collective-permute-start.10 = (bf16[32,1024]{1,0:T(8,128)(2,1)S(1)}, bf16[32,1024]{1,0:T(8,128)(2,1)S(1)}, u32[]{:S(2)}, u32[]{:S(2)}) collective-permute-start(bf16[32,1024]{1,0:T(8,128)(2,1)S(1)} %get-tuple-element.23), channel_id=1, source_target_pairs={{0,20},{4,16},{8,28},{12,24},{16,4},{20,0},{24,12},{28,8},{1,21},{... | collective-permute-start | bytes 196616 | tf_op jit(solution)/shard_map/ppermute | solution.py:337
  65.6 5.7 %collective-permute-start.9 = (bf16[32,1024]{1,0:T(8,128)(2,1)S(1)}, bf16[32,1024]{1,0:T(8,128)(2,1)S(1)}, u32[]{:S(2)}, u32[]{:S(2)}) collective-permute-start(bf16[32,1024]{1,0:T(8,128)(2,1)S(1)} %get-tuple-element.24), channel_id=1, source_target_pairs={{0,16},{4,20},{8,24},{12,28},{16,0},{20,4},{24,8},{28,12},{1,17},{... | collective-permute-start | bytes 196616 | tf_op jit(solution)/shard_map/ppermute | solution.py:337
  66.1 5.1 %collective-permute-start.8 = (bf16[32,1024]{1,0:T(8,128)(2,1)S(1)}, bf16[32,1024]{1,0:T(8,128)(2,1)S(1)}, u32[]{:S(2)}, u32[]{:S(2)}) collective-permute-start(bf16[32,1024]{1,0:T(8,128)(2,1)S(1)} %get-tuple-element.25), channel_id=1, source_target_pairs={{0,12},{4,8},{8,4},{12,0},{16,28},{20,24},{24,20},{28,16},{1,13},{... | collective-permute-start | bytes 196616 | tf_op jit(solution)/shard_map/ppermute | solution.py:337
  66.9 5.0 %copy-start.10 = (bf16[32,1024]{1,0:T(8,128)(2,1)}, bf16[32,1024]{1,0:T(8,128)(2,1)S(1)}, u32[]{:S(2)}) copy-start(bf16[32,1024]{1,0:T(8,128)(2,1)S(1)} %collective-permute-done.12.refs_6_) | copy-start | bytes 196612
  66.9 4.9 %collective-permute-start.7 = (bf16[32,1024]{1,0:T(8,128)(2,1)S(1)}, bf16[32,1024]{1,0:T(8,128)(2,1)S(1)}, u32[]{:S(2)}, u32[]{:S(2)}) collective-permute-start(bf16[32,1024]{1,0:T(8,128)(2,1)S(1)} %get-tuple-element.26), channel_id=1, source_target_pairs={{0,8},{4,12},{8,0},{12,4},{16,24},{20,28},{24,16},{28,20},{1,9},{5... | collective-permute-start | bytes 196616 | tf_op jit(solution)/shard_map/ppermute | solution.py:337
  67.7 4.2 %copy-start.11 = (bf16[32,1024]{1,0:T(8,128)(2,1)}, bf16[32,1024]{1,0:T(8,128)(2,1)S(1)}, u32[]{:S(2)}) copy-start(bf16[32,1024]{1,0:T(8,128)(2,1)S(1)} %collective-permute-done.11.refs_5_) | copy-start | bytes 196612
  67.8 4.1 %collective-permute-start.6 = (bf16[32,1024]{1,0:T(8,128)(2,1)S(1)}, bf16[32,1024]{1,0:T(8,128)(2,1)S(1)}, u32[]{:S(2)}, u32[]{:S(2)}) collective-permute-start(bf16[32,1024]{1,0:T(8,128)(2,1)S(1)} %get-tuple-element.27), channel_id=1, source_target_pairs={{0,4},{4,0},{8,12},{12,8},{16,20},{20,16},{24,28},{28,24},{1,5},{5... | collective-permute-start | bytes 196616 | tf_op jit(solution)/shard_map/ppermute | solution.py:337
  69.8 2.2 %copy-start.12 = (bf16[32,1024]{1,0:T(8,128)(2,1)}, bf16[32,1024]{1,0:T(8,128)(2,1)S(1)}, u32[]{:S(2)}) copy-start(bf16[32,1024]{1,0:T(8,128)(2,1)S(1)} %collective-permute-done.10.refs_4_) | copy-start | bytes 196612
  71.2 0.7 copy-start.13
  71.2 0.7 copy-start.14
  71.9 0.6 copy-start.15
  71.9 0.6 copy-start.16
  74.4 6.1 %collective-permute-start.19 = (f32[32,768]{1,0:T(8,128)}, f32[32,768]{1,0:T(8,128)S(1)}, u32[]{:S(2)}, u32[]{:S(2)}) collective-permute-start(f32[32,768]{1,0:T(8,128)} %sum.1.refs_0_), channel_id=1, source_target_pairs={{0,28},{4,24},{8,20},{12,16},{16,12},{20,8},{24,4},{28,0},{1,29},{... | collective-permute-start | bytes 294920 | tf_op jit(solution)/shard_map/ppermute | solution.py:344
  75.6 7.2 %collective-permute-start.18 = (f32[32,768]{1,0:T(8,128)}, f32[32,768]{1,0:T(8,128)S(1)}, u32[]{:S(2)}, u32[]{:S(2)}) collective-permute-start(f32[32,768]{1,0:T(8,128)} %sum.1.refs_0_), channel_id=1, source_target_pairs={{0,24},{4,28},{8,16},{12,20},{16,8},{20,12},{24,0},{28,4},{1,25},{... | collective-permute-start | bytes 294920 | tf_op jit(solution)/shard_map/ppermute | solution.py:344
  76.9 7.9 %collective-permute-start.17 = (f32[32,768]{1,0:T(8,128)}, f32[32,768]{1,0:T(8,128)S(1)}, u32[]{:S(2)}, u32[]{:S(2)}) collective-permute-start(f32[32,768]{1,0:T(8,128)} %sum.1.refs_0_), channel_id=1, source_target_pairs={{0,20},{4,16},{8,28},{12,24},{16,4},{20,0},{24,12},{28,8},{1,21},{... | collective-permute-start | bytes 294920 | tf_op jit(solution)/shard_map/ppermute | solution.py:344
  78.3 8.7 %collective-permute-start.16 = (f32[32,768]{1,0:T(8,128)}, f32[32,768]{1,0:T(8,128)S(1)}, u32[]{:S(2)}, u32[]{:S(2)}) collective-permute-start(f32[32,768]{1,0:T(8,128)} %sum.1.refs_0_), channel_id=1, source_target_pairs={{0,16},{4,20},{8,24},{12,28},{16,0},{20,4},{24,8},{28,12},{1,17},{... | collective-permute-start | bytes 294920 | tf_op jit(solution)/shard_map/ppermute | solution.py:344
  78.8 8.1 %collective-permute-start.15 = (f32[32,768]{1,0:T(8,128)}, f32[32,768]{1,0:T(8,128)S(1)}, u32[]{:S(2)}, u32[]{:S(2)}) collective-permute-start(f32[32,768]{1,0:T(8,128)} %sum.1.refs_0_), channel_id=1, source_target_pairs={{0,12},{4,8},{8,4},{12,0},{16,28},{20,24},{24,20},{28,16},{1,13},{... | collective-permute-start | bytes 294920 | tf_op jit(solution)/shard_map/ppermute | solution.py:344
  80.5 6.5 %copy-start.3 = (f32[32,768]{1,0:T(8,128)}, f32[32,768]{1,0:T(8,128)S(1)}, u32[]{:S(2)}) copy-start(f32[32,768]{1,0:T(8,128)S(1)} %collective-permute-done.19.refs_7_) | copy-start | bytes 294916
  80.5 6.5 %collective-permute-start.14 = (f32[32,768]{1,0:T(8,128)}, f32[32,768]{1,0:T(8,128)S(1)}, u32[]{:S(2)}, u32[]{:S(2)}) collective-permute-start(f32[32,768]{1,0:T(8,128)} %sum.1.refs_0_), channel_id=1, source_target_pairs={{0,8},{4,12},{8,0},{12,4},{16,24},{20,28},{24,16},{28,20},{1,9},{5... | collective-permute-start | bytes 294920 | tf_op jit(solution)/shard_map/ppermute | solution.py:344
  82.8 4.2 %copy-start.4 = (f32[32,768]{1,0:T(8,128)}, f32[32,768]{1,0:T(8,128)S(1)}, u32[]{:S(2)}) copy-start(f32[32,768]{1,0:T(8,128)S(1)} %collective-permute-done.18.refs_6_) | copy-start | bytes 294916
  82.8 4.2 %collective-permute-start.13 = (f32[32,768]{1,0:T(8,128)}, f32[32,768]{1,0:T(8,128)S(1)}, u32[]{:S(2)}, u32[]{:S(2)}) collective-permute-start(f32[32,768]{1,0:T(8,128)} %sum.1.refs_0_), channel_id=1, source_target_pairs={{0,4},{4,0},{8,12},{12,8},{16,20},{20,16},{24,28},{28,24},{1,5},{5... | collective-permute-start | bytes 294920 | tf_op jit(solution)/shard_map/ppermute | solution.py:344
  84.8 2.2 %copy-start.5 = (f32[32,768]{1,0:T(8,128)}, f32[32,768]{1,0:T(8,128)S(1)}, u32[]{:S(2)}) copy-start(f32[32,768]{1,0:T(8,128)S(1)} %collective-permute-done.17.refs_5_) | copy-start | bytes 294916
  86.9 0.6 copy-start.6
  87.0 0.7 copy-start.7
  87.0 0.6 copy-start.8
  87.7 0.6 copy-start.9
where the time goes:
time: 91.1 us; the launch traced here: 90.5 us
  Pallas kernels  45.9 us (50%)
  starting transfers between devices  22.5 us (25%)
  waiting for transfers between devices  15.7 us (17%)
  local copies, waits for them, and re-layouts  4.17 us (5%)
  other arithmetic  1.47 us (2%)
    pallas_call x1, Pallas kernels, block_call(): pl.pallas_call(functools.partial(block_kernel, n_ka, n_dp), out_shape=(ja...  41.8 us
    ppermute x7, waiting for transfers between devices, body(): lax.ppermute(summed, 'dp', routes(s, n_dp))  6.69 us
    ppermute x7, starting transfers between devices, body(): lax.ppermute(pieces[s - 1], 'dp', routes(s, n_dp))  6.4 us
    ppermute x7, starting transfers between devices, body(): lax.ppermute(summed, 'dp', routes(s, n_dp))  5.89 us
    ppermute x3, starting transfers between devices, body(): lax.ppermute(kvec, 'ka', routes(s, n_ka))  5.78 us
    ppermute x3, waiting for transfers between devices, body(): lax.ppermute(kvec, 'ka', routes(s, n_ka))  4.86 us
    ppermute x3, starting transfers between devices, body(): lax.ppermute(kfilt, 'ka', routes(s, n_ka))  4.39 us
    ppermute x7, waiting for transfers between devices, body(): lax.ppermute(pieces[s - 1], 'dp', routes(s, n_dp))  3.84 us
  transfers between devices with their start and end apart: 20, of which 12 were waited for; matrix products, arithmetic and copies ran while one was open for 2% of the time, Pallas kernels for 0%

commit v1 on v0

v1 whole, which is shorter than its diff:
```python
import functools

import jax
import jax.numpy as jnp
from jax import lax
from jax.experimental import pallas as pl
from jax.experimental.pallas import tpu as pltpu
from jax.sharding import PartitionSpec as P

F32 = jnp.float32
BF16 = jnp.bfloat16
LANES = 128
TILE = 256
MOST = 1024
LIMIT = 24 << 20
SMALL = 6 << 20
FLOPS_PER_MICRO = 1 << 30
LOG2_E = 1.4426950408889634
COS_TERMS = (
    0.9999999890590228,
    -19.73920449945383,
    64.93911745989081,
    -85.45013953079767,
    60.167630950263465,
    -25.967599245923743,
    6.52865815775625,
)
SIN_TERMS = (
    6.283184916495428,
    -41.34158923268831,
    81.59994332977429,
    -76.61447253115396,
    41.34288235413569,
    -12.471243534350362,
)
ROUNDER = 12582912.0


def mm(lhs, rhs, lhs_dim=1, rhs_dim=0):
    return lax.dot_general(
        lhs, rhs, (((lhs_dim,), (rhs_dim,)), ((), ())), preferred_element_type=F32
    )


def horner(terms, square):
    value = terms[-1] * square + terms[-2]
    for term in terms[-3::-1]:
        value = value * square + term
    return value


def routes(step, count):
    if count & (count - 1) == 0:
        return [(i, i ^ step) for i in range(count)]
    return [(i, (i + step) % count) for i in range(count)]


def tile_of(size, most):
    tile = most
    while size % tile:
        tile //= 2
    return tile


def column_to_lanes(row):
    return jnp.broadcast_to(row, (8, row.shape[1])).T


def span_of(bounds, cell):
    first = bounds[1, cell]
    start = lax.div(first, LANES) * LANES
    count = bounds[0, cell]
    steps = lax.div(first - start + count + (TILE - 1), TILE)
    return pl.multiple_of(start, LANES), steps, count


def most_steps(atoms):
    return -(-(min(MOST, atoms) + LANES - 1) // TILE)


def by_steps(steps, most, action):
    for n in range(1, most + 1):
        pl.when(steps == n)(functools.partial(action, n))


def gather_cell(cell, start, steps, most, ids, source, waves, store):
    def action(n):
        at = pl.ds(start, n * TILE)
        member = (ids[:, at] == cell).astype(F32).astype(BF16)
        store(mm(source[:, at] * member, waves[:, at], 1, 1))

    by_steps(steps, most, action)


def spread_cell(cell, start, steps, most, ids, weights, waves, out):
    def action(n):
        for t in range(n):
            at = pl.ds(pl.multiple_of(start + t * TILE, LANES), TILE)
            value = mm(weights[...], waves[:, at])
            out[:, at] = jnp.where(ids[:, at] == cell, value, out[:, at])

    by_steps(steps, most, action)


def inverse_count(count):
    return 1.0 / jnp.full((1, 1), count, jnp.int32).astype(F32)


def shape_of(cell, quad, width_cols):
    exponent = quad[pl.ds(cell, 1), :] * width_cols[:, 0:1]
    return jnp.exp2(exponent)


def waves_kernel(n_ka, *refs):
    bounds, feats, coords, ids_in, recip, w_in = refs[:6]
    kvecs = refs[6 : 6 + n_ka]
    waves, factors, quad, ids, kcols, proj_t = refs[6 + n_ka :]
    atoms, chan = feats.shape
    own = kvecs[0].shape[1]
    k_all = own * n_ka
    cells = recip.shape[0]

    rows = jnp.concatenate([k[...] for k in kvecs], axis=1).astype(F32)
    rows = jnp.concatenate([rows, jnp.zeros((5, k_all), F32)], axis=0)
    kcols[...] = rows.T
    squared = jnp.zeros((cells, k_all), F32)
    for r in range(3):
        part = recip[:, 3 * r : 3 * r + 1] * rows[0:1, :]
        part = part + recip[:, 3 * r + 1 : 3 * r + 2] * rows[1:2, :]
        part = part + recip[:, 3 * r + 2 : 3 * r + 3] * rows[2:3, :]
        squared = squared + part * part
    quad[...] = squared
    ids[:, :atoms] = ids_in[...]
    ids[:, atoms:] = jnp.full((1, LANES), -1, jnp.int32)
    waves[:, atoms:] = jnp.zeros((2 * k_all, LANES), BF16)
    proj_t[:, atoms:] = jnp.zeros((chan, LANES), BF16)

    wide = tile_of(atoms, 1024)

    def phase_rows(i, carry):
        row = pl.multiple_of(i * 16, 16)
        kv = kcols[pl.ds(row, 16), :]
        for start in range(0, atoms, wide):
            frac = coords[:, start : start + wide]
            turns = kv[:, 0:1] * frac[0:1, :] + kv[:, 1:2] * frac[1:2, :]
            turns = turns + kv[:, 2:3] * frac[2:3, :]
            turns = turns - ((turns + ROUNDER) - ROUNDER)
            square = turns * turns
            waves[pl.ds(row, 16), start : start + wide] = horner(COS_TERMS, square).astype(BF16)
            waves[pl.ds(pl.multiple_of(k_all + row, 16), 16), start : start + wide] = (
                horner(SIN_TERMS, square) * turns
            ).astype(BF16)
        return carry

    lax.fori_loop(0, k_all // 16, phase_rows, 0)

    def project(t, carry):
        at = pl.ds(pl.multiple_of(t * TILE, TILE), TILE)
        proj_t[:, at] = mm(w_in[...], feats[at, :], 0, 1).astype(BF16)
        return carry

    lax.fori_loop(0, atoms // TILE, project, 0)

    def cell_step(cell, carry):
        start, steps, _ = span_of(bounds, cell)

        def store(value):
            factors[cell] = value

        gather_cell(cell, start, steps, most_steps(atoms), ids, proj_t, waves, store)
        return carry

    lax.fori_loop(0, cells, cell_step, 0)


def message_kernel(n_ka, *refs):
    bounds, ids, quad, waves, factors, spread, cotan, w_out = refs[:8]
    kfilts = refs[8 : 8 + n_ka]
    act_t, mgrad_t, raw_out, raw_half, filt_t, width_cols, weights, mess_t = refs[8 + n_ka :]
    atoms, chan = cotan.shape
    own = kfilts[0].shape[0]
    k_all = own * n_ka
    cells = quad.shape[0]
    for j in range(n_ka):
        filt_t[:, j * own : (j + 1) * own] = kfilts[j][...].T
    width_cols[...] = column_to_lanes(spread[...] * (-LOG2_E))

    def cell_step(cell, carry):
        start, steps, count = span_of(bounds, cell)
        filt = filt_t[...] * (shape_of(cell, quad, width_cols) * inverse_count(count))
        weights[:, :k_all] = (filt * factors[cell, :, :k_all]).astype(BF16)
        weights[:, k_all:] = (filt * factors[cell, :, k_all:]).astype(BF16)
        spread_cell(cell, start, steps, most_steps(atoms), ids, weights, waves, mess_t)
        return carry

    lax.fori_loop(0, cells, cell_step, 0)

    mgrad_t[:, atoms:] = jnp.zeros((chan, LANES), BF16)
    raw_out[...] = jnp.zeros_like(raw_out)

    def middle(t, carry):
        at = pl.ds(pl.multiple_of(t * TILE, TILE), TILE)
        message = mess_t[:, at]
        sigma = jax.nn.sigmoid(message)
        activated = (message * sigma).astype(BF16)
        act_t[:, at] = activated
        cot = cotan[at, :]
        act_grad = mm(w_out[...], cot, 1, 1)
        mgrad_t[:, at] = (act_grad * (sigma * (1.0 + message * (1.0 - sigma)))).astype(BF16)
        raw_out[...] += mm(activated, cot)
        return carry

    lax.fori_loop(0, atoms // TILE, middle, 0)
    raw_half[...] = raw_out[...].astype(BF16)


def adjoint_kernel(n_ka, *refs):
    bounds, ids, quad, waves, factors, mgrad_t, spread = refs[:7]
    kfilts = refs[7 : 7 + n_ka]
    weights, filter_grad, filter_half, filt_t, width_cols, total, grad_t = refs[7 + n_ka :]
    chan = mgrad_t.shape[0]
    atoms = mgrad_t.shape[1] - LANES
    own = kfilts[0].shape[0]
    k_all = own * n_ka
    cells = quad.shape[0]
    for j in range(n_ka):
        filt_t[:, j * own : (j + 1) * own] = kfilts[j][...].T
    width_cols[...] = column_to_lanes(spread[...] * (-LOG2_E))
    grad_t[...] = jnp.zeros_like(grad_t)

    def cell_step(cell, carry):
        start, steps, count = span_of(bounds, cell)

        def store(value):
            total[...] = value

        gather_cell(cell, start, steps, most_steps(atoms), ids, mgrad_t, waves, store)
        scaled = shape_of(cell, quad, width_cols) * inverse_count(count)
        filt = filt_t[...] * scaled
        weights[cell, :, :k_all] = (filt * total[:, :k_all]).astype(BF16)
        weights[cell, :, k_all:] = (filt * total[:, k_all:]).astype(BF16)
        grad_t[...] += scaled[:, :own] * (
            factors[cell, :, :own] * total[:, :own]
            + factors[cell, :, k_all : k_all + own] * total[:, k_all : k_all + own]
        )
        return carry

    lax.fori_loop(0, cells, cell_step, 0)
    result = grad_t[...].T
    filter_grad[...] = result
    filter_half[...] = result.astype(BF16)


def update_kernel(bounds, ids, waves, weights, feats, update_t, raw_in_t, total_t):
    cells, chan, _ = weights.shape
    atoms = feats.shape[0]

    def cell_step(cell, carry):
        start, steps, _ = span_of(bounds, cell)
        spread_cell(
            cell, start, steps, most_steps(atoms), ids, weights.at[cell], waves, total_t
        )
        return carry

    lax.fori_loop(0, cells, cell_step, 0)
    raw_in_t[...] = jnp.zeros_like(raw_in_t)

    def last(t, carry):
        at = pl.ds(pl.multiple_of(t * TILE, TILE), TILE)
        update = total_t[:, at].astype(BF16)
        update_t[:, at] = update
        raw_in_t[...] += mm(update, feats[at, :])
        return carry

    lax.fori_loop(0, atoms // TILE, last, 0)


def residual_kernel(transposed, base, values_t, weight, out):
    rows = base.shape[0]

    def step(t, carry):
        at = pl.ds(pl.multiple_of(t * TILE, TILE), TILE)
        value = mm(values_t[:, at].T, weight[...], 1, 1 if transposed else 0)
        out[at, :] = (base[at, :].astype(F32) + value).astype(BF16)
        return carry

    lax.fori_loop(0, rows // TILE, step, 0)


def chip_kernel(raw_in_t, other_in, out_sum, out_near, filt_sum, filt_near, in_sum, in_half, w_sum, f_sum, f_squares):
    value = raw_in_t[...] + other_in[...]
    in_sum[...] = value
    in_half[...] = value.astype(BF16)
    w_sum[...] = out_sum[...] + out_near[...]
    filt = filt_sum[...] + filt_near[...]
    f_sum[...] = filt
    f_squares[...] = jnp.broadcast_to(
        jnp.sum(jnp.sum(filt * filt, axis=0, keepdims=True), axis=1, keepdims=True),
        f_squares.shape,
    )


def total_of(first, others):
    value = first[...]
    for other in others:
        value = value + other[...].astype(F32)
    return value


def add_kernel(*refs):
    refs[-1][...] = total_of(refs[0], refs[1:-1])


def final_kernel(n_chip, n_ka, *refs):
    in_parts = refs[:n_chip]
    raw_out, filt = refs[n_chip : n_chip + 2]
    squares = refs[n_chip + 2 : n_chip + 2 + n_ka]
    g_in, g_out, g_filt = refs[n_chip + 2 + n_ka :]
    raw_in = total_of(in_parts[0], in_parts[1:])
    out = raw_out[...]
    both = raw_in * raw_in + out * out
    weight_squares = jnp.sum(jnp.sum(both, axis=0, keepdims=True), axis=1, keepdims=True)
    weight_scale = lax.rsqrt(weight_squares / (2 * raw_in.size) + 1e-06)
    filter_squares = total_of(squares[0], squares[1:])[0:1, 0:1]
    filter_scale = lax.rsqrt(filter_squares / (n_ka * filt.size) + 1e-06)
    g_in[...] = (raw_in * weight_scale).T
    g_out[...] = out * weight_scale
    g_filt[...] = filt[...] * filter_scale


def call(kernel, name, operands, smem, outs, scratch=(), limit=SMALL, micros=2):
    vmem = pl.BlockSpec(memory_space=pltpu.VMEM)
    return pl.pallas_call(
        kernel,
        out_shape=tuple(jax.ShapeDtypeStruct(*o) for o in outs),
        in_specs=[pl.BlockSpec(memory_space=pltpu.SMEM)] * smem + [vmem] * (len(operands) - smem),
        out_specs=tuple(vmem for _ in outs),
        scratch_shapes=list(scratch),
        compiler_params=pltpu.CompilerParams(vmem_limit_bytes=limit),
        cost_estimate=pl.CostEstimate(
            flops=micros * FLOPS_PER_MICRO, bytes_accessed=0, transcendentals=0
        ),
        name=name,
    )(*operands)


def body(feats, coords, cell_ids, recip, kvec, w_in, w_out, kfilt, spread, cotan):
    n_ka = lax.axis_size("ka")
    n_dp = lax.axis_size("dp")
    atoms, chan = feats.shape
    own = kvec.shape[1]
    k_all = own * n_ka
    cells = recip.shape[1]
    long = atoms + LANES
    recip, spread = recip[0], spread[None]
    kvecs = [kvec] + [lax.ppermute(kvec, "ka", routes(s, n_ka)) for s in range(1, n_ka)]
    kfilts = [kfilt] + [lax.ppermute(kfilt, "ka", routes(s, n_ka)) for s in range(1, n_ka)]
    numbers = jnp.arange(cells, dtype=jnp.int32)[:, None]
    bounds = jnp.stack(
        [
            jnp.sum((cell_ids == numbers).astype(jnp.int32), axis=1),
            jnp.sum((cell_ids < numbers).astype(jnp.int32), axis=1),
        ]
    )
    vm = pltpu.VMEM
    waves, factors, quad, ids = call(
        functools.partial(waves_kernel, n_ka),
        "waves",
        (bounds, feats, coords, cell_ids, recip, w_in, *kvecs),
        1,
        [((2 * k_all, long), BF16), ((cells, chan, 2 * k_all), F32), ((cells, k_all), F32), ((1, long), jnp.int32)],
        [vm((k_all, 8), F32), vm((chan, long), BF16)],
        LIMIT,
        8,
    )
    act_t, mgrad_t, raw_out, raw_half = call(
        functools.partial(message_kernel, n_ka),
        "message",
        (bounds, ids, quad, waves, factors, spread, cotan, w_out, *kfilts),
        1,
        [((chan, atoms), BF16), ((chan, long), BF16), ((chan, chan), F32), ((chan, chan), BF16)],
        [vm((chan, k_all), F32), vm((chan, 8), F32), vm((chan, 2 * k_all), BF16), vm((chan, long), F32)],
        LIMIT,
        8,
    )
    chips = [2 * s for s in range(1, n_dp // 2)]
    out_parts = [lax.ppermute(raw_half, "dp", routes(s, n_dp)) for s in chips]
    weights, filter_grad, filter_half = call(
        functools.partial(adjoint_kernel, n_ka),
        "adjoint",
        (bounds, ids, quad, waves, factors, mgrad_t, spread, *kfilts),
        1,
        [((cells, chan, 2 * k_all), BF16), ((own, chan), F32), ((own, chan), BF16)],
        [vm((chan, k_all), F32), vm((chan, 8), F32), vm((chan, 2 * k_all), F32), vm((chan, own), F32)],
        LIMIT,
        8,
    )
    filt_parts = [lax.ppermute(filter_half, "dp", routes(s, n_dp)) for s in chips]
    (out_sum,) = call(add_kernel, "outsum", (raw_out, *out_parts), 0, [((chan, chan), F32)])
    out_near = lax.ppermute(out_sum, "dp", routes(1, n_dp))
    update_t, raw_in_t = call(
        update_kernel,
        "update",
        (bounds, ids, waves, weights, feats),
        1,
        [((chan, atoms), BF16), ((chan, chan), F32)],
        [vm((chan, long), F32)],
        LIMIT,
        8,
    )
    other_in = lax.ppermute(raw_in_t, "dp", routes(1, n_dp))
    (filt_sum,) = call(add_kernel, "filtsum", (filter_grad, *filt_parts), 0, [((own, chan), F32)])
    filt_near = lax.ppermute(filt_sum, "dp", routes(1, n_dp))
    (feat_grad,) = call(
        functools.partial(residual_kernel, True), "featgrad", (cotan, update_t, w_in), 0,
        [((atoms, chan), BF16)],
    )
    in_sum, in_half, w_sum, f_sum, f_squares = call(
        chip_kernel,
        "chip",
        (raw_in_t, other_in, out_sum, out_near, filt_sum, filt_near),
        0,
        [((chan, chan), F32), ((chan, chan), BF16), ((chan, chan), F32), ((own, chan), F32), ((8, LANES), F32)],
    )
    squares = [f_squares] + [lax.ppermute(f_squares, "ka", routes(s, n_ka)) for s in range(1, n_ka)]
    in_parts = [in_sum] + [lax.ppermute(in_half, "dp", routes(s, n_dp)) for s in chips]
    (mixed,) = call(
        functools.partial(residual_kernel, False), "mixed", (feats, act_t, w_out), 0,
        [((atoms, chan), BF16)],
    )
    grads = call(
        functools.partial(final_kernel, len(in_parts), n_ka),
        "final",
        (*in_parts, w_sum, f_sum, *squares),
        0,
        [((chan, chan), F32), ((chan, chan), F32), ((own, chan), F32)],
    )
    return (mixed, feat_grad, *grads)


def solution(mesh):
    placed = (
        P("dp", None),
        P(None, "dp"),
        P("dp", None),
        P("dp", None, None),
        P(None, "ka"),
        P(),
        P(),
        P("ka", None),
        P(),
        P("dp", None),
    )
    return jax.shard_map(
        body,
        mesh=mesh,
        in_specs=placed,
        out_specs=(P("dp", None), P("dp", None), P(), P(), P("ka", None)),
        check_vma=False,
    )
```

time: 91.1 us -> 80.2 us (0.88)
  waiting for transfers between devices: 15.7 us -> 6.87 us
  Pallas kernels: 45.9 us -> 40.5 us
  starting transfers between devices: 22.5 us -> 25.8 us
    pallas_call x3 -> x10, Pallas kernels: 45.9 us -> 40.5 us  [call(): pl.pallas_call(kernel, out_shape=tuple((jax.ShapeDtypeStruct(*o) for o in...]
    ppermute x3, waiting for transfers between devices: 4.86 us -> 0.36 us  [body(): lax.ppermute(kvec, 'ka', routes(s, n_ka))]
    ppermute x14 -> x15, waiting for transfers between devices: 10.5 us -> 6.51 us  [the longest x3 3.08 us: body(): lax.ppermute(filter_half, 'dp', routes(s, n_dp))]
    ppermute x14 -> x15, starting transfers between devices: 12.3 us -> 15.6 us  [the longest x3 4.39 us: body(): lax.ppermute(f_squares, 'ka', routes(s, n_ka))]
    unnamed x42 -> x24, local copies, waits for them, and re-layouts: 3.11 us -> 4.97 us
    squeeze x1 -> x0, local copies, waits for them, and re-layouts: 1.06 us -> none  [body(): pieces[s - 1]]
  transfers between devices with their start and end apart: 20 -> 21, of which waited for: 12 -> 5; matrix products, arithmetic and copies ran while one was open for 2% -> 1% of each run, Pallas kernels for 0% -> 31%
where the time goes in v1:
time: 80.2 us; the launch traced here: 79.9 us
  Pallas kernels  40.5 us (50%)
  starting transfers between devices  25.8 us (32%)
  waiting for transfers between devices  6.87 us (9%)
  local copies, waits for them, and re-layouts  4.97 us (6%)
  other arithmetic  0.87 us (1%)
    pallas_call x10, Pallas kernels, call(): pl.pallas_call(kernel, out_shape=tuple((jax.ShapeDtypeStruct(*o) for o in...  40.5 us
    ppermute x3, starting transfers between devices, body(): lax.ppermute(kvec, 'ka', routes(s, n_ka))  5.71 us
    unnamed x24, local copies, waits for them, and re-layouts  4.97 us
    ppermute x3, starting transfers between devices, body(): lax.ppermute(kfilt, 'ka', routes(s, n_ka))  4.47 us
    ppermute x3, starting transfers between devices, body(): lax.ppermute(f_squares, 'ka', routes(s, n_ka))  4.39 us
    ppermute x3, starting transfers between devices, body(): lax.ppermute(filter_half, 'dp', routes(s, n_dp))  3.63 us
    ppermute x3, starting transfers between devices, body(): lax.ppermute(in_half, 'dp', routes(s, n_dp))  3.49 us
    ppermute x3, starting transfers between devices, body(): out_parts = [lax.ppermute(raw_half, 'dp', routes(s, n_dp)) for s in chips]  3.49 us
  transfers between devices with their start and end apart: 21, of which 5 were waited for; matrix products, arithmetic and copies ran while one was open for 1% of the time, Pallas kernels for 31%

profile of v1, /device:TPU:0, one launch (start us, length us, event | category | flops | bytes accessed | tf_op | source)
XLA Modules:
  0.0 79.9 jit_solution(9169260716006191610)
XLA Ops:
  0.6 4.1 %collective-permute-start.1 = (s32[3,128]{1,0:T(4,128)}, s32[3,128]{1,0:T(4,128)S(1)}, u32[]{:S(2)}, u32[]{:S(2)}) collective-permute-start(s32[3,128]{1,0:T(4,128)} %refs_6_.2), channel_id=1, source_target_pairs={{0,2},{1,3},{2,0},{3,1},{4,6},{5,7},{6,4},{7,5},{8,10},{9,11},{10,... | collective-permute-start | bytes 4616 | tf_op jit(solution)/shard_map/ppermute | solution.py:356
  4.8 1.6 %collective-permute-start = (s32[3,128]{1,0:T(4,128)}, s32[3,128]{1,0:T(4,128)S(1)}, u32[]{:S(2)}, u32[]{:S(2)}) collective-permute-start(s32[3,128]{1,0:T(4,128)} %refs_6_.2), channel_id=1, source_target_pairs={{0,1},{1,0},{2,3},{3,2},{4,5},{5,4},{6,7},{7,6},{8,9},{9,8},{10,11... | collective-permute-start | bytes 4616 | tf_op jit(solution)/shard_map/ppermute | solution.py:356
  6.3 0.0 collective-permute-start.2
  6.3 3.8 %collective-permute-start.5 = (f32[128,256]{1,0:T(8,128)}, f32[128,256]{1,0:T(8,128)S(1)}, u32[]{:S(2)}, u32[]{:S(2)}) collective-permute-start(f32[128,256]{1,0:T(8,128)} %refs_7_.3), channel_id=1, source_target_pairs={{0,3},{1,2},{2,1},{3,0},{4,7},{5,6},{6,5},{7,4},{8,11},{9,10},{10,... | collective-permute-start | bytes 393224 | tf_op jit(solution)/shard_map/ppermute | solution.py:357
  10.2 0.0 collective-permute-start.4
  10.2 0.9 %convert_reduce_fusion.1 = (s32[8]{0:T(128)S(1)}, s32[8]{0:T(128)S(1)}) fusion(s32[2048]{0:T(1024)} %bitcast.5), kind=kLoop, calls=%fused_computation.2 | loop fusion | flops 98288 | bytes 8256 | tf_op jit(solution)/shard_map/reduce_sum | solution.py:361
  11.0 0.0 collective-permute-done.1.refs_8_
  11.0 0.7 collective-permute-start.3
  11.7 0.0 collective-permute-done.refs_7_
  11.7 0.4 collective-permute-done.2.refs_9_
  12.1 0.7 copy-done
  12.8 1.2 %copy-done.1 = bf16[2048,256]{1,0:T(8,128)(2,1)S(1)} copy-done((bf16[2048,256]{1,0:T(8,128)(2,1)S(1)}, bf16[2048,256]{1,0:T(8,128)(2,1)}, u32[]{:S(2)}) %copy-start.1) | copy-done | bytes 1048600
  14.0 0.9 %copy-done.6 = bf16[256,256]{1,0:T(8,128)(2,1)S(1)} copy-done((bf16[256,256]{1,0:T(8,128)(2,1)S(1)}, bf16[256,256]{1,0:T(8,128)(2,1)}, u32[]{:S(2)}) %copy-start.6) | copy-done | bytes 131096
  14.9 0.8 copy-done.8
  15.6 0.7 copy-done.9
  16.3 0.7 copy-done.10
  17.0 13.2 %waves.1 = (bf16[1024,2176]{1,0:T(8,128)(2,1)S(1)}, f32[8,256,1024]{2,1,0:T(8,128)S(1)}, f32[8,512]{1,0:T(8,128)S(1)}, s32[1,2176]{1,0:T(1,128)S(1)}) custom-call(s32[2,8]{1,0:T(2,128)S(1)} %pad_add_fusion.refs_0_.bounds, bf16[2048,256]{1,0:T(8,128)(2,1)S(1)} %copy-done.1, f32[3,2048]{1,0:T(4,128)S(1)} %copy-done.8, s32[1,2048]{1,0:T(1,128)S(1)} %copy-done, ...), custom_call_target="tpu_custom_call" | custom-call | flops 8589934592 | tf_op jit(solution)/shard_map/waves/pallas_call | solution.py:333
  30.3 0.0 collective-permute-done.5.refs_11_.refs_10_
  30.3 0.0 collective-permute-done.4.refs_10_.refs_9_
  30.3 0.0 collective-permute-done.3.refs_9_.refs_8_
  30.3 0.0 copy-done.3
  30.3 0.0 copy-done.4
  30.3 0.0 copy-done.5
  30.3 0.0 copy-done.11
  30.3 8.1 %message.1 = (bf16[256,2048]{1,0:T(8,128)(2,1)S(1)}, bf16[256,2176]{1,0:T(8,128)(2,1)S(1)}, f32[256,256]{1,0:T(8,128)S(1)}, bf16[256,256]{1,0:T(8,128)(2,1)S(1)}) custom-call(s32[2,8]{1,0:T(2,128)S(1)} %pad_add_fusion.refs_0_.bounds, s32[1,2176]{1,0:T(1,128)S(1)} %get-tuple-element.26.refs_1_.ids, f32[8,512]{1,0:T(8,128)S(1)} %get-tuple-element.27.refs_2_, ...), custom_call_target="tpu_custom_call" | custom-call | flops 8589934592 | tf_op jit(solution)/shard_map/message/pallas_call | solution.py:333
  38.5 0.0 copy-start.2
  38.5 6.3 %adjoint.1 = (bf16[8,256,1024]{2,1,0:T(8,128)(2,1)S(1)}, f32[128,256]{1,0:T(8,128)S(1)}, bf16[128,256]{1,0:T(8,128)(2,1)S(1)}) custom-call(s32[2,8]{1,0:T(2,128)S(1)} %pad_add_fusion.refs_0_.bounds, s32[1,2176]{1,0:T(1,128)S(1)} %get-tuple-element.26.refs_1_.ids, f32[8,512]{1,0:T(8,128)S(1)} %get-tuple-element.27.refs_2_, ...), custom_call_target="tpu_custom_call" | custom-call | flops 8589934592 | tf_op jit(solution)/shard_map/adjoint/pallas_call | solution.py:333
  44.8 2.1 %collective-permute-start.13 = (bf16[128,256]{1,0:T(8,128)(2,1)S(1)}, bf16[128,256]{1,0:T(8,128)(2,1)S(1)}, u32[]{:S(2)}, u32[]{:S(2)}) collective-permute-start(bf16[128,256]{1,0:T(8,128)(2,1)S(1)} %get-tuple-element.38), channel_id=1, source_target_pairs={{0,24},{4,28},{8,16},{12,20},{16,8},{20,12},{24,0},{28,4},{1,25},{... | collective-permute-start | bytes 196616 | tf_op jit(solution)/shard_map/ppermute | solution.py:398
  46.9 0.9 %collective-permute-start.12 = (bf16[128,256]{1,0:T(8,128)(2,1)S(1)}, bf16[128,256]{1,0:T(8,128)(2,1)S(1)}, u32[]{:S(2)}, u32[]{:S(2)}) collective-permute-start(bf16[128,256]{1,0:T(8,128)(2,1)S(1)} %get-tuple-element.38), channel_id=1, source_target_pairs={{0,16},{4,20},{8,24},{12,28},{16,0},{20,4},{24,8},{28,12},{1,17},{... | collective-permute-start | bytes 196616 | tf_op jit(solution)/shard_map/ppermute | solution.py:398
  47.8 1.9 %collective-permute-start.9 = (bf16[256,256]{1,0:T(8,128)(2,1)S(1)}, bf16[256,256]{1,0:T(8,128)(2,1)S(1)}, u32[]{:S(2)}, u32[]{:S(2)}) collective-permute-start(bf16[256,256]{1,0:T(8,128)(2,1)S(1)} %get-tuple-element.36), channel_id=1, source_target_pairs={{0,24},{4,28},{8,16},{12,20},{16,8},{20,12},{24,0},{28,4},{1,25},{... | collective-permute-start | bytes 393224 | tf_op jit(solution)/shard_map/ppermute | solution.py:387
  49.8 0.0 collective-permute-start.8
  49.8 1.5 %collective-permute-start.7 = (bf16[256,256]{1,0:T(8,128)(2,1)S(1)}, bf16[256,256]{1,0:T(8,128)(2,1)S(1)}, u32[]{:S(2)}, u32[]{:S(2)}) collective-permute-start(bf16[256,256]{1,0:T(8,128)(2,1)S(1)} %get-tuple-element.36), channel_id=1, source_target_pairs={{0,8},{4,12},{8,0},{12,4},{16,24},{20,28},{24,16},{28,20},{1,9},{5... | collective-permute-start | bytes 393224 | tf_op jit(solution)/shard_map/ppermute | solution.py:387
  51.3 0.0 copy-done.2
  51.3 5.8 %update.1 = (bf16[256,2048]{1,0:T(8,128)(2,1)S(1)}, f32[256,256]{1,0:T(8,128)S(1)}) custom-call(s32[2,8]{1,0:T(2,128)S(1)} %pad_add_fusion.refs_0_.bounds, s32[1,2176]{1,0:T(1,128)S(1)} %get-tuple-element.26.refs_1_.ids, bf16[1024,2176]{1,0:T(8,128)(2,1)S(1)} %get-tuple-element.28.refs_3_.waves, bf16[8,256,1024]{2,1,0:T(8,128)(2,1)S(1)} %get-tuple-element.32.weights, ...), custom_call_target="tpu_custom_call" | custom-call | flops 8589934592 | tf_op jit(solution)/shard_map/update/pallas_call | solution.py:333
  57.2 0.0 collective-permute-done.9.refs_3_
  57.2 0.6 collective-permute-start.11
  57.8 0.0 collective-permute-done.8.refs_2_
  57.8 0.0 collective-permute-start.6
  57.8 0.0 collective-permute-done.7.refs_1_
  57.8 0.1 outsum.1.out_sum
  57.9 0.6 collective-permute-start.10
  58.4 0.0 collective-permute-done.13.refs_3_
  58.4 0.0 collective-permute-done.12.refs_2_
  58.4 3.1 %collective-permute-done.11.refs_1_ = bf16[128,256]{1,0:T(8,128)(2,1)S(1)} collective-permute-done((bf16[128,256]{1,0:T(8,128)(2,1)S(1)}, bf16[128,256]{1,0:T(8,128)(2,1)S(1)}, u32[]{:S(2)}, u32[]{:S(2)}) %collective-permute-start.11) | collective-permute-done | bytes 65568 | tf_op jit(solution)/shard_map/ppermute | solution.py:398
  61.6 0.1 collective-permute-start.14
  61.6 1.3 %collective-permute-done.14.filt_near = f32[128,256]{1,0:T(8,128)S(1)} collective-permute-done((f32[128,256]{1,0:T(8,128)S(1)}, f32[128,256]{1,0:T(8,128)S(1)}, u32[]{:S(2)}, u32[]{:S(2)}) %collective-permute-start.14) | collective-permute-done | bytes 131104 | tf_op jit(solution)/shard_map/ppermute | solution.py:413
  63.0 0.0 collective-permute-done.6.other_in
  63.0 0.0 collective-permute-done.10.out_near
  63.0 0.2 chip.1
  63.2 3.5 %collective-permute-start.20 = (f32[8,128]{1,0:T(8,128)S(1)}, f32[8,128]{1,0:T(8,128)S(1)}, u32[]{:S(2)}, u32[]{:S(2)}) collective-permute-start(f32[8,128]{1,0:T(8,128)S(1)} %get-tuple-element.43.refs_6_), channel_id=1, source_target_pairs={{0,3},{1,2},{2,1},{3,0},{4,7},{5,6},{6,5},{7,4},{8,11},{9,10},{10,... | collective-permute-start | bytes 12296 | tf_op jit(solution)/shard_map/ppermute | solution.py:425
  66.6 2.8 %mixed.1 = bf16[2048,256]{1,0:T(8,128)(2,1)} custom-call(bf16[2048,256]{1,0:T(8,128)(2,1)S(1)} %copy-done.2, bf16[256,2048]{1,0:T(8,128)(2,1)S(1)} %get-tuple-element.30.values_t, bf16[256,256]{1,0:T(8,128)(2,1)S(1)} %copy-done.5), custom_call_target="tpu_custom_call" | custom-call | flops 2147483648 | tf_op jit(solution)/shard_map/mixed/pallas_call | solution.py:333
  69.5 0.0 collective-permute-start.19
  69.5 0.9 %collective-permute-start.18 = (f32[8,128]{1,0:T(8,128)S(1)}, f32[8,128]{1,0:T(8,128)S(1)}, u32[]{:S(2)}, u32[]{:S(2)}) collective-permute-start(f32[8,128]{1,0:T(8,128)S(1)} %get-tuple-element.43.refs_6_), channel_id=1, source_target_pairs={{0,1},{1,0},{2,3},{3,2},{4,5},{5,4},{6,7},{7,6},{8,9},{9,8},{10,11... | collective-permute-start | bytes 12296 | tf_op jit(solution)/shard_map/ppermute | solution.py:425
  70.4 1.8 %collective-permute-start.17 = (bf16[256,256]{1,0:T(8,128)(2,1)S(1)}, bf16[256,256]{1,0:T(8,128)(2,1)S(1)}, u32[]{:S(2)}, u32[]{:S(2)}) collective-permute-start(bf16[256,256]{1,0:T(8,128)(2,1)S(1)} %get-tuple-element.40), channel_id=1, source_target_pairs={{0,24},{4,28},{8,16},{12,20},{16,8},{20,12},{24,0},{28,4},{1,25},{... | collective-permute-start | bytes 393224 | tf_op jit(solution)/shard_map/ppermute | solution.py:426
  72.2 0.2 collective-permute-start.16
  72.4 0.0 collective-permute-done.20.refs_9_
  72.4 1.5 %collective-permute-start.15 = (bf16[256,256]{1,0:T(8,128)(2,1)S(1)}, bf16[256,256]{1,0:T(8,128)(2,1)S(1)}, u32[]{:S(2)}, u32[]{:S(2)}) collective-permute-start(bf16[256,256]{1,0:T(8,128)(2,1)S(1)} %get-tuple-element.40), channel_id=1, source_target_pairs={{0,8},{4,12},{8,0},{12,4},{16,24},{20,28},{24,16},{28,20},{1,9},{5... | collective-permute-start | bytes 393224 | tf_op jit(solution)/shard_map/ppermute | solution.py:426
  73.9 2.9 %featgrad.1 = bf16[2048,256]{1,0:T(8,128)(2,1)} custom-call(bf16[2048,256]{1,0:T(8,128)(2,1)S(1)} %copy-done.3, bf16[256,2048]{1,0:T(8,128)(2,1)S(1)} %get-tuple-element.33.values_t, bf16[256,256]{1,0:T(8,128)(2,1)S(1)} %copy-done.7), custom_call_target="tpu_custom_call" | custom-call | flops 2147483648 | tf_op jit(solution)/shard_map/featgrad/pallas_call | solution.py:333
  76.7 0.0 collective-permute-done.19.refs_8_
  76.7 0.0 collective-permute-done.18.refs_7_
  76.8 0.8 collective-permute-done.17.refs_3_
  77.5 1.3 %collective-permute-done.16.refs_2_ = bf16[256,256]{1,0:T(8,128)(2,1)S(1)} collective-permute-done((bf16[256,256]{1,0:T(8,128)(2,1)S(1)}, bf16[256,256]{1,0:T(8,128)(2,1)S(1)}, u32[]{:S(2)}, u32[]{:S(2)}) %collective-permute-start.16) | collective-permute-done | bytes 131104 | tf_op jit(solution)/shard_map/ppermute | solution.py:426
  78.8 0.0 collective-permute-done.15.refs_1_
  78.8 1.1 %final.1 = (f32[256,256]{1,0:T(8,128)}, f32[256,256]{1,0:T(8,128)}, f32[128,256]{1,0:T(8,128)}) custom-call(f32[256,256]{1,0:T(8,128)S(1)} %get-tuple-element.39.refs_0_, bf16[256,256]{1,0:T(8,128)(2,1)S(1)} %collective-permute-done.15.refs_1_, bf16[256,256]{1,0:T(8,128)(2,1)S(1)} %collective-permute-done.16.refs_2_, ...), custom_call_target="tpu_custom_call" | custom-call | flops 2147483648 | tf_op jit(solution)/shard_map/final/pallas_call | solution.py:333
  (14 shorter events, 0.1 us)
Async XLA Ops:
  0.6 10.4 %collective-permute-start.1 = (s32[3,128]{1,0:T(4,128)}, s32[3,128]{1,0:T(4,128)S(1)}, u32[]{:S(2)}, u32[]{:S(2)}) collective-permute-start(s32[3,128]{1,0:T(4,128)} %refs_6_.2), channel_id=1, source_target_pairs={{0,2},{1,3},{2,0},{3,1},{4,6},{5,7},{6,4},{7,5},{8,10},{9,11},{10,... | collective-permute-start | bytes 4616 | tf_op jit(solution)/shard_map/ppermute | solution.py:356
  4.8 6.9 %collective-permute-start = (s32[3,128]{1,0:T(4,128)}, s32[3,128]{1,0:T(4,128)S(1)}, u32[]{:S(2)}, u32[]{:S(2)}) collective-permute-start(s32[3,128]{1,0:T(4,128)} %refs_6_.2), channel_id=1, source_target_pairs={{0,1},{1,0},{2,3},{3,2},{4,5},{5,4},{6,7},{7,6},{8,9},{9,8},{10,11... | collective-permute-start | bytes 4616 | tf_op jit(solution)/shard_map/ppermute | solution.py:356
  6.3 5.7 %collective-permute-start.2 = (s32[3,128]{1,0:T(4,128)}, s32[3,128]{1,0:T(4,128)S(1)}, u32[]{:S(2)}, u32[]{:S(2)}) collective-permute-start(s32[3,128]{1,0:T(4,128)} %refs_6_.2), channel_id=1, source_target_pairs={{0,3},{1,2},{2,1},{3,0},{4,7},{5,6},{6,5},{7,4},{8,11},{9,10},{10,... | collective-permute-start | bytes 4616 | tf_op jit(solution)/shard_map/ppermute | solution.py:356
  6.3 23.9 %collective-permute-start.5 = (f32[128,256]{1,0:T(8,128)}, f32[128,256]{1,0:T(8,128)S(1)}, u32[]{:S(2)}, u32[]{:S(2)}) collective-permute-start(f32[128,256]{1,0:T(8,128)} %refs_7_.3), channel_id=1, source_target_pairs={{0,3},{1,2},{2,1},{3,0},{4,7},{5,6},{6,5},{7,4},{8,11},{9,10},{10,... | collective-permute-start | bytes 393224 | tf_op jit(solution)/shard_map/ppermute | solution.py:357
  10.2 20.1 %collective-permute-start.4 = (f32[128,256]{1,0:T(8,128)}, f32[128,256]{1,0:T(8,128)S(1)}, u32[]{:S(2)}, u32[]{:S(2)}) collective-permute-start(f32[128,256]{1,0:T(8,128)} %refs_7_.3), channel_id=1, source_target_pairs={{0,2},{1,3},{2,0},{3,1},{4,6},{5,7},{6,4},{7,5},{8,10},{9,11},{10,... | collective-permute-start | bytes 393224 | tf_op jit(solution)/shard_map/ppermute | solution.py:357
  11.0 19.2 %collective-permute-start.3 = (f32[128,256]{1,0:T(8,128)}, f32[128,256]{1,0:T(8,128)S(1)}, u32[]{:S(2)}, u32[]{:S(2)}) collective-permute-start(f32[128,256]{1,0:T(8,128)} %refs_7_.3), channel_id=1, source_target_pairs={{0,1},{1,0},{2,3},{3,2},{4,5},{5,4},{6,7},{7,6},{8,9},{9,8},{10,11... | collective-permute-start | bytes 393224 | tf_op jit(solution)/shard_map/ppermute | solution.py:357
  12.1 0.7 copy-start
  12.8 1.2 %copy-start.1 = (bf16[2048,256]{1,0:T(8,128)(2,1)S(1)}, bf16[2048,256]{1,0:T(8,128)(2,1)}, u32[]{:S(2)}) copy-start(bf16[2048,256]{1,0:T(8,128)(2,1)} %feats.1) | copy-start | bytes 3145732
  14.0 0.9 %copy-start.6 = (bf16[256,256]{1,0:T(8,128)(2,1)S(1)}, bf16[256,256]{1,0:T(8,128)(2,1)}, u32[]{:S(2)}) copy-start(bf16[256,256]{1,0:T(8,128)(2,1)} %weight.3) | copy-start | bytes 393220
  14.9 0.8 copy-start.8
  15.6 0.7 copy-start.9
  16.3 0.7 copy-start.10
  17.0 13.3 %copy-start.3 = (bf16[2048,256]{1,0:T(8,128)(2,1)S(1)}, bf16[2048,256]{1,0:T(8,128)(2,1)}, u32[]{:S(2)}) copy-start(bf16[2048,256]{1,0:T(8,128)(2,1)} %base.3) | copy-start | bytes 3145732
  17.0 13.3 %copy-start.4 = (f32[128,256]{1,0:T(8,128)S(1)}, f32[128,256]{1,0:T(8,128)}, u32[]{:S(2)}) copy-start(f32[128,256]{1,0:T(8,128)} %refs_7_.3) | copy-start | bytes 393220
  17.0 13.3 %copy-start.5 = (bf16[256,256]{1,0:T(8,128)(2,1)S(1)}, bf16[256,256]{1,0:T(8,128)(2,1)}, u32[]{:S(2)}) copy-start(bf16[256,256]{1,0:T(8,128)(2,1)} %weight.2) | copy-start | bytes 393220
  17.0 13.3 %copy-start.11 = (f32[256]{0:T(256)S(1)}, f32[256]{0:T(256)}, u32[]{:S(2)}) copy-start(f32[256]{0:T(256)} %param.18) | copy-start | bytes 3076
  38.5 12.9 %copy-start.2 = (bf16[2048,256]{1,0:T(8,128)(2,1)S(1)}, bf16[2048,256]{1,0:T(8,128)(2,1)}, u32[]{:S(2)}) copy-start(bf16[2048,256]{1,0:T(8,128)(2,1)} %feats.1) | copy-start | bytes 3145732
  44.8 13.6 %collective-permute-start.13 = (bf16[128,256]{1,0:T(8,128)(2,1)S(1)}, bf16[128,256]{1,0:T(8,128)(2,1)S(1)}, u32[]{:S(2)}, u32[]{:S(2)}) collective-permute-start(bf16[128,256]{1,0:T(8,128)(2,1)S(1)} %get-tuple-element.38), channel_id=1, source_target_pairs={{0,24},{4,28},{8,16},{12,20},{16,8},{20,12},{24,0},{28,4},{1,25},{... | collective-permute-start | bytes 196616 | tf_op jit(solution)/shard_map/ppermute | solution.py:398
  46.9 11.5 %collective-permute-start.12 = (bf16[128,256]{1,0:T(8,128)(2,1)S(1)}, bf16[128,256]{1,0:T(8,128)(2,1)S(1)}, u32[]{:S(2)}, u32[]{:S(2)}) collective-permute-start(bf16[128,256]{1,0:T(8,128)(2,1)S(1)} %get-tuple-element.38), channel_id=1, source_target_pairs={{0,16},{4,20},{8,24},{12,28},{16,0},{20,4},{24,8},{28,12},{1,17},{... | collective-permute-start | bytes 196616 | tf_op jit(solution)/shard_map/ppermute | solution.py:398
  47.8 9.3 %collective-permute-start.9 = (bf16[256,256]{1,0:T(8,128)(2,1)S(1)}, bf16[256,256]{1,0:T(8,128)(2,1)S(1)}, u32[]{:S(2)}, u32[]{:S(2)}) collective-permute-start(bf16[256,256]{1,0:T(8,128)(2,1)S(1)} %get-tuple-element.36), channel_id=1, source_target_pairs={{0,24},{4,28},{8,16},{12,20},{16,8},{20,12},{24,0},{28,4},{1,25},{... | collective-permute-start | bytes 393224 | tf_op jit(solution)/shard_map/ppermute | solution.py:387
  49.8 8.0 %collective-permute-start.8 = (bf16[256,256]{1,0:T(8,128)(2,1)S(1)}, bf16[256,256]{1,0:T(8,128)(2,1)S(1)}, u32[]{:S(2)}, u32[]{:S(2)}) collective-permute-start(bf16[256,256]{1,0:T(8,128)(2,1)S(1)} %get-tuple-element.36), channel_id=1, source_target_pairs={{0,16},{4,20},{8,24},{12,28},{16,0},{20,4},{24,8},{28,12},{1,17},{... | collective-permute-start | bytes 393224 | tf_op jit(solution)/shard_map/ppermute | solution.py:387
  49.8 8.0 %collective-permute-start.7 = (bf16[256,256]{1,0:T(8,128)(2,1)S(1)}, bf16[256,256]{1,0:T(8,128)(2,1)S(1)}, u32[]{:S(2)}, u32[]{:S(2)}) collective-permute-start(bf16[256,256]{1,0:T(8,128)(2,1)S(1)} %get-tuple-element.36), channel_id=1, source_target_pairs={{0,8},{4,12},{8,0},{12,4},{16,24},{20,28},{24,16},{28,20},{1,9},{5... | collective-permute-start | bytes 393224 | tf_op jit(solution)/shard_map/ppermute | solution.py:387
  57.2 4.3 %collective-permute-start.11 = (bf16[128,256]{1,0:T(8,128)(2,1)S(1)}, bf16[128,256]{1,0:T(8,128)(2,1)S(1)}, u32[]{:S(2)}, u32[]{:S(2)}) collective-permute-start(bf16[128,256]{1,0:T(8,128)(2,1)S(1)} %get-tuple-element.38), channel_id=1, source_target_pairs={{0,8},{4,12},{8,0},{12,4},{16,24},{20,28},{24,16},{28,20},{1,9},{5... | collective-permute-start | bytes 196616 | tf_op jit(solution)/shard_map/ppermute | solution.py:398
  57.8 5.2 %collective-permute-start.6 = (f32[256,256]{1,0:T(8,128)S(1)}, f32[256,256]{1,0:T(8,128)S(1)}, u32[]{:S(2)}, u32[]{:S(2)}) collective-permute-start(f32[256,256]{1,0:T(8,128)S(1)} %get-tuple-element.34.raw_in_t), channel_id=1, source_target_pairs={{0,4},{4,0},{8,12},{12,8},{16,20},{20,16},{24,28},{28,24},{1,5},{5... | collective-permute-start | bytes 786440 | tf_op jit(solution)/shard_map/ppermute | solution.py:411
  57.9 5.1 %collective-permute-start.10 = (f32[256,256]{1,0:T(8,128)S(1)}, f32[256,256]{1,0:T(8,128)S(1)}, u32[]{:S(2)}, u32[]{:S(2)}) collective-permute-start(f32[256,256]{1,0:T(8,128)S(1)} %outsum.1.out_sum), channel_id=1, source_target_pairs={{0,4},{4,0},{8,12},{12,8},{16,20},{20,16},{24,28},{28,24},{1,5},{5... | collective-permute-start | bytes 786440 | tf_op jit(solution)/shard_map/ppermute | solution.py:400
  61.6 1.4 %collective-permute-start.14 = (f32[128,256]{1,0:T(8,128)S(1)}, f32[128,256]{1,0:T(8,128)S(1)}, u32[]{:S(2)}, u32[]{:S(2)}) collective-permute-start(f32[128,256]{1,0:T(8,128)S(1)} %filtsum.1.filt_sum), channel_id=1, source_target_pairs={{0,4},{4,0},{8,12},{12,8},{16,20},{20,16},{24,28},{28,24},{1,5},{5... | collective-permute-start | bytes 393224 | tf_op jit(solution)/shard_map/ppermute | solution.py:413
  63.2 10.7 %copy-start.7 = (bf16[256,256]{1,0:T(8,128)(2,1)S(1)}, bf16[256,256]{1,0:T(8,128)(2,1)}, u32[]{:S(2)}) copy-start(bf16[256,256]{1,0:T(8,128)(2,1)} %weight.3) | copy-start | bytes 393220
  63.2 9.2 %collective-permute-start.20 = (f32[8,128]{1,0:T(8,128)S(1)}, f32[8,128]{1,0:T(8,128)S(1)}, u32[]{:S(2)}, u32[]{:S(2)}) collective-permute-start(f32[8,128]{1,0:T(8,128)S(1)} %get-tuple-element.43.refs_6_), channel_id=1, source_target_pairs={{0,3},{1,2},{2,1},{3,0},{4,7},{5,6},{6,5},{7,4},{8,11},{9,10},{10,... | collective-permute-start | bytes 12296 | tf_op jit(solution)/shard_map/ppermute | solution.py:425
  69.5 7.3 %collective-permute-start.19 = (f32[8,128]{1,0:T(8,128)S(1)}, f32[8,128]{1,0:T(8,128)S(1)}, u32[]{:S(2)}, u32[]{:S(2)}) collective-permute-start(f32[8,128]{1,0:T(8,128)S(1)} %get-tuple-element.43.refs_6_), channel_id=1, source_target_pairs={{0,2},{1,3},{2,0},{3,1},{4,6},{5,7},{6,4},{7,5},{8,10},{9,11},{10,... | collective-permute-start | bytes 12296 | tf_op jit(solution)/shard_map/ppermute | solution.py:425
  69.5 7.3 %collective-permute-start.18 = (f32[8,128]{1,0:T(8,128)S(1)}, f32[8,128]{1,0:T(8,128)S(1)}, u32[]{:S(2)}, u32[]{:S(2)}) collective-permute-start(f32[8,128]{1,0:T(8,128)S(1)} %get-tuple-element.43.refs_6_), channel_id=1, source_target_pairs={{0,1},{1,0},{2,3},{3,2},{4,5},{5,4},{6,7},{7,6},{8,9},{9,8},{10,11... | collective-permute-start | bytes 12296 | tf_op jit(solution)/shard_map/ppermute | solution.py:425
  70.4 7.1 %collective-permute-start.17 = (bf16[256,256]{1,0:T(8,128)(2,1)S(1)}, bf16[256,256]{1,0:T(8,128)(2,1)S(1)}, u32[]{:S(2)}, u32[]{:S(2)}) collective-permute-start(bf16[256,256]{1,0:T(8,128)(2,1)S(1)} %get-tuple-element.40), channel_id=1, source_target_pairs={{0,24},{4,28},{8,16},{12,20},{16,8},{20,12},{24,0},{28,4},{1,25},{... | collective-permute-start | bytes 393224 | tf_op jit(solution)/shard_map/ppermute | solution.py:426
  72.2 6.6 %collective-permute-start.16 = (bf16[256,256]{1,0:T(8,128)(2,1)S(1)}, bf16[256,256]{1,0:T(8,128)(2,1)S(1)}, u32[]{:S(2)}, u32[]{:S(2)}) collective-permute-start(bf16[256,256]{1,0:T(8,128)(2,1)S(1)} %get-tuple-element.40), channel_id=1, source_target_pairs={{0,16},{4,20},{8,24},{12,28},{16,0},{20,4},{24,8},{28,12},{1,17},{... | collective-permute-start | bytes 393224 | tf_op jit(solution)/shard_map/ppermute | solution.py:426
  72.4 6.4 %collective-permute-start.15 = (bf16[256,256]{1,0:T(8,128)(2,1)S(1)}, bf16[256,256]{1,0:T(8,128)(2,1)S(1)}, u32[]{:S(2)}, u32[]{:S(2)}) collective-permute-start(bf16[256,256]{1,0:T(8,128)(2,1)S(1)} %get-tuple-element.40), channel_id=1, source_target_pairs={{0,8},{4,12},{8,0},{12,4},{16,24},{20,28},{24,16},{28,20},{1,9},{5... | collective-permute-start | bytes 393224 | tf_op jit(solution)/shard_map/ppermute | solution.py:426

commit v2 on v1

--- a/solution.py
+++ b/solution.py
@@ -6,6 +6,7 @@
 from jax.experimental import pallas as pl
 from jax.experimental.pallas import tpu as pltpu
 from jax.sharding import PartitionSpec as P
+
 
 F32 = jnp.float32
 BF16 = jnp.bfloat16
@@ -14,6 +15,7 @@
 MOST = 1024
 LIMIT = 24 << 20
 SMALL = 6 << 20
+PREPARE = 16 << 20
 FLOPS_PER_MICRO = 1 << 30
 LOG2_E = 1.4426950408889634
 COS_TERMS = (
@@ -106,35 +108,14 @@
     return 1.0 / jnp.full((1, 1), count, jnp.int32).astype(F32)
 
 
-def shape_of(cell, quad, width_cols):
-    exponent = quad[pl.ds(cell, 1), :] * width_cols[:, 0:1]
+def shape_of(cell, quad, width_cols, first, size):
+    exponent = quad[pl.ds(cell, 1), :][:, first : first + size] * width_cols[:, 0:1]
     return jnp.exp2(exponent)
 
 
-def waves_kernel(n_ka, *refs):
-    bounds, feats, coords, ids_in, recip, w_in = refs[:6]
-    kvecs = refs[6 : 6 + n_ka]
-    waves, factors, quad, ids, kcols, proj_t = refs[6 + n_ka :]
-    atoms, chan = feats.shape
-    own = kvecs[0].shape[1]
-    k_all = own * n_ka
-    cells = recip.shape[0]
-
-    rows = jnp.concatenate([k[...] for k in kvecs], axis=1).astype(F32)
-    rows = jnp.concatenate([rows, jnp.zeros((5, k_all), F32)], axis=0)
-    kcols[...] = rows.T
-    squared = jnp.zeros((cells, k_all), F32)
-    for r in range(3):
-        part = recip[:, 3 * r : 3 * r + 1] * rows[0:1, :]
-        part = part + recip[:, 3 * r + 1 : 3 * r + 2] * rows[1:2, :]
-        part = part + recip[:, 3 * r + 2 : 3 * r + 3] * rows[2:3, :]
-        squared = squared + part * part
-    quad[...] = squared
-    ids[:, :atoms] = ids_in[...]
-    ids[:, atoms:] = jnp.full((1, LANES), -1, jnp.int32)
-    waves[:, atoms:] = jnp.zeros((2 * k_all, LANES), BF16)
-    proj_t[:, atoms:] = jnp.zeros((chan, LANES), BF16)
-
+def fill_waves(waves, base, kcols, coords):
+    own = kcols.shape[0]
+    atoms = coords.shape[1]
     wide = tile_of(atoms, 1024)
 
     def phase_rows(i, carry):
@@ -146,13 +127,47 @@
             turns = turns + kv[:, 2:3] * frac[2:3, :]
             turns = turns - ((turns + ROUNDER) - ROUNDER)
             square = turns * turns
-            waves[pl.ds(row, 16), start : start + wide] = horner(COS_TERMS, square).astype(BF16)
-            waves[pl.ds(pl.multiple_of(k_all + row, 16), 16), start : start + wide] = (
+            waves[pl.ds(pl.multiple_of(base + row, 16), 16), start : start + wide] = horner(
+                COS_TERMS, square
+            ).astype(BF16)
+            waves[pl.ds(pl.multiple_of(base + own + row, 16), 16), start : start + wide] = (
                 horner(SIN_TERMS, square) * turns
             ).astype(BF16)
         return carry
 
-    lax.fori_loop(0, k_all // 16, phase_rows, 0)
+    lax.fori_loop(0, own // 16, phase_rows, 0)
+
+
+def vector_columns(kvec):
+    rows = kvec[...].astype(F32)
+    return jnp.concatenate([rows, jnp.zeros((5, rows.shape[1]), F32)], axis=0).T
+
+
+def prepare_kernel(
+    feats_hbm, coords_hbm, ids_hbm, recip_hbm, kvec_hbm, w_in_hbm,
+    waves, proj_t, ids, coords, recip, kvec, feats, w_in, kcols, sems,
+):
+    atoms, chan = feats.shape
+    moves = (
+        (kvec_hbm, kvec),
+        (coords_hbm, coords),
+        (w_in_hbm, w_in),
+        (feats_hbm, feats),
+        (ids_hbm, ids.at[:, :atoms]),
+        (recip_hbm, recip),
+    )
+    copies = [pltpu.make_async_copy(a, b, sems.at[i]) for i, (a, b) in enumerate(moves)]
+    for copy in copies:
+        copy.start()
+    ids[:, atoms:] = jnp.full((1, LANES), -1, jnp.int32)
+    waves[:, atoms:] = jnp.zeros((waves.shape[0], LANES), BF16)
+    proj_t[:, atoms:] = jnp.zeros((chan, LANES), BF16)
+    copies[0].wait()
+    copies[1].wait()
+    kcols[...] = vector_columns(kvec)
+    fill_waves(waves, 0, kcols, coords)
+    copies[2].wait()
+    copies[3].wait()
 
     def project(t, carry):
         at = pl.ds(pl.multiple_of(t * TILE, TILE), TILE)
@@ -160,6 +175,31 @@
         return carry
 
     lax.fori_loop(0, atoms // TILE, project, 0)
+    copies[4].wait()
+    copies[5].wait()
+
+
+def waves_kernel(n_ka, *refs):
+    bounds, own_waves, proj_t, ids, coords, recip = refs[:6]
+    kvecs = refs[6 : 6 + n_ka]
+    waves, factors, quad, kcols = refs[6 + n_ka :]
+    atoms = coords.shape[1]
+    own = kvecs[0].shape[1]
+    cells = recip.shape[0]
+    waves[: 2 * own, :] = own_waves[...]
+    waves[2 * own :, atoms:] = jnp.zeros((2 * own * (n_ka - 1), LANES), BF16)
+    for j in range(1, n_ka):
+        kcols[...] = vector_columns(kvecs[j])
+        fill_waves(waves, 2 * own * j, kcols, coords)
+    for j in range(n_ka):
+        rows = kvecs[j][...].astype(F32)
+        squared = jnp.zeros((cells, own), F32)
+        for r in range(3):
+            part = recip[:, 3 * r : 3 * r + 1] * rows[0:1, :]
+            part = part + recip[:, 3 * r + 1 : 3 * r + 2] * rows[1:2, :]
+            part = part + recip[:, 3 * r + 2 : 3 * r + 3] * rows[2:3, :]
+            squared = squared + part * part
+        quad[:, own * j : own * (j + 1)] = squared
 
     def cell_step(cell, carry):
         start, steps, _ = span_of(bounds, cell)
@@ -179,7 +219,6 @@
     act_t, mgrad_t, raw_out, raw_half, filt_t, width_cols, weights, mess_t = refs[8 + n_ka :]
     atoms, chan = cotan.shape
     own = kfilts[0].shape[0]
-    k_all = own * n_ka
     cells = quad.shape[0]
     for j in range(n_ka):
         filt_t[:, j * own : (j + 1) * own] = kfilts[j][...].T
@@ -187,9 +226,12 @@
 
     def cell_step(cell, carry):
         start, steps, count = span_of(bounds, cell)
-        filt = filt_t[...] * (shape_of(cell, quad, width_cols) * inverse_count(count))
-        weights[:, :k_all] = (filt * factors[cell, :, :k_all]).astype(BF16)
-        weights[:, k_all:] = (filt * factors[cell, :, k_all:]).astype(BF16)
+        inverse = inverse_count(count)
+        for j in range(n_ka):
+            scaled = shape_of(cell, quad, width_cols, j * own, own) * inverse
+            filt = filt_t[:, own * j : own * (j + 1)] * scaled
+            for at in (slice(2 * own * j, own * (2 * j + 1)), slice(own * (2 * j + 1), 2 * own * (j + 1))):
+                weights[:, at] = (filt * factors[cell, :, at]).astype(BF16)
         spread_cell(cell, start, steps, most_steps(atoms), ids, weights, waves, mess_t)
         return carry
 
@@ -218,10 +260,8 @@
     bounds, ids, quad, waves, factors, mgrad_t, spread = refs[:7]
     kfilts = refs[7 : 7 + n_ka]
     weights, filter_grad, filter_half, filt_t, width_cols, total, grad_t = refs[7 + n_ka :]
-    chan = mgrad_t.shape[0]
     atoms = mgrad_t.shape[1] - LANES
     own = kfilts[0].shape[0]
-    k_all = own * n_ka
     cells = quad.shape[0]
     for j in range(n_ka):
         filt_t[:, j * own : (j + 1) * own] = kfilts[j][...].T
@@ -235,14 +275,18 @@
             total[...] = value
 
         gather_cell(cell, start, steps, most_steps(atoms), ids, mgrad_t, waves, store)
-        scaled = shape_of(cell, quad, width_cols) * inverse_count(count)
-        filt = filt_t[...] * scaled
-        weights[cell, :, :k_all] = (filt * total[:, :k_all]).astype(BF16)
-        weights[cell, :, k_all:] = (filt * total[:, k_all:]).astype(BF16)
-        grad_t[...] += scaled[:, :own] * (
-            factors[cell, :, :own] * total[:, :own]
-            + factors[cell, :, k_all : k_all + own] * total[:, k_all : k_all + own]
-        )
+        inverse = inverse_count(count)
+        for j in range(n_ka):
+            scaled = shape_of(cell, quad, width_cols, j * own, own) * inverse
+            filt = filt_t[:, own * j : own * (j + 1)] * scaled
+            real = slice(2 * own * j, own * (2 * j + 1))
+            imag = slice(own * (2 * j + 1), 2 * own * (j + 1))
+            weights[cell, :, real] = (filt * total[:, real]).astype(BF16)
+            weights[cell, :, imag] = (filt * total[:, imag]).astype(BF16)
+            if j == 0:
+                grad_t[...] += scaled * (
+                    factors[cell, :, real] * total[:, real] + factors[cell, :, imag] * total[:, imag]
+                )
         return carry
 
     lax.fori_loop(0, cells, cell_step, 0)
@@ -252,7 +296,7 @@
 
 
 def update_kernel(bounds, ids, waves, weights, feats, update_t, raw_in_t, total_t):
-    cells, chan, _ = weights.shape
+    cells, _, _ = weights.shape
     atoms = feats.shape[0]
 
     def cell_step(cell, carry):
@@ -276,23 +320,45 @@
 
 
 def residual_kernel(transposed, base, values_t, weight, out):
-    rows = base.shape[0]
-
-    def step(t, carry):
-        at = pl.ds(pl.multiple_of(t * TILE, TILE), TILE)
-        value = mm(values_t[:, at].T, weight[...], 1, 1 if transposed else 0)
-        out[at, :] = (base[at, :].astype(F32) + value).astype(BF16)
-        return carry
-
-    lax.fori_loop(0, rows // TILE, step, 0)
-
-
-def chip_kernel(raw_in_t, other_in, out_sum, out_near, filt_sum, filt_near, in_sum, in_half, w_sum, f_sum, f_squares):
-    value = raw_in_t[...] + other_in[...]
+    value = mm(values_t[...].T, weight[...], 1, 1 if transposed else 0)
+    out[...] = (base[...].astype(F32) + value).astype(BF16)
+
+
+def residual(transposed, base, values_t, weight):
+    rows, chan = base.shape
+    step = tile_of(rows, 512)
+    by_rows = pl.BlockSpec((step, chan), lambda i: (i, 0))
+    return pl.pallas_call(
+        functools.partial(residual_kernel, transposed),
+        out_shape=jax.ShapeDtypeStruct((rows, chan), BF16),
+        grid=(rows // step,),
+        in_specs=[
+            by_rows,
+            pl.BlockSpec((chan, step), lambda i: (0, i)),
+            pl.BlockSpec((chan, chan), lambda i: (0, 0)),
+        ],
+        out_specs=by_rows,
+        compiler_params=pltpu.CompilerParams(vmem_limit_bytes=SMALL),
+        cost_estimate=pl.CostEstimate(
+            flops=2 * FLOPS_PER_MICRO, bytes_accessed=0, transcendentals=0
+        ),
+    )(base, values_t, weight)
+
+
+def join_kernel(raw_in_t, filt, *refs):
+    pack = refs[-1]
+    chan = raw_in_t.shape[0]
+    pack[:chan, :] = raw_in_t[...]
+    pack[chan:, :] = total_of(filt, refs[:-1])
+
+
+def chip_kernel(pack, near, out_sum, out_near, in_sum, in_half, w_sum, f_sum, f_squares):
+    chan = out_sum.shape[0]
+    value = pack[:chan, :] + near[:chan, :]
     in_sum[...] = value
     in_half[...] = value.astype(BF16)
     w_sum[...] = out_sum[...] + out_near[...]
-    filt = filt_sum[...] + filt_near[...]
+    filt = pack[chan:, :] + near[chan:, :]
     f_sum[...] = filt
     f_squares[...] = jnp.broadcast_to(
         jnp.sum(jnp.sum(filt * filt, axis=0, keepdims=True), axis=1, keepdims=True),
@@ -328,23 +394,26 @@
     g_filt[...] = filt[...] * filter_scale
 
 
-def call(kernel, name, operands, smem, outs, scratch=(), limit=SMALL, micros=2):
+def call(kernel, operands, smem, outs, scratch=(), limit=SMALL, micros=2, space=pltpu.VMEM):
     vmem = pl.BlockSpec(memory_space=pltpu.VMEM)
     return pl.pallas_call(
         kernel,
         out_shape=tuple(jax.ShapeDtypeStruct(*o) for o in outs),
-        in_specs=[pl.BlockSpec(memory_space=pltpu.SMEM)] * smem + [vmem] * (len(operands) - smem),
+        in_specs=[pl.BlockSpec(memory_space=pltpu.SMEM)] * smem + [pl.BlockSpec(memory_space=space)] * (len(operands) - smem),
         out_specs=tuple(vmem for _ in outs),
         scratch_shapes=list(scratch),
         compiler_params=pltpu.CompilerParams(vmem_limit_bytes=limit),
         cost_estimate=pl.CostEstimate(
             flops=micros * FLOPS_PER_MICRO, bytes_accessed=0, transcendentals=0
         ),
-        name=name,
     )(*operands)
 
 
-def body(feats, coords, cell_ids, recip, kvec, w_in, w_out, kfilt, spread, cotan):
+def send(value, axis, step):
+    return lax.ppermute(value, axis, routes(step, lax.axis_size(axis)))
+
+
+def block(feats, coords, cell_ids, recip, kvec, w_in, w_out, kfilt, spread, cotan):
     n_ka = lax.axis_size("ka")
     n_dp = lax.axis_size("dp")
     atoms, chan = feats.shape
@@ -353,8 +422,11 @@
     cells = recip.shape[1]
     long = atoms + LANES
     recip, spread = recip[0], spread[None]
-    kvecs = [kvec] + [lax.ppermute(kvec, "ka", routes(s, n_ka)) for s in range(1, n_ka)]
-    kfilts = [kfilt] + [lax.ppermute(kfilt, "ka", routes(s, n_ka)) for s in range(1, n_ka)]
+    others = range(1, n_ka)
+    chips = range(2, n_dp, 2)
+    vm = pltpu.VMEM
+    kvecs = [send(kvec, "ka", s) for s in others]
+    kfilts = [kfilt] + [send(kfilt, "ka", s) for s in others]
     numbers = jnp.arange(cells, dtype=jnp.int32)[:, None]
     bounds = jnp.stack(
         [
@@ -362,20 +434,43 @@
             jnp.sum((cell_ids < numbers).astype(jnp.int32), axis=1),
         ]
     )
-    vm = pltpu.VMEM
-    waves, factors, quad, ids = call(
+    held = [
+        pltpu.with_memory_space_constraint(x, pltpu.HBM)
+        for x in (feats, coords, cell_ids, recip, kvec, w_in)
+    ]
+    waves, proj_t, ids, coords, recip, kvec = call(
+        prepare_kernel,
+        held,
+        0,
+        [
+            ((2 * own, long), BF16),
+            ((chan, long), BF16),
+            ((1, long), jnp.int32),
+            (coords.shape, F32),
+            (recip.shape, F32),
+            (kvec.shape, jnp.int32),
+        ],
+        [
+            vm((atoms, chan), BF16),
+            vm((chan, chan), BF16),
+            vm((own, 8), F32),
+            pltpu.SemaphoreType.DMA((6,)),
+        ],
+        PREPARE,
+        4,
+        pltpu.HBM,
+    )
+    waves, factors, quad = call(
         functools.partial(waves_kernel, n_ka),
-        "waves",
-        (bounds, feats, coords, cell_ids, recip, w_in, *kvecs),
+        (bounds, waves, proj_t, ids, coords, recip, kvec, *kvecs),
         1,
-        [((2 * k_all, long), BF16), ((cells, chan, 2 * k_all), F32), ((cells, k_all), F32), ((1, long), jnp.int32)],
-        [vm((k_all, 8), F32), vm((chan, long), BF16)],
+        [((2 * k_all, long), BF16), ((cells, chan, 2 * k_all), F32), ((cells, k_all), F32)],
+        [vm((own, 8), F32)],
         LIMIT,
         8,
     )
     act_t, mgrad_t, raw_out, raw_half = call(
         functools.partial(message_kernel, n_ka),
-        "message",
         (bounds, ids, quad, waves, factors, spread, cotan, w_out, *kfilts),
         1,
         [((chan, atoms), BF16), ((chan, long), BF16), ((chan, chan), F32), ((chan, chan), BF16)],
@@ -383,11 +478,9 @@
         LIMIT,
         8,
     )
-    chips = [2 * s for s in range(1, n_dp // 2)]
-    out_parts = [lax.ppermute(raw_half, "dp", routes(s, n_dp)) for s in chips]
+    out_parts = [send(raw_half, "dp", s) for s in chips]
     weights, filter_grad, filter_half = call(
         functools.partial(adjoint_kernel, n_ka),
-        "adjoint",
         (bounds, ids, quad, waves, factors, mgrad_t, spread, *kfilts),
         1,
         [((cells, chan, 2 * k_all), BF16), ((own, chan), F32), ((own, chan), BF16)],
@@ -395,12 +488,11 @@
         LIMIT,
         8,
     )
-    filt_parts = [lax.ppermute(filter_half, "dp", routes(s, n_dp)) for s in chips]
-    (out_sum,) = call(add_kernel, "outsum", (raw_out, *out_parts), 0, [((chan, chan), F32)])
-    out_near = lax.ppermute(out_sum, "dp", routes(1, n_dp))
+    filt_parts = [send(filter_half, "dp", s) for s in chips]
+    (out_sum,) = call(add_kernel, (raw_out, *out_parts), 0, [((chan, chan), F32)])
+    out_near = send(out_sum, "dp", 1)
     update_t, raw_in_t = call(
         update_kernel,
-        "update",
         (bounds, ids, waves, weights, feats),
         1,
         [((chan, atoms), BF16), ((chan, chan), F32)],
@@ -408,29 +500,28 @@
         LIMIT,
         8,
     )
-    other_in = lax.ppermute(raw_in_t, "dp", routes(1, n_dp))
-    (filt_sum,) = call(add_kernel, "filtsum", (filter_grad, *filt_parts), 0, [((own, chan), F32)])
-    filt_near = lax.ppermute(filt_sum, "dp", routes(1, n_dp))
-    (feat_grad,) = call(
-        functools.partial(residual_kernel, True), "featgrad", (cotan, update_t, w_in), 0,
-        [((atoms, chan), BF16)],
-    )
+    (pack,) = call(
+        join_kernel, (raw_in_t, filter_grad, *filt_parts), 0, [((chan + own, chan), F32)]
+    )
+    near = send(pack, "dp", 1)
+    feat_grad = residual(True, cotan, update_t, w_in)
     in_sum, in_half, w_sum, f_sum, f_squares = call(
         chip_kernel,
-        "chip",
-        (raw_in_t, other_in, out_sum, out_near, filt_sum, filt_near),
+        (pack, near, out_sum, out_near),
         0,
-        [((chan, chan), F32), ((chan, chan), BF16), ((chan, chan), F32), ((own, chan), F32), ((8, LANES), F32)],
-    )
-    squares = [f_squares] + [lax.ppermute(f_squares, "ka", routes(s, n_ka)) for s in range(1, n_ka)]
-    in_parts = [in_sum] + [lax.ppermute(in_half, "dp", routes(s, n_dp)) for s in chips]
-    (mixed,) = call(
-        functools.partial(residual_kernel, False), "mixed", (feats, act_t, w_out), 0,
-        [((atoms, chan), BF16)],
-    )
+        [
+            ((chan, chan), F32),
+            ((chan, chan), BF16),
+            ((chan, chan), F32),
+            ((own, chan), F32),
+            ((8, LANES), F32),
+        ],
+    )
+    squares = [f_squares] + [send(f_squares, "ka", s) for s in others]
+    in_parts = [in_sum] + [send(in_half, "dp", s) for s in chips]
+    mixed = residual(False, feats, act_t, w_out)
     grads = call(
         functools.partial(final_kernel, len(in_parts), n_ka),
-        "final",
         (*in_parts, w_sum, f_sum, *squares),
         0,
         [((chan, chan), F32), ((chan, chan), F32), ((own, chan), F32)],
@@ -452,7 +543,7 @@
         P("dp", None),
     )
     return jax.shard_map(
-        body,
+        block,
         mesh=mesh,
         in_specs=placed,
         out_specs=(P("dp", None), P("dp", None), P(), P(), P("ka", None)),

time: 80.2 us -> 76.8 us (0.958)
  local copies, waits for them, and re-layouts: 4.97 us -> 0.03 us
  waiting for transfers between devices: 6.87 us -> 8.78 us
    unnamed x24 -> x12, local copies, waits for them, and re-layouts: 4.97 us -> 0.03 us
    pallas_call x0 -> x2, Pallas kernels: none -> 4.61 us  [residual(): pl.pallas_call(functools.partial(residual_kernel, transposed), out_shape=...]
    pallas_call x10 -> x9, Pallas kernels: 40.5 us -> 36 us  [call(): pl.pallas_call(kernel, out_shape=tuple((jax.ShapeDtypeStruct(*o) for o in...]
    ppermute x21 -> x20, waiting for transfers between devices: 6.87 us -> 8.78 us  [send(): return lax.ppermute(value, axis, routes(step, lax.axis_size(axis)))]
    ppermute x21 -> x20, starting transfers between devices: 25.8 us -> 25.5 us  [send(): return lax.ppermute(value, axis, routes(step, lax.axis_size(axis)))]
  transfers between devices with their start and end apart: 21 -> 20, of which waited for: 5 -> 5; matrix products, arithmetic and copies ran while one was open for 1% -> 1% of each run, Pallas kernels for 31% -> 32%
where the time goes in v2:
time: 76.8 us; the launch traced here: 76.6 us
  Pallas kernels  40.6 us (53%)
  starting transfers between devices  25.5 us (33%)
  waiting for transfers between devices  8.78 us (11%)
  other arithmetic  0.86 us (1%)
  between operations  0.84 us (1%)
    pallas_call x9, Pallas kernels, call(): pl.pallas_call(kernel, out_shape=tuple((jax.ShapeDtypeStruct(*o) for o in...  36 us
    ppermute x20, starting transfers between devices, send(): return lax.ppermute(value, axis, routes(step, lax.axis_size(axis)))  25.5 us
    ppermute x20, waiting for transfers between devices, send(): return lax.ppermute(value, axis, routes(step, lax.axis_size(axis)))  8.78 us
    pallas_call x2, Pallas kernels, residual(): pl.pallas_call(functools.partial(residual_kernel, transposed), out_shape=...  4.61 us
  transfers between devices with their start and end apart: 20, of which 5 were waited for; matrix products, arithmetic and copies ran while one was open for 1% of the time, Pallas kernels for 32%

profile of v2, /device:TPU:0, one launch (start us, length us, event | category | flops | bytes accessed | tf_op | source)
XLA Modules:
  0.0 76.6 jit_solution(15555357779013256979)
XLA Ops:
  0.6 3.1 %collective-permute-start = (s32[3,128]{1,0:T(4,128)}, s32[3,128]{1,0:T(4,128)S(1)}, u32[]{:S(2)}, u32[]{:S(2)}) collective-permute-start(s32[3,128]{1,0:T(4,128)} %kvec_hbm.1), channel_id=1, source_target_pairs={{0,1},{1,0},{2,3},{3,2},{4,5},{5,4},{6,7},{7,6},{8,9},{9,8},{10,11... | collective-permute-start | bytes 4616 | tf_op jit(solution)/shard_map/ppermute | solution.py:413
  3.7 2.5 %collective-permute-start.2 = (s32[3,128]{1,0:T(4,128)}, s32[3,128]{1,0:T(4,128)S(1)}, u32[]{:S(2)}, u32[]{:S(2)}) collective-permute-start(s32[3,128]{1,0:T(4,128)} %kvec_hbm.1), channel_id=1, source_target_pairs={{0,3},{1,2},{2,1},{3,0},{4,7},{5,6},{6,5},{7,4},{8,11},{9,10},{10,... | collective-permute-start | bytes 4616 | tf_op jit(solution)/shard_map/ppermute | solution.py:413
  6.2 0.1 collective-permute-start.1
  6.3 2.9 %collective-permute-start.5 = (f32[128,256]{1,0:T(8,128)}, f32[128,256]{1,0:T(8,128)S(1)}, u32[]{:S(2)}, u32[]{:S(2)}) collective-permute-start(f32[128,256]{1,0:T(8,128)} %refs_7_.3), channel_id=1, source_target_pairs={{0,3},{1,2},{2,1},{3,0},{4,7},{5,6},{6,5},{7,4},{8,11},{9,10},{10,... | collective-permute-start | bytes 393224 | tf_op jit(solution)/shard_map/ppermute | solution.py:413
  9.3 0.3 collective-permute-start.4
  9.6 0.9 %convert_reduce_fusion.1 = (s32[8]{0:T(128)S(1)}, s32[8]{0:T(128)S(1)}) fusion(s32[2048]{0:T(1024)} %bitcast.7), kind=kLoop, calls=%fused_computation.2 | loop fusion | flops 98288 | bytes 8256 | tf_op jit(solution)/shard_map/reduce_sum | solution.py:433
  10.5 0.0 copy-start.2
  10.5 4.5 %shard_map.137 = (bf16[256,2176]{1,0:T(8,128)(2,1)S(1)}, bf16[256,2176]{1,0:T(8,128)(2,1)S(1)}, s32[1,2176]{1,0:T(1,128)S(1)}, f32[3,2048]{1,0:T(4,128)S(1)}, f32[8,9]{1,0:T(8,128)S(1)}, /*index=5*/s32[3,128]{1,0:T(4,128)S(1)}) custom-call(bf16[2048,256]{1,0:T(8,128)(2,1)} %feats.1, f32[3,2048]{1,0:T(4,128)} %coords_hbm.1, s32[1,2048]{1,0:T(1,128)} %ids_hbm.1, ...), custom_call_target="tpu_custom_call" | custom-call | flops 4294967296 | tf_op jit(solution)/shard_map/pallas_call | solution.py:399
  15.0 0.0 collective-permute-done.refs_7_
  15.0 0.0 copy-done.2
  15.1 1.2 %collective-permute-start.3 = (f32[128,256]{1,0:T(8,128)S(1)}, f32[128,256]{1,0:T(8,128)S(1)}, u32[]{:S(2)}, u32[]{:S(2)}) collective-permute-start(f32[128,256]{1,0:T(8,128)S(1)} %copy-done.2), channel_id=1, source_target_pairs={{0,1},{1,0},{2,3},{3,2},{4,5},{5,4},{6,7},{7,6},{8,9},{9,8},{10,11... | collective-permute-start | bytes 393224 | tf_op jit(solution)/shard_map/ppermute | solution.py:413
  16.3 0.0 collective-permute-done.2.refs_9_
  16.3 0.0 collective-permute-done.1.refs_8_
  16.3 0.0 copy-start.1
  16.3 0.0 copy-start.3
  16.3 0.0 copy-start.5
  16.3 9.9 %shard_map.138 = (bf16[1024,2176]{1,0:T(8,128)(2,1)S(1)}, f32[8,256,1024]{2,1,0:T(8,128)S(1)}, f32[8,512]{1,0:T(8,128)S(1)}) custom-call(s32[2,8]{1,0:T(2,128)S(1)} %pad_add_fusion.refs_0_.bounds, bf16[256,2176]{1,0:T(8,128)(2,1)S(1)} %get-tuple-element.32.refs_1_, bf16[256,2176]{1,0:T(8,128)(2,1)S(1)} %get-tuple-element.33.refs_2_, ...), custom_call_target="tpu_custom_call" | custom-call | flops 8589934592 | tf_op jit(solution)/shard_map/pallas_call | solution.py:399
  26.2 0.0 collective-permute-done.5.refs_11_.refs_10_
  26.2 0.0 collective-permute-done.4.refs_10_.refs_9_
  26.2 0.0 collective-permute-done.3.refs_9_.refs_8_
  26.2 0.0 copy-done.1
  26.2 0.0 copy-done.3
  26.2 0.0 copy-done.5
  26.2 8.2 %shard_map.139 = (bf16[256,2048]{1,0:T(8,128)(2,1)S(1)}, bf16[256,2176]{1,0:T(8,128)(2,1)S(1)}, f32[256,256]{1,0:T(8,128)S(1)}, bf16[256,256]{1,0:T(8,128)(2,1)S(1)}) custom-call(s32[2,8]{1,0:T(2,128)S(1)} %pad_add_fusion.refs_0_.bounds, s32[1,2176]{1,0:T(1,128)S(1)} %get-tuple-element.31.refs_3_.refs_1_.ids, f32[8,512]{1,0:T(8,128)S(1)} %get-tuple-element.37.refs_2_, ...), custom_call_target="tpu_custom_call" | custom-call | flops 8589934592 | tf_op jit(solution)/shard_map/pallas_call | solution.py:399
  34.4 0.0 copy-start
  34.5 6.4 %shard_map.141 = (bf16[8,256,1024]{2,1,0:T(8,128)(2,1)S(1)}, f32[128,256]{1,0:T(8,128)S(1)}, bf16[128,256]{1,0:T(8,128)(2,1)S(1)}) custom-call(s32[2,8]{1,0:T(2,128)S(1)} %pad_add_fusion.refs_0_.bounds, s32[1,2176]{1,0:T(1,128)S(1)} %get-tuple-element.31.refs_3_.refs_1_.ids, f32[8,512]{1,0:T(8,128)S(1)} %get-tuple-element.37.refs_2_, ...), custom_call_target="tpu_custom_call" | custom-call | flops 8589934592 | tf_op jit(solution)/shard_map/pallas_call | solution.py:399
  40.8 2.9 %collective-permute-start.8 = (bf16[128,256]{1,0:T(8,128)(2,1)S(1)}, bf16[128,256]{1,0:T(8,128)(2,1)S(1)}, u32[]{:S(2)}, u32[]{:S(2)}) collective-permute-start(bf16[128,256]{1,0:T(8,128)(2,1)S(1)} %get-tuple-element.46), channel_id=1, source_target_pairs={{0,24},{4,28},{8,16},{12,20},{16,8},{20,12},{24,0},{28,4},{1,25},{... | collective-permute-start | bytes 196616 | tf_op jit(solution)/shard_map/ppermute | solution.py:413
  43.8 0.5 collective-permute-start.7
  44.3 0.1 collective-permute-start.6
  44.4 2.8 %collective-permute-start.12 = (bf16[256,256]{1,0:T(8,128)(2,1)S(1)}, bf16[256,256]{1,0:T(8,128)(2,1)S(1)}, u32[]{:S(2)}, u32[]{:S(2)}) collective-permute-start(bf16[256,256]{1,0:T(8,128)(2,1)S(1)} %get-tuple-element.48), channel_id=1, source_target_pairs={{0,24},{4,28},{8,16},{12,20},{16,8},{20,12},{24,0},{28,4},{1,25},{... | collective-permute-start | bytes 393224 | tf_op jit(solution)/shard_map/ppermute | solution.py:413
  47.3 0.5 collective-permute-start.11
  47.8 0.0 copy-done
  47.8 5.7 %shard_map.142 = (bf16[256,2048]{1,0:T(8,128)(2,1)S(1)}, f32[256,256]{1,0:T(8,128)S(1)}) custom-call(s32[2,8]{1,0:T(2,128)S(1)} %pad_add_fusion.refs_0_.bounds, s32[1,2176]{1,0:T(1,128)S(1)} %get-tuple-element.31.refs_3_.refs_1_.ids, bf16[1024,2176]{1,0:T(8,128)(2,1)S(1)} %get-tuple-element.38.refs_3_.waves, ...), custom_call_target="tpu_custom_call" | custom-call | flops 8589934592 | tf_op jit(solution)/shard_map/pallas_call | solution.py:399
  53.4 0.0 collective-permute-done.8.refs_2_
  53.5 0.4 collective-permute-start.10
  53.8 0.0 collective-permute-done.7.refs_1_
  53.8 0.0 collective-permute-done.6.refs_0_
  53.8 0.1 shard_map.144.pack
  53.9 0.1 collective-permute-start.9
  54.0 0.0 collective-permute-done.12.refs_3_
  54.0 0.0 collective-permute-done.11.refs_2_
  54.0 4.5 %collective-permute-done.10.refs_1_ = bf16[256,256]{1,0:T(8,128)(2,1)S(1)} collective-permute-done((bf16[256,256]{1,0:T(8,128)(2,1)S(1)}, bf16[256,256]{1,0:T(8,128)(2,1)S(1)}, u32[]{:S(2)}, u32[]{:S(2)}) %collective-permute-start.10) | collective-permute-done | bytes 131104 | tf_op jit(solution)/shard_map/ppermute | solution.py:413
  58.5 0.1 shard_map.145.out_sum
  58.6 0.1 collective-permute-start.13
  58.6 1.5 %collective-permute-done.13.out_near = f32[256,256]{1,0:T(8,128)S(1)} collective-permute-done((f32[256,256]{1,0:T(8,128)S(1)}, f32[256,256]{1,0:T(8,128)S(1)}, u32[]{:S(2)}, u32[]{:S(2)}) %collective-permute-start.13) | collective-permute-done | bytes 262176 | tf_op jit(solution)/shard_map/ppermute | solution.py:413
  60.2 0.0 collective-permute-done.9.near
  60.2 0.2 shard_map.146
  60.3 0.0 copy-start.4
  60.3 2.9 %collective-permute-start.19 = (f32[8,128]{1,0:T(8,128)S(1)}, f32[8,128]{1,0:T(8,128)S(1)}, u32[]{:S(2)}, u32[]{:S(2)}) collective-permute-start(f32[8,128]{1,0:T(8,128)S(1)} %get-tuple-element.53.refs_6_), channel_id=1, source_target_pairs={{0,3},{1,2},{2,1},{3,0},{4,7},{5,6},{6,5},{7,4},{8,11},{9,10},{10,... | collective-permute-start | bytes 12296 | tf_op jit(solution)/shard_map/ppermute | solution.py:413
  63.2 2.3 %shard_map.140 = bf16[2048,256]{1,0:T(8,128)(2,1)} custom-call(bf16[2048,256]{1,0:T(8,128)(2,1)S(1)} %copy-done, bf16[256,2048]{1,0:T(8,128)(2,1)S(1)} %get-tuple-element.40.values_t, bf16[256,256]{1,0:T(8,128)(2,1)S(1)} %copy-done.3), custom_call_target="tpu_custom_call" | custom-call | flops 2147483648 | tf_op jit(solution)/shard_map/pallas_call | solution.py:331
  65.5 0.0 collective-permute-start.18
  65.5 1.5 %collective-permute-start.17 = (f32[8,128]{1,0:T(8,128)S(1)}, f32[8,128]{1,0:T(8,128)S(1)}, u32[]{:S(2)}, u32[]{:S(2)}) collective-permute-start(f32[8,128]{1,0:T(8,128)S(1)} %get-tuple-element.53.refs_6_), channel_id=1, source_target_pairs={{0,1},{1,0},{2,3},{3,2},{4,5},{5,4},{6,7},{7,6},{8,9},{9,8},{10,11... | collective-permute-start | bytes 12296 | tf_op jit(solution)/shard_map/ppermute | solution.py:413
  67.0 1.2 %collective-permute-start.16 = (bf16[256,256]{1,0:T(8,128)(2,1)S(1)}, bf16[256,256]{1,0:T(8,128)(2,1)S(1)}, u32[]{:S(2)}, u32[]{:S(2)}) collective-permute-start(bf16[256,256]{1,0:T(8,128)(2,1)S(1)} %get-tuple-element.50), channel_id=1, source_target_pairs={{0,24},{4,28},{8,16},{12,20},{16,8},{20,12},{24,0},{28,4},{1,25},{... | collective-permute-start | bytes 393224 | tf_op jit(solution)/shard_map/ppermute | solution.py:413
  68.3 0.5 collective-permute-start.15
  68.8 0.0 collective-permute-done.19.refs_9_
  68.8 1.7 %collective-permute-start.14 = (bf16[256,256]{1,0:T(8,128)(2,1)S(1)}, bf16[256,256]{1,0:T(8,128)(2,1)S(1)}, u32[]{:S(2)}, u32[]{:S(2)}) collective-permute-start(bf16[256,256]{1,0:T(8,128)(2,1)S(1)} %get-tuple-element.50), channel_id=1, source_target_pairs={{0,8},{4,12},{8,0},{12,4},{16,24},{20,28},{24,16},{28,20},{1,9},{5... | collective-permute-start | bytes 393224 | tf_op jit(solution)/shard_map/ppermute | solution.py:413
  70.5 0.0 copy-done.4
  70.5 2.3 %shard_map.143 = bf16[2048,256]{1,0:T(8,128)(2,1)} custom-call(bf16[2048,256]{1,0:T(8,128)(2,1)S(1)} %copy-done.1, bf16[256,2048]{1,0:T(8,128)(2,1)S(1)} %get-tuple-element.43.values_t, bf16[256,256]{1,0:T(8,128)(2,1)S(1)} %copy-done.4), custom_call_target="tpu_custom_call" | custom-call | flops 2147483648 | tf_op jit(solution)/shard_map/pallas_call | solution.py:331
  72.8 0.0 collective-permute-done.18.refs_8_
  72.8 0.0 collective-permute-done.17.refs_7_
  72.8 1.2 %collective-permute-done.16.refs_3_ = bf16[256,256]{1,0:T(8,128)(2,1)S(1)} collective-permute-done((bf16[256,256]{1,0:T(8,128)(2,1)S(1)}, bf16[256,256]{1,0:T(8,128)(2,1)S(1)}, u32[]{:S(2)}, u32[]{:S(2)}) %collective-permute-start.16) | collective-permute-done | bytes 131104 | tf_op jit(solution)/shard_map/ppermute | solution.py:413
  74.0 1.4 %collective-permute-done.15.refs_2_ = bf16[256,256]{1,0:T(8,128)(2,1)S(1)} collective-permute-done((bf16[256,256]{1,0:T(8,128)(2,1)S(1)}, bf16[256,256]{1,0:T(8,128)(2,1)S(1)}, u32[]{:S(2)}, u32[]{:S(2)}) %collective-permute-start.15) | collective-permute-done | bytes 131104 | tf_op jit(solution)/shard_map/ppermute | solution.py:413
  75.4 0.1 collective-permute-done.14.refs_1_
  75.5 1.1 %shard_map.147 = (f32[256,256]{1,0:T(8,128)}, f32[256,256]{1,0:T(8,128)}, f32[128,256]{1,0:T(8,128)}) custom-call(f32[256,256]{1,0:T(8,128)S(1)} %get-tuple-element.49.refs_0_, bf16[256,256]{1,0:T(8,128)(2,1)S(1)} %collective-permute-done.14.refs_1_, bf16[256,256]{1,0:T(8,128)(2,1)S(1)} %collective-permute-done.15.refs_2_, ...), custom_call_target="tpu_custom_call" | custom-call | flops 2147483648 | tf_op jit(solution)/shard_map/pallas_call | solution.py:399
  (1 shorter events, 0.0 us)
Async XLA Ops:
  0.6 14.4 %collective-permute-start = (s32[3,128]{1,0:T(4,128)}, s32[3,128]{1,0:T(4,128)S(1)}, u32[]{:S(2)}, u32[]{:S(2)}) collective-permute-start(s32[3,128]{1,0:T(4,128)} %kvec_hbm.1), channel_id=1, source_target_pairs={{0,1},{1,0},{2,3},{3,2},{4,5},{5,4},{6,7},{7,6},{8,9},{9,8},{10,11... | collective-permute-start | bytes 4616 | tf_op jit(solution)/shard_map/ppermute | solution.py:413
  3.7 12.5 %collective-permute-start.2 = (s32[3,128]{1,0:T(4,128)}, s32[3,128]{1,0:T(4,128)S(1)}, u32[]{:S(2)}, u32[]{:S(2)}) collective-permute-start(s32[3,128]{1,0:T(4,128)} %kvec_hbm.1), channel_id=1, source_target_pairs={{0,3},{1,2},{2,1},{3,0},{4,7},{5,6},{6,5},{7,4},{8,11},{9,10},{10,... | collective-permute-start | bytes 4616 | tf_op jit(solution)/shard_map/ppermute | solution.py:413
  6.2 10.0 %collective-permute-start.1 = (s32[3,128]{1,0:T(4,128)}, s32[3,128]{1,0:T(4,128)S(1)}, u32[]{:S(2)}, u32[]{:S(2)}) collective-permute-start(s32[3,128]{1,0:T(4,128)} %kvec_hbm.1), channel_id=1, source_target_pairs={{0,2},{1,3},{2,0},{3,1},{4,6},{5,7},{6,4},{7,5},{8,10},{9,11},{10,... | collective-permute-start | bytes 4616 | tf_op jit(solution)/shard_map/ppermute | solution.py:413
  6.3 19.8 %collective-permute-start.5 = (f32[128,256]{1,0:T(8,128)}, f32[128,256]{1,0:T(8,128)S(1)}, u32[]{:S(2)}, u32[]{:S(2)}) collective-permute-start(f32[128,256]{1,0:T(8,128)} %refs_7_.3), channel_id=1, source_target_pairs={{0,3},{1,2},{2,1},{3,0},{4,7},{5,6},{6,5},{7,4},{8,11},{9,10},{10,... | collective-permute-start | bytes 393224 | tf_op jit(solution)/shard_map/ppermute | solution.py:413
  9.3 16.9 %collective-permute-start.4 = (f32[128,256]{1,0:T(8,128)}, f32[128,256]{1,0:T(8,128)S(1)}, u32[]{:S(2)}, u32[]{:S(2)}) collective-permute-start(f32[128,256]{1,0:T(8,128)} %refs_7_.3), channel_id=1, source_target_pairs={{0,2},{1,3},{2,0},{3,1},{4,6},{5,7},{6,4},{7,5},{8,10},{9,11},{10,... | collective-permute-start | bytes 393224 | tf_op jit(solution)/shard_map/ppermute | solution.py:413
  10.5 4.6 %copy-start.2 = (f32[128,256]{1,0:T(8,128)S(1)}, f32[128,256]{1,0:T(8,128)}, u32[]{:S(2)}) copy-start(f32[128,256]{1,0:T(8,128)} %refs_7_.3) | copy-start | bytes 393220
  15.1 11.1 %collective-permute-start.3 = (f32[128,256]{1,0:T(8,128)S(1)}, f32[128,256]{1,0:T(8,128)S(1)}, u32[]{:S(2)}, u32[]{:S(2)}) collective-permute-start(f32[128,256]{1,0:T(8,128)S(1)} %copy-done.2), channel_id=1, source_target_pairs={{0,1},{1,0},{2,3},{3,2},{4,5},{5,4},{6,7},{7,6},{8,9},{9,8},{10,11... | collective-permute-start | bytes 393224 | tf_op jit(solution)/shard_map/ppermute | solution.py:413
  16.3 10.0 %copy-start.1 = (bf16[2048,256]{1,0:T(8,128)(2,1)S(1)}, bf16[2048,256]{1,0:T(8,128)(2,1)}, u32[]{:S(2)}) copy-start(bf16[2048,256]{1,0:T(8,128)(2,1)} %base.3) | copy-start | bytes 3145732
  16.3 10.0 %copy-start.3 = (bf16[256,256]{1,0:T(8,128)(2,1)S(1)}, bf16[256,256]{1,0:T(8,128)(2,1)}, u32[]{:S(2)}) copy-start(bf16[256,256]{1,0:T(8,128)(2,1)} %weight.2) | copy-start | bytes 393220
  16.3 10.0 %copy-start.5 = (f32[256]{0:T(256)S(1)}, f32[256]{0:T(256)}, u32[]{:S(2)}) copy-start(f32[256]{0:T(256)} %param.18) | copy-start | bytes 3076
  34.4 13.3 %copy-start = (bf16[2048,256]{1,0:T(8,128)(2,1)S(1)}, bf16[2048,256]{1,0:T(8,128)(2,1)}, u32[]{:S(2)}) copy-start(bf16[2048,256]{1,0:T(8,128)(2,1)} %feats.1) | copy-start | bytes 3145732
  40.8 12.6 %collective-permute-start.8 = (bf16[128,256]{1,0:T(8,128)(2,1)S(1)}, bf16[128,256]{1,0:T(8,128)(2,1)S(1)}, u32[]{:S(2)}, u32[]{:S(2)}) collective-permute-start(bf16[128,256]{1,0:T(8,128)(2,1)S(1)} %get-tuple-element.46), channel_id=1, source_target_pairs={{0,24},{4,28},{8,16},{12,20},{16,8},{20,12},{24,0},{28,4},{1,25},{... | collective-permute-start | bytes 196616 | tf_op jit(solution)/shard_map/ppermute | solution.py:413
  43.8 10.0 %collective-permute-start.7 = (bf16[128,256]{1,0:T(8,128)(2,1)S(1)}, bf16[128,256]{1,0:T(8,128)(2,1)S(1)}, u32[]{:S(2)}, u32[]{:S(2)}) collective-permute-start(bf16[128,256]{1,0:T(8,128)(2,1)S(1)} %get-tuple-element.46), channel_id=1, source_target_pairs={{0,16},{4,20},{8,24},{12,28},{16,0},{20,4},{24,8},{28,12},{1,17},{... | collective-permute-start | bytes 196616 | tf_op jit(solution)/shard_map/ppermute | solution.py:413
  44.3 9.5 %collective-permute-start.6 = (bf16[128,256]{1,0:T(8,128)(2,1)S(1)}, bf16[128,256]{1,0:T(8,128)(2,1)S(1)}, u32[]{:S(2)}, u32[]{:S(2)}) collective-permute-start(bf16[128,256]{1,0:T(8,128)(2,1)S(1)} %get-tuple-element.46), channel_id=1, source_target_pairs={{0,8},{4,12},{8,0},{12,4},{16,24},{20,28},{24,16},{28,20},{1,9},{5... | collective-permute-start | bytes 196616 | tf_op jit(solution)/shard_map/ppermute | solution.py:413
  44.4 9.5 %collective-permute-start.12 = (bf16[256,256]{1,0:T(8,128)(2,1)S(1)}, bf16[256,256]{1,0:T(8,128)(2,1)S(1)}, u32[]{:S(2)}, u32[]{:S(2)}) collective-permute-start(bf16[256,256]{1,0:T(8,128)(2,1)S(1)} %get-tuple-element.48), channel_id=1, source_target_pairs={{0,24},{4,28},{8,16},{12,20},{16,8},{20,12},{24,0},{28,4},{1,25},{... | collective-permute-start | bytes 393224 | tf_op jit(solution)/shard_map/ppermute | solution.py:413
  47.3 6.7 %collective-permute-start.11 = (bf16[256,256]{1,0:T(8,128)(2,1)S(1)}, bf16[256,256]{1,0:T(8,128)(2,1)S(1)}, u32[]{:S(2)}, u32[]{:S(2)}) collective-permute-start(bf16[256,256]{1,0:T(8,128)(2,1)S(1)} %get-tuple-element.48), channel_id=1, source_target_pairs={{0,16},{4,20},{8,24},{12,28},{16,0},{20,4},{24,8},{28,12},{1,17},{... | collective-permute-start | bytes 393224 | tf_op jit(solution)/shard_map/ppermute | solution.py:413
  53.5 5.0 %collective-permute-start.10 = (bf16[256,256]{1,0:T(8,128)(2,1)S(1)}, bf16[256,256]{1,0:T(8,128)(2,1)S(1)}, u32[]{:S(2)}, u32[]{:S(2)}) collective-permute-start(bf16[256,256]{1,0:T(8,128)(2,1)S(1)} %get-tuple-element.48), channel_id=1, source_target_pairs={{0,8},{4,12},{8,0},{12,4},{16,24},{20,28},{24,16},{28,20},{1,9},{5... | collective-permute-start | bytes 393224 | tf_op jit(solution)/shard_map/ppermute | solution.py:413
  53.9 6.3 %collective-permute-start.9 = (f32[384,256]{1,0:T(8,128)S(1)}, f32[384,256]{1,0:T(8,128)S(1)}, u32[]{:S(2)}, u32[]{:S(2)}) collective-permute-start(f32[384,256]{1,0:T(8,128)S(1)} %shard_map.144.pack), channel_id=1, source_target_pairs={{0,4},{4,0},{8,12},{12,8},{16,20},{20,16},{24,28},{28,24},{1,5},{5... | collective-permute-start | bytes 1179656 | tf_op jit(solution)/shard_map/ppermute | solution.py:413
  58.6 1.6 %collective-permute-start.13 = (f32[256,256]{1,0:T(8,128)S(1)}, f32[256,256]{1,0:T(8,128)S(1)}, u32[]{:S(2)}, u32[]{:S(2)}) collective-permute-start(f32[256,256]{1,0:T(8,128)S(1)} %shard_map.145.out_sum), channel_id=1, source_target_pairs={{0,4},{4,0},{8,12},{12,8},{16,20},{20,16},{24,28},{28,24},{1,5},{5... | collective-permute-start | bytes 786440 | tf_op jit(solution)/shard_map/ppermute | solution.py:413
  60.3 10.2 %copy-start.4 = (bf16[256,256]{1,0:T(8,128)(2,1)S(1)}, bf16[256,256]{1,0:T(8,128)(2,1)}, u32[]{:S(2)}) copy-start(bf16[256,256]{1,0:T(8,128)(2,1)} %weight.3) | copy-start | bytes 393220
  60.3 8.5 %collective-permute-start.19 = (f32[8,128]{1,0:T(8,128)S(1)}, f32[8,128]{1,0:T(8,128)S(1)}, u32[]{:S(2)}, u32[]{:S(2)}) collective-permute-start(f32[8,128]{1,0:T(8,128)S(1)} %get-tuple-element.53.refs_6_), channel_id=1, source_target_pairs={{0,3},{1,2},{2,1},{3,0},{4,7},{5,6},{6,5},{7,4},{8,11},{9,10},{10,... | collective-permute-start | bytes 12296 | tf_op jit(solution)/shard_map/ppermute | solution.py:413
  65.5 7.3 %collective-permute-start.18 = (f32[8,128]{1,0:T(8,128)S(1)}, f32[8,128]{1,0:T(8,128)S(1)}, u32[]{:S(2)}, u32[]{:S(2)}) collective-permute-start(f32[8,128]{1,0:T(8,128)S(1)} %get-tuple-element.53.refs_6_), channel_id=1, source_target_pairs={{0,2},{1,3},{2,0},{3,1},{4,6},{5,7},{6,4},{7,5},{8,10},{9,11},{10,... | collective-permute-start | bytes 12296 | tf_op jit(solution)/shard_map/ppermute | solution.py:413
  65.5 7.3 %collective-permute-start.17 = (f32[8,128]{1,0:T(8,128)S(1)}, f32[8,128]{1,0:T(8,128)S(1)}, u32[]{:S(2)}, u32[]{:S(2)}) collective-permute-start(f32[8,128]{1,0:T(8,128)S(1)} %get-tuple-element.53.refs_6_), channel_id=1, source_target_pairs={{0,1},{1,0},{2,3},{3,2},{4,5},{5,4},{6,7},{7,6},{8,9},{9,8},{10,11... | collective-permute-start | bytes 12296 | tf_op jit(solution)/shard_map/ppermute | solution.py:413
  67.0 7.0 %collective-permute-start.16 = (bf16[256,256]{1,0:T(8,128)(2,1)S(1)}, bf16[256,256]{1,0:T(8,128)(2,1)S(1)}, u32[]{:S(2)}, u32[]{:S(2)}) collective-permute-start(bf16[256,256]{1,0:T(8,128)(2,1)S(1)} %get-tuple-element.50), channel_id=1, source_target_pairs={{0,24},{4,28},{8,16},{12,20},{16,8},{20,12},{24,0},{28,4},{1,25},{... | collective-permute-start | bytes 393224 | tf_op jit(solution)/shard_map/ppermute | solution.py:413
  68.3 7.2 %collective-permute-start.15 = (bf16[256,256]{1,0:T(8,128)(2,1)S(1)}, bf16[256,256]{1,0:T(8,128)(2,1)S(1)}, u32[]{:S(2)}, u32[]{:S(2)}) collective-permute-start(bf16[256,256]{1,0:T(8,128)(2,1)S(1)} %get-tuple-element.50), channel_id=1, source_target_pairs={{0,16},{4,20},{8,24},{12,28},{16,0},{20,4},{24,8},{28,12},{1,17},{... | collective-permute-start | bytes 393224 | tf_op jit(solution)/shard_map/ppermute | solution.py:413
  68.8 6.8 %collective-permute-start.14 = (bf16[256,256]{1,0:T(8,128)(2,1)S(1)}, bf16[256,256]{1,0:T(8,128)(2,1)S(1)}, u32[]{:S(2)}, u32[]{:S(2)}) collective-permute-start(bf16[256,256]{1,0:T(8,128)(2,1)S(1)} %get-tuple-element.50), channel_id=1, source_target_pairs={{0,8},{4,12},{8,0},{12,4},{16,24},{20,28},{24,16},{28,20},{1,9},{5... | collective-permute-start | bytes 393224 | tf_op jit(solution)/shard_map/ppermute | solution.py:413

commit v3 on v2

--- a/solution.py
+++ b/solution.py
@@ -15,7 +15,6 @@
 MOST = 1024
 LIMIT = 24 << 20
 SMALL = 6 << 20
-PREPARE = 16 << 20
 FLOPS_PER_MICRO = 1 << 30
 LOG2_E = 1.4426950408889634
 COS_TERMS = (
@@ -140,34 +139,62 @@
 
 def vector_columns(kvec):
     rows = kvec[...].astype(F32)
-    return jnp.concatenate([rows, jnp.zeros((5, rows.shape[1]), F32)], axis=0).T
-
-
-def prepare_kernel(
-    feats_hbm, coords_hbm, ids_hbm, recip_hbm, kvec_hbm, w_in_hbm,
-    waves, proj_t, ids, coords, recip, kvec, feats, w_in, kcols, sems,
-):
-    atoms, chan = feats.shape
-    moves = (
-        (kvec_hbm, kvec),
-        (coords_hbm, coords),
-        (w_in_hbm, w_in),
-        (feats_hbm, feats),
-        (ids_hbm, ids.at[:, :atoms]),
-        (recip_hbm, recip),
-    )
+    if rows.shape[0] == 3:
+        rows = jnp.concatenate([rows, jnp.zeros((5, rows.shape[1]), F32)], axis=0)
+    return rows.T
+
+
+def start_copies(sems, *moves):
     copies = [pltpu.make_async_copy(a, b, sems.at[i]) for i, (a, b) in enumerate(moves)]
     for copy in copies:
         copy.start()
+    return copies
+
+
+def prepare_kernel(
+    coords_hbm, ids_hbm, recip_hbm, kvec_hbm, kfilt_hbm,
+    waves, ids, coords, recip, kvec, kfilt, kcols, sems,
+):
+    atoms = coords.shape[1]
+    copies = start_copies(
+        sems,
+        (kvec_hbm, kvec),
+        (coords_hbm, coords),
+        (ids_hbm, ids.at[:, :atoms]),
+        (recip_hbm, recip),
+        (kfilt_hbm, kfilt),
+    )
     ids[:, atoms:] = jnp.full((1, LANES), -1, jnp.int32)
     waves[:, atoms:] = jnp.zeros((waves.shape[0], LANES), BF16)
-    proj_t[:, atoms:] = jnp.zeros((chan, LANES), BF16)
     copies[0].wait()
     copies[1].wait()
     kcols[...] = vector_columns(kvec)
     fill_waves(waves, 0, kcols, coords)
-    copies[2].wait()
-    copies[3].wait()
+    for copy in copies[2:]:
+        copy.wait()
+
+
+def pair_kernel(kvec, other_kvec, kfilt, other_kfilt, kvecs, kfilts):
+    count = kvec.shape[0]
+    for j in range(count):
+        for at, source in ((j, kvec), (j + count, other_kvec)):
+            rows = source[j].astype(F32)
+            if rows.shape[0] == 3:
+                rows = jnp.concatenate([rows, jnp.zeros((5, rows.shape[1]), F32)], axis=0)
+            kvecs[at] = rows
+        kfilts[j] = kfilt[j]
+        kfilts[j + count] = other_kfilt[j]
+
+
+def project_kernel(coords, kvecs, feats_hbm, w_in_hbm, waves, proj_t, feats, w_in, kcols, sems):
+    atoms, chan = feats.shape
+    copies = start_copies(sems, (w_in_hbm, w_in), (feats_hbm, feats))
+    waves[:, atoms:] = jnp.zeros((waves.shape[0], LANES), BF16)
+    proj_t[:, atoms:] = jnp.zeros((chan, LANES), BF16)
+    kcols[...] = vector_columns(kvecs.at[1])
+    fill_waves(waves, 0, kcols, coords)
+    for copy in copies:
+        copy.wait()
 
     def project(t, carry):
         at = pl.ds(pl.multiple_of(t * TILE, TILE), TILE)
@@ -175,24 +202,23 @@
         return carry
 
     lax.fori_loop(0, atoms // TILE, project, 0)
-    copies[4].wait()
-    copies[5].wait()
 
 
 def waves_kernel(n_ka, *refs):
-    bounds, own_waves, proj_t, ids, coords, recip = refs[:6]
-    kvecs = refs[6 : 6 + n_ka]
-    waves, factors, quad, kcols = refs[6 + n_ka :]
+    bounds, first, second, proj_t, ids, coords, recip = refs[:7]
+    waves, factors, quad, kcols = refs[-4:]
+    kvecs = [ref.at[j] for ref in refs[7:-4] for j in range(ref.shape[0])]
     atoms = coords.shape[1]
     own = kvecs[0].shape[1]
     cells = recip.shape[0]
-    waves[: 2 * own, :] = own_waves[...]
-    waves[2 * own :, atoms:] = jnp.zeros((2 * own * (n_ka - 1), LANES), BF16)
-    for j in range(1, n_ka):
+    waves[: 2 * own, :] = first[...]
+    waves[2 * own : 4 * own, :] = second[...]
+    waves[4 * own :, atoms:] = jnp.zeros((2 * own * (n_ka - 2), LANES), BF16)
+    for j in range(2, n_ka):
         kcols[...] = vector_columns(kvecs[j])
         fill_waves(waves, 2 * own * j, kcols, coords)
     for j in range(n_ka):
-        rows = kvecs[j][...].astype(F32)
+        rows = kvecs[j][...]
         squared = jnp.zeros((cells, own), F32)
         for r in range(3):
             part = recip[:, 3 * r : 3 * r + 1] * rows[0:1, :]
@@ -213,15 +239,22 @@
     lax.fori_loop(0, cells, cell_step, 0)
 
 
+def filters_first(filt_t, kfilts):
+    chunk = 0
+    for ref in kfilts:
+        own = ref.shape[1]
+        for j in range(ref.shape[0]):
+            filt_t[:, chunk * own : (chunk + 1) * own] = ref[j].T
+            chunk += 1
+    return own
+
+
 def message_kernel(n_ka, *refs):
     bounds, ids, quad, waves, factors, spread, cotan, w_out = refs[:8]
-    kfilts = refs[8 : 8 + n_ka]
-    act_t, mgrad_t, raw_out, raw_half, filt_t, width_cols, weights, mess_t = refs[8 + n_ka :]
+    act_t, mgrad_t, raw_out, raw_half, filt_t, width_cols, weights, mess_t = refs[-8:]
     atoms, chan = cotan.shape
-    own = kfilts[0].shape[0]
     cells = quad.shape[0]
-    for j in range(n_ka):
-        filt_t[:, j * own : (j + 1) * own] = kfilts[j][...].T
+    own = filters_first(filt_t, refs[8:-8])
     width_cols[...] = column_to_lanes(spread[...] * (-LOG2_E))
 
     def cell_step(cell, carry):
@@ -258,13 +291,10 @@
 
 def adjoint_kernel(n_ka, *refs):
     bounds, ids, quad, waves, factors, mgrad_t, spread = refs[:7]
-    kfilts = refs[7 : 7 + n_ka]
-    weights, filter_grad, filter_half, filt_t, width_cols, total, grad_t = refs[7 + n_ka :]
+    weights, filter_grad, filter_half, filt_t, width_cols, total, grad_t = refs[-7:]
     atoms = mgrad_t.shape[1] - LANES
-    own = kfilts[0].shape[0]
     cells = quad.shape[0]
-    for j in range(n_ka):
-        filt_t[:, j * own : (j + 1) * own] = kfilts[j][...].T
+    own = filters_first(filt_t, refs[7:-7])
     width_cols[...] = column_to_lanes(spread[...] * (-LOG2_E))
     grad_t[...] = jnp.zeros_like(grad_t)
 
@@ -345,20 +375,21 @@
     )(base, values_t, weight)
 
 
-def join_kernel(raw_in_t, filt, *refs):
+def join_kernel(raw_in_t, raw_out, filt, *refs):
     pack = refs[-1]
     chan = raw_in_t.shape[0]
     pack[:chan, :] = raw_in_t[...]
-    pack[chan:, :] = total_of(filt, refs[:-1])
-
-
-def chip_kernel(pack, near, out_sum, out_near, in_sum, in_half, w_sum, f_sum, f_squares):
-    chan = out_sum.shape[0]
+    pack[chan : 2 * chan, :] = total_of(raw_out, refs[0:1])
+    pack[2 * chan :, :] = total_of(filt, refs[1:-1])
+
+
+def chip_kernel(pack, near, in_sum, in_half, w_sum, f_sum, f_squares):
+    chan = in_sum.shape[0]
     value = pack[:chan, :] + near[:chan, :]
     in_sum[...] = value
     in_half[...] = value.astype(BF16)
-    w_sum[...] = out_sum[...] + out_near[...]
-    filt = pack[chan:, :] + near[chan:, :]
+    w_sum[...] = pack[chan : 2 * chan, :] + near[chan : 2 * chan, :]
+    filt = pack[2 * chan :, :] + near[2 * chan :, :]
     f_sum[...] = filt
     f_squares[...] = jnp.broadcast_to(
         jnp.sum(jnp.sum(filt * filt, axis=0, keepdims=True), axis=1, keepdims=True),
@@ -373,22 +404,21 @@
     return value
 
 
-def add_kernel(*refs):
-    refs[-1][...] = total_of(refs[0], refs[1:-1])
+def add_kernel(first, second, *outs):
+    value = first[...] + second[...].astype(F32)
+    for out in outs:
+        out[...] = value.astype(out.dtype)
 
 
 def final_kernel(n_chip, n_ka, *refs):
     in_parts = refs[:n_chip]
-    raw_out, filt = refs[n_chip : n_chip + 2]
-    squares = refs[n_chip + 2 : n_chip + 2 + n_ka]
-    g_in, g_out, g_filt = refs[n_chip + 2 + n_ka :]
+    raw_out, filt, squares, g_in, g_out, g_filt = refs[n_chip:]
     raw_in = total_of(in_parts[0], in_parts[1:])
     out = raw_out[...]
     both = raw_in * raw_in + out * out
     weight_squares = jnp.sum(jnp.sum(both, axis=0, keepdims=True), axis=1, keepdims=True)
     weight_scale = lax.rsqrt(weight_squares / (2 * raw_in.size) + 1e-06)
-    filter_squares = total_of(squares[0], squares[1:])[0:1, 0:1]
-    filter_scale = lax.rsqrt(filter_squares / (n_ka * filt.size) + 1e-06)
+    filter_scale = lax.rsqrt(squares[0:1, 0:1] / (n_ka * filt.size) + 1e-06)
     g_in[...] = (raw_in * weight_scale).T
     g_out[...] = out * weight_scale
     g_filt[...] = filt[...] * filter_scale
@@ -396,10 +426,12 @@
 
 def call(kernel, operands, smem, outs, scratch=(), limit=SMALL, micros=2, space=pltpu.VMEM):
     vmem = pl.BlockSpec(memory_space=pltpu.VMEM)
+    rest = len(operands) - smem
+    spaces = space if isinstance(space, tuple) else (space,) * rest
     return pl.pallas_call(
         kernel,
         out_shape=tuple(jax.ShapeDtypeStruct(*o) for o in outs),
-        in_specs=[pl.BlockSpec(memory_space=pltpu.SMEM)] * smem + [pl.BlockSpec(memory_space=space)] * (len(operands) - smem),
+        in_specs=[pl.BlockSpec(memory_space=x) for x in (pltpu.SMEM,) * smem + spaces],
         out_specs=tuple(vmem for _ in outs),
         scratch_shapes=list(scratch),
         compiler_params=pltpu.CompilerParams(vmem_limit_bytes=limit),
@@ -409,8 +441,16 @@
     )(*operands)
 
 
+def in_hbm(value):
+    return pltpu.with_memory_space_constraint(value, pltpu.HBM)
+
+
 def send(value, axis, step):
     return lax.ppermute(value, axis, routes(step, lax.axis_size(axis)))
+
+
+def doubling(first, size):
+    return [first << i for i in range(size.bit_length()) if first << i < size]
 
 
 def block(feats, coords, cell_ids, recip, kvec, w_in, w_out, kfilt, spread, cotan):
@@ -422,11 +462,11 @@
     cells = recip.shape[1]
     long = atoms + LANES
     recip, spread = recip[0], spread[None]
-    others = range(1, n_ka)
     chips = range(2, n_dp, 2)
     vm = pltpu.VMEM
-    kvecs = [send(kvec, "ka", s) for s in others]
-    kfilts = [kfilt] + [send(kfilt, "ka", s) for s in others]
+    dma = pltpu.SemaphoreType.DMA
+    near_kvec = send(kvec[None], "ka", 1)
+    near_kfilt = send(kfilt[None], "ka", 1)
     numbers = jnp.arange(cells, dtype=jnp.int32)[:, None]
     bounds = jnp.stack(
         [
@@ -434,35 +474,53 @@
             jnp.sum((cell_ids < numbers).astype(jnp.int32), axis=1),
         ]
     )
-    held = [
-        pltpu.with_memory_space_constraint(x, pltpu.HBM)
-        for x in (feats, coords, cell_ids, recip, kvec, w_in)
-    ]
-    waves, proj_t, ids, coords, recip, kvec = call(
+    first, ids, coords, recip, kvec, kfilt = call(
         prepare_kernel,
-        held,
+        [in_hbm(x) for x in (coords, cell_ids, recip, kvec, kfilt)],
         0,
         [
             ((2 * own, long), BF16),
-            ((chan, long), BF16),
             ((1, long), jnp.int32),
             (coords.shape, F32),
             (recip.shape, F32),
             (kvec.shape, jnp.int32),
+            (kfilt.shape, F32),
         ],
-        [
-            vm((atoms, chan), BF16),
-            vm((chan, chan), BF16),
-            vm((own, 8), F32),
-            pltpu.SemaphoreType.DMA((6,)),
-        ],
-        PREPARE,
-        4,
+        [vm((own, 8), F32), dma((5,))],
+        SMALL,
+        3,
         pltpu.HBM,
+    )
+    kvecs, kfilts = call(
+        pair_kernel,
+        (kvec[None], near_kvec, kfilt[None], near_kfilt),
+        0,
+        [((2, 8, own), F32), ((2, own, chan), F32)],
+    )
+    far_kvecs, far_kfilts = [kvecs], [kfilts]
+    for s in doubling(2, n_ka):
+        if s > 2:
+            kvecs, kfilts = call(
+                pair_kernel,
+                (kvecs, far_kvecs[-1], kfilts, far_kfilts[-1]),
+                0,
+                [((s, 8, own), F32), ((s, own, chan), F32)],
+            )
+        far_kvecs.append(send(kvecs, "ka", s))
+        far_kfilts.append(send(kfilts, "ka", s))
+    second, proj_t = call(
+        project_kernel,
+        (coords, far_kvecs[0], in_hbm(feats), in_hbm(w_in)),
+        0,
+        [((2 * own, long), BF16), ((chan, long), BF16)],
+        [vm((atoms, chan), BF16), vm((chan, chan), BF16), vm((own, 8), F32), dma((2,))],
+        SMALL,
+        3,
+        (pltpu.VMEM, pltpu.VMEM, pltpu.HBM, pltpu.HBM),
     )
     waves, factors, quad = call(
         functools.partial(waves_kernel, n_ka),
-        (bounds, waves, proj_t, ids, coords, recip, kvec, *kvecs),
+        (bounds, first, second, proj_t, ids, coords, recip, *far_kvecs),
         1,
         [((2 * k_all, long), BF16), ((cells, chan, 2 * k_all), F32), ((cells, k_all), F32)],
         [vm((own, 8), F32)],
@@ -471,17 +529,18 @@
     )
     act_t, mgrad_t, raw_out, raw_half = call(
         functools.partial(message_kernel, n_ka),
-        (bounds, ids, quad, waves, factors, spread, cotan, w_out, *kfilts),
+        (bounds, ids, quad, waves, factors, spread, cotan, w_out, *far_kfilts),
         1,
         [((chan, atoms), BF16), ((chan, long), BF16), ((chan, chan), F32), ((chan, chan), BF16)],
         [vm((chan, k_all), F32), vm((chan, 8), F32), vm((chan, 2 * k_all), BF16), vm((chan, long), F32)],
         LIMIT,
         8,
     )
-    out_parts = [send(raw_half, "dp", s) for s in chips]
+    out_steps = doubling(2, n_dp)
+    out_part = send(raw_half, "dp", out_steps[0])
     weights, filter_grad, filter_half = call(
         functools.partial(adjoint_kernel, n_ka),
-        (bounds, ids, quad, waves, factors, mgrad_t, spread, *kfilts),
+        (bounds, ids, quad, waves, factors, mgrad_t, spread, *far_kfilts),
         1,
         [((cells, chan, 2 * k_all), BF16), ((own, chan), F32), ((own, chan), BF16)],
         [vm((chan, k_all), F32), vm((chan, 8), F32), vm((chan, 2 * k_all), F32), vm((chan, own), F32)],
@@ -489,8 +548,11 @@
         8,
     )
     filt_parts = [send(filter_half, "dp", s) for s in chips]
-    (out_sum,) = call(add_kernel, (raw_out, *out_parts), 0, [((chan, chan), F32)])
-    out_near = send(out_sum, "dp", 1)
+    for s in out_steps[1:]:
+        raw_out, raw_half = call(
+            add_kernel, (raw_out, out_part), 0, [((chan, chan), F32), ((chan, chan), BF16)]
+        )
+        out_part = send(raw_half, "dp", s)
     update_t, raw_in_t = call(
         update_kernel,
         (bounds, ids, waves, weights, feats),
@@ -501,13 +563,16 @@
         8,
     )
     (pack,) = call(
-        join_kernel, (raw_in_t, filter_grad, *filt_parts), 0, [((chan + own, chan), F32)]
+        join_kernel,
+        (raw_in_t, raw_out, filter_grad, out_part, *filt_parts),
+        0,
+        [((2 * chan + own, chan), F32)],
     )
     near = send(pack, "dp", 1)
     feat_grad = residual(True, cotan, update_t, w_in)
-    in_sum, in_half, w_sum, f_sum, f_squares = call(
+    in_sum, in_half, w_sum, f_sum, squares = call(
         chip_kernel,
-        (pack, near, out_sum, out_near),
+        (pack, near),
         0,
         [
             ((chan, chan), F32),
@@ -517,12 +582,13 @@
             ((8, LANES), F32),
         ],
     )
-    squares = [f_squares] + [send(f_squares, "ka", s) for s in others]
     in_parts = [in_sum] + [send(in_half, "dp", s) for s in chips]
+    for s in doubling(1, n_ka):
+        (squares,) = call(add_kernel, (squares, send(squares, "ka", s)), 0, [((8, LANES), F32)])
     mixed = residual(False, feats, act_t, w_out)
     grads = call(
         functools.partial(final_kernel, len(in_parts), n_ka),
-        (*in_parts, w_sum, f_sum, *squares),
+        (*in_parts, w_sum, f_sum, squares),
         0,
         [((chan, chan), F32), ((chan, chan), F32), ((own, chan), F32)],
     )

time: 76.8 us -> 73.4 us (0.956)
  starting transfers between devices: 25.5 us -> 17.3 us
  waiting for transfers between devices: 8.78 us -> 14.3 us
    ppermute x20 -> x15, starting transfers between devices: 25.5 us -> 17.3 us  [send(): return lax.ppermute(value, axis, routes(step, lax.axis_size(axis)))]
    ppermute x20 -> x15, waiting for transfers between devices: 8.78 us -> 14.3 us  [send(): return lax.ppermute(value, axis, routes(step, lax.axis_size(axis)))]
    pallas_call x9 -> x13, Pallas kernels: 36 us -> 36 us  [call(): pl.pallas_call(kernel, out_shape=tuple((jax.ShapeDtypeStruct(*o) for o in...]
  transfers between devices with their start and end apart: 20 -> 15, of which waited for: 5 -> 6; matrix products, arithmetic and copies ran while one was open for 1% -> 0% of each run, Pallas kernels for 32% -> 42%
where the time goes in v3:
time: 73.4 us; the launch traced here: 73.3 us
  Pallas kernels  40.7 us (55%)
  starting transfers between devices  17.3 us (24%)
  waiting for transfers between devices  14.3 us (19%)
  between operations  0.8 us (1%)
    pallas_call x13, Pallas kernels, call(): pl.pallas_call(kernel, out_shape=tuple((jax.ShapeDtypeStruct(*o) for o in...  36 us
    ppermute x15, starting transfers between devices, send(): return lax.ppermute(value, axis, routes(step, lax.axis_size(axis)))  17.3 us
    ppermute x15, waiting for transfers between devices, send(): return lax.ppermute(value, axis, routes(step, lax.axis_size(axis)))  14.3 us
    pallas_call x2, Pallas kernels, residual(): pl.pallas_call(functools.partial(residual_kernel, transposed), out_shape=...  4.62 us
  transfers between devices with their start and end apart: 15, of which 6 were waited for; matrix products, arithmetic and copies ran while one was open for 0% of the time, Pallas kernels for 42%

profile of v3, /device:TPU:0, one launch (start us, length us, event | category | flops | bytes accessed | tf_op | source)
XLA Modules:
  0.0 73.3 jit_solution(9121348343406893706)
XLA Ops:
  0.6 3.1 %collective-permute-start = (s32[1,3,128]{2,1,0:T(4,128)}, s32[1,3,128]{2,1,0:T(4,128)S(1)}, u32[]{:S(2)}, u32[]{:S(2)}) collective-permute-start(s32[1,3,128]{2,1,0:T(4,128)} %bitcast.18), channel_id=1, source_target_pairs={{0,1},{1,0},{2,3},{3,2},{4,5},{5,4},{6,7},{7,6},{8,9},{9,8},{10,11... | collective-permute-start | bytes 4616 | tf_op jit(solution)/shard_map/ppermute | solution.py:449
  3.8 0.1 collective-permute-start.1
  3.8 0.0 copy-start.5
  3.8 2.7 %shard_map.137 = (bf16[256,2176]{1,0:T(8,128)(2,1)S(1)}, s32[1,2176]{1,0:T(1,128)S(1)}, f32[3,2048]{1,0:T(4,128)S(1)}, f32[8,9]{1,0:T(8,128)S(1)}, s32[3,128]{1,0:T(4,128)S(1)}, /*index=5*/f32[128,256]{1,0:T(8,128)S(1)}) custom-call(f32[3,2048]{1,0:T(4,128)} %coords_hbm.1, s32[1,2048]{1,0:T(1,128)} %ids_hbm.1, f32[8,9]{1,0:T(8,128)} %bitcast.17, ...), custom_call_target="tpu_custom_call" | custom-call | flops 3221225472 | tf_op jit(solution)/shard_map/pallas_call | solution.py:431
  6.5 0.0 copy-done.5
  6.5 0.2 convert_reduce_fusion.1
  6.7 0.0 collective-permute-done.other_kvec
  6.7 2.2 %collective-permute-done.1.other_kfilt = f32[1,128,256]{2,1,0:T(8,128)S(1)} collective-permute-done((f32[1,128,256]{2,1,0:T(8,128)}, f32[1,128,256]{2,1,0:T(8,128)S(1)}, u32[]{:S(2)}, u32[]{:S(2)}) %collective-permute-start.1) | collective-permute-done | bytes 131104 | tf_op jit(solution)/shard_map/ppermute | solution.py:449
  9.0 2.7 %collective-permute-start.2 = (f32[2,8,128]{2,1,0:T(8,128)S(1)}, f32[2,8,128]{2,1,0:T(8,128)S(1)}, u32[]{:S(2)}, u32[]{:S(2)}) collective-permute-start(f32[2,8,128]{2,1,0:T(8,128)S(1)} %get-tuple-element.42.kvecs.refs_7_), channel_id=1, source_target_pairs={{0,2},{1,3},{2,0},{3,1},{4,6},{5,7},{6,4},{7,5},{8,10},{9,11},{10,... | collective-permute-start | bytes 24584 | tf_op jit(solution)/shard_map/ppermute | solution.py:449
  11.6 0.3 collective-permute-start.3
  11.9 3.7 %shard_map.139 = (bf16[256,2176]{1,0:T(8,128)(2,1)S(1)}, bf16[256,2176]{1,0:T(8,128)(2,1)S(1)}) custom-call(f32[3,2048]{1,0:T(4,128)S(1)} %get-tuple-element.39.coords.refs_5_, f32[2,8,128]{2,1,0:T(8,128)S(1)} %get-tuple-element.42.kvecs.refs_7_, bf16[2048,256]{1,0:T(8,128)(2,1)} %feats.1, bf16[256,256]{1,0:T(8,128)(2,1)} %weight.3), custom_call_target="tpu_custom_call" | custom-call | flops 3221225472 | tf_op jit(solution)/shard_map/pallas_call | solution.py:431
  15.6 3.6 %collective-permute-done.2.refs_8_ = f32[2,8,128]{2,1,0:T(8,128)S(1)} collective-permute-done((f32[2,8,128]{2,1,0:T(8,128)S(1)}, f32[2,8,128]{2,1,0:T(8,128)S(1)}, u32[]{:S(2)}, u32[]{:S(2)}) %collective-permute-start.2) | collective-permute-done | bytes 8224 | tf_op jit(solution)/shard_map/ppermute | solution.py:449
  19.3 0.0 copy-start.1
  19.3 0.0 copy-start.2
  19.3 0.0 copy-start.4
  19.3 8.0 %shard_map.140 = (bf16[1024,2176]{1,0:T(8,128)(2,1)S(1)}, f32[8,256,1024]{2,1,0:T(8,128)S(1)}, f32[8,512]{1,0:T(8,128)S(1)}) custom-call(s32[2,8]{1,0:T(2,128)S(1)} %pad_add_fusion.refs_0_.bounds, bf16[256,2176]{1,0:T(8,128)(2,1)S(1)} %get-tuple-element.38.refs_1_, bf16[256,2176]{1,0:T(8,128)(2,1)S(1)} %get-tuple-element.43.refs_2_, ...), custom_call_target="tpu_custom_call" | custom-call | flops 8589934592 | tf_op jit(solution)/shard_map/pallas_call | solution.py:431
  27.3 0.0 collective-permute-done.3.refs_9_.refs_8_
  27.3 0.0 copy-done.1
  27.3 0.0 copy-done.2
  27.3 0.0 copy-done.4
  27.4 8.2 %shard_map.141 = (bf16[256,2048]{1,0:T(8,128)(2,1)S(1)}, bf16[256,2176]{1,0:T(8,128)(2,1)S(1)}, f32[256,256]{1,0:T(8,128)S(1)}, bf16[256,256]{1,0:T(8,128)(2,1)S(1)}) custom-call(s32[2,8]{1,0:T(2,128)S(1)} %pad_add_fusion.refs_0_.bounds, s32[1,2176]{1,0:T(1,128)S(1)} %get-tuple-element.37.refs_4_.refs_1_.ids, f32[8,512]{1,0:T(8,128)S(1)} %get-tuple-element.46.refs_2_, ...), custom_call_target="tpu_custom_call" | custom-call | flops 8589934592 | tf_op jit(solution)/shard_map/pallas_call | solution.py:431
  35.6 1.9 %collective-permute-start.4 = (bf16[256,256]{1,0:T(8,128)(2,1)S(1)}, bf16[256,256]{1,0:T(8,128)(2,1)S(1)}, u32[]{:S(2)}, u32[]{:S(2)}) collective-permute-start(bf16[256,256]{1,0:T(8,128)(2,1)S(1)} %get-tuple-element.56), channel_id=1, source_target_pairs={{0,8},{4,12},{8,0},{12,4},{16,24},{20,28},{24,16},{28,20},{1,9},{5... | collective-permute-start | bytes 393224 | tf_op jit(solution)/shard_map/ppermute | solution.py:449
  37.5 6.4 %shard_map.143 = (bf16[8,256,1024]{2,1,0:T(8,128)(2,1)S(1)}, f32[128,256]{1,0:T(8,128)S(1)}, bf16[128,256]{1,0:T(8,128)(2,1)S(1)}) custom-call(s32[2,8]{1,0:T(2,128)S(1)} %pad_add_fusion.refs_0_.bounds, s32[1,2176]{1,0:T(1,128)S(1)} %get-tuple-element.37.refs_4_.refs_1_.ids, f32[8,512]{1,0:T(8,128)S(1)} %get-tuple-element.46.refs_2_, ...), custom_call_target="tpu_custom_call" | custom-call | flops 8589934592 | tf_op jit(solution)/shard_map/pallas_call | solution.py:431
  43.9 1.4 %collective-permute-start.8 = (bf16[128,256]{1,0:T(8,128)(2,1)S(1)}, bf16[128,256]{1,0:T(8,128)(2,1)S(1)}, u32[]{:S(2)}, u32[]{:S(2)}) collective-permute-start(bf16[128,256]{1,0:T(8,128)(2,1)S(1)} %get-tuple-element.60), channel_id=1, source_target_pairs={{0,24},{4,28},{8,16},{12,20},{16,8},{20,12},{24,0},{28,4},{1,25},{... | collective-permute-start | bytes 196616 | tf_op jit(solution)/shard_map/ppermute | solution.py:449
  45.3 0.4 collective-permute-start.7
  45.7 1.7 %collective-permute-start.6 = (bf16[128,256]{1,0:T(8,128)(2,1)S(1)}, bf16[128,256]{1,0:T(8,128)(2,1)S(1)}, u32[]{:S(2)}, u32[]{:S(2)}) collective-permute-start(bf16[128,256]{1,0:T(8,128)(2,1)S(1)} %get-tuple-element.60), channel_id=1, source_target_pairs={{0,8},{4,12},{8,0},{12,4},{16,24},{20,28},{24,16},{28,20},{1,9},{5... | collective-permute-start | bytes 196616 | tf_op jit(solution)/shard_map/ppermute | solution.py:449
  47.4 0.0 collective-permute-done.4.second
  47.4 0.0 copy-start
  47.5 1.6 %collective-permute-start.5 = (bf16[256,256]{1,0:T(8,128)(2,1)S(1)}, bf16[256,256]{1,0:T(8,128)(2,1)S(1)}, u32[]{:S(2)}, u32[]{:S(2)}) collective-permute-start(bf16[256,256]{1,0:T(8,128)(2,1)S(1)} %get-tuple-element.59), channel_id=1, source_target_pairs={{0,16},{4,20},{8,24},{12,28},{16,0},{20,4},{24,8},{28,12},{1,17},{... | collective-permute-start | bytes 393224 | tf_op jit(solution)/shard_map/ppermute | solution.py:449
  49.1 0.0 copy-done
  49.1 5.7 %shard_map.144 = (bf16[256,2048]{1,0:T(8,128)(2,1)S(1)}, f32[256,256]{1,0:T(8,128)S(1)}) custom-call(s32[2,8]{1,0:T(2,128)S(1)} %pad_add_fusion.refs_0_.bounds, s32[1,2176]{1,0:T(1,128)S(1)} %get-tuple-element.37.refs_4_.refs_1_.ids, bf16[1024,2176]{1,0:T(8,128)(2,1)S(1)} %get-tuple-element.47.refs_3_.waves, ...), custom_call_target="tpu_custom_call" | custom-call | flops 8589934592 | tf_op jit(solution)/shard_map/pallas_call | solution.py:431
  54.8 0.0 collective-permute-done.8.refs_3_
  54.8 0.0 collective-permute-done.7.refs_2_
  54.8 0.0 collective-permute-done.6.refs_1_
  54.8 0.0 collective-permute-done.5.refs_0_
  54.8 0.1 shard_map.147.pack
  54.9 0.1 collective-permute-start.9
  55.0 2.1 %collective-permute-done.9.near = f32[640,256]{1,0:T(8,128)S(1)} collective-permute-done((f32[640,256]{1,0:T(8,128)S(1)}, f32[640,256]{1,0:T(8,128)S(1)}, u32[]{:S(2)}, u32[]{:S(2)}) %collective-permute-start.9) | collective-permute-done | bytes 655392 | tf_op jit(solution)/shard_map/ppermute | solution.py:449
  57.1 0.2 shard_map.148
  57.2 0.0 collective-permute-start.13
  57.2 2.3 %shard_map.142 = bf16[2048,256]{1,0:T(8,128)(2,1)} custom-call(bf16[2048,256]{1,0:T(8,128)(2,1)S(1)} %copy-done, bf16[256,2048]{1,0:T(8,128)(2,1)S(1)} %get-tuple-element.50.values_t, bf16[256,256]{1,0:T(8,128)(2,1)S(1)} %copy-done.2), custom_call_target="tpu_custom_call" | custom-call | flops 2147483648 | tf_op jit(solution)/shard_map/pallas_call | solution.py:361
  59.5 0.0 copy-start.3
  59.5 1.3 %collective-permute-done.13.second = f32[8,128]{1,0:T(8,128)S(1)} collective-permute-done((f32[8,128]{1,0:T(8,128)S(1)}, f32[8,128]{1,0:T(8,128)S(1)}, u32[]{:S(2)}, u32[]{:S(2)}) %collective-permute-start.13) | collective-permute-done | bytes 4128 | tf_op jit(solution)/shard_map/ppermute | solution.py:449
  60.8 0.5 collective-permute-start.14
  61.3 0.0 copy-done.3
  61.3 2.3 %shard_map.145 = bf16[2048,256]{1,0:T(8,128)(2,1)} custom-call(bf16[2048,256]{1,0:T(8,128)(2,1)S(1)} %copy-done.1, bf16[256,2048]{1,0:T(8,128)(2,1)S(1)} %get-tuple-element.53.values_t, bf16[256,256]{1,0:T(8,128)(2,1)S(1)} %copy-done.3), custom_call_target="tpu_custom_call" | custom-call | flops 2147483648 | tf_op jit(solution)/shard_map/pallas_call | solution.py:361
  63.6 1.1 %collective-permute-start.12 = (bf16[256,256]{1,0:T(8,128)(2,1)S(1)}, bf16[256,256]{1,0:T(8,128)(2,1)S(1)}, u32[]{:S(2)}, u32[]{:S(2)}) collective-permute-start(bf16[256,256]{1,0:T(8,128)(2,1)S(1)} %get-tuple-element.62), channel_id=1, source_target_pairs={{0,24},{4,28},{8,16},{12,20},{16,8},{20,12},{24,0},{28,4},{1,25},{... | collective-permute-start | bytes 393224 | tf_op jit(solution)/shard_map/ppermute | solution.py:449
  64.7 0.9 %collective-permute-start.11 = (bf16[256,256]{1,0:T(8,128)(2,1)S(1)}, bf16[256,256]{1,0:T(8,128)(2,1)S(1)}, u32[]{:S(2)}, u32[]{:S(2)}) collective-permute-start(bf16[256,256]{1,0:T(8,128)(2,1)S(1)} %get-tuple-element.62), channel_id=1, source_target_pairs={{0,16},{4,20},{8,24},{12,28},{16,0},{20,4},{24,8},{28,12},{1,17},{... | collective-permute-start | bytes 393224 | tf_op jit(solution)/shard_map/ppermute | solution.py:449
  65.6 1.5 %collective-permute-start.10 = (bf16[256,256]{1,0:T(8,128)(2,1)S(1)}, bf16[256,256]{1,0:T(8,128)(2,1)S(1)}, u32[]{:S(2)}, u32[]{:S(2)}) collective-permute-start(bf16[256,256]{1,0:T(8,128)(2,1)S(1)} %get-tuple-element.62), channel_id=1, source_target_pairs={{0,8},{4,12},{8,0},{12,4},{16,24},{20,28},{24,16},{28,20},{1,9},{5... | collective-permute-start | bytes 393224 | tf_op jit(solution)/shard_map/ppermute | solution.py:449
  67.1 0.0 collective-permute-done.14.second
  67.1 3.8 %collective-permute-done.12.refs_3_ = bf16[256,256]{1,0:T(8,128)(2,1)S(1)} collective-permute-done((bf16[256,256]{1,0:T(8,128)(2,1)S(1)}, bf16[256,256]{1,0:T(8,128)(2,1)S(1)}, u32[]{:S(2)}, u32[]{:S(2)}) %collective-permute-start.12) | collective-permute-done | bytes 131104 | tf_op jit(solution)/shard_map/ppermute | solution.py:449
  70.9 1.4 %collective-permute-done.11.refs_2_ = bf16[256,256]{1,0:T(8,128)(2,1)S(1)} collective-permute-done((bf16[256,256]{1,0:T(8,128)(2,1)S(1)}, bf16[256,256]{1,0:T(8,128)(2,1)S(1)}, u32[]{:S(2)}, u32[]{:S(2)}) %collective-permute-start.11) | collective-permute-done | bytes 131104 | tf_op jit(solution)/shard_map/ppermute | solution.py:449
  72.2 0.0 collective-permute-done.10.refs_1_
  72.2 1.1 %shard_map.151 = (f32[256,256]{1,0:T(8,128)}, f32[256,256]{1,0:T(8,128)}, f32[128,256]{1,0:T(8,128)}) custom-call(f32[256,256]{1,0:T(8,128)S(1)} %get-tuple-element.61.refs_0_, bf16[256,256]{1,0:T(8,128)(2,1)S(1)} %collective-permute-done.10.refs_1_, bf16[256,256]{1,0:T(8,128)(2,1)S(1)} %collective-permute-done.11.refs_2_, ...), custom_call_target="tpu_custom_call" | custom-call | flops 2147483648 | tf_op jit(solution)/shard_map/pallas_call | solution.py:431
  (5 shorter events, 0.1 us)
Async XLA Ops:
  0.6 6.1 %collective-permute-start = (s32[1,3,128]{2,1,0:T(4,128)}, s32[1,3,128]{2,1,0:T(4,128)S(1)}, u32[]{:S(2)}, u32[]{:S(2)}) collective-permute-start(s32[1,3,128]{2,1,0:T(4,128)} %bitcast.18), channel_id=1, source_target_pairs={{0,1},{1,0},{2,3},{3,2},{4,5},{5,4},{6,7},{7,6},{8,9},{9,8},{10,11... | collective-permute-start | bytes 4616 | tf_op jit(solution)/shard_map/ppermute | solution.py:449
  3.8 5.2 %collective-permute-start.1 = (f32[1,128,256]{2,1,0:T(8,128)}, f32[1,128,256]{2,1,0:T(8,128)S(1)}, u32[]{:S(2)}, u32[]{:S(2)}) collective-permute-start(f32[1,128,256]{2,1,0:T(8,128)} %bitcast.16), channel_id=1, source_target_pairs={{0,1},{1,0},{2,3},{3,2},{4,5},{5,4},{6,7},{7,6},{8,9},{9,8},{10,11... | collective-permute-start | bytes 393224 | tf_op jit(solution)/shard_map/ppermute | solution.py:449
  3.8 2.7 %copy-start.5 = (s32[1,2048]{1,0:T(1,128)S(1)}, s32[1,2048]{1,0:T(1,128)}, u32[]{:S(2)}) copy-start(s32[1,2048]{1,0:T(1,128)} %ids_hbm.1) | copy-start | bytes 24580
  9.0 10.3 %collective-permute-start.2 = (f32[2,8,128]{2,1,0:T(8,128)S(1)}, f32[2,8,128]{2,1,0:T(8,128)S(1)}, u32[]{:S(2)}, u32[]{:S(2)}) collective-permute-start(f32[2,8,128]{2,1,0:T(8,128)S(1)} %get-tuple-element.42.kvecs.refs_7_), channel_id=1, source_target_pairs={{0,2},{1,3},{2,0},{3,1},{4,6},{5,7},{6,4},{7,5},{8,10},{9,11},{10,... | collective-permute-start | bytes 24584 | tf_op jit(solution)/shard_map/ppermute | solution.py:449
  11.6 15.7 %collective-permute-start.3 = (f32[2,128,256]{2,1,0:T(8,128)S(1)}, f32[2,128,256]{2,1,0:T(8,128)S(1)}, u32[]{:S(2)}, u32[]{:S(2)}) collective-permute-start(f32[2,128,256]{2,1,0:T(8,128)S(1)} %get-tuple-element.49.refs_8_.refs_7_), channel_id=1, source_target_pairs={{0,2},{1,3},{2,0},{3,1},{4,6},{5,7},{6,4},{7,5},{8,10},{9,11},{10,... | collective-permute-start | bytes 786440 | tf_op jit(solution)/shard_map/ppermute | solution.py:449
  19.3 8.1 %copy-start.1 = (bf16[2048,256]{1,0:T(8,128)(2,1)S(1)}, bf16[2048,256]{1,0:T(8,128)(2,1)}, u32[]{:S(2)}) copy-start(bf16[2048,256]{1,0:T(8,128)(2,1)} %base.3) | copy-start | bytes 3145732
  19.3 8.1 %copy-start.2 = (bf16[256,256]{1,0:T(8,128)(2,1)S(1)}, bf16[256,256]{1,0:T(8,128)(2,1)}, u32[]{:S(2)}) copy-start(bf16[256,256]{1,0:T(8,128)(2,1)} %weight.2) | copy-start | bytes 393220
  19.3 8.1 %copy-start.4 = (f32[256]{0:T(256)S(1)}, f32[256]{0:T(256)}, u32[]{:S(2)}) copy-start(f32[256]{0:T(256)} %param.18) | copy-start | bytes 3076
  35.6 11.9 %collective-permute-start.4 = (bf16[256,256]{1,0:T(8,128)(2,1)S(1)}, bf16[256,256]{1,0:T(8,128)(2,1)S(1)}, u32[]{:S(2)}, u32[]{:S(2)}) collective-permute-start(bf16[256,256]{1,0:T(8,128)(2,1)S(1)} %get-tuple-element.56), channel_id=1, source_target_pairs={{0,8},{4,12},{8,0},{12,4},{16,24},{20,28},{24,16},{28,20},{1,9},{5... | collective-permute-start | bytes 393224 | tf_op jit(solution)/shard_map/ppermute | solution.py:449
  43.9 10.9 %collective-permute-start.8 = (bf16[128,256]{1,0:T(8,128)(2,1)S(1)}, bf16[128,256]{1,0:T(8,128)(2,1)S(1)}, u32[]{:S(2)}, u32[]{:S(2)}) collective-permute-start(bf16[128,256]{1,0:T(8,128)(2,1)S(1)} %get-tuple-element.60), channel_id=1, source_target_pairs={{0,24},{4,28},{8,16},{12,20},{16,8},{20,12},{24,0},{28,4},{1,25},{... | collective-permute-start | bytes 196616 | tf_op jit(solution)/shard_map/ppermute | solution.py:449
  45.3 9.5 %collective-permute-start.7 = (bf16[128,256]{1,0:T(8,128)(2,1)S(1)}, bf16[128,256]{1,0:T(8,128)(2,1)S(1)}, u32[]{:S(2)}, u32[]{:S(2)}) collective-permute-start(bf16[128,256]{1,0:T(8,128)(2,1)S(1)} %get-tuple-element.60), channel_id=1, source_target_pairs={{0,16},{4,20},{8,24},{12,28},{16,0},{20,4},{24,8},{28,12},{1,17},{... | collective-permute-start | bytes 196616 | tf_op jit(solution)/shard_map/ppermute | solution.py:449
  45.7 9.1 %collective-permute-start.6 = (bf16[128,256]{1,0:T(8,128)(2,1)S(1)}, bf16[128,256]{1,0:T(8,128)(2,1)S(1)}, u32[]{:S(2)}, u32[]{:S(2)}) collective-permute-start(bf16[128,256]{1,0:T(8,128)(2,1)S(1)} %get-tuple-element.60), channel_id=1, source_target_pairs={{0,8},{4,12},{8,0},{12,4},{16,24},{20,28},{24,16},{28,20},{1,9},{5... | collective-permute-start | bytes 196616 | tf_op jit(solution)/shard_map/ppermute | solution.py:449
  47.4 1.7 %copy-start = (bf16[2048,256]{1,0:T(8,128)(2,1)S(1)}, bf16[2048,256]{1,0:T(8,128)(2,1)}, u32[]{:S(2)}) copy-start(bf16[2048,256]{1,0:T(8,128)(2,1)} %feats.1) | copy-start | bytes 3145732
  47.5 7.3 %collective-permute-start.5 = (bf16[256,256]{1,0:T(8,128)(2,1)S(1)}, bf16[256,256]{1,0:T(8,128)(2,1)S(1)}, u32[]{:S(2)}, u32[]{:S(2)}) collective-permute-start(bf16[256,256]{1,0:T(8,128)(2,1)S(1)} %get-tuple-element.59), channel_id=1, source_target_pairs={{0,16},{4,20},{8,24},{12,28},{16,0},{20,4},{24,8},{28,12},{1,17},{... | collective-permute-start | bytes 393224 | tf_op jit(solution)/shard_map/ppermute | solution.py:449
  54.9 2.2 %collective-permute-start.9 = (f32[640,256]{1,0:T(8,128)S(1)}, f32[640,256]{1,0:T(8,128)S(1)}, u32[]{:S(2)}, u32[]{:S(2)}) collective-permute-start(f32[640,256]{1,0:T(8,128)S(1)} %shard_map.147.pack), channel_id=1, source_target_pairs={{0,4},{4,0},{8,12},{12,8},{16,20},{20,16},{24,28},{28,24},{1,5},{5... | collective-permute-start | bytes 1966088 | tf_op jit(solution)/shard_map/ppermute | solution.py:449
  57.2 3.6 %collective-permute-start.13 = (f32[8,128]{1,0:T(8,128)S(1)}, f32[8,128]{1,0:T(8,128)S(1)}, u32[]{:S(2)}, u32[]{:S(2)}) collective-permute-start(f32[8,128]{1,0:T(8,128)S(1)} %get-tuple-element.65.first), channel_id=1, source_target_pairs={{0,1},{1,0},{2,3},{3,2},{4,5},{5,4},{6,7},{7,6},{8,9},{9,8},{10,11... | collective-permute-start | bytes 12296 | tf_op jit(solution)/shard_map/ppermute | solution.py:449
  59.5 1.8 %copy-start.3 = (bf16[256,256]{1,0:T(8,128)(2,1)S(1)}, bf16[256,256]{1,0:T(8,128)(2,1)}, u32[]{:S(2)}) copy-start(bf16[256,256]{1,0:T(8,128)(2,1)} %weight.3) | copy-start | bytes 393220
  60.8 6.3 %collective-permute-start.14 = (f32[8,128]{1,0:T(8,128)S(1)}, f32[8,128]{1,0:T(8,128)S(1)}, u32[]{:S(2)}, u32[]{:S(2)}) collective-permute-start(f32[8,128]{1,0:T(8,128)S(1)} %shard_map.149.first), channel_id=1, source_target_pairs={{0,2},{1,3},{2,0},{3,1},{4,6},{5,7},{6,4},{7,5},{8,10},{9,11},{10,... | collective-permute-start | bytes 12296 | tf_op jit(solution)/shard_map/ppermute | solution.py:449
  63.6 7.3 %collective-permute-start.12 = (bf16[256,256]{1,0:T(8,128)(2,1)S(1)}, bf16[256,256]{1,0:T(8,128)(2,1)S(1)}, u32[]{:S(2)}, u32[]{:S(2)}) collective-permute-start(bf16[256,256]{1,0:T(8,128)(2,1)S(1)} %get-tuple-element.62), channel_id=1, source_target_pairs={{0,24},{4,28},{8,16},{12,20},{16,8},{20,12},{24,0},{28,4},{1,25},{... | collective-permute-start | bytes 393224 | tf_op jit(solution)/shard_map/ppermute | solution.py:449
  64.7 7.5 %collective-permute-start.11 = (bf16[256,256]{1,0:T(8,128)(2,1)S(1)}, bf16[256,256]{1,0:T(8,128)(2,1)S(1)}, u32[]{:S(2)}, u32[]{:S(2)}) collective-permute-start(bf16[256,256]{1,0:T(8,128)(2,1)S(1)} %get-tuple-element.62), channel_id=1, source_target_pairs={{0,16},{4,20},{8,24},{12,28},{16,0},{20,4},{24,8},{28,12},{1,17},{... | collective-permute-start | bytes 393224 | tf_op jit(solution)/shard_map/ppermute | solution.py:449
  65.6 6.6 %collective-permute-start.10 = (bf16[256,256]{1,0:T(8,128)(2,1)S(1)}, bf16[256,256]{1,0:T(8,128)(2,1)S(1)}, u32[]{:S(2)}, u32[]{:S(2)}) collective-permute-start(bf16[256,256]{1,0:T(8,128)(2,1)S(1)} %get-tuple-element.62), channel_id=1, source_target_pairs={{0,8},{4,12},{8,0},{12,4},{16,24},{20,28},{24,16},{28,20},{1,9},{5... | collective-permute-start | bytes 393224 | tf_op jit(solution)/shard_map/ppermute | solution.py:449

commit v4 on v3

--- a/solution.py
+++ b/solution.py
@@ -93,14 +93,44 @@
     by_steps(steps, most, action)
 
 
-def spread_cell(cell, start, steps, most, ids, weights, waves, out):
-    def action(n):
-        for t in range(n):
-            at = pl.ds(pl.multiple_of(start + t * TILE, LANES), TILE)
-            value = mm(weights[...], waves[:, at])
-            out[:, at] = jnp.where(ids[:, at] == cell, value, out[:, at])
-
-    by_steps(steps, most, action)
+def weigh(cell, n_ka, bounds, quad, filt_t, width_cols, sums, weights):
+    own = filt_t.shape[1] // n_ka
+    inverse = inverse_count(bounds[0, cell])
+    for j in range(n_ka):
+        scaled = shape_of(cell, quad, width_cols, j * own, own) * inverse
+        filt = filt_t[:, own * j : own * (j + 1)] * scaled
+        for half in (2 * j, 2 * j + 1):
+            at = slice(own * half, own * (half + 1))
+            weights[:, at] = (filt * sums[cell, :, at]).astype(BF16)
+
+
+def spread_cells(n_ka, bounds, ids, quad, filt_t, width_cols, sums, waves, even, odd, out):
+    cells = quad.shape[0]
+    most = most_steps(out.shape[1] - LANES)
+
+    def one(cell, weights, after, target):
+        start, steps, _ = span_of(bounds, cell)
+
+        def action(n):
+            if after is not None:
+                weigh(after, n_ka, bounds, quad, filt_t, width_cols, sums, target)
+            for t in range(n):
+                at = pl.ds(pl.multiple_of(start + t * TILE, LANES), TILE)
+                value = mm(weights[...], waves[:, at])
+                out[:, at] = jnp.where(ids[:, at] == cell, value, out[:, at])
+
+        by_steps(steps, most, action)
+
+    weigh(0, n_ka, bounds, quad, filt_t, width_cols, sums, even)
+
+    def two(i, carry):
+        one(2 * i, even, jnp.minimum(2 * i + 1, cells - 1), odd)
+        one(2 * i + 1, odd, jnp.minimum(2 * i + 2, cells - 1), even)
+        return carry
+
+    lax.fori_loop(0, cells // 2, two, 0)
+    if cells % 2:
+        one(cells - 1, even, None, None)
 
 
 def inverse_count(count):
@@ -251,25 +281,11 @@
 
 def message_kernel(n_ka, *refs):
     bounds, ids, quad, waves, factors, spread, cotan, w_out = refs[:8]
-    act_t, mgrad_t, raw_out, raw_half, filt_t, width_cols, weights, mess_t = refs[-8:]
+    act_t, mgrad_t, raw_out, raw_half, filt_t, width_cols, even, odd, mess_t = refs[-9:]
     atoms, chan = cotan.shape
-    cells = quad.shape[0]
-    own = filters_first(filt_t, refs[8:-8])
+    filters_first(filt_t, refs[8:-9])
     width_cols[...] = column_to_lanes(spread[...] * (-LOG2_E))
-
-    def cell_step(cell, carry):
-        start, steps, count = span_of(bounds, cell)
-        inverse = inverse_count(count)
-        for j in range(n_ka):
-            scaled = shape_of(cell, quad, width_cols, j * own, own) * inverse
-            filt = filt_t[:, own * j : own * (j + 1)] * scaled
-            for at in (slice(2 * own * j, own * (2 * j + 1)), slice(own * (2 * j + 1), 2 * own * (j + 1))):
-                weights[:, at] = (filt * factors[cell, :, at]).astype(BF16)
-        spread_cell(cell, start, steps, most_steps(atoms), ids, weights, waves, mess_t)
-        return carry
-
-    lax.fori_loop(0, cells, cell_step, 0)
-
+    spread_cells(n_ka, bounds, ids, quad, filt_t, width_cols, factors, waves, even, odd, mess_t)
     mgrad_t[:, atoms:] = jnp.zeros((chan, LANES), BF16)
     raw_out[...] = jnp.zeros_like(raw_out)
 
@@ -291,10 +307,10 @@
 
 def adjoint_kernel(n_ka, *refs):
     bounds, ids, quad, waves, factors, mgrad_t, spread = refs[:7]
-    weights, filter_grad, filter_half, filt_t, width_cols, total, grad_t = refs[-7:]
+    sums, filter_grad, filter_half, width_cols, grad_t = refs[7:]
     atoms = mgrad_t.shape[1] - LANES
-    cells = quad.shape[0]
-    own = filters_first(filt_t, refs[7:-7])
+    cells, k_all = quad.shape
+    own = k_all // n_ka
     width_cols[...] = column_to_lanes(spread[...] * (-LOG2_E))
     grad_t[...] = jnp.zeros_like(grad_t)
 
@@ -302,21 +318,14 @@
         start, steps, count = span_of(bounds, cell)
 
         def store(value):
-            total[...] = value
+            sums[cell] = value
 
         gather_cell(cell, start, steps, most_steps(atoms), ids, mgrad_t, waves, store)
-        inverse = inverse_count(count)
-        for j in range(n_ka):
-            scaled = shape_of(cell, quad, width_cols, j * own, own) * inverse
-            filt = filt_t[:, own * j : own * (j + 1)] * scaled
-            real = slice(2 * own * j, own * (2 * j + 1))
-            imag = slice(own * (2 * j + 1), 2 * own * (j + 1))
-            weights[cell, :, real] = (filt * total[:, real]).astype(BF16)
-            weights[cell, :, imag] = (filt * total[:, imag]).astype(BF16)
-            if j == 0:
-                grad_t[...] += scaled * (
-                    factors[cell, :, real] * total[:, real] + factors[cell, :, imag] * total[:, imag]
-                )
+        scaled = shape_of(cell, quad, width_cols, 0, own) * inverse_count(count)
+        grad_t[...] += scaled * (
+            factors[cell, :, :own] * sums[cell, :, :own]
+            + factors[cell, :, own : 2 * own] * sums[cell, :, own : 2 * own]
+        )
         return carry
 
     lax.fori_loop(0, cells, cell_step, 0)
@@ -325,28 +334,22 @@
     filter_half[...] = result.astype(BF16)
 
 
-def update_kernel(bounds, ids, waves, weights, feats, update_t, raw_in_t, total_t):
-    cells, _, _ = weights.shape
-    atoms = feats.shape[0]
-
-    def cell_step(cell, carry):
-        start, steps, _ = span_of(bounds, cell)
-        spread_cell(
-            cell, start, steps, most_steps(atoms), ids, weights.at[cell], waves, total_t
-        )
-        return carry
-
-    lax.fori_loop(0, cells, cell_step, 0)
-    raw_in_t[...] = jnp.zeros_like(raw_in_t)
-
-    def last(t, carry):
-        at = pl.ds(pl.multiple_of(t * TILE, TILE), TILE)
-        update = total_t[:, at].astype(BF16)
-        update_t[:, at] = update
-        raw_in_t[...] += mm(update, feats[at, :])
-        return carry
-
-    lax.fori_loop(0, atoms // TILE, last, 0)
+def update_kernel(n_ka, *refs):
+    bounds, ids, quad, waves, sums, spread = refs[:6]
+    update_t = refs[-11]
+    filt_t, width_cols, even, odd, total_t, sems = refs[-6:]
+    copies = start_copies(sems, *zip(refs[-15:-11], refs[-10:-6]))
+    atoms = update_t.shape[1]
+    filters_first(filt_t, refs[6:-15])
+    width_cols[...] = column_to_lanes(spread[...] * (-LOG2_E))
+    spread_cells(n_ka, bounds, ids, quad, filt_t, width_cols, sums, waves, even, odd, total_t)
+    update_t[...] = total_t[:, :atoms].astype(BF16)
+    for copy in copies:
+        copy.wait()
+
+
+def gradient_kernel(update_t, feats, raw_in_t):
+    raw_in_t[...] = mm(update_t[...], feats[...])
 
 
 def residual_kernel(transposed, base, values_t, weight, out):
@@ -375,26 +378,31 @@
     )(base, values_t, weight)
 
 
-def join_kernel(raw_in_t, raw_out, filt, *refs):
-    pack = refs[-1]
+def join_kernel(raw_in_t, raw_out, other_out, pack):
     chan = raw_in_t.shape[0]
     pack[:chan, :] = raw_in_t[...]
-    pack[chan : 2 * chan, :] = total_of(raw_out, refs[0:1])
-    pack[2 * chan :, :] = total_of(filt, refs[1:-1])
-
-
-def chip_kernel(pack, near, in_sum, in_half, w_sum, f_sum, f_squares):
+    pack[chan:, :] = total_of(raw_out, (other_out,))
+
+
+def filter_kernel(*refs):
+    refs[-1][...] = total_of(refs[0], refs[1:-1])
+
+
+def squares_kernel(filt, near, f_sum, f_squares):
+    value = filt[...] + near[...]
+    f_sum[...] = value
+    f_squares[...] = jnp.broadcast_to(
+        jnp.sum(jnp.sum(value * value, axis=0, keepdims=True), axis=1, keepdims=True),
+        f_squares.shape,
+    )
+
+
+def chip_kernel(pack, near, in_sum, in_half, w_sum):
     chan = in_sum.shape[0]
     value = pack[:chan, :] + near[:chan, :]
     in_sum[...] = value
     in_half[...] = value.astype(BF16)
-    w_sum[...] = pack[chan : 2 * chan, :] + near[chan : 2 * chan, :]
-    filt = pack[2 * chan :, :] + near[2 * chan :, :]
-    f_sum[...] = filt
-    f_squares[...] = jnp.broadcast_to(
-        jnp.sum(jnp.sum(filt * filt, axis=0, keepdims=True), axis=1, keepdims=True),
-        f_squares.shape,
-    )
+    w_sum[...] = pack[chan:, :] + near[chan:, :]
 
 
 def total_of(first, others):
@@ -527,25 +535,26 @@
         LIMIT,
         8,
     )
+    halves = [vm((chan, 2 * k_all), BF16)] * 2
     act_t, mgrad_t, raw_out, raw_half = call(
         functools.partial(message_kernel, n_ka),
         (bounds, ids, quad, waves, factors, spread, cotan, w_out, *far_kfilts),
         1,
         [((chan, atoms), BF16), ((chan, long), BF16), ((chan, chan), F32), ((chan, chan), BF16)],
-        [vm((chan, k_all), F32), vm((chan, 8), F32), vm((chan, 2 * k_all), BF16), vm((chan, long), F32)],
+        [vm((chan, k_all), F32), vm((chan, 8), F32), *halves, vm((chan, long), F32)],
         LIMIT,
         8,
     )
     out_steps = doubling(2, n_dp)
     out_part = send(raw_half, "dp", out_steps[0])
-    weights, filter_grad, filter_half = call(
+    sums, filter_grad, filter_half = call(
         functools.partial(adjoint_kernel, n_ka),
-        (bounds, ids, quad, waves, factors, mgrad_t, spread, *far_kfilts),
+        (bounds, ids, quad, waves, factors, mgrad_t, spread),
         1,
-        [((cells, chan, 2 * k_all), BF16), ((own, chan), F32), ((own, chan), BF16)],
-        [vm((chan, k_all), F32), vm((chan, 8), F32), vm((chan, 2 * k_all), F32), vm((chan, own), F32)],
+        [((cells, chan, 2 * k_all), F32), ((own, chan), F32), ((own, chan), BF16)],
+        [vm((chan, 8), F32), vm((chan, own), F32)],
         LIMIT,
-        8,
+        6,
     )
     filt_parts = [send(filter_half, "dp", s) for s in chips]
     for s in out_steps[1:]:
@@ -553,38 +562,39 @@
             add_kernel, (raw_out, out_part), 0, [((chan, chan), F32), ((chan, chan), BF16)]
         )
         out_part = send(raw_half, "dp", s)
-    update_t, raw_in_t = call(
-        update_kernel,
-        (bounds, ids, waves, weights, feats),
+    held = (feats, cotan, w_in, w_out)
+    update_t, feats, cotan, w_in, w_out = call(
+        functools.partial(update_kernel, n_ka),
+        (bounds, ids, quad, waves, sums, spread, *far_kfilts, *map(in_hbm, held)),
         1,
-        [((chan, atoms), BF16), ((chan, chan), F32)],
-        [vm((chan, long), F32)],
+        [((chan, atoms), BF16), *((x.shape, BF16) for x in held)],
+        [vm((chan, k_all), F32), vm((chan, 8), F32), *halves, vm((chan, long), F32), dma((4,))],
         LIMIT,
         8,
-    )
-    (pack,) = call(
-        join_kernel,
-        (raw_in_t, raw_out, filter_grad, out_part, *filt_parts),
-        0,
-        [((2 * chan + own, chan), F32)],
-    )
+        (pltpu.VMEM,) * (5 + len(far_kfilts)) + (pltpu.HBM,) * 4,
+    )
+    (filt_sum,) = call(filter_kernel, (filter_grad, *filt_parts), 0, [((own, chan), F32)])
+    filt_near = send(filt_sum, "dp", 1)
+    (raw_in_t,) = call(gradient_kernel, (update_t, feats), 0, [((chan, chan), F32)])
+    (pack,) = call(join_kernel, (raw_in_t, raw_out, out_part), 0, [((2 * chan, chan), F32)])
     near = send(pack, "dp", 1)
+    f_sum, squares = call(
+        squares_kernel, (filt_sum, filt_near), 0, [((own, chan), F32), ((8, LANES), F32)]
+    )
+    square_steps = doubling(1, n_ka)
+    square_part = send(squares, "ka", square_steps[0])
     feat_grad = residual(True, cotan, update_t, w_in)
-    in_sum, in_half, w_sum, f_sum, squares = call(
+    in_sum, in_half, w_sum = call(
         chip_kernel,
         (pack, near),
         0,
-        [
-            ((chan, chan), F32),
-            ((chan, chan), BF16),
-            ((chan, chan), F32),
-            ((own, chan), F32),
-            ((8, LANES), F32),
-        ],
+        [((chan, chan), F32), ((chan, chan), BF16), ((chan, chan), F32)],
     )
     in_parts = [in_sum] + [send(in_half, "dp", s) for s in chips]
-    for s in doubling(1, n_ka):
-        (squares,) = call(add_kernel, (squares, send(squares, "ka", s)), 0, [((8, LANES), F32)])
+    for s in square_steps[1:] + [0]:
+        (squares,) = call(add_kernel, (squares, square_part), 0, [((8, LANES), F32)])
+        if s:
+            square_part = send(squares, "ka", s)
     mixed = residual(False, feats, act_t, w_out)
     grads = call(
         functools.partial(final_kernel, len(in_parts), n_ka),

time: 73.4 us -> 73.4 us (level)
  Pallas kernels: 40.7 us -> 38.7 us
  waiting for transfers between devices: 14.3 us -> 16.1 us
    pallas_call x13 -> x16, Pallas kernels: 36 us -> 34.1 us  [call(): pl.pallas_call(kernel, out_shape=tuple((jax.ShapeDtypeStruct(*o) for o in...]
    ppermute x15 -> x16, waiting for transfers between devices: 14.3 us -> 16.1 us  [send(): return lax.ppermute(value, axis, routes(step, lax.axis_size(axis)))]
    ppermute x15 -> x16, starting transfers between devices: 17.3 us -> 17.4 us  [send(): return lax.ppermute(value, axis, routes(step, lax.axis_size(axis)))]
  transfers between devices with their start and end apart: 15 -> 16, of which waited for: 6 -> 8; matrix products, arithmetic and copies ran while one was open for 0% -> 0% of each run, Pallas kernels for 42% -> 34%
where the time goes in v4:
time: 73.4 us; the launch traced here: 73.2 us
  Pallas kernels  38.7 us (53%)
  starting transfers between devices  17.4 us (24%)
  waiting for transfers between devices  16.1 us (22%)
  between operations  0.81 us (1%)
    pallas_call x16, Pallas kernels, call(): pl.pallas_call(kernel, out_shape=tuple((jax.ShapeDtypeStruct(*o) for o in...  34.1 us
    ppermute x16, starting transfers between devices, send(): return lax.ppermute(value, axis, routes(step, lax.axis_size(axis)))  17.4 us
    ppermute x16, waiting for transfers between devices, send(): return lax.ppermute(value, axis, routes(step, lax.axis_size(axis)))  16.1 us
    pallas_call x2, Pallas kernels, residual(): pl.pallas_call(functools.partial(residual_kernel, transposed), out_shape=...  4.64 us
  transfers between devices with their start and end apart: 16, of which 8 were waited for; matrix products, arithmetic and copies ran while one was open for 0% of the time, Pallas kernels for 34%

profile of v4, /device:TPU:0, one launch (start us, length us, event | category | flops | bytes accessed | tf_op | source)
XLA Modules:
  0.0 73.2 jit_solution(13311457858171897968)
XLA Ops:
  0.6 3.1 %collective-permute-start = (s32[1,3,128]{2,1,0:T(4,128)}, s32[1,3,128]{2,1,0:T(4,128)S(1)}, u32[]{:S(2)}, u32[]{:S(2)}) collective-permute-start(s32[1,3,128]{2,1,0:T(4,128)} %bitcast.19), channel_id=1, source_target_pairs={{0,1},{1,0},{2,3},{3,2},{4,5},{5,4},{6,7},{7,6},{8,9},{9,8},{10,11... | collective-permute-start | bytes 4616 | tf_op jit(solution)/shard_map/ppermute | solution.py:457
  3.8 0.1 collective-permute-start.1
  3.8 0.0 copy-start.3
  3.8 2.7 %shard_map.137 = (bf16[256,2176]{1,0:T(8,128)(2,1)S(1)}, s32[1,2176]{1,0:T(1,128)S(1)}, f32[3,2048]{1,0:T(4,128)S(1)}, f32[8,9]{1,0:T(8,128)S(1)}, s32[3,128]{1,0:T(4,128)S(1)}, /*index=5*/f32[128,256]{1,0:T(8,128)S(1)}) custom-call(f32[3,2048]{1,0:T(4,128)} %coords_hbm.1, s32[1,2048]{1,0:T(1,128)} %ids_hbm.1, f32[8,9]{1,0:T(8,128)} %bitcast.18, ...), custom_call_target="tpu_custom_call" | custom-call | flops 3221225472 | tf_op jit(solution)/shard_map/pallas_call | solution.py:439
  6.5 0.0 copy-done.3
  6.5 0.2 convert_reduce_fusion.1
  6.7 0.0 collective-permute-done.other_kvec
  6.7 2.2 %collective-permute-done.1.other_kfilt = f32[1,128,256]{2,1,0:T(8,128)S(1)} collective-permute-done((f32[1,128,256]{2,1,0:T(8,128)}, f32[1,128,256]{2,1,0:T(8,128)S(1)}, u32[]{:S(2)}, u32[]{:S(2)}) %collective-permute-start.1) | collective-permute-done | bytes 131104 | tf_op jit(solution)/shard_map/ppermute | solution.py:457
  9.0 2.7 %collective-permute-start.2 = (f32[2,8,128]{2,1,0:T(8,128)S(1)}, f32[2,8,128]{2,1,0:T(8,128)S(1)}, u32[]{:S(2)}, u32[]{:S(2)}) collective-permute-start(f32[2,8,128]{2,1,0:T(8,128)S(1)} %get-tuple-element.45.kvecs.refs_7_), channel_id=1, source_target_pairs={{0,2},{1,3},{2,0},{3,1},{4,6},{5,7},{6,4},{7,5},{8,10},{9,11},{10,... | collective-permute-start | bytes 24584 | tf_op jit(solution)/shard_map/ppermute | solution.py:457
  11.6 0.3 collective-permute-start.3
  11.9 3.7 %shard_map.139 = (bf16[256,2176]{1,0:T(8,128)(2,1)S(1)}, bf16[256,2176]{1,0:T(8,128)(2,1)S(1)}) custom-call(f32[3,2048]{1,0:T(4,128)S(1)} %get-tuple-element.42.coords.refs_5_, f32[2,8,128]{2,1,0:T(8,128)S(1)} %get-tuple-element.45.kvecs.refs_7_, bf16[2048,256]{1,0:T(8,128)(2,1)} %refs_8_.1, bf16[256,256]{1,0:T(8,128)(2,1)} %refs_10_.1), custom_call_target="tpu_custom_call" | custom-call | flops 3221225472 | tf_op jit(solution)/shard_map/pallas_call | solution.py:439
  15.7 3.6 %collective-permute-done.2.refs_8_ = f32[2,8,128]{2,1,0:T(8,128)S(1)} collective-permute-done((f32[2,8,128]{2,1,0:T(8,128)S(1)}, f32[2,8,128]{2,1,0:T(8,128)S(1)}, u32[]{:S(2)}, u32[]{:S(2)}) %collective-permute-start.2) | collective-permute-done | bytes 8224 | tf_op jit(solution)/shard_map/ppermute | solution.py:457
  19.3 0.0 copy-start
  19.3 0.0 copy-start.1
  19.3 0.0 copy-start.2
  19.3 8.1 %shard_map.140 = (bf16[1024,2176]{1,0:T(8,128)(2,1)S(1)}, f32[8,256,1024]{2,1,0:T(8,128)S(1)}, f32[8,512]{1,0:T(8,128)S(1)}) custom-call(s32[2,8]{1,0:T(2,128)S(1)} %pad_add_fusion.refs_0_, bf16[256,2176]{1,0:T(8,128)(2,1)S(1)} %get-tuple-element.41.refs_1_, bf16[256,2176]{1,0:T(8,128)(2,1)S(1)} %get-tuple-element.46.refs_2_, ...), custom_call_target="tpu_custom_call" | custom-call | flops 8589934592 | tf_op jit(solution)/shard_map/pallas_call | solution.py:439
  27.4 0.0 collective-permute-done.3.refs_9_.refs_7_
  27.4 0.0 copy-done
  27.4 0.0 copy-done.1
  27.4 0.0 copy-done.2
  27.4 7.1 %shard_map.141 = (bf16[256,2048]{1,0:T(8,128)(2,1)S(1)}, bf16[256,2176]{1,0:T(8,128)(2,1)S(1)}, f32[256,256]{1,0:T(8,128)S(1)}, bf16[256,256]{1,0:T(8,128)(2,1)S(1)}) custom-call(s32[2,8]{1,0:T(2,128)S(1)} %pad_add_fusion.refs_0_, s32[1,2176]{1,0:T(1,128)S(1)} %get-tuple-element.40.refs_4_.refs_1_, f32[8,512]{1,0:T(8,128)S(1)} %get-tuple-element.49.refs_2_, ...), custom_call_target="tpu_custom_call" | custom-call | flops 8589934592 | tf_op jit(solution)/shard_map/pallas_call | solution.py:439
  34.6 5.4 %shard_map.142 = (f32[8,256,1024]{2,1,0:T(8,128)S(1)}, f32[128,256]{1,0:T(8,128)S(1)}, bf16[128,256]{1,0:T(8,128)(2,1)S(1)}) custom-call(s32[2,8]{1,0:T(2,128)S(1)} %pad_add_fusion.refs_0_, s32[1,2176]{1,0:T(1,128)S(1)} %get-tuple-element.40.refs_4_.refs_1_, f32[8,512]{1,0:T(8,128)S(1)} %get-tuple-element.49.refs_2_, ...), custom_call_target="tpu_custom_call" | custom-call | flops 6442450944 | tf_op jit(solution)/shard_map/pallas_call | solution.py:439
  40.0 3.1 %collective-permute-start.12 = (bf16[128,256]{1,0:T(8,128)(2,1)S(1)}, bf16[128,256]{1,0:T(8,128)(2,1)S(1)}, u32[]{:S(2)}, u32[]{:S(2)}) collective-permute-start(bf16[128,256]{1,0:T(8,128)(2,1)S(1)} %get-tuple-element.69), channel_id=1, source_target_pairs={{0,24},{4,28},{8,16},{12,20},{16,8},{20,12},{24,0},{28,4},{1,25},{... | collective-permute-start | bytes 196616 | tf_op jit(solution)/shard_map/ppermute | solution.py:457
  43.1 0.5 collective-permute-start.11
  43.6 0.1 collective-permute-start.10
  43.7 1.9 %collective-permute-start.4 = (bf16[256,256]{1,0:T(8,128)(2,1)S(1)}, bf16[256,256]{1,0:T(8,128)(2,1)S(1)}, u32[]{:S(2)}, u32[]{:S(2)}) collective-permute-start(bf16[256,256]{1,0:T(8,128)(2,1)S(1)} %get-tuple-element.62), channel_id=1, source_target_pairs={{0,8},{4,12},{8,0},{12,4},{16,24},{20,28},{24,16},{28,20},{1,9},{5... | collective-permute-start | bytes 393224 | tf_op jit(solution)/shard_map/ppermute | solution.py:457
  45.6 5.2 %shard_map.143 = (bf16[256,2048]{1,0:T(8,128)(2,1)S(1)}, bf16[2048,256]{1,0:T(8,128)(2,1)S(1)}, bf16[2048,256]{1,0:T(8,128)(2,1)S(1)}, bf16[256,256]{1,0:T(8,128)(2,1)S(1)}, bf16[256,256]{1,0:T(8,128)(2,1)S(1)}) custom-call(s32[2,8]{1,0:T(2,128)S(1)} %pad_add_fusion.refs_0_, s32[1,2176]{1,0:T(1,128)S(1)} %get-tuple-element.40.refs_4_.refs_1_, ...), custom_call_target="tpu_custom_call" | custom-call | flops 8589934592 | tf_op jit(solution)/shard_map/pallas_call | solution.py:439
  50.8 0.4 shard_map.146.raw_in_t
  51.3 2.3 %shard_map.144 = bf16[2048,256]{1,0:T(8,128)(2,1)} custom-call(bf16[2048,256]{1,0:T(8,128)(2,1)S(1)} %get-tuple-element.55.base.feats, bf16[256,2048]{1,0:T(8,128)(2,1)S(1)} %get-tuple-element.56.values_t, bf16[256,256]{1,0:T(8,128)(2,1)S(1)} %get-tuple-element.57.weight), custom_call_target="tpu_custom_call" | custom-call | flops 2147483648 | tf_op jit(solution)/shard_map/pallas_call | solution.py:364
  53.6 0.0 collective-permute-done.4.second
  53.6 1.6 %collective-permute-start.5 = (bf16[256,256]{1,0:T(8,128)(2,1)S(1)}, bf16[256,256]{1,0:T(8,128)(2,1)S(1)}, u32[]{:S(2)}, u32[]{:S(2)}) collective-permute-start(bf16[256,256]{1,0:T(8,128)(2,1)S(1)} %get-tuple-element.64), channel_id=1, source_target_pairs={{0,16},{4,20},{8,24},{12,28},{16,0},{20,4},{24,8},{28,12},{1,17},{... | collective-permute-start | bytes 393224 | tf_op jit(solution)/shard_map/ppermute | solution.py:457
  55.2 0.0 collective-permute-done.12.refs_3_
  55.2 0.0 collective-permute-done.11.refs_2_
  55.2 0.0 collective-permute-done.10.refs_1_
  55.3 0.1 collective-permute-start.13
  55.3 3.3 %collective-permute-done.5.other_out = bf16[256,256]{1,0:T(8,128)(2,1)S(1)} collective-permute-done((bf16[256,256]{1,0:T(8,128)(2,1)S(1)}, bf16[256,256]{1,0:T(8,128)(2,1)S(1)}, u32[]{:S(2)}, u32[]{:S(2)}) %collective-permute-start.5) | collective-permute-done | bytes 131104 | tf_op jit(solution)/shard_map/ppermute | solution.py:457
  58.7 0.1 collective-permute-start.6
  58.8 0.0 collective-permute-done.13.near
  58.8 0.1 shard_map.151
  58.9 0.0 collective-permute-start.14
  58.9 2.3 %shard_map.145 = bf16[2048,256]{1,0:T(8,128)(2,1)} custom-call(bf16[2048,256]{1,0:T(8,128)(2,1)S(1)} %get-tuple-element.58.base, bf16[256,2048]{1,0:T(8,128)(2,1)S(1)} %get-tuple-element.59.values_t.update_t, bf16[256,256]{1,0:T(8,128)(2,1)S(1)} %get-tuple-element.60.weight), custom_call_target="tpu_custom_call" | custom-call | flops 2147483648 | tf_op jit(solution)/shard_map/pallas_call | solution.py:364
  61.2 1.3 %collective-permute-done.14.second = f32[8,128]{1,0:T(8,128)S(1)} collective-permute-done((f32[8,128]{1,0:T(8,128)S(1)}, f32[8,128]{1,0:T(8,128)S(1)}, u32[]{:S(2)}, u32[]{:S(2)}) %collective-permute-start.14) | collective-permute-done | bytes 4128 | tf_op jit(solution)/shard_map/ppermute | solution.py:457
  62.5 0.4 collective-permute-start.15
  62.9 0.0 collective-permute-done.6.near
  62.9 0.1 shard_map.149
  63.0 1.3 %collective-permute-start.9 = (bf16[256,256]{1,0:T(8,128)(2,1)S(1)}, bf16[256,256]{1,0:T(8,128)(2,1)S(1)}, u32[]{:S(2)}, u32[]{:S(2)}) collective-permute-start(bf16[256,256]{1,0:T(8,128)(2,1)S(1)} %get-tuple-element.66), channel_id=1, source_target_pairs={{0,24},{4,28},{8,16},{12,20},{16,8},{20,12},{24,0},{28,4},{1,25},{... | collective-permute-start | bytes 393224 | tf_op jit(solution)/shard_map/ppermute | solution.py:457
  64.3 0.5 collective-permute-start.8
  64.8 1.8 %collective-permute-start.7 = (bf16[256,256]{1,0:T(8,128)(2,1)S(1)}, bf16[256,256]{1,0:T(8,128)(2,1)S(1)}, u32[]{:S(2)}, u32[]{:S(2)}) collective-permute-start(bf16[256,256]{1,0:T(8,128)(2,1)S(1)} %get-tuple-element.66), channel_id=1, source_target_pairs={{0,8},{4,12},{8,0},{12,4},{16,24},{20,28},{24,16},{28,20},{1,9},{5... | collective-permute-start | bytes 393224 | tf_op jit(solution)/shard_map/ppermute | solution.py:457
  66.5 0.5 collective-permute-done.15.second
  67.0 3.3 %collective-permute-done.9.refs_3_ = bf16[256,256]{1,0:T(8,128)(2,1)S(1)} collective-permute-done((bf16[256,256]{1,0:T(8,128)(2,1)S(1)}, bf16[256,256]{1,0:T(8,128)(2,1)S(1)}, u32[]{:S(2)}, u32[]{:S(2)}) %collective-permute-start.9) | collective-permute-done | bytes 131104 | tf_op jit(solution)/shard_map/ppermute | solution.py:457
  70.3 1.7 %collective-permute-done.8.refs_2_ = bf16[256,256]{1,0:T(8,128)(2,1)S(1)} collective-permute-done((bf16[256,256]{1,0:T(8,128)(2,1)S(1)}, bf16[256,256]{1,0:T(8,128)(2,1)S(1)}, u32[]{:S(2)}, u32[]{:S(2)}) %collective-permute-start.8) | collective-permute-done | bytes 131104 | tf_op jit(solution)/shard_map/ppermute | solution.py:457
  72.1 0.1 collective-permute-done.7.refs_1_
  72.2 1.1 %shard_map.154 = (f32[256,256]{1,0:T(8,128)}, f32[256,256]{1,0:T(8,128)}, f32[128,256]{1,0:T(8,128)}) custom-call(f32[256,256]{1,0:T(8,128)S(1)} %get-tuple-element.65.refs_0_, bf16[256,256]{1,0:T(8,128)(2,1)S(1)} %collective-permute-done.7.refs_1_, bf16[256,256]{1,0:T(8,128)(2,1)S(1)} %collective-permute-done.8.refs_2_, ...), custom_call_target="tpu_custom_call" | custom-call | flops 2147483648 | tf_op jit(solution)/shard_map/pallas_call | solution.py:439
  (7 shorter events, 0.1 us)
Async XLA Ops:
  0.6 6.1 %collective-permute-start = (s32[1,3,128]{2,1,0:T(4,128)}, s32[1,3,128]{2,1,0:T(4,128)S(1)}, u32[]{:S(2)}, u32[]{:S(2)}) collective-permute-start(s32[1,3,128]{2,1,0:T(4,128)} %bitcast.19), channel_id=1, source_target_pairs={{0,1},{1,0},{2,3},{3,2},{4,5},{5,4},{6,7},{7,6},{8,9},{9,8},{10,11... | collective-permute-start | bytes 4616 | tf_op jit(solution)/shard_map/ppermute | solution.py:457
  3.8 5.2 %collective-permute-start.1 = (f32[1,128,256]{2,1,0:T(8,128)}, f32[1,128,256]{2,1,0:T(8,128)S(1)}, u32[]{:S(2)}, u32[]{:S(2)}) collective-permute-start(f32[1,128,256]{2,1,0:T(8,128)} %bitcast.17), channel_id=1, source_target_pairs={{0,1},{1,0},{2,3},{3,2},{4,5},{5,4},{6,7},{7,6},{8,9},{9,8},{10,11... | collective-permute-start | bytes 393224 | tf_op jit(solution)/shard_map/ppermute | solution.py:457
  3.8 2.7 %copy-start.3 = (s32[1,2048]{1,0:T(1,128)S(1)}, s32[1,2048]{1,0:T(1,128)}, u32[]{:S(2)}) copy-start(s32[1,2048]{1,0:T(1,128)} %ids_hbm.1) | copy-start | bytes 24580
  9.0 10.3 %collective-permute-start.2 = (f32[2,8,128]{2,1,0:T(8,128)S(1)}, f32[2,8,128]{2,1,0:T(8,128)S(1)}, u32[]{:S(2)}, u32[]{:S(2)}) collective-permute-start(f32[2,8,128]{2,1,0:T(8,128)S(1)} %get-tuple-element.45.kvecs.refs_7_), channel_id=1, source_target_pairs={{0,2},{1,3},{2,0},{3,1},{4,6},{5,7},{6,4},{7,5},{8,10},{9,11},{10,... | collective-permute-start | bytes 24584 | tf_op jit(solution)/shard_map/ppermute | solution.py:457
  11.6 15.8 %collective-permute-start.3 = (f32[2,128,256]{2,1,0:T(8,128)S(1)}, f32[2,128,256]{2,1,0:T(8,128)S(1)}, u32[]{:S(2)}, u32[]{:S(2)}) collective-permute-start(f32[2,128,256]{2,1,0:T(8,128)S(1)} %get-tuple-element.52.refs_8_.refs_6_), channel_id=1, source_target_pairs={{0,2},{1,3},{2,0},{3,1},{4,6},{5,7},{6,4},{7,5},{8,10},{9,11},{10,... | collective-permute-start | bytes 786440 | tf_op jit(solution)/shard_map/ppermute | solution.py:457
  19.3 8.1 %copy-start = (bf16[2048,256]{1,0:T(8,128)(2,1)S(1)}, bf16[2048,256]{1,0:T(8,128)(2,1)}, u32[]{:S(2)}) copy-start(bf16[2048,256]{1,0:T(8,128)(2,1)} %refs_9_.1) | copy-start | bytes 3145732
  19.3 8.1 %copy-start.1 = (bf16[256,256]{1,0:T(8,128)(2,1)S(1)}, bf16[256,256]{1,0:T(8,128)(2,1)}, u32[]{:S(2)}) copy-start(bf16[256,256]{1,0:T(8,128)(2,1)} %refs_11_.1) | copy-start | bytes 393220
  19.3 8.1 %copy-start.2 = (f32[256]{0:T(256)S(1)}, f32[256]{0:T(256)}, u32[]{:S(2)}) copy-start(f32[256]{0:T(256)} %param.18) | copy-start | bytes 3076
  40.0 15.2 %collective-permute-start.12 = (bf16[128,256]{1,0:T(8,128)(2,1)S(1)}, bf16[128,256]{1,0:T(8,128)(2,1)S(1)}, u32[]{:S(2)}, u32[]{:S(2)}) collective-permute-start(bf16[128,256]{1,0:T(8,128)(2,1)S(1)} %get-tuple-element.69), channel_id=1, source_target_pairs={{0,24},{4,28},{8,16},{12,20},{16,8},{20,12},{24,0},{28,4},{1,25},{... | collective-permute-start | bytes 196616 | tf_op jit(solution)/shard_map/ppermute | solution.py:457
  43.1 12.2 %collective-permute-start.11 = (bf16[128,256]{1,0:T(8,128)(2,1)S(1)}, bf16[128,256]{1,0:T(8,128)(2,1)S(1)}, u32[]{:S(2)}, u32[]{:S(2)}) collective-permute-start(bf16[128,256]{1,0:T(8,128)(2,1)S(1)} %get-tuple-element.69), channel_id=1, source_target_pairs={{0,16},{4,20},{8,24},{12,28},{16,0},{20,4},{24,8},{28,12},{1,17},{... | collective-permute-start | bytes 196616 | tf_op jit(solution)/shard_map/ppermute | solution.py:457
  43.6 11.7 %collective-permute-start.10 = (bf16[128,256]{1,0:T(8,128)(2,1)S(1)}, bf16[128,256]{1,0:T(8,128)(2,1)S(1)}, u32[]{:S(2)}, u32[]{:S(2)}) collective-permute-start(bf16[128,256]{1,0:T(8,128)(2,1)S(1)} %get-tuple-element.69), channel_id=1, source_target_pairs={{0,8},{4,12},{8,0},{12,4},{16,24},{20,28},{24,16},{28,20},{1,9},{5... | collective-permute-start | bytes 196616 | tf_op jit(solution)/shard_map/ppermute | solution.py:457
  43.7 9.9 %collective-permute-start.4 = (bf16[256,256]{1,0:T(8,128)(2,1)S(1)}, bf16[256,256]{1,0:T(8,128)(2,1)S(1)}, u32[]{:S(2)}, u32[]{:S(2)}) collective-permute-start(bf16[256,256]{1,0:T(8,128)(2,1)S(1)} %get-tuple-element.62), channel_id=1, source_target_pairs={{0,8},{4,12},{8,0},{12,4},{16,24},{20,28},{24,16},{28,20},{1,9},{5... | collective-permute-start | bytes 393224 | tf_op jit(solution)/shard_map/ppermute | solution.py:457
  53.6 5.0 %collective-permute-start.5 = (bf16[256,256]{1,0:T(8,128)(2,1)S(1)}, bf16[256,256]{1,0:T(8,128)(2,1)S(1)}, u32[]{:S(2)}, u32[]{:S(2)}) collective-permute-start(bf16[256,256]{1,0:T(8,128)(2,1)S(1)} %get-tuple-element.64), channel_id=1, source_target_pairs={{0,16},{4,20},{8,24},{12,28},{16,0},{20,4},{24,8},{28,12},{1,17},{... | collective-permute-start | bytes 393224 | tf_op jit(solution)/shard_map/ppermute | solution.py:457
  55.3 3.5 %collective-permute-start.13 = (f32[128,256]{1,0:T(8,128)S(1)}, f32[128,256]{1,0:T(8,128)S(1)}, u32[]{:S(2)}, u32[]{:S(2)}) collective-permute-start(f32[128,256]{1,0:T(8,128)S(1)} %shard_map.150.filt), channel_id=1, source_target_pairs={{0,4},{4,0},{8,12},{12,8},{16,20},{20,16},{24,28},{28,24},{1,5},{5... | collective-permute-start | bytes 393224 | tf_op jit(solution)/shard_map/ppermute | solution.py:457
  58.7 4.2 %collective-permute-start.6 = (f32[512,256]{1,0:T(8,128)S(1)}, f32[512,256]{1,0:T(8,128)S(1)}, u32[]{:S(2)}, u32[]{:S(2)}) collective-permute-start(f32[512,256]{1,0:T(8,128)S(1)} %shard_map.148.pack), channel_id=1, source_target_pairs={{0,4},{4,0},{8,12},{12,8},{16,20},{20,16},{24,28},{28,24},{1,5},{5... | collective-permute-start | bytes 1572872 | tf_op jit(solution)/shard_map/ppermute | solution.py:457
  58.9 3.6 %collective-permute-start.14 = (f32[8,128]{1,0:T(8,128)S(1)}, f32[8,128]{1,0:T(8,128)S(1)}, u32[]{:S(2)}, u32[]{:S(2)}) collective-permute-start(f32[8,128]{1,0:T(8,128)S(1)} %get-tuple-element.71.first), channel_id=1, source_target_pairs={{0,1},{1,0},{2,3},{3,2},{4,5},{5,4},{6,7},{7,6},{8,9},{9,8},{10,11... | collective-permute-start | bytes 12296 | tf_op jit(solution)/shard_map/ppermute | solution.py:457
  62.5 4.5 %collective-permute-start.15 = (f32[8,128]{1,0:T(8,128)S(1)}, f32[8,128]{1,0:T(8,128)S(1)}, u32[]{:S(2)}, u32[]{:S(2)}) collective-permute-start(f32[8,128]{1,0:T(8,128)S(1)} %shard_map.152.first), channel_id=1, source_target_pairs={{0,2},{1,3},{2,0},{3,1},{4,6},{5,7},{6,4},{7,5},{8,10},{9,11},{10,... | collective-permute-start | bytes 12296 | tf_op jit(solution)/shard_map/ppermute | solution.py:457
  63.0 7.4 %collective-permute-start.9 = (bf16[256,256]{1,0:T(8,128)(2,1)S(1)}, bf16[256,256]{1,0:T(8,128)(2,1)S(1)}, u32[]{:S(2)}, u32[]{:S(2)}) collective-permute-start(bf16[256,256]{1,0:T(8,128)(2,1)S(1)} %get-tuple-element.66), channel_id=1, source_target_pairs={{0,24},{4,28},{8,16},{12,20},{16,8},{20,12},{24,0},{28,4},{1,25},{... | collective-permute-start | bytes 393224 | tf_op jit(solution)/shard_map/ppermute | solution.py:457
  64.3 7.8 %collective-permute-start.8 = (bf16[256,256]{1,0:T(8,128)(2,1)S(1)}, bf16[256,256]{1,0:T(8,128)(2,1)S(1)}, u32[]{:S(2)}, u32[]{:S(2)}) collective-permute-start(bf16[256,256]{1,0:T(8,128)(2,1)S(1)} %get-tuple-element.66), channel_id=1, source_target_pairs={{0,16},{4,20},{8,24},{12,28},{16,0},{20,4},{24,8},{28,12},{1,17},{... | collective-permute-start | bytes 393224 | tf_op jit(solution)/shard_map/ppermute | solution.py:457
  64.8 7.4 %collective-permute-start.7 = (bf16[256,256]{1,0:T(8,128)(2,1)S(1)}, bf16[256,256]{1,0:T(8,128)(2,1)S(1)}, u32[]{:S(2)}, u32[]{:S(2)}) collective-permute-start(bf16[256,256]{1,0:T(8,128)(2,1)S(1)} %get-tuple-element.66), channel_id=1, source_target_pairs={{0,8},{4,12},{8,0},{12,4},{16,24},{20,28},{24,16},{28,20},{1,9},{5... | collective-permute-start | bytes 393224 | tf_op jit(solution)/shard_map/ppermute | solution.py:457

commit v5 on v4

--- a/solution.py
+++ b/solution.py
@@ -84,15 +84,6 @@
         pl.when(steps == n)(functools.partial(action, n))
 
 
-def gather_cell(cell, start, steps, most, ids, source, waves, store):
-    def action(n):
-        at = pl.ds(start, n * TILE)
-        member = (ids[:, at] == cell).astype(F32).astype(BF16)
-        store(mm(source[:, at] * member, waves[:, at], 1, 1))
-
-    by_steps(steps, most, action)
-
-
 def weigh(cell, n_ka, bounds, quad, filt_t, width_cols, sums, weights):
     own = filt_t.shape[1] // n_ka
     inverse = inverse_count(bounds[0, cell])
@@ -142,29 +133,28 @@
     return jnp.exp2(exponent)
 
 
-def fill_waves(waves, base, kcols, coords):
-    own = kcols.shape[0]
+def fill_slice(waves, base, own, kcols, first, row, coords):
     atoms = coords.shape[1]
     wide = tile_of(atoms, 1024)
-
-    def phase_rows(i, carry):
-        row = pl.multiple_of(i * 16, 16)
-        kv = kcols[pl.ds(row, 16), :]
-        for start in range(0, atoms, wide):
-            frac = coords[:, start : start + wide]
-            turns = kv[:, 0:1] * frac[0:1, :] + kv[:, 1:2] * frac[1:2, :]
-            turns = turns + kv[:, 2:3] * frac[2:3, :]
-            turns = turns - ((turns + ROUNDER) - ROUNDER)
-            square = turns * turns
-            waves[pl.ds(pl.multiple_of(base + row, 16), 16), start : start + wide] = horner(
-                COS_TERMS, square
-            ).astype(BF16)
-            waves[pl.ds(pl.multiple_of(base + own + row, 16), 16), start : start + wide] = (
-                horner(SIN_TERMS, square) * turns
-            ).astype(BF16)
-        return carry
-
-    lax.fori_loop(0, own // 16, phase_rows, 0)
+    row = pl.multiple_of(row, 16)
+    kv = kcols[pl.ds(pl.multiple_of(first + row, 16), 16), :]
+    for start in range(0, atoms, wide):
+        frac = coords[:, start : start + wide]
+        turns = kv[:, 0:1] * frac[0:1, :] + kv[:, 1:2] * frac[1:2, :]
+        turns = turns + kv[:, 2:3] * frac[2:3, :]
+        turns = turns - ((turns + ROUNDER) - ROUNDER)
+        square = turns * turns
+        waves[pl.ds(pl.multiple_of(base + row, 16), 16), start : start + wide] = horner(
+            COS_TERMS, square
+        ).astype(BF16)
+        waves[pl.ds(pl.multiple_of(base + own + row, 16), 16), start : start + wide] = (
+            horner(SIN_TERMS, square) * turns
+        ).astype(BF16)
+
+
+def rows_of_share(index, shares, own):
+    each = -(-own // (16 * shares))
+    return [16 * jnp.minimum(index * each + p, own // 16 - 1) for p in range(each)]
 
 
 def vector_columns(kvec):
@@ -183,9 +173,10 @@
 
 def prepare_kernel(
     coords_hbm, ids_hbm, recip_hbm, kvec_hbm, kfilt_hbm,
-    waves, ids, coords, recip, kvec, kfilt, kcols, sems,
+    waves, ids, coords, recip, kvec, kfilt, bounds, kcols, sems,
 ):
     atoms = coords.shape[1]
+    own = kvec.shape[1]
     copies = start_copies(
         sems,
         (kvec_hbm, kvec),
@@ -196,15 +187,27 @@
     )
     ids[:, atoms:] = jnp.full((1, LANES), -1, jnp.int32)
     waves[:, atoms:] = jnp.zeros((waves.shape[0], LANES), BF16)
-    copies[0].wait()
-    copies[1].wait()
+    for copy in copies[:3]:
+        copy.wait()
     kcols[...] = vector_columns(kvec)
-    fill_waves(waves, 0, kcols, coords)
-    for copy in copies[2:]:
+    numbers = ids[:, :atoms]
+    before = 0
+    for cell in range(bounds.shape[1]):
+        count = jnp.sum((numbers == cell).astype(F32)).astype(jnp.int32)
+        bounds[0, cell] = count
+        bounds[1, cell] = before
+        before = before + count
+
+    def phase_rows(i, carry):
+        fill_slice(waves, 0, own, kcols, 0, 16 * i, coords)
+        return carry
+
+    lax.fori_loop(0, own // 16, phase_rows, 0)
+    for copy in copies[3:]:
         copy.wait()
 
 
-def pair_kernel(kvec, other_kvec, kfilt, other_kfilt, kvecs, kfilts):
+def pair_kernel(kvec, other_kvec, kvecs):
     count = kvec.shape[0]
     for j in range(count):
         for at, source in ((j, kvec), (j + count, other_kvec)):
@@ -212,26 +215,33 @@
             if rows.shape[0] == 3:
                 rows = jnp.concatenate([rows, jnp.zeros((5, rows.shape[1]), F32)], axis=0)
             kvecs[at] = rows
-        kfilts[j] = kfilt[j]
-        kfilts[j + count] = other_kfilt[j]
+
+
+def stack_kernel(near, far, out):
+    count = near.shape[0]
+    out[:count] = near[...].astype(out.dtype)
+    out[count:] = far[...].astype(out.dtype)
 
 
 def project_kernel(coords, kvecs, feats_hbm, w_in_hbm, waves, proj_t, feats, w_in, kcols, sems):
     atoms, chan = feats.shape
+    own = kcols.shape[0]
     copies = start_copies(sems, (w_in_hbm, w_in), (feats_hbm, feats))
     waves[:, atoms:] = jnp.zeros((waves.shape[0], LANES), BF16)
     proj_t[:, atoms:] = jnp.zeros((chan, LANES), BF16)
     kcols[...] = vector_columns(kvecs.at[1])
-    fill_waves(waves, 0, kcols, coords)
     for copy in copies:
         copy.wait()
+    tiles = atoms // TILE
 
     def project(t, carry):
         at = pl.ds(pl.multiple_of(t * TILE, TILE), TILE)
         proj_t[:, at] = mm(w_in[...], feats[at, :], 0, 1).astype(BF16)
+        for row in rows_of_share(t, tiles, own):
+            fill_slice(waves, 0, own, kcols, 0, row, coords)
         return carry
 
-    lax.fori_loop(0, atoms // TILE, project, 0)
+    lax.fori_loop(0, tiles, project, 0)
 
 
 def waves_kernel(n_ka, *refs):
@@ -241,12 +251,9 @@
     atoms = coords.shape[1]
     own = kvecs[0].shape[1]
     cells = recip.shape[0]
-    waves[: 2 * own, :] = first[...]
-    waves[2 * own : 4 * own, :] = second[...]
-    waves[4 * own :, atoms:] = jnp.zeros((2 * own * (n_ka - 2), LANES), BF16)
+    most = most_steps(atoms)
     for j in range(2, n_ka):
-        kcols[...] = vector_columns(kvecs[j])
-        fill_waves(waves, 2 * own * j, kcols, coords)
+        kcols[(j - 2) * own : (j - 1) * own, :] = vector_columns(kvecs[j])
     for j in range(n_ka):
         rows = kvecs[j][...]
         squared = jnp.zeros((cells, own), F32)
@@ -256,17 +263,39 @@
             part = part + recip[:, 3 * r + 2 : 3 * r + 3] * rows[2:3, :]
             squared = squared + part * part
         quad[:, own * j : own * (j + 1)] = squared
-
-    def cell_step(cell, carry):
+    waves[4 * own :, atoms:] = jnp.zeros((2 * own * (n_ka - 2), LANES), BF16)
+
+    def early(cell, carry):
         start, steps, _ = span_of(bounds, cell)
 
-        def store(value):
-            factors[cell] = value
-
-        gather_cell(cell, start, steps, most_steps(atoms), ids, proj_t, waves, store)
+        def action(n):
+            at = pl.ds(start, n * TILE)
+            lhs = proj_t[:, at] * (ids[:, at] == cell).astype(F32).astype(BF16)
+            factors[cell, :, : 2 * own] = mm(lhs, first[:, at], 1, 1)
+            factors[cell, :, 2 * own : 4 * own] = mm(lhs, second[:, at], 1, 1)
+            for j in range(2, n_ka):
+                for row in rows_of_share(cell, cells, own):
+                    fill_slice(waves, 2 * own * j, own, kcols, (j - 2) * own, row, coords)
+
+        by_steps(steps, most, action)
         return carry
 
-    lax.fori_loop(0, cells, cell_step, 0)
+    lax.fori_loop(0, cells, early, 0)
+    waves[: 2 * own, :] = first[...]
+    waves[2 * own : 4 * own, :] = second[...]
+
+    def late(cell, carry):
+        start, steps, _ = span_of(bounds, cell)
+
+        def action(n):
+            at = pl.ds(start, n * TILE)
+            lhs = proj_t[:, at] * (ids[:, at] == cell).astype(F32).astype(BF16)
+            factors[cell, :, 4 * own :] = mm(lhs, waves[4 * own :, at], 1, 1)
+
+        by_steps(steps, most, action)
+        return carry
+
+    lax.fori_loop(0, cells, late, 0)
 
 
 def filters_first(filt_t, kfilts):
@@ -274,7 +303,7 @@
     for ref in kfilts:
         own = ref.shape[1]
         for j in range(ref.shape[0]):
-            filt_t[:, chunk * own : (chunk + 1) * own] = ref[j].T
+            filt_t[:, chunk * own : (chunk + 1) * own] = ref[j].astype(F32).T
             chunk += 1
     return own
 
@@ -289,8 +318,10 @@
     mgrad_t[:, atoms:] = jnp.zeros((chan, LANES), BF16)
     raw_out[...] = jnp.zeros_like(raw_out)
 
+    wide = tile_of(atoms, 2 * TILE)
+
     def middle(t, carry):
-        at = pl.ds(pl.multiple_of(t * TILE, TILE), TILE)
+        at = pl.ds(pl.multiple_of(t * wide, wide), wide)
         message = mess_t[:, at]
         sigma = jax.nn.sigmoid(message)
         activated = (message * sigma).astype(BF16)
@@ -301,7 +332,7 @@
         raw_out[...] += mm(activated, cot)
         return carry
 
-    lax.fori_loop(0, atoms // TILE, middle, 0)
+    lax.fori_loop(0, atoms // wide, middle, 0)
     raw_half[...] = raw_out[...].astype(BF16)
 
 
@@ -314,21 +345,35 @@
     width_cols[...] = column_to_lanes(spread[...] * (-LOG2_E))
     grad_t[...] = jnp.zeros_like(grad_t)
 
-    def cell_step(cell, carry):
-        start, steps, count = span_of(bounds, cell)
-
-        def store(value):
-            sums[cell] = value
-
-        gather_cell(cell, start, steps, most_steps(atoms), ids, mgrad_t, waves, store)
-        scaled = shape_of(cell, quad, width_cols, 0, own) * inverse_count(count)
+    most = most_steps(atoms)
+
+    def collect(cell):
+        scaled = shape_of(cell, quad, width_cols, 0, own) * inverse_count(bounds[0, cell])
         grad_t[...] += scaled * (
             factors[cell, :, :own] * sums[cell, :, :own]
             + factors[cell, :, own : 2 * own] * sums[cell, :, own : 2 * own]
         )
+
+    def gather(cell, before):
+        start, steps, _ = span_of(bounds, cell)
+
+        def action(n):
+            if before is not None:
+                collect(before)
+            at = pl.ds(start, n * TILE)
+            lhs = mgrad_t[:, at] * (ids[:, at] == cell).astype(F32).astype(BF16)
+            sums[cell] = mm(lhs, waves[:, at], 1, 1)
+
+        by_steps(steps, most, action)
+
+    gather(0, None)
+
+    def cell_step(cell, carry):
+        gather(cell, cell - 1)
         return carry
 
-    lax.fori_loop(0, cells, cell_step, 0)
+    lax.fori_loop(1, cells, cell_step, 0)
+    collect(cells - 1)
     result = grad_t[...].T
     filter_grad[...] = result
     filter_half[...] = result.astype(BF16)
@@ -381,11 +426,23 @@
 def join_kernel(raw_in_t, raw_out, other_out, pack):
     chan = raw_in_t.shape[0]
     pack[:chan, :] = raw_in_t[...]
-    pack[chan:, :] = total_of(raw_out, (other_out,))
+    pack[chan:, :] = raw_out[...] + other_out[:chan, :].astype(F32)
+
+
+def out_kernel(raw_out, other_out, filter_half, out_sum, packed):
+    chan = raw_out.shape[0]
+    value = raw_out[...] + other_out[:chan, :].astype(F32)
+    out_sum[...] = value
+    packed[:chan, :] = value.astype(BF16)
+    packed[chan:, :] = filter_half[...]
 
 
 def filter_kernel(*refs):
-    refs[-1][...] = total_of(refs[0], refs[1:-1])
+    own = refs[0].shape[0]
+    value = refs[0][...]
+    for ref in refs[1:-1]:
+        value = value + ref[ref.shape[0] - own :, :].astype(F32)
+    refs[-1][...] = value
 
 
 def squares_kernel(filt, near, f_sum, f_squares):
@@ -432,7 +489,9 @@
     g_filt[...] = filt[...] * filter_scale
 
 
-def call(kernel, operands, smem, outs, scratch=(), limit=SMALL, micros=2, space=pltpu.VMEM):
+def call(
+    kernel, operands, smem, outs, scratch=(), limit=SMALL, micros=2, space=pltpu.VMEM, smem_outs=0
+):
     vmem = pl.BlockSpec(memory_space=pltpu.VMEM)
     rest = len(operands) - smem
     spaces = space if isinstance(space, tuple) else (space,) * rest
@@ -440,7 +499,8 @@
         kernel,
         out_shape=tuple(jax.ShapeDtypeStruct(*o) for o in outs),
         in_specs=[pl.BlockSpec(memory_space=x) for x in (pltpu.SMEM,) * smem + spaces],
-        out_specs=tuple(vmem for _ in outs),
+        out_specs=(vmem,) * (len(outs) - smem_outs)
+        + (pl.BlockSpec(memory_space=pltpu.SMEM),) * smem_outs,
         scratch_shapes=list(scratch),
         compiler_params=pltpu.CompilerParams(vmem_limit_bytes=limit),
         cost_estimate=pl.CostEstimate(
@@ -475,14 +535,7 @@
     dma = pltpu.SemaphoreType.DMA
     near_kvec = send(kvec[None], "ka", 1)
     near_kfilt = send(kfilt[None], "ka", 1)
-    numbers = jnp.arange(cells, dtype=jnp.int32)[:, None]
-    bounds = jnp.stack(
-        [
-            jnp.sum((cell_ids == numbers).astype(jnp.int32), axis=1),
-            jnp.sum((cell_ids < numbers).astype(jnp.int32), axis=1),
-        ]
-    )
-    first, ids, coords, recip, kvec, kfilt = call(
+    first, ids, coords, recip, kvec, kfilt, bounds = call(
         prepare_kernel,
         [in_hbm(x) for x in (coords, cell_ids, recip, kvec, kfilt)],
         0,
@@ -493,29 +546,22 @@
             (recip.shape, F32),
             (kvec.shape, jnp.int32),
             (kfilt.shape, F32),
+            ((2, cells), jnp.int32),
         ],
         [vm((own, 8), F32), dma((5,))],
         SMALL,
         3,
         pltpu.HBM,
-    )
-    kvecs, kfilts = call(
-        pair_kernel,
-        (kvec[None], near_kvec, kfilt[None], near_kfilt),
-        0,
-        [((2, 8, own), F32), ((2, own, chan), F32)],
-    )
-    far_kvecs, far_kfilts = [kvecs], [kfilts]
-    for s in doubling(2, n_ka):
+        smem_outs=1,
+    )
+    kfilt = kfilt[None]
+    (kvecs,) = call(pair_kernel, (kvec[None], near_kvec), 0, [((2, 8, own), F32)])
+    far_kvecs, far_kfilts = [kvecs], [kfilt, near_kfilt]
+    ka_steps = doubling(2, n_ka)
+    for s in ka_steps:
         if s > 2:
-            kvecs, kfilts = call(
-                pair_kernel,
-                (kvecs, far_kvecs[-1], kfilts, far_kfilts[-1]),
-                0,
-                [((s, 8, own), F32), ((s, own, chan), F32)],
-            )
+            (kvecs,) = call(pair_kernel, (kvecs, far_kvecs[-1]), 0, [((s, 8, own), F32)])
         far_kvecs.append(send(kvecs, "ka", s))
-        far_kfilts.append(send(kfilts, "ka", s))
     second, proj_t = call(
         project_kernel,
         (coords, far_kvecs[0], in_hbm(feats), in_hbm(w_in)),
@@ -526,12 +572,16 @@
         3,
         (pltpu.VMEM, pltpu.VMEM, pltpu.HBM, pltpu.HBM),
     )
+    kfilts = kfilt
+    for s in ka_steps:
+        (kfilts,) = call(stack_kernel, (kfilts, far_kfilts[-1]), 0, [((s, own, chan), BF16)])
+        far_kfilts.append(send(kfilts, "ka", s))
     waves, factors, quad = call(
         functools.partial(waves_kernel, n_ka),
         (bounds, first, second, proj_t, ids, coords, recip, *far_kvecs),
         1,
         [((2 * k_all, long), BF16), ((cells, chan, 2 * k_all), F32), ((cells, k_all), F32)],
-        [vm((own, 8), F32)],
+        [vm((k_all - 2 * own, 8), F32)],
         LIMIT,
         8,
     )
@@ -556,10 +606,20 @@
         LIMIT,
         6,
     )
-    filt_parts = [send(filter_half, "dp", s) for s in chips]
-    for s in out_steps[1:]:
+    raw_out, packed = call(
+        out_kernel,
+        (raw_out, out_part, filter_half),
+        0,
+        [((chan, chan), F32), ((chan + own, chan), BF16)],
+    )
+    filt_parts = [send(packed if s == 4 else filter_half, "dp", s) for s in chips]
+    out_part = filt_parts[1]
+    for s in out_steps[2:]:
         raw_out, raw_half = call(
-            add_kernel, (raw_out, out_part), 0, [((chan, chan), F32), ((chan, chan), BF16)]
+            out_kernel,
+            (raw_out, out_part, filter_half),
+            0,
+            [((chan, chan), F32), ((chan + own, chan), BF16)],
         )
         out_part = send(raw_half, "dp", s)
     held = (feats, cotan, w_in, w_out)

time: 73.4 us -> 66.8 us (0.910)
  waiting for transfers between devices: 16.1 us -> 8.27 us
  starting transfers between devices: 17.4 us -> 20.2 us
  Pallas kernels: 38.7 us -> 37.3 us
    ppermute x16 -> x15, waiting for transfers between devices: 16.1 us -> 8.27 us  [send(): return lax.ppermute(value, axis, routes(step, lax.axis_size(axis)))]
    ppermute x16 -> x15, starting transfers between devices: 17.4 us -> 20.2 us  [send(): return lax.ppermute(value, axis, routes(step, lax.axis_size(axis)))]
    pallas_call x16 -> x17, Pallas kernels: 34.1 us -> 32.7 us  [call(): pl.pallas_call(kernel, out_shape=tuple((jax.ShapeDtypeStruct(*o) for o in...]
  transfers between devices with their start and end apart: 16 -> 15, of which waited for: 8 -> 5; matrix products, arithmetic and copies ran while one was open for 0% -> 0% of each run, Pallas kernels for 34% -> 38%
where the time goes in v5:
time: 66.8 us; the launch traced here: 66.6 us
  Pallas kernels  37.3 us (56%)
  starting transfers between devices  20.2 us (30%)
  waiting for transfers between devices  8.27 us (12%)
  between operations  0.8 us (1%)
    pallas_call x17, Pallas kernels, call(): pl.pallas_call(kernel, out_shape=tuple((jax.ShapeDtypeStruct(*o) for o in...  32.7 us
    ppermute x15, starting transfers between devices, send(): return lax.ppermute(value, axis, routes(step, lax.axis_size(axis)))  20.2 us
    ppermute x15, waiting for transfers between devices, send(): return lax.ppermute(value, axis, routes(step, lax.axis_size(axis)))  8.27 us
    pallas_call x2, Pallas kernels, residual(): pl.pallas_call(functools.partial(residual_kernel, transposed), out_shape=...  4.61 us
  transfers between devices with their start and end apart: 15, of which 5 were waited for; matrix products, arithmetic and copies ran while one was open for 0% of the time, Pallas kernels for 38%

profile of v5, /device:TPU:0, one launch (start us, length us, event | category | flops | bytes accessed | tf_op | source)
XLA Modules:
  0.0 66.6 jit_solution(5473101125587546699)
XLA Ops:
  0.6 3.1 %collective-permute-start = (s32[1,3,128]{2,1,0:T(4,128)}, s32[1,3,128]{2,1,0:T(4,128)S(1)}, u32[]{:S(2)}, u32[]{:S(2)}) collective-permute-start(s32[1,3,128]{2,1,0:T(4,128)} %bitcast.15), channel_id=1, source_target_pairs={{0,1},{1,0},{2,3},{3,2},{4,5},{5,4},{6,7},{7,6},{8,9},{9,8},{10,11... | collective-permute-start | bytes 4616 | tf_op jit(solution)/shard_map/ppermute | solution.py:517
  3.8 0.1 collective-permute-start.2
  3.8 3.4 %shard_map.137 = (bf16[256,2176]{1,0:T(8,128)(2,1)S(1)}, s32[1,2176]{1,0:T(1,128)S(1)}, f32[3,2048]{1,0:T(4,128)S(1)}, f32[8,9]{1,0:T(8,128)S(1)}, s32[3,128]{1,...) custom-call(f32[3,2048]{1,0:T(4,128)} %coords_hbm.1, s32[1,2048]{1,0:T(1,128)} %ids_hbm.1, f32[8,9]{1,0:T(8,128)} %bitcast.14, ...), custom_call_target="tpu_custom_call" | custom-call | flops 3221225472 | tf_op jit(solution)/shard_map/pallas_call | solution.py:498
  7.2 0.0 collective-permute-done.other_kvec
  7.2 3.0 %collective-permute-start.1 = (f32[2,8,128]{2,1,0:T(8,128)S(1)}, f32[2,8,128]{2,1,0:T(8,128)S(1)}, u32[]{:S(2)}, u32[]{:S(2)}) collective-permute-start(f32[2,8,128]{2,1,0:T(8,128)S(1)} %shard_map.138.kvecs.refs_7_), channel_id=1, source_target_pairs={{0,2},{1,3},{2,0},{3,1},{4,6},{5,7},{6,4},{7,5},{8,10},{9,11},{10,... | collective-permute-start | bytes 24584 | tf_op jit(solution)/shard_map/ppermute | solution.py:517
  10.3 3.5 %shard_map.139 = (bf16[256,2176]{1,0:T(8,128)(2,1)S(1)}, bf16[256,2176]{1,0:T(8,128)(2,1)S(1)}) custom-call(f32[3,2048]{1,0:T(4,128)S(1)} %get-tuple-element.42.coords.refs_5_, f32[2,8,128]{2,1,0:T(8,128)S(1)} %shard_map.138.kvecs.refs_7_, bf16[2048,256]{1,0:T(8,128)(2,1)} %refs_9_.1, bf16[256,256]{1,0:T(8,128)(2,1)} %refs_11_.1), custom_call_target="tpu_custom_call" | custom-call | flops 3221225472 | tf_op jit(solution)/shard_map/pallas_call | solution.py:498
  13.8 0.0 collective-permute-done.2.far.refs_9_.refs_7_
  13.8 0.1 collective-permute-start.3
  13.9 0.0 collective-permute-done.1.refs_8_
  13.9 0.0 copy-start
  13.9 0.0 copy-start.1
  13.9 0.0 copy-start.2
  13.9 7.7 %shard_map.140 = (bf16[1024,2176]{1,0:T(8,128)(2,1)S(1)}, f32[8,256,1024]{2,1,0:T(8,128)S(1)}, f32[8,512]{1,0:T(8,128)S(1)}) custom-call(s32[2,8]{1,0:T(2,128)S(1)} %get-tuple-element.39.refs_0_, bf16[256,2176]{1,0:T(8,128)(2,1)S(1)} %get-tuple-element.41.refs_1_, bf16[256,2176]{1,0:T(8,128)(2,1)S(1)} %get-tuple-element.44.refs_2_, ...), custom_call_target="tpu_custom_call" | custom-call | flops 8589934592 | tf_op jit(solution)/shard_map/pallas_call | solution.py:498
  21.7 0.3 collective-permute-done.3.refs_10_.refs_8_
  22.0 0.0 copy-done
  22.0 0.0 copy-done.1
  22.0 0.0 copy-done.2
  22.0 6.4 %shard_map.142 = (bf16[256,2048]{1,0:T(8,128)(2,1)S(1)}, bf16[256,2176]{1,0:T(8,128)(2,1)S(1)}, f32[256,256]{1,0:T(8,128)S(1)}, bf16[256,256]{1,0:T(8,128)(2,1)S(1)}) custom-call(s32[2,8]{1,0:T(2,128)S(1)} %get-tuple-element.39.refs_0_, s32[1,2176]{1,0:T(1,128)S(1)} %get-tuple-element.40.refs_4_.refs_1_, f32[8,512]{1,0:T(8,128)S(1)} %get-tuple-element.47.refs_2_, ...), custom_call_target="tpu_custom_call" | custom-call | flops 8589934592 | tf_op jit(solution)/shard_map/pallas_call | solution.py:498
  28.4 4.6 %shard_map.143 = (f32[8,256,1024]{2,1,0:T(8,128)S(1)}, f32[128,256]{1,0:T(8,128)S(1)}, bf16[128,256]{1,0:T(8,128)(2,1)S(1)}) custom-call(s32[2,8]{1,0:T(2,128)S(1)} %get-tuple-element.39.refs_0_, s32[1,2176]{1,0:T(1,128)S(1)} %get-tuple-element.40.refs_4_.refs_1_, f32[8,512]{1,0:T(8,128)S(1)} %get-tuple-element.47.refs_2_, ...), custom_call_target="tpu_custom_call" | custom-call | flops 6442450944 | tf_op jit(solution)/shard_map/pallas_call | solution.py:498
  33.1 2.9 %collective-permute-start.11 = (bf16[128,256]{1,0:T(8,128)(2,1)S(1)}, bf16[128,256]{1,0:T(8,128)(2,1)S(1)}, u32[]{:S(2)}, u32[]{:S(2)}) collective-permute-start(bf16[128,256]{1,0:T(8,128)(2,1)S(1)} %get-tuple-element.61.filter_half), channel_id=1, source_target_pairs={{0,24},{4,28},{8,16},{12,20},{16,8},{20,12},{24,0},{28,4},{1,25},{... | collective-permute-start | bytes 196616 | tf_op jit(solution)/shard_map/ppermute | solution.py:517
  36.0 0.1 collective-permute-start.10
  36.1 1.9 %collective-permute-start.4 = (bf16[256,256]{1,0:T(8,128)(2,1)S(1)}, bf16[256,256]{1,0:T(8,128)(2,1)S(1)}, u32[]{:S(2)}, u32[]{:S(2)}) collective-permute-start(bf16[256,256]{1,0:T(8,128)(2,1)S(1)} %get-tuple-element.60), channel_id=1, source_target_pairs={{0,8},{4,12},{8,0},{12,4},{16,24},{20,28},{24,16},{28,20},{1,9},{5... | collective-permute-start | bytes 393224 | tf_op jit(solution)/shard_map/ppermute | solution.py:517
  38.0 5.2 %shard_map.144 = (bf16[256,2048]{1,0:T(8,128)(2,1)S(1)}, bf16[2048,256]{1,0:T(8,128)(2,1)S(1)}, bf16[2048,256]{1,0:T(8,128)(2,1)S(1)}, bf16[256,256]{1,0:T(8,128)(2,1)S(1)}, bf16[256,256]{1,0:T(8,128)(2,1)S(1)}) custom-call(s32[2,8]{1,0:T(2,128)S(1)} %get-tuple-element.39.refs_0_, s32[1,2176]{1,0:T(1,128)S(1)} %get-tuple-element.40.refs_4_.refs_1_, ...), custom_call_target="tpu_custom_call" | custom-call | flops 8589934592 | tf_op jit(solution)/shard_map/pallas_call | solution.py:498
  43.2 0.4 shard_map.147.raw_in_t
  43.7 0.0 collective-permute-done.4.other_out
  43.7 0.6 collective-permute-start.5
  44.3 2.3 %shard_map.145 = bf16[2048,256]{1,0:T(8,128)(2,1)} custom-call(bf16[2048,256]{1,0:T(8,128)(2,1)S(1)} %get-tuple-element.53.base.feats, bf16[256,2048]{1,0:T(8,128)(2,1)S(1)} %get-tuple-element.54.values_t, bf16[256,256]{1,0:T(8,128)(2,1)S(1)} %get-tuple-element.55.weight), custom_call_target="tpu_custom_call" | custom-call | flops 2147483648 | tf_op jit(solution)/shard_map/pallas_call | solution.py:409
  46.6 0.0 collective-permute-done.11.refs_3_
  46.6 0.0 collective-permute-done.10.refs_1_
  46.6 2.8 %collective-permute-done.5.other_out.refs_2_ = bf16[384,256]{1,0:T(8,128)(2,1)S(1)} collective-permute-done((bf16[384,256]{1,0:T(8,128)(2,1)S(1)}, bf16[384,256]{1,0:T(8,128)(2,1)S(1)}, u32[]{:S(2)}, u32[]{:S(2)}) %collective-permute-start.5) | collective-permute-done | bytes 196640 | tf_op jit(solution)/shard_map/ppermute | solution.py:517
  49.5 0.1 collective-permute-start.12
  49.6 0.6 collective-permute-start.6
  50.2 0.7 %collective-permute-done.12.near = f32[128,256]{1,0:T(8,128)S(1)} collective-permute-done((f32[128,256]{1,0:T(8,128)S(1)}, f32[128,256]{1,0:T(8,128)S(1)}, u32[]{:S(2)}, u32[]{:S(2)}) %collective-permute-start.12) | collective-permute-done | bytes 131104 | tf_op jit(solution)/shard_map/ppermute | solution.py:517
  50.9 0.1 shard_map.152
  51.0 1.6 %collective-permute-start.13 = (f32[8,128]{1,0:T(8,128)S(1)}, f32[8,128]{1,0:T(8,128)S(1)}, u32[]{:S(2)}, u32[]{:S(2)}) collective-permute-start(f32[8,128]{1,0:T(8,128)S(1)} %get-tuple-element.69.first), channel_id=1, source_target_pairs={{0,1},{1,0},{2,3},{3,2},{4,5},{5,4},{6,7},{7,6},{8,9},{9,8},{10,11... | collective-permute-start | bytes 12296 | tf_op jit(solution)/shard_map/ppermute | solution.py:517
  52.6 2.3 %shard_map.146 = bf16[2048,256]{1,0:T(8,128)(2,1)} custom-call(bf16[2048,256]{1,0:T(8,128)(2,1)S(1)} %get-tuple-element.56.base, bf16[256,2048]{1,0:T(8,128)(2,1)S(1)} %get-tuple-element.57.values_t.update_t, bf16[256,256]{1,0:T(8,128)(2,1)S(1)} %get-tuple-element.58.weight), custom_call_target="tpu_custom_call" | custom-call | flops 2147483648 | tf_op jit(solution)/shard_map/pallas_call | solution.py:409
  54.9 0.0 collective-permute-done.13.second
  54.9 2.6 %collective-permute-start.14 = (f32[8,128]{1,0:T(8,128)S(1)}, f32[8,128]{1,0:T(8,128)S(1)}, u32[]{:S(2)}, u32[]{:S(2)}) collective-permute-start(f32[8,128]{1,0:T(8,128)S(1)} %shard_map.153.first), channel_id=1, source_target_pairs={{0,2},{1,3},{2,0},{3,1},{4,6},{5,7},{6,4},{7,5},{8,10},{9,11},{10,... | collective-permute-start | bytes 12296 | tf_op jit(solution)/shard_map/ppermute | solution.py:517
  57.5 0.0 collective-permute-done.6.near
  57.5 0.1 shard_map.150
  57.6 0.3 collective-permute-start.9
  57.9 1.4 %collective-permute-start.8 = (bf16[256,256]{1,0:T(8,128)(2,1)S(1)}, bf16[256,256]{1,0:T(8,128)(2,1)S(1)}, u32[]{:S(2)}, u32[]{:S(2)}) collective-permute-start(bf16[256,256]{1,0:T(8,128)(2,1)S(1)} %get-tuple-element.65), channel_id=1, source_target_pairs={{0,16},{4,20},{8,24},{12,28},{16,0},{20,4},{24,8},{28,12},{1,17},{... | collective-permute-start | bytes 393224 | tf_op jit(solution)/shard_map/ppermute | solution.py:517
  59.3 1.8 %collective-permute-start.7 = (bf16[256,256]{1,0:T(8,128)(2,1)S(1)}, bf16[256,256]{1,0:T(8,128)(2,1)S(1)}, u32[]{:S(2)}, u32[]{:S(2)}) collective-permute-start(bf16[256,256]{1,0:T(8,128)(2,1)S(1)} %get-tuple-element.65), channel_id=1, source_target_pairs={{0,8},{4,12},{8,0},{12,4},{16,24},{20,28},{24,16},{28,20},{1,9},{5... | collective-permute-start | bytes 393224 | tf_op jit(solution)/shard_map/ppermute | solution.py:517
  61.1 0.0 collective-permute-done.14.second
  61.1 3.8 %collective-permute-done.9.refs_3_ = bf16[256,256]{1,0:T(8,128)(2,1)S(1)} collective-permute-done((bf16[256,256]{1,0:T(8,128)(2,1)S(1)}, bf16[256,256]{1,0:T(8,128)(2,1)S(1)}, u32[]{:S(2)}, u32[]{:S(2)}) %collective-permute-start.9) | collective-permute-done | bytes 131104 | tf_op jit(solution)/shard_map/ppermute | solution.py:517
  64.9 0.6 collective-permute-done.8.refs_2_
  65.5 0.0 collective-permute-done.7.refs_1_
  65.5 1.1 %shard_map.155 = (f32[256,256]{1,0:T(8,128)}, f32[256,256]{1,0:T(8,128)}, f32[128,256]{1,0:T(8,128)}) custom-call(f32[256,256]{1,0:T(8,128)S(1)} %get-tuple-element.64.refs_0_, bf16[256,256]{1,0:T(8,128)(2,1)S(1)} %collective-permute-done.7.refs_1_, bf16[256,256]{1,0:T(8,128)(2,1)S(1)} %collective-permute-done.8.refs_2_, ...), custom_call_target="tpu_custom_call" | custom-call | flops 2147483648 | tf_op jit(solution)/shard_map/pallas_call | solution.py:498
  (7 shorter events, 0.2 us)
Async XLA Ops:
  0.6 6.6 %collective-permute-start = (s32[1,3,128]{2,1,0:T(4,128)}, s32[1,3,128]{2,1,0:T(4,128)S(1)}, u32[]{:S(2)}, u32[]{:S(2)}) collective-permute-start(s32[1,3,128]{2,1,0:T(4,128)} %bitcast.15), channel_id=1, source_target_pairs={{0,1},{1,0},{2,3},{3,2},{4,5},{5,4},{6,7},{7,6},{8,9},{9,8},{10,11... | collective-permute-start | bytes 4616 | tf_op jit(solution)/shard_map/ppermute | solution.py:517
  3.8 10.0 %collective-permute-start.2 = (f32[1,128,256]{2,1,0:T(8,128)}, f32[1,128,256]{2,1,0:T(8,128)S(1)}, u32[]{:S(2)}, u32[]{:S(2)}) collective-permute-start(f32[1,128,256]{2,1,0:T(8,128)} %bitcast.13), channel_id=1, source_target_pairs={{0,1},{1,0},{2,3},{3,2},{4,5},{5,4},{6,7},{7,6},{8,9},{9,8},{10,11... | collective-permute-start | bytes 393224 | tf_op jit(solution)/shard_map/ppermute | solution.py:517
  7.2 6.7 %collective-permute-start.1 = (f32[2,8,128]{2,1,0:T(8,128)S(1)}, f32[2,8,128]{2,1,0:T(8,128)S(1)}, u32[]{:S(2)}, u32[]{:S(2)}) collective-permute-start(f32[2,8,128]{2,1,0:T(8,128)S(1)} %shard_map.138.kvecs.refs_7_), channel_id=1, source_target_pairs={{0,2},{1,3},{2,0},{3,1},{4,6},{5,7},{6,4},{7,5},{8,10},{9,11},{10,... | collective-permute-start | bytes 24584 | tf_op jit(solution)/shard_map/ppermute | solution.py:517
  13.8 8.2 %collective-permute-start.3 = (bf16[2,128,256]{2,1,0:T(8,128)(2,1)S(1)}, bf16[2,128,256]{2,1,0:T(8,128)(2,1)S(1)}, u32[]{:S(2)}, u32[]{:S(2)}) collective-permute-start(bf16[2,128,256]{2,1,0:T(8,128)(2,1)S(1)} %shard_map.141), channel_id=1, source_target_pairs={{0,2},{1,3},{2,0},{3,1},{4,6},{5,7},{6,4},{7,5},{8,10},{9,11},{10,... | collective-permute-start | bytes 393224 | tf_op jit(solution)/shard_map/ppermute | solution.py:517
  13.9 8.1 %copy-start = (bf16[2048,256]{1,0:T(8,128)(2,1)S(1)}, bf16[2048,256]{1,0:T(8,128)(2,1)}, u32[]{:S(2)}) copy-start(bf16[2048,256]{1,0:T(8,128)(2,1)} %refs_10_.1) | copy-start | bytes 3145732
  13.9 8.1 %copy-start.1 = (bf16[256,256]{1,0:T(8,128)(2,1)S(1)}, bf16[256,256]{1,0:T(8,128)(2,1)}, u32[]{:S(2)}) copy-start(bf16[256,256]{1,0:T(8,128)(2,1)} %refs_12_.1) | copy-start | bytes 393220
  13.9 8.1 %copy-start.2 = (f32[256]{0:T(256)S(1)}, f32[256]{0:T(256)}, u32[]{:S(2)}) copy-start(f32[256]{0:T(256)} %param.18) | copy-start | bytes 3076
  33.1 13.6 %collective-permute-start.11 = (bf16[128,256]{1,0:T(8,128)(2,1)S(1)}, bf16[128,256]{1,0:T(8,128)(2,1)S(1)}, u32[]{:S(2)}, u32[]{:S(2)}) collective-permute-start(bf16[128,256]{1,0:T(8,128)(2,1)S(1)} %get-tuple-element.61.filter_half), channel_id=1, source_target_pairs={{0,24},{4,28},{8,16},{12,20},{16,8},{20,12},{24,0},{28,4},{1,25},{... | collective-permute-start | bytes 196616 | tf_op jit(solution)/shard_map/ppermute | solution.py:517
  36.0 10.6 %collective-permute-start.10 = (bf16[128,256]{1,0:T(8,128)(2,1)S(1)}, bf16[128,256]{1,0:T(8,128)(2,1)S(1)}, u32[]{:S(2)}, u32[]{:S(2)}) collective-permute-start(bf16[128,256]{1,0:T(8,128)(2,1)S(1)} %get-tuple-element.61.filter_half), channel_id=1, source_target_pairs={{0,8},{4,12},{8,0},{12,4},{16,24},{20,28},{24,16},{28,20},{1,9},{5... | collective-permute-start | bytes 196616 | tf_op jit(solution)/shard_map/ppermute | solution.py:517
  36.1 7.6 %collective-permute-start.4 = (bf16[256,256]{1,0:T(8,128)(2,1)S(1)}, bf16[256,256]{1,0:T(8,128)(2,1)S(1)}, u32[]{:S(2)}, u32[]{:S(2)}) collective-permute-start(bf16[256,256]{1,0:T(8,128)(2,1)S(1)} %get-tuple-element.60), channel_id=1, source_target_pairs={{0,8},{4,12},{8,0},{12,4},{16,24},{20,28},{24,16},{28,20},{1,9},{5... | collective-permute-start | bytes 393224 | tf_op jit(solution)/shard_map/ppermute | solution.py:517
  43.7 5.7 %collective-permute-start.5 = (bf16[384,256]{1,0:T(8,128)(2,1)S(1)}, bf16[384,256]{1,0:T(8,128)(2,1)S(1)}, u32[]{:S(2)}, u32[]{:S(2)}) collective-permute-start(bf16[384,256]{1,0:T(8,128)(2,1)S(1)} %get-tuple-element.63), channel_id=1, source_target_pairs={{0,16},{4,20},{8,24},{12,28},{16,0},{20,4},{24,8},{28,12},{1,17},{... | collective-permute-start | bytes 589832 | tf_op jit(solution)/shard_map/ppermute | solution.py:517
  49.5 1.4 %collective-permute-start.12 = (f32[128,256]{1,0:T(8,128)S(1)}, f32[128,256]{1,0:T(8,128)S(1)}, u32[]{:S(2)}, u32[]{:S(2)}) collective-permute-start(f32[128,256]{1,0:T(8,128)S(1)} %shard_map.151.filt), channel_id=1, source_target_pairs={{0,4},{4,0},{8,12},{12,8},{16,20},{20,16},{24,28},{28,24},{1,5},{5... | collective-permute-start | bytes 393224 | tf_op jit(solution)/shard_map/ppermute | solution.py:517
  49.6 7.9 %collective-permute-start.6 = (f32[512,256]{1,0:T(8,128)S(1)}, f32[512,256]{1,0:T(8,128)S(1)}, u32[]{:S(2)}, u32[]{:S(2)}) collective-permute-start(f32[512,256]{1,0:T(8,128)S(1)} %shard_map.149.pack), channel_id=1, source_target_pairs={{0,4},{4,0},{8,12},{12,8},{16,20},{20,16},{24,28},{28,24},{1,5},{5... | collective-permute-start | bytes 1572872 | tf_op jit(solution)/shard_map/ppermute | solution.py:517
  51.0 3.9 %collective-permute-start.13 = (f32[8,128]{1,0:T(8,128)S(1)}, f32[8,128]{1,0:T(8,128)S(1)}, u32[]{:S(2)}, u32[]{:S(2)}) collective-permute-start(f32[8,128]{1,0:T(8,128)S(1)} %get-tuple-element.69.first), channel_id=1, source_target_pairs={{0,1},{1,0},{2,3},{3,2},{4,5},{5,4},{6,7},{7,6},{8,9},{9,8},{10,11... | collective-permute-start | bytes 12296 | tf_op jit(solution)/shard_map/ppermute | solution.py:517
  54.9 6.2 %collective-permute-start.14 = (f32[8,128]{1,0:T(8,128)S(1)}, f32[8,128]{1,0:T(8,128)S(1)}, u32[]{:S(2)}, u32[]{:S(2)}) collective-permute-start(f32[8,128]{1,0:T(8,128)S(1)} %shard_map.153.first), channel_id=1, source_target_pairs={{0,2},{1,3},{2,0},{3,1},{4,6},{5,7},{6,4},{7,5},{8,10},{9,11},{10,... | collective-permute-start | bytes 12296 | tf_op jit(solution)/shard_map/ppermute | solution.py:517
  57.6 7.3 %collective-permute-start.9 = (bf16[256,256]{1,0:T(8,128)(2,1)S(1)}, bf16[256,256]{1,0:T(8,128)(2,1)S(1)}, u32[]{:S(2)}, u32[]{:S(2)}) collective-permute-start(bf16[256,256]{1,0:T(8,128)(2,1)S(1)} %get-tuple-element.65), channel_id=1, source_target_pairs={{0,24},{4,28},{8,16},{12,20},{16,8},{20,12},{24,0},{28,4},{1,25},{... | collective-permute-start | bytes 393224 | tf_op jit(solution)/shard_map/ppermute | solution.py:517
  57.9 7.6 %collective-permute-start.8 = (bf16[256,256]{1,0:T(8,128)(2,1)S(1)}, bf16[256,256]{1,0:T(8,128)(2,1)S(1)}, u32[]{:S(2)}, u32[]{:S(2)}) collective-permute-start(bf16[256,256]{1,0:T(8,128)(2,1)S(1)} %get-tuple-element.65), channel_id=1, source_target_pairs={{0,16},{4,20},{8,24},{12,28},{16,0},{20,4},{24,8},{28,12},{1,17},{... | collective-permute-start | bytes 393224 | tf_op jit(solution)/shard_map/ppermute | solution.py:517
  59.3 6.2 %collective-permute-start.7 = (bf16[256,256]{1,0:T(8,128)(2,1)S(1)}, bf16[256,256]{1,0:T(8,128)(2,1)S(1)}, u32[]{:S(2)}, u32[]{:S(2)}) collective-permute-start(bf16[256,256]{1,0:T(8,128)(2,1)S(1)} %get-tuple-element.65), channel_id=1, source_target_pairs={{0,8},{4,12},{8,0},{12,4},{16,24},{20,28},{24,16},{28,20},{1,9},{5... | collective-permute-start | bytes 393224 | tf_op jit(solution)/shard_map/ppermute | solution.py:517

commit v6 on v5

--- a/solution.py
+++ b/solution.py
@@ -190,6 +190,7 @@
     for copy in copies[:3]:
         copy.wait()
     kcols[...] = vector_columns(kvec)
+    fill_slice(waves, 0, own, kcols, 0, 0, coords)
     numbers = ids[:, :atoms]
     before = 0
     for cell in range(bounds.shape[1]):
@@ -202,7 +203,7 @@
         fill_slice(waves, 0, own, kcols, 0, 16 * i, coords)
         return carry
 
-    lax.fori_loop(0, own // 16, phase_rows, 0)
+    lax.fori_loop(1, own // 16, phase_rows, 0)
     for copy in copies[3:]:
         copy.wait()
 
@@ -276,13 +277,15 @@
             for j in range(2, n_ka):
                 for row in rows_of_share(cell, cells, own):
                     fill_slice(waves, 2 * own * j, own, kcols, (j - 2) * own, row, coords)
+            for row in rows_of_share(cell, cells, 2 * own):
+                from_rows = pl.ds(pl.multiple_of(row, 16), 16)
+                waves[from_rows, :] = first[from_rows, :]
+                waves[pl.ds(pl.multiple_of(2 * own + row, 16), 16), :] = second[from_rows, :]
 
         by_steps(steps, most, action)
         return carry
 
     lax.fori_loop(0, cells, early, 0)
-    waves[: 2 * own, :] = first[...]
-    waves[2 * own : 4 * own, :] = second[...]
 
     def late(cell, carry):
         start, steps, _ = span_of(bounds, cell)
@@ -397,25 +400,32 @@
     raw_in_t[...] = mm(update_t[...], feats[...])
 
 
-def residual_kernel(transposed, base, values_t, weight, out):
-    value = mm(values_t[...].T, weight[...], 1, 1 if transposed else 0)
-    out[...] = (base[...].astype(F32) + value).astype(BF16)
+def residual_kernel(transposed, base, values_t, weight, out_hbm, out, sems):
+    rows = base.shape[0]
+    step = tile_of(rows, 512)
+    copies = []
+    for t in range(rows // step):
+        at = slice(t * step, (t + 1) * step)
+        value = mm(values_t[:, at].T, weight[...], 1, 1 if transposed else 0)
+        out[at, :] = (base[at, :].astype(F32) + value).astype(BF16)
+        copies.append(pltpu.make_async_copy(out.at[at, :], out_hbm.at[at, :], sems.at[t]))
+        copies[-1].start()
+    for copy in copies:
+        copy.wait()
 
 
 def residual(transposed, base, values_t, weight):
     rows, chan = base.shape
-    step = tile_of(rows, 512)
-    by_rows = pl.BlockSpec((step, chan), lambda i: (i, 0))
+    vmem = pl.BlockSpec(memory_space=pltpu.VMEM)
     return pl.pallas_call(
         functools.partial(residual_kernel, transposed),
         out_shape=jax.ShapeDtypeStruct((rows, chan), BF16),
-        grid=(rows // step,),
-        in_specs=[
-            by_rows,
-            pl.BlockSpec((chan, step), lambda i: (0, i)),
-            pl.BlockSpec((chan, chan), lambda i: (0, 0)),
+        in_specs=[vmem] * 3,
+        out_specs=pl.BlockSpec(memory_space=pltpu.HBM),
+        scratch_shapes=[
+            pltpu.VMEM((rows, chan), BF16),
+            pltpu.SemaphoreType.DMA((rows // tile_of(rows, 512),)),
         ],
-        out_specs=by_rows,
         compiler_params=pltpu.CompilerParams(vmem_limit_bytes=SMALL),
         cost_estimate=pl.CostEstimate(
             flops=2 * FLOPS_PER_MICRO, bytes_accessed=0, transcendentals=0
@@ -423,10 +433,8 @@
     )(base, values_t, weight)
 
 
-def join_kernel(raw_in_t, raw_out, other_out, pack):
-    chan = raw_in_t.shape[0]
-    pack[:chan, :] = raw_in_t[...]
-    pack[chan:, :] = raw_out[...] + other_out[:chan, :].astype(F32)
+def last_out_kernel(raw_out, other_out, out_sum):
+    out_sum[...] = raw_out[...] + other_out[: raw_out.shape[0], :].astype(F32)
 
 
 def out_kernel(raw_out, other_out, filter_half, out_sum, packed):
@@ -454,12 +462,10 @@
     )
 
 
-def chip_kernel(pack, near, in_sum, in_half, w_sum):
-    chan = in_sum.shape[0]
-    value = pack[:chan, :] + near[:chan, :]
+def chip_kernel(raw_in_t, near, in_sum, in_half):
+    value = raw_in_t[...] + near[...]
     in_sum[...] = value
     in_half[...] = value.astype(BF16)
-    w_sum[...] = pack[chan:, :] + near[chan:, :]
 
 
 def total_of(first, others):
@@ -477,9 +483,9 @@
 
 def final_kernel(n_chip, n_ka, *refs):
     in_parts = refs[:n_chip]
-    raw_out, filt, squares, g_in, g_out, g_filt = refs[n_chip:]
+    raw_out, near_out, filt, squares, g_in, g_out, g_filt = refs[n_chip:]
     raw_in = total_of(in_parts[0], in_parts[1:])
-    out = raw_out[...]
+    out = raw_out[...] + near_out[...]
     both = raw_in * raw_in + out * out
     weight_squares = jnp.sum(jnp.sum(both, axis=0, keepdims=True), axis=1, keepdims=True)
     weight_scale = lax.rsqrt(weight_squares / (2 * raw_in.size) + 1e-06)
@@ -574,7 +580,7 @@
     )
     kfilts = kfilt
     for s in ka_steps:
-        (kfilts,) = call(stack_kernel, (kfilts, far_kfilts[-1]), 0, [((s, own, chan), BF16)])
+        (kfilts,) = call(stack_kernel, (kfilts, far_kfilts[-1]), 0, [((s, own, chan), F32)])
         far_kfilts.append(send(kfilts, "ka", s))
     waves, factors, quad = call(
         functools.partial(waves_kernel, n_ka),
@@ -636,29 +642,27 @@
     (filt_sum,) = call(filter_kernel, (filter_grad, *filt_parts), 0, [((own, chan), F32)])
     filt_near = send(filt_sum, "dp", 1)
     (raw_in_t,) = call(gradient_kernel, (update_t, feats), 0, [((chan, chan), F32)])
-    (pack,) = call(join_kernel, (raw_in_t, raw_out, out_part), 0, [((2 * chan, chan), F32)])
-    near = send(pack, "dp", 1)
+    near = send(raw_in_t, "dp", 1)
+    (out_sum,) = call(last_out_kernel, (raw_out, out_part), 0, [((chan, chan), F32)])
     f_sum, squares = call(
         squares_kernel, (filt_sum, filt_near), 0, [((own, chan), F32), ((8, LANES), F32)]
     )
     square_steps = doubling(1, n_ka)
     square_part = send(squares, "ka", square_steps[0])
     feat_grad = residual(True, cotan, update_t, w_in)
-    in_sum, in_half, w_sum = call(
-        chip_kernel,
-        (pack, near),
-        0,
-        [((chan, chan), F32), ((chan, chan), BF16), ((chan, chan), F32)],
+    in_sum, in_half = call(
+        chip_kernel, (raw_in_t, near), 0, [((chan, chan), F32), ((chan, chan), BF16)]
     )
     in_parts = [in_sum] + [send(in_half, "dp", s) for s in chips]
     for s in square_steps[1:] + [0]:
         (squares,) = call(add_kernel, (squares, square_part), 0, [((8, LANES), F32)])
         if s:
             square_part = send(squares, "ka", s)
+    near_out = send(out_sum, "dp", 1)
     mixed = residual(False, feats, act_t, w_out)
     grads = call(
         functools.partial(final_kernel, len(in_parts), n_ka),
-        (*in_parts, w_sum, f_sum, squares),
+        (*in_parts, out_sum, near_out, f_sum, squares),
         0,
         [((chan, chan), F32), ((chan, chan), F32), ((own, chan), F32)],
     )

time: 66.8 us -> 70.9 us (1.061)
  waiting for transfers between devices: 8.27 us -> 18.5 us
  starting transfers between devices: 20.2 us -> 15.9 us
  Pallas kernels: 37.3 us -> 35.4 us
    ppermute x15 -> x16, waiting for transfers between devices: 8.27 us -> 18.5 us  [send(): return lax.ppermute(value, axis, routes(step, lax.axis_size(axis)))]
    ppermute x15 -> x16, starting transfers between devices: 20.2 us -> 15.9 us  [send(): return lax.ppermute(value, axis, routes(step, lax.axis_size(axis)))]
    pallas_call x2, Pallas kernels: 4.61 us -> 2.69 us  [residual(): pl.pallas_call(functools.partial(residual_kernel, transposed), out_shape=...]
  transfers between devices with their start and end apart: 15 -> 16, of which waited for: 5 -> 6; matrix products, arithmetic and copies ran while one was open for 0% -> 0% of each run, Pallas kernels for 38% -> 33%
where the time goes in v6:
time: 70.9 us; the launch traced here: 70.7 us
  Pallas kernels  35.4 us (50%)
  waiting for transfers between devices  18.5 us (26%)
  starting transfers between devices  15.9 us (22%)
  between operations  0.84 us (1%)
    pallas_call x17, Pallas kernels, call(): pl.pallas_call(kernel, out_shape=tuple((jax.ShapeDtypeStruct(*o) for o in...  32.7 us
    ppermute x16, waiting for transfers between devices, send(): return lax.ppermute(value, axis, routes(step, lax.axis_size(axis)))  18.5 us
    ppermute x16, starting transfers between devices, send(): return lax.ppermute(value, axis, routes(step, lax.axis_size(axis)))  15.9 us
    pallas_call x2, Pallas kernels, residual(): pl.pallas_call(functools.partial(residual_kernel, transposed), out_shape=...  2.69 us
  transfers between devices with their start and end apart: 16, of which 6 were waited for; matrix products, arithmetic and copies ran while one was open for 0% of the time, Pallas kernels for 33%

profile of v6, /device:TPU:0, one launch (start us, length us, event | category | flops | bytes accessed | tf_op | source)
XLA Modules:
  0.0 70.7 jit_solution(7392120173978522117)
XLA Ops:
  0.6 3.1 %collective-permute-start = (s32[1,3,128]{2,1,0:T(4,128)}, s32[1,3,128]{2,1,0:T(4,128)S(1)}, u32[]{:S(2)}, u32[]{:S(2)}) collective-permute-start(s32[1,3,128]{2,1,0:T(4,128)} %bitcast.15), channel_id=1, source_target_pairs={{0,1},{1,0},{2,3},{3,2},{4,5},{5,4},{6,7},{7,6},{8,9},{9,8},{10,11... | collective-permute-start | bytes 4616 | tf_op jit(solution)/shard_map/ppermute | solution.py:523
  3.8 0.1 collective-permute-start.2
  3.8 3.3 %shard_map.137 = (bf16[256,2176]{1,0:T(8,128)(2,1)S(1)}, s32[1,2176]{1,0:T(1,128)S(1)}, f32[3,2048]{1,0:T(4,128)S(1)}, f32[8,9]{1,0:T(8,128)S(1)}, s32[3,128]{1,...) custom-call(f32[3,2048]{1,0:T(4,128)} %coords_hbm.1, s32[1,2048]{1,0:T(1,128)} %ids_hbm.1, f32[8,9]{1,0:T(8,128)} %bitcast.14, ...), custom_call_target="tpu_custom_call" | custom-call | flops 3221225472 | tf_op jit(solution)/shard_map/pallas_call | solution.py:504
  7.1 0.0 collective-permute-done.other_kvec
  7.1 3.0 %collective-permute-start.1 = (f32[2,8,128]{2,1,0:T(8,128)S(1)}, f32[2,8,128]{2,1,0:T(8,128)S(1)}, u32[]{:S(2)}, u32[]{:S(2)}) collective-permute-start(f32[2,8,128]{2,1,0:T(8,128)S(1)} %shard_map.138.kvecs.refs_7_), channel_id=1, source_target_pairs={{0,2},{1,3},{2,0},{3,1},{4,6},{5,7},{6,4},{7,5},{8,10},{9,11},{10,... | collective-permute-start | bytes 24584 | tf_op jit(solution)/shard_map/ppermute | solution.py:523
  10.1 3.5 %shard_map.139 = (bf16[256,2176]{1,0:T(8,128)(2,1)S(1)}, bf16[256,2176]{1,0:T(8,128)(2,1)S(1)}) custom-call(f32[3,2048]{1,0:T(4,128)S(1)} %get-tuple-element.41.coords.refs_5_, f32[2,8,128]{2,1,0:T(8,128)S(1)} %shard_map.138.kvecs.refs_7_, bf16[2048,256]{1,0:T(8,128)(2,1)} %refs_9_.1, bf16[256,256]{1,0:T(8,128)(2,1)} %refs_11_.1), custom_call_target="tpu_custom_call" | custom-call | flops 3221225472 | tf_op jit(solution)/shard_map/pallas_call | solution.py:504
  13.7 0.0 collective-permute-done.2.far.refs_9_.refs_7_
  13.7 0.1 collective-permute-start.3
  13.8 0.0 collective-permute-done.1.refs_8_
  13.8 0.0 copy-start
  13.8 0.0 copy-start.1
  13.8 0.0 copy-start.2
  13.8 7.8 %shard_map.140 = (bf16[1024,2176]{1,0:T(8,128)(2,1)S(1)}, f32[8,256,1024]{2,1,0:T(8,128)S(1)}, f32[8,512]{1,0:T(8,128)S(1)}) custom-call(s32[2,8]{1,0:T(2,128)S(1)} %get-tuple-element.38.refs_0_, bf16[256,2176]{1,0:T(8,128)(2,1)S(1)} %get-tuple-element.40.refs_1_, bf16[256,2176]{1,0:T(8,128)(2,1)S(1)} %get-tuple-element.43.refs_2_, ...), custom_call_target="tpu_custom_call" | custom-call | flops 8589934592 | tf_op jit(solution)/shard_map/pallas_call | solution.py:504
  21.6 5.9 %collective-permute-done.3.refs_10_.refs_8_ = f32[2,128,256]{2,1,0:T(8,128)S(1)} collective-permute-done((f32[2,128,256]{2,1,0:T(8,128)S(1)}, f32[2,128,256]{2,1,0:T(8,128)S(1)}, u32[]{:S(2)}, u32[]{:S(2)}) %collective-permute-start.3) | collective-permute-done | bytes 262176 | tf_op jit(solution)/shard_map/ppermute | solution.py:523
  27.5 0.0 copy-done
  27.5 0.0 copy-done.1
  27.5 0.0 copy-done.2
  27.5 6.5 %shard_map.142 = (bf16[256,2048]{1,0:T(8,128)(2,1)S(1)}, bf16[256,2176]{1,0:T(8,128)(2,1)S(1)}, f32[256,256]{1,0:T(8,128)S(1)}, bf16[256,256]{1,0:T(8,128)(2,1)S(1)}) custom-call(s32[2,8]{1,0:T(2,128)S(1)} %get-tuple-element.38.refs_0_, s32[1,2176]{1,0:T(1,128)S(1)} %get-tuple-element.39.refs_4_.refs_1_, f32[8,512]{1,0:T(8,128)S(1)} %get-tuple-element.46.refs_2_, ...), custom_call_target="tpu_custom_call" | custom-call | flops 8589934592 | tf_op jit(solution)/shard_map/pallas_call | solution.py:504
  34.0 4.7 %shard_map.143 = (f32[8,256,1024]{2,1,0:T(8,128)S(1)}, f32[128,256]{1,0:T(8,128)S(1)}, bf16[128,256]{1,0:T(8,128)(2,1)S(1)}) custom-call(s32[2,8]{1,0:T(2,128)S(1)} %get-tuple-element.38.refs_0_, s32[1,2176]{1,0:T(1,128)S(1)} %get-tuple-element.39.refs_4_.refs_1_, f32[8,512]{1,0:T(8,128)S(1)} %get-tuple-element.46.refs_2_, ...), custom_call_target="tpu_custom_call" | custom-call | flops 6442450944 | tf_op jit(solution)/shard_map/pallas_call | solution.py:504
  38.6 2.8 %collective-permute-start.12 = (bf16[128,256]{1,0:T(8,128)(2,1)S(1)}, bf16[128,256]{1,0:T(8,128)(2,1)S(1)}, u32[]{:S(2)}, u32[]{:S(2)}) collective-permute-start(bf16[128,256]{1,0:T(8,128)(2,1)S(1)} %get-tuple-element.62.filter_half), channel_id=1, source_target_pairs={{0,24},{4,28},{8,16},{12,20},{16,8},{20,12},{24,0},{28,4},{1,25},{... | collective-permute-start | bytes 196616 | tf_op jit(solution)/shard_map/ppermute | solution.py:523
  41.4 0.2 collective-permute-start.11
  41.6 1.8 %collective-permute-start.8 = (bf16[256,256]{1,0:T(8,128)(2,1)S(1)}, bf16[256,256]{1,0:T(8,128)(2,1)S(1)}, u32[]{:S(2)}, u32[]{:S(2)}) collective-permute-start(bf16[256,256]{1,0:T(8,128)(2,1)S(1)} %get-tuple-element.61), channel_id=1, source_target_pairs={{0,8},{4,12},{8,0},{12,4},{16,24},{20,28},{24,16},{28,20},{1,9},{5... | collective-permute-start | bytes 393224 | tf_op jit(solution)/shard_map/ppermute | solution.py:523
  43.4 5.2 %shard_map.144 = (bf16[256,2048]{1,0:T(8,128)(2,1)S(1)}, bf16[2048,256]{1,0:T(8,128)(2,1)S(1)}, bf16[2048,256]{1,0:T(8,128)(2,1)S(1)}, bf16[256,256]{1,0:T(8,128)(2,1)S(1)}, bf16[256,256]{1,0:T(8,128)(2,1)S(1)}) custom-call(s32[2,8]{1,0:T(2,128)S(1)} %get-tuple-element.38.refs_0_, s32[1,2176]{1,0:T(1,128)S(1)} %get-tuple-element.39.refs_4_.refs_1_, ...), custom_call_target="tpu_custom_call" | custom-call | flops 8589934592 | tf_op jit(solution)/shard_map/pallas_call | solution.py:504
  48.7 0.4 shard_map.147.raw_in_t
  49.1 0.1 collective-permute-start.4
  49.2 0.0 collective-permute-done.8.other_out
  49.3 0.5 collective-permute-start.9
  49.8 1.3 %shard_map.145 = bf16[2048,256]{1,0:T(8,128)(2,1)} custom-call(bf16[2048,256]{1,0:T(8,128)(2,1)S(1)} %get-tuple-element.52.base.feats, bf16[256,2048]{1,0:T(8,128)(2,1)S(1)} %get-tuple-element.53.values_t, bf16[256,256]{1,0:T(8,128)(2,1)S(1)} %get-tuple-element.54.weight), custom_call_target="tpu_custom_call" | custom-call | flops 2147483648 | tf_op jit(solution)/shard_map/pallas_call | solution.py:420
  51.1 0.0 collective-permute-done.12.refs_3_
  51.2 0.0 collective-permute-done.11.refs_1_
  51.2 5.5 %collective-permute-done.9.other_out.refs_2_ = bf16[384,256]{1,0:T(8,128)(2,1)S(1)} collective-permute-done((bf16[384,256]{1,0:T(8,128)(2,1)S(1)}, bf16[384,256]{1,0:T(8,128)(2,1)S(1)}, u32[]{:S(2)}, u32[]{:S(2)}) %collective-permute-start.9) | collective-permute-done | bytes 196640 | tf_op jit(solution)/shard_map/ppermute | solution.py:523
  56.7 0.1 collective-permute-start.13
  56.7 1.4 %shard_map.146 = bf16[2048,256]{1,0:T(8,128)(2,1)} custom-call(bf16[2048,256]{1,0:T(8,128)(2,1)S(1)} %get-tuple-element.55.base, bf16[256,2048]{1,0:T(8,128)(2,1)S(1)} %get-tuple-element.56.values_t.update_t, bf16[256,256]{1,0:T(8,128)(2,1)S(1)} %get-tuple-element.57.weight), custom_call_target="tpu_custom_call" | custom-call | flops 2147483648 | tf_op jit(solution)/shard_map/pallas_call | solution.py:420
  58.1 0.0 collective-permute-done.13.near
  58.1 0.1 shard_map.152
  58.2 0.0 collective-permute-start.14
  58.3 0.6 collective-permute-start.10
  58.8 3.0 %collective-permute-done.14.second = f32[8,128]{1,0:T(8,128)S(1)} collective-permute-done((f32[8,128]{1,0:T(8,128)S(1)}, f32[8,128]{1,0:T(8,128)S(1)}, u32[]{:S(2)}, u32[]{:S(2)}) %collective-permute-start.14) | collective-permute-done | bytes 4128 | tf_op jit(solution)/shard_map/ppermute | solution.py:523
  61.8 0.0 collective-permute-start.15
  61.8 0.0 collective-permute-done.4.near
  61.9 0.4 collective-permute-start.7
  62.3 1.4 %collective-permute-start.6 = (bf16[256,256]{1,0:T(8,128)(2,1)S(1)}, bf16[256,256]{1,0:T(8,128)(2,1)S(1)}, u32[]{:S(2)}, u32[]{:S(2)}) collective-permute-start(bf16[256,256]{1,0:T(8,128)(2,1)S(1)} %get-tuple-element.59), channel_id=1, source_target_pairs={{0,16},{4,20},{8,24},{12,28},{16,0},{20,4},{24,8},{28,12},{1,17},{... | collective-permute-start | bytes 393224 | tf_op jit(solution)/shard_map/ppermute | solution.py:523
  63.8 1.7 %collective-permute-start.5 = (bf16[256,256]{1,0:T(8,128)(2,1)S(1)}, bf16[256,256]{1,0:T(8,128)(2,1)S(1)}, u32[]{:S(2)}, u32[]{:S(2)}) collective-permute-start(bf16[256,256]{1,0:T(8,128)(2,1)S(1)} %get-tuple-element.59), channel_id=1, source_target_pairs={{0,8},{4,12},{8,0},{12,4},{16,24},{20,28},{24,16},{28,20},{1,9},{5... | collective-permute-start | bytes 393224 | tf_op jit(solution)/shard_map/ppermute | solution.py:523
  65.4 0.9 %collective-permute-done.15.second = f32[8,128]{1,0:T(8,128)S(1)} collective-permute-done((f32[8,128]{1,0:T(8,128)S(1)}, f32[8,128]{1,0:T(8,128)S(1)}, u32[]{:S(2)}, u32[]{:S(2)}) %collective-permute-start.15) | collective-permute-done | bytes 4128 | tf_op jit(solution)/shard_map/ppermute | solution.py:523
  66.4 2.7 %collective-permute-done.7.refs_3_ = bf16[256,256]{1,0:T(8,128)(2,1)S(1)} collective-permute-done((bf16[256,256]{1,0:T(8,128)(2,1)S(1)}, bf16[256,256]{1,0:T(8,128)(2,1)S(1)}, u32[]{:S(2)}, u32[]{:S(2)}) %collective-permute-start.7) | collective-permute-done | bytes 131104 | tf_op jit(solution)/shard_map/ppermute | solution.py:523
  69.1 0.5 collective-permute-done.6.refs_2_
  69.6 0.0 collective-permute-done.5.refs_1_
  69.6 0.0 collective-permute-done.10.refs_5_
  69.6 1.1 %shard_map.155 = (f32[256,256]{1,0:T(8,128)}, f32[256,256]{1,0:T(8,128)}, f32[128,256]{1,0:T(8,128)}) custom-call(f32[256,256]{1,0:T(8,128)S(1)} %get-tuple-element.58.refs_0_, bf16[256,256]{1,0:T(8,128)(2,1)S(1)} %collective-permute-done.5.refs_1_, bf16[256,256]{1,0:T(8,128)(2,1)S(1)} %collective-permute-done.6.refs_2_, ...), custom_call_target="tpu_custom_call" | custom-call | flops 2147483648 | tf_op jit(solution)/shard_map/pallas_call | solution.py:504
  (8 shorter events, 0.2 us)
Async XLA Ops:
  0.6 6.5 %collective-permute-start = (s32[1,3,128]{2,1,0:T(4,128)}, s32[1,3,128]{2,1,0:T(4,128)S(1)}, u32[]{:S(2)}, u32[]{:S(2)}) collective-permute-start(s32[1,3,128]{2,1,0:T(4,128)} %bitcast.15), channel_id=1, source_target_pairs={{0,1},{1,0},{2,3},{3,2},{4,5},{5,4},{6,7},{7,6},{8,9},{9,8},{10,11... | collective-permute-start | bytes 4616 | tf_op jit(solution)/shard_map/ppermute | solution.py:523
  3.8 9.9 %collective-permute-start.2 = (f32[1,128,256]{2,1,0:T(8,128)}, f32[1,128,256]{2,1,0:T(8,128)S(1)}, u32[]{:S(2)}, u32[]{:S(2)}) collective-permute-start(f32[1,128,256]{2,1,0:T(8,128)} %bitcast.13), channel_id=1, source_target_pairs={{0,1},{1,0},{2,3},{3,2},{4,5},{5,4},{6,7},{7,6},{8,9},{9,8},{10,11... | collective-permute-start | bytes 393224 | tf_op jit(solution)/shard_map/ppermute | solution.py:523
  7.1 6.7 %collective-permute-start.1 = (f32[2,8,128]{2,1,0:T(8,128)S(1)}, f32[2,8,128]{2,1,0:T(8,128)S(1)}, u32[]{:S(2)}, u32[]{:S(2)}) collective-permute-start(f32[2,8,128]{2,1,0:T(8,128)S(1)} %shard_map.138.kvecs.refs_7_), channel_id=1, source_target_pairs={{0,2},{1,3},{2,0},{3,1},{4,6},{5,7},{6,4},{7,5},{8,10},{9,11},{10,... | collective-permute-start | bytes 24584 | tf_op jit(solution)/shard_map/ppermute | solution.py:523
  13.7 13.8 %collective-permute-start.3 = (f32[2,128,256]{2,1,0:T(8,128)S(1)}, f32[2,128,256]{2,1,0:T(8,128)S(1)}, u32[]{:S(2)}, u32[]{:S(2)}) collective-permute-start(f32[2,128,256]{2,1,0:T(8,128)S(1)} %shard_map.141), channel_id=1, source_target_pairs={{0,2},{1,3},{2,0},{3,1},{4,6},{5,7},{6,4},{7,5},{8,10},{9,11},{10,... | collective-permute-start | bytes 786440 | tf_op jit(solution)/shard_map/ppermute | solution.py:523
  13.8 13.7 %copy-start = (bf16[2048,256]{1,0:T(8,128)(2,1)S(1)}, bf16[2048,256]{1,0:T(8,128)(2,1)}, u32[]{:S(2)}) copy-start(bf16[2048,256]{1,0:T(8,128)(2,1)} %refs_10_.1) | copy-start | bytes 3145732
  13.8 13.7 %copy-start.1 = (bf16[256,256]{1,0:T(8,128)(2,1)S(1)}, bf16[256,256]{1,0:T(8,128)(2,1)}, u32[]{:S(2)}) copy-start(bf16[256,256]{1,0:T(8,128)(2,1)} %refs_12_.1) | copy-start | bytes 393220
  13.8 13.7 %copy-start.2 = (f32[256]{0:T(256)S(1)}, f32[256]{0:T(256)}, u32[]{:S(2)}) copy-start(f32[256]{0:T(256)} %param.18) | copy-start | bytes 3076
  38.6 12.5 %collective-permute-start.12 = (bf16[128,256]{1,0:T(8,128)(2,1)S(1)}, bf16[128,256]{1,0:T(8,128)(2,1)S(1)}, u32[]{:S(2)}, u32[]{:S(2)}) collective-permute-start(bf16[128,256]{1,0:T(8,128)(2,1)S(1)} %get-tuple-element.62.filter_half), channel_id=1, source_target_pairs={{0,24},{4,28},{8,16},{12,20},{16,8},{20,12},{24,0},{28,4},{1,25},{... | collective-permute-start | bytes 196616 | tf_op jit(solution)/shard_map/ppermute | solution.py:523
  41.4 9.7 %collective-permute-start.11 = (bf16[128,256]{1,0:T(8,128)(2,1)S(1)}, bf16[128,256]{1,0:T(8,128)(2,1)S(1)}, u32[]{:S(2)}, u32[]{:S(2)}) collective-permute-start(bf16[128,256]{1,0:T(8,128)(2,1)S(1)} %get-tuple-element.62.filter_half), channel_id=1, source_target_pairs={{0,8},{4,12},{8,0},{12,4},{16,24},{20,28},{24,16},{28,20},{1,9},{5... | collective-permute-start | bytes 196616 | tf_op jit(solution)/shard_map/ppermute | solution.py:523
  41.6 7.6 %collective-permute-start.8 = (bf16[256,256]{1,0:T(8,128)(2,1)S(1)}, bf16[256,256]{1,0:T(8,128)(2,1)S(1)}, u32[]{:S(2)}, u32[]{:S(2)}) collective-permute-start(bf16[256,256]{1,0:T(8,128)(2,1)S(1)} %get-tuple-element.61), channel_id=1, source_target_pairs={{0,8},{4,12},{8,0},{12,4},{16,24},{20,28},{24,16},{28,20},{1,9},{5... | collective-permute-start | bytes 393224 | tf_op jit(solution)/shard_map/ppermute | solution.py:523
  49.1 12.7 %collective-permute-start.4 = (f32[256,256]{1,0:T(8,128)S(1)}, f32[256,256]{1,0:T(8,128)S(1)}, u32[]{:S(2)}, u32[]{:S(2)}) collective-permute-start(f32[256,256]{1,0:T(8,128)S(1)} %shard_map.147.raw_in_t), channel_id=1, source_target_pairs={{0,4},{4,0},{8,12},{12,8},{16,20},{20,16},{24,28},{28,24},{1,5},{5... | collective-permute-start | bytes 786440 | tf_op jit(solution)/shard_map/ppermute | solution.py:523
  49.3 7.4 %collective-permute-start.9 = (bf16[384,256]{1,0:T(8,128)(2,1)S(1)}, bf16[384,256]{1,0:T(8,128)(2,1)S(1)}, u32[]{:S(2)}, u32[]{:S(2)}) collective-permute-start(bf16[384,256]{1,0:T(8,128)(2,1)S(1)} %get-tuple-element.64), channel_id=1, source_target_pairs={{0,16},{4,20},{8,24},{12,28},{16,0},{20,4},{24,8},{28,12},{1,17},{... | collective-permute-start | bytes 589832 | tf_op jit(solution)/shard_map/ppermute | solution.py:523
  56.7 1.5 %collective-permute-start.13 = (f32[128,256]{1,0:T(8,128)S(1)}, f32[128,256]{1,0:T(8,128)S(1)}, u32[]{:S(2)}, u32[]{:S(2)}) collective-permute-start(f32[128,256]{1,0:T(8,128)S(1)} %shard_map.151.filt), channel_id=1, source_target_pairs={{0,4},{4,0},{8,12},{12,8},{16,20},{20,16},{24,28},{28,24},{1,5},{5... | collective-permute-start | bytes 393224 | tf_op jit(solution)/shard_map/ppermute | solution.py:523
  58.2 3.6 %collective-permute-start.14 = (f32[8,128]{1,0:T(8,128)S(1)}, f32[8,128]{1,0:T(8,128)S(1)}, u32[]{:S(2)}, u32[]{:S(2)}) collective-permute-start(f32[8,128]{1,0:T(8,128)S(1)} %get-tuple-element.67.first), channel_id=1, source_target_pairs={{0,1},{1,0},{2,3},{3,2},{4,5},{5,4},{6,7},{7,6},{8,9},{9,8},{10,11... | collective-permute-start | bytes 12296 | tf_op jit(solution)/shard_map/ppermute | solution.py:523
  58.3 11.3 %collective-permute-start.10 = (f32[256,256]{1,0:T(8,128)S(1)}, f32[256,256]{1,0:T(8,128)S(1)}, u32[]{:S(2)}, u32[]{:S(2)}) collective-permute-start(f32[256,256]{1,0:T(8,128)S(1)} %shard_map.150.refs_4_), channel_id=1, source_target_pairs={{0,4},{4,0},{8,12},{12,8},{16,20},{20,16},{24,28},{28,24},{1,5},{5... | collective-permute-start | bytes 786440 | tf_op jit(solution)/shard_map/ppermute | solution.py:523
  61.8 4.5 %collective-permute-start.15 = (f32[8,128]{1,0:T(8,128)S(1)}, f32[8,128]{1,0:T(8,128)S(1)}, u32[]{:S(2)}, u32[]{:S(2)}) collective-permute-start(f32[8,128]{1,0:T(8,128)S(1)} %shard_map.153.first), channel_id=1, source_target_pairs={{0,2},{1,3},{2,0},{3,1},{4,6},{5,7},{6,4},{7,5},{8,10},{9,11},{10,... | collective-permute-start | bytes 12296 | tf_op jit(solution)/shard_map/ppermute | solution.py:523
  61.9 7.2 %collective-permute-start.7 = (bf16[256,256]{1,0:T(8,128)(2,1)S(1)}, bf16[256,256]{1,0:T(8,128)(2,1)S(1)}, u32[]{:S(2)}, u32[]{:S(2)}) collective-permute-start(bf16[256,256]{1,0:T(8,128)(2,1)S(1)} %get-tuple-element.59), channel_id=1, source_target_pairs={{0,24},{4,28},{8,16},{12,20},{16,8},{20,12},{24,0},{28,4},{1,25},{... | collective-permute-start | bytes 393224 | tf_op jit(solution)/shard_map/ppermute | solution.py:523
  62.3 7.3 %collective-permute-start.6 = (bf16[256,256]{1,0:T(8,128)(2,1)S(1)}, bf16[256,256]{1,0:T(8,128)(2,1)S(1)}, u32[]{:S(2)}, u32[]{:S(2)}) collective-permute-start(bf16[256,256]{1,0:T(8,128)(2,1)S(1)} %get-tuple-element.59), channel_id=1, source_target_pairs={{0,16},{4,20},{8,24},{12,28},{16,0},{20,4},{24,8},{28,12},{1,17},{... | collective-permute-start | bytes 393224 | tf_op jit(solution)/shard_map/ppermute | solution.py:523
  63.8 5.8 %collective-permute-start.5 = (bf16[256,256]{1,0:T(8,128)(2,1)S(1)}, bf16[256,256]{1,0:T(8,128)(2,1)S(1)}, u32[]{:S(2)}, u32[]{:S(2)}) collective-permute-start(bf16[256,256]{1,0:T(8,128)(2,1)S(1)} %get-tuple-element.59), channel_id=1, source_target_pairs={{0,8},{4,12},{8,0},{12,4},{16,24},{20,28},{24,16},{28,20},{1,9},{5... | collective-permute-start | bytes 393224 | tf_op jit(solution)/shard_map/ppermute | solution.py:523

commit v7 on v6

--- a/solution.py
+++ b/solution.py
@@ -84,6 +84,14 @@
         pl.when(steps == n)(functools.partial(action, n))
 
 
+def lanes_of(sums, cell, half, own):
+    for ref in sums:
+        held = ref.shape[2] // own
+        if half < held:
+            return ref[cell, :, own * half : own * (half + 1)]
+        half -= held
+
+
 def weigh(cell, n_ka, bounds, quad, filt_t, width_cols, sums, weights):
     own = filt_t.shape[1] // n_ka
     inverse = inverse_count(bounds[0, cell])
@@ -91,8 +99,7 @@
         scaled = shape_of(cell, quad, width_cols, j * own, own) * inverse
         filt = filt_t[:, own * j : own * (j + 1)] * scaled
         for half in (2 * j, 2 * j + 1):
-            at = slice(own * half, own * (half + 1))
-            weights[:, at] = (filt * sums[cell, :, at]).astype(BF16)
+            weights[half] = (filt * lanes_of(sums, cell, half, own)).astype(BF16)
 
 
 def spread_cells(n_ka, bounds, ids, quad, filt_t, width_cols, sums, waves, even, odd, out):
@@ -105,9 +112,10 @@
         def action(n):
             if after is not None:
                 weigh(after, n_ka, bounds, quad, filt_t, width_cols, sums, target)
+            lhs = jnp.concatenate([weights[h] for h in range(2 * n_ka)], axis=1)
             for t in range(n):
                 at = pl.ds(pl.multiple_of(start + t * TILE, LANES), TILE)
-                value = mm(weights[...], waves[:, at])
+                value = mm(lhs, waves[:, at])
                 out[:, at] = jnp.where(ids[:, at] == cell, value, out[:, at])
 
         by_steps(steps, most, action)
@@ -218,10 +226,17 @@
             kvecs[at] = rows
 
 
-def stack_kernel(near, far, out):
+def half_kernel(core, near, far, out):
     count = near.shape[0]
-    out[:count] = near[...].astype(out.dtype)
-    out[count:] = far[...].astype(out.dtype)
+    half = out.shape[2]
+    if near.shape[2] == half:
+        out[:count] = near[...]
+        out[count:] = far[...]
+    else:
+        at = pl.ds(pl.multiple_of(core[0] * half, half), half)
+        for j in range(count):
+            out[j] = near[j, :, at]
+            out[j + count] = far[j, :, at]
 
 
 def project_kernel(coords, kvecs, feats_hbm, w_in_hbm, waves, proj_t, feats, w_in, kcols, sems):
@@ -287,37 +302,51 @@
 
     lax.fori_loop(0, cells, early, 0)
 
+
+def late_kernel(bounds, proj_t, ids, waves, sums):
+    cells, _, width = sums.shape
+    atoms = proj_t.shape[1] - LANES
+    first = waves.shape[0] - width
+
     def late(cell, carry):
         start, steps, _ = span_of(bounds, cell)
 
         def action(n):
             at = pl.ds(start, n * TILE)
             lhs = proj_t[:, at] * (ids[:, at] == cell).astype(F32).astype(BF16)
-            factors[cell, :, 4 * own :] = mm(lhs, waves[4 * own :, at], 1, 1)
-
-        by_steps(steps, most, action)
+            sums[cell] = mm(lhs, waves[first:, at], 1, 1)
+
+        by_steps(steps, most_steps(atoms), action)
         return carry
 
     lax.fori_loop(0, cells, late, 0)
 
 
-def filters_first(filt_t, kfilts):
+def filters_first(filt_t, core, nears, fars, others):
     chunk = 0
-    for ref in kfilts:
+    half = filt_t.shape[0] // 2
+    for ref in nears:
         own = ref.shape[1]
-        for j in range(ref.shape[0]):
-            filt_t[:, chunk * own : (chunk + 1) * own] = ref[j].astype(F32).T
+        filt_t[:, chunk * own : (chunk + 1) * own] = ref[0].T
+        chunk += 1
+    for mine, other in zip(fars, others):
+        for j in range(mine.shape[0]):
+            at = slice(chunk * own, (chunk + 1) * own)
+            filt_t[pl.ds(pl.multiple_of(core * half, half), half), at] = mine[j].T
+            filt_t[pl.ds(pl.multiple_of((1 - core) * half, half), half), at] = other[j].T
             chunk += 1
     return own
 
 
 def message_kernel(n_ka, *refs):
-    bounds, ids, quad, waves, factors, spread, cotan, w_out = refs[:8]
+    bounds, core, ids, quad, waves, low, high, spread, cotan, w_out = refs[:10]
     act_t, mgrad_t, raw_out, raw_half, filt_t, width_cols, even, odd, mess_t = refs[-9:]
     atoms, chan = cotan.shape
-    filters_first(filt_t, refs[8:-9])
+    filters = refs[10:-9]
+    steps = (len(filters) - 2) // 2
+    filters_first(filt_t, core[0], filters[:2], filters[2 : 2 + steps], filters[2 + steps :])
     width_cols[...] = column_to_lanes(spread[...] * (-LOG2_E))
-    spread_cells(n_ka, bounds, ids, quad, filt_t, width_cols, factors, waves, even, odd, mess_t)
+    spread_cells(n_ka, bounds, ids, quad, filt_t, width_cols, (low, high), waves, even, odd, mess_t)
     mgrad_t[:, atoms:] = jnp.zeros((chan, LANES), BF16)
     raw_out[...] = jnp.zeros_like(raw_out)
 
@@ -383,14 +412,16 @@
 
 
 def update_kernel(n_ka, *refs):
-    bounds, ids, quad, waves, sums, spread = refs[:6]
+    bounds, core, ids, quad, waves, sums, spread = refs[:7]
     update_t = refs[-11]
     filt_t, width_cols, even, odd, total_t, sems = refs[-6:]
     copies = start_copies(sems, *zip(refs[-15:-11], refs[-10:-6]))
     atoms = update_t.shape[1]
-    filters_first(filt_t, refs[6:-15])
+    filters = refs[7:-15]
+    steps = (len(filters) - 2) // 2
+    filters_first(filt_t, core[0], filters[:2], filters[2 : 2 + steps], filters[2 + steps :])
     width_cols[...] = column_to_lanes(spread[...] * (-LOG2_E))
-    spread_cells(n_ka, bounds, ids, quad, filt_t, width_cols, sums, waves, even, odd, total_t)
+    spread_cells(n_ka, bounds, ids, quad, filt_t, width_cols, (sums,), waves, even, odd, total_t)
     update_t[...] = total_t[:, :atoms].astype(BF16)
     for copy in copies:
         copy.wait()
@@ -562,7 +593,7 @@
     )
     kfilt = kfilt[None]
     (kvecs,) = call(pair_kernel, (kvec[None], near_kvec), 0, [((2, 8, own), F32)])
-    far_kvecs, far_kfilts = [kvecs], [kfilt, near_kfilt]
+    far_kvecs = [kvecs]
     ka_steps = doubling(2, n_ka)
     for s in ka_steps:
         if s > 2:
@@ -578,24 +609,38 @@
         3,
         (pltpu.VMEM, pltpu.VMEM, pltpu.HBM, pltpu.HBM),
     )
-    kfilts = kfilt
+    core = lax.rem(lax.axis_index("dp"), 2).astype(jnp.int32).reshape(1)
+    kfilts, far = kfilt, near_kfilt
+    halves_far = []
     for s in ka_steps:
-        (kfilts,) = call(stack_kernel, (kfilts, far_kfilts[-1]), 0, [((s, own, chan), F32)])
-        far_kfilts.append(send(kfilts, "ka", s))
-    waves, factors, quad = call(
+        (kfilts,) = call(half_kernel, (core, kfilts, far), 1, [((s, own, chan // 2), F32)])
+        far = send(kfilts, "ka", s)
+        halves_far.append(far)
+    waves, low, quad = call(
         functools.partial(waves_kernel, n_ka),
         (bounds, first, second, proj_t, ids, coords, recip, *far_kvecs),
         1,
-        [((2 * k_all, long), BF16), ((cells, chan, 2 * k_all), F32), ((cells, k_all), F32)],
+        [((2 * k_all, long), BF16), ((cells, chan, 4 * own), F32), ((cells, k_all), F32)],
         [vm((k_all - 2 * own, 8), F32)],
         LIMIT,
         8,
     )
-    halves = [vm((chan, 2 * k_all), BF16)] * 2
+    halves_other = [send(x, "dp", 1) for x in halves_far]
+    (high,) = call(
+        late_kernel,
+        (bounds, proj_t, ids, waves),
+        1,
+        [((cells, chan, 2 * k_all - 4 * own), F32)],
+        [],
+        SMALL,
+        3,
+    )
+    far_kfilts = [kfilt, near_kfilt, *halves_far, *halves_other]
+    halves = [vm((2 * n_ka, chan, own), BF16)] * 2
     act_t, mgrad_t, raw_out, raw_half = call(
         functools.partial(message_kernel, n_ka),
-        (bounds, ids, quad, waves, factors, spread, cotan, w_out, *far_kfilts),
-        1,
+        (bounds, core, ids, quad, waves, low, high, spread, cotan, w_out, *far_kfilts),
+        2,
         [((chan, atoms), BF16), ((chan, long), BF16), ((chan, chan), F32), ((chan, chan), BF16)],
         [vm((chan, k_all), F32), vm((chan, 8), F32), *halves, vm((chan, long), F32)],
         LIMIT,
@@ -605,7 +650,7 @@
     out_part = send(raw_half, "dp", out_steps[0])
     sums, filter_grad, filter_half = call(
         functools.partial(adjoint_kernel, n_ka),
-        (bounds, ids, quad, waves, factors, mgrad_t, spread),
+        (bounds, ids, quad, waves, low, mgrad_t, spread),
         1,
         [((cells, chan, 2 * k_all), F32), ((own, chan), F32), ((own, chan), BF16)],
         [vm((chan, 8), F32), vm((chan, own), F32)],
@@ -631,8 +676,8 @@
     held = (feats, cotan, w_in, w_out)
     update_t, feats, cotan, w_in, w_out = call(
         functools.partial(update_kernel, n_ka),
-        (bounds, ids, quad, waves, sums, spread, *far_kfilts, *map(in_hbm, held)),
-        1,
+        (bounds, core, ids, quad, waves, sums, spread, *far_kfilts, *map(in_hbm, held)),
+        2,
         [((chan, atoms), BF16), *((x.shape, BF16) for x in held)],
         [vm((chan, k_all), F32), vm((chan, 8), F32), *halves, vm((chan, long), F32), dma((4,))],
         LIMIT,
@@ -644,6 +689,7 @@
     (raw_in_t,) = call(gradient_kernel, (update_t, feats), 0, [((chan, chan), F32)])
     near = send(raw_in_t, "dp", 1)
     (out_sum,) = call(last_out_kernel, (raw_out, out_part), 0, [((chan, chan), F32)])
+    near_out = send(out_sum, "dp", 1)
     f_sum, squares = call(
         squares_kernel, (filt_sum, filt_near), 0, [((own, chan), F32), ((8, LANES), F32)]
     )
@@ -658,7 +704,6 @@
         (squares,) = call(add_kernel, (squares, square_part), 0, [((8, LANES), F32)])
         if s:
             square_part = send(squares, "ka", s)
-    near_out = send(out_sum, "dp", 1)
     mixed = residual(False, feats, act_t, w_out)
     grads = call(
         functools.partial(final_kernel, len(in_parts), n_ka),

time: 70.9 us -> 68.5 us (0.966)
  waiting for transfers between devices: 18.5 us -> 15.7 us
    ppermute x16 -> x17, waiting for transfers between devices: 18.5 us -> 15.7 us  [send(): return lax.ppermute(value, axis, routes(step, lax.axis_size(axis)))]
    pallas_call x17 -> x18, Pallas kernels: 32.7 us -> 33.1 us  [call(): pl.pallas_call(kernel, out_shape=tuple((jax.ShapeDtypeStruct(*o) for o in...]
    ppermute x16 -> x17, starting transfers between devices: 15.9 us -> 16 us  [send(): return lax.ppermute(value, axis, routes(step, lax.axis_size(axis)))]
  transfers between devices with their start and end apart: 16 -> 17, of which waited for: 6 -> 6; matrix products, arithmetic and copies ran while one was open for 0% -> 0% of each run, Pallas kernels for 33% -> 35%
where the time goes in v7:
time: 68.5 us; the launch traced here: 68.3 us
  Pallas kernels  35.8 us (52%)
  starting transfers between devices  16 us (23%)
  waiting for transfers between devices  15.7 us (23%)
  between operations  0.87 us (1%)
    pallas_call x18, Pallas kernels, call(): pl.pallas_call(kernel, out_shape=tuple((jax.ShapeDtypeStruct(*o) for o in...  33.1 us
    ppermute x17, starting transfers between devices, send(): return lax.ppermute(value, axis, routes(step, lax.axis_size(axis)))  16 us
    ppermute x17, waiting for transfers between devices, send(): return lax.ppermute(value, axis, routes(step, lax.axis_size(axis)))  15.7 us
    pallas_call x2, Pallas kernels, residual(): pl.pallas_call(functools.partial(residual_kernel, transposed), out_shape=...  2.69 us
  transfers between devices with their start and end apart: 17, of which 6 were waited for; matrix products, arithmetic and copies ran while one was open for 0% of the time, Pallas kernels for 35%

profile of v7, /device:TPU:0, one launch (start us, length us, event | category | flops | bytes accessed | tf_op | source)
XLA Modules:
  0.0 68.3 jit_solution(8722794511905019411)
XLA Ops:
  0.6 3.1 %collective-permute-start = (s32[1,3,128]{2,1,0:T(4,128)}, s32[1,3,128]{2,1,0:T(4,128)S(1)}, u32[]{:S(2)}, u32[]{:S(2)}) collective-permute-start(s32[1,3,128]{2,1,0:T(4,128)} %bitcast.16), channel_id=1, source_target_pairs={{0,1},{1,0},{2,3},{3,2},{4,5},{5,4},{6,7},{7,6},{8,9},{9,8},{10,11... | collective-permute-start | bytes 4616 | tf_op jit(solution)/shard_map/ppermute | solution.py:554
  3.8 0.1 collective-permute-start.2
  3.8 3.2 %shard_map.137 = (bf16[256,2176]{1,0:T(8,128)(2,1)S(1)}, s32[1,2176]{1,0:T(1,128)S(1)}, f32[3,2048]{1,0:T(4,128)S(1)}, f32[8,9]{1,0:T(8,128)S(1)}, s32[3,128]{1,...) custom-call(f32[3,2048]{1,0:T(4,128)} %coords_hbm.1, s32[1,2048]{1,0:T(1,128)} %ids_hbm.1, f32[8,9]{1,0:T(8,128)} %bitcast.15, ...), custom_call_target="tpu_custom_call" | custom-call | flops 3221225472 | tf_op jit(solution)/shard_map/pallas_call | solution.py:535
  7.1 0.0 collective-permute-done.other_kvec
  7.1 3.0 %collective-permute-start.1 = (f32[2,8,128]{2,1,0:T(8,128)S(1)}, f32[2,8,128]{2,1,0:T(8,128)S(1)}, u32[]{:S(2)}, u32[]{:S(2)}) collective-permute-start(f32[2,8,128]{2,1,0:T(8,128)S(1)} %shard_map.138.kvecs.refs_7_), channel_id=1, source_target_pairs={{0,2},{1,3},{2,0},{3,1},{4,6},{5,7},{6,4},{7,5},{8,10},{9,11},{10,... | collective-permute-start | bytes 24584 | tf_op jit(solution)/shard_map/ppermute | solution.py:554
  10.1 3.5 %shard_map.139 = (bf16[256,2176]{1,0:T(8,128)(2,1)S(1)}, bf16[256,2176]{1,0:T(8,128)(2,1)S(1)}) custom-call(f32[3,2048]{1,0:T(4,128)S(1)} %get-tuple-element.41.coords.refs_5_, f32[2,8,128]{2,1,0:T(8,128)S(1)} %shard_map.138.kvecs.refs_7_, bf16[2048,256]{1,0:T(8,128)(2,1)} %refs_11_.1, bf16[256,256]{1,0:T(8,128)(2,1)} %refs_13_.1), custom_call_target="tpu_custom_call" | custom-call | flops 3221225472 | tf_op jit(solution)/shard_map/pallas_call | solution.py:535
  13.7 0.0 collective-permute-done.2.far.refs_11_.refs_8_
  13.7 0.1 collective-permute-start.3
  13.8 0.0 collective-permute-done.1.refs_8_
  13.8 5.0 %shard_map.140 = (bf16[1024,2176]{1,0:T(8,128)(2,1)S(1)}, f32[8,256,512]{2,1,0:T(8,128)S(1)}, f32[8,512]{1,0:T(8,128)S(1)}) custom-call(s32[2,8]{1,0:T(2,128)S(1)} %get-tuple-element.38.refs_0_.bounds, bf16[256,2176]{1,0:T(8,128)(2,1)S(1)} %get-tuple-element.40.refs_1_, bf16[256,2176]{1,0:T(8,128)(2,1)S(1)} %get-tuple-element.43.refs_2_, ...), custom_call_target="tpu_custom_call" | custom-call | flops 8589934592 | tf_op jit(solution)/shard_map/pallas_call | solution.py:535
  18.8 3.1 %collective-permute-done.3.refs_12_.refs_9_ = f32[2,128,128]{2,1,0:T(8,128)S(1)} collective-permute-done((f32[2,128,128]{2,1,0:T(8,128)S(1)}, f32[2,128,128]{2,1,0:T(8,128)S(1)}, u32[]{:S(2)}, u32[]{:S(2)}) %collective-permute-start.3) | collective-permute-done | bytes 131104 | tf_op jit(solution)/shard_map/ppermute | solution.py:554
  21.9 0.0 collective-permute-start.4
  21.9 0.0 copy-start
  21.9 0.0 copy-start.1
  21.9 0.0 copy-start.2
  21.9 3.3 %shard_map.141.refs_6_ = f32[8,256,512]{2,1,0:T(8,128)S(1)} custom-call(s32[2,8]{1,0:T(2,128)S(1)} %get-tuple-element.38.refs_0_.bounds, bf16[256,2176]{1,0:T(8,128)(2,1)S(1)} %get-tuple-element.44.refs_3_.proj_t, s32[1,2176]{1,0:T(1,128)S(1)} %get-tuple-element.39.refs_4_.ids.refs_2_.refs_1_, bf16[1024,2176]{1,0:T(8,128)(2,1)S(1)} %get-tuple-element.47.waves.refs_4_.refs_3_), custom_call_target="tpu_custom_call" | custom-call | flops 3221225472 | tf_op jit(solution)/shard_map/pallas_call | solution.py:535
  25.2 0.0 collective-permute-done.4.refs_13_.refs_10_
  25.2 0.0 copy-done
  25.2 0.0 copy-done.1
  25.2 0.0 copy-done.2
  25.2 6.4 %shard_map.143 = (bf16[256,2048]{1,0:T(8,128)(2,1)S(1)}, bf16[256,2176]{1,0:T(8,128)(2,1)S(1)}, f32[256,256]{1,0:T(8,128)S(1)}, bf16[256,256]{1,0:T(8,128)(2,1)S(1)}) custom-call(s32[2,8]{1,0:T(2,128)S(1)} %get-tuple-element.38.refs_0_.bounds, s32[1]{0:T(128)} %bitcast.1.core.refs_1_, s32[1,2176]{1,0:T(1,128)S(1)} %get-tuple-element.39.refs_4_.ids.refs_2_.refs_1_, ...), custom_call_target="tpu_custom_call" | custom-call | flops 8589934592 | tf_op jit(solution)/shard_map/pallas_call | solution.py:535
  31.6 4.7 %shard_map.144 = (f32[8,256,1024]{2,1,0:T(8,128)S(1)}, f32[128,256]{1,0:T(8,128)S(1)}, bf16[128,256]{1,0:T(8,128)(2,1)S(1)}) custom-call(s32[2,8]{1,0:T(2,128)S(1)} %get-tuple-element.38.refs_0_.bounds, s32[1,2176]{1,0:T(1,128)S(1)} %get-tuple-element.39.refs_4_.ids.refs_2_.refs_1_, f32[8,512]{1,0:T(8,128)S(1)} %get-tuple-element.46.refs_3_.refs_2_, ...), custom_call_target="tpu_custom_call" | custom-call | flops 6442450944 | tf_op jit(solution)/shard_map/pallas_call | solution.py:535
  36.2 2.9 %collective-permute-start.13 = (bf16[128,256]{1,0:T(8,128)(2,1)S(1)}, bf16[128,256]{1,0:T(8,128)(2,1)S(1)}, u32[]{:S(2)}, u32[]{:S(2)}) collective-permute-start(bf16[128,256]{1,0:T(8,128)(2,1)S(1)} %get-tuple-element.62.filter_half), channel_id=1, source_target_pairs={{0,24},{4,28},{8,16},{12,20},{16,8},{20,12},{24,0},{28,4},{1,25},{... | collective-permute-start | bytes 196616 | tf_op jit(solution)/shard_map/ppermute | solution.py:554
  39.1 0.2 collective-permute-start.12
  39.3 1.9 %collective-permute-start.9 = (bf16[256,256]{1,0:T(8,128)(2,1)S(1)}, bf16[256,256]{1,0:T(8,128)(2,1)S(1)}, u32[]{:S(2)}, u32[]{:S(2)}) collective-permute-start(bf16[256,256]{1,0:T(8,128)(2,1)S(1)} %get-tuple-element.61), channel_id=1, source_target_pairs={{0,8},{4,12},{8,0},{12,4},{16,24},{20,28},{24,16},{28,20},{1,9},{5... | collective-permute-start | bytes 393224 | tf_op jit(solution)/shard_map/ppermute | solution.py:554
  41.1 5.2 %shard_map.145 = (bf16[256,2048]{1,0:T(8,128)(2,1)S(1)}, bf16[2048,256]{1,0:T(8,128)(2,1)S(1)}, bf16[2048,256]{1,0:T(8,128)(2,1)S(1)}, bf16[256,256]{1,0:T(8,128)(2,1)S(1)}, bf16[256,256]{1,0:T(8,128)(2,1)S(1)}) custom-call(s32[2,8]{1,0:T(2,128)S(1)} %get-tuple-element.38.refs_0_.bounds, s32[1]{0:T(128)} %bitcast.1.core.refs_1_, ...), custom_call_target="tpu_custom_call" | custom-call | flops 8589934592 | tf_op jit(solution)/shard_map/pallas_call | solution.py:535
  46.3 0.4 shard_map.148.raw_in_t
  46.8 0.1 collective-permute-start.5
  46.9 0.0 collective-permute-done.9.other_out
  46.9 0.6 collective-permute-start.10
  47.5 1.3 %shard_map.146 = bf16[2048,256]{1,0:T(8,128)(2,1)} custom-call(bf16[2048,256]{1,0:T(8,128)(2,1)S(1)} %get-tuple-element.52.base.feats, bf16[256,2048]{1,0:T(8,128)(2,1)S(1)} %get-tuple-element.53.values_t, bf16[256,256]{1,0:T(8,128)(2,1)S(1)} %get-tuple-element.54.weight), custom_call_target="tpu_custom_call" | custom-call | flops 2147483648 | tf_op jit(solution)/shard_map/pallas_call | solution.py:451
  48.8 0.0 collective-permute-done.13.refs_3_
  48.8 0.0 collective-permute-done.12.refs_1_
  48.8 5.4 %collective-permute-done.10.other_out.refs_2_ = bf16[384,256]{1,0:T(8,128)(2,1)S(1)} collective-permute-done((bf16[384,256]{1,0:T(8,128)(2,1)S(1)}, bf16[384,256]{1,0:T(8,128)(2,1)S(1)}, u32[]{:S(2)}, u32[]{:S(2)}) %collective-permute-start.10) | collective-permute-done | bytes 196640 | tf_op jit(solution)/shard_map/ppermute | solution.py:554
  54.3 0.1 collective-permute-start.14
  54.4 1.4 %shard_map.147 = bf16[2048,256]{1,0:T(8,128)(2,1)} custom-call(bf16[2048,256]{1,0:T(8,128)(2,1)S(1)} %get-tuple-element.55.base, bf16[256,2048]{1,0:T(8,128)(2,1)S(1)} %get-tuple-element.56.values_t.update_t, bf16[256,256]{1,0:T(8,128)(2,1)S(1)} %get-tuple-element.57.weight), custom_call_target="tpu_custom_call" | custom-call | flops 2147483648 | tf_op jit(solution)/shard_map/pallas_call | solution.py:451
  55.7 0.0 collective-permute-done.14.near
  55.8 0.1 shard_map.153
  55.9 0.0 collective-permute-start.15
  55.9 0.6 collective-permute-start.11
  56.5 3.0 %collective-permute-done.15.second = f32[8,128]{1,0:T(8,128)S(1)} collective-permute-done((f32[8,128]{1,0:T(8,128)S(1)}, f32[8,128]{1,0:T(8,128)S(1)}, u32[]{:S(2)}, u32[]{:S(2)}) %collective-permute-start.15) | collective-permute-done | bytes 4128 | tf_op jit(solution)/shard_map/ppermute | solution.py:554
  59.5 0.0 collective-permute-start.16
  59.5 0.0 collective-permute-done.5.near
  59.5 0.3 collective-permute-start.8
  59.9 1.5 %collective-permute-start.7 = (bf16[256,256]{1,0:T(8,128)(2,1)S(1)}, bf16[256,256]{1,0:T(8,128)(2,1)S(1)}, u32[]{:S(2)}, u32[]{:S(2)}) collective-permute-start(bf16[256,256]{1,0:T(8,128)(2,1)S(1)} %get-tuple-element.59), channel_id=1, source_target_pairs={{0,16},{4,20},{8,24},{12,28},{16,0},{20,4},{24,8},{28,12},{1,17},{... | collective-permute-start | bytes 393224 | tf_op jit(solution)/shard_map/ppermute | solution.py:554
  61.4 1.7 %collective-permute-start.6 = (bf16[256,256]{1,0:T(8,128)(2,1)S(1)}, bf16[256,256]{1,0:T(8,128)(2,1)S(1)}, u32[]{:S(2)}, u32[]{:S(2)}) collective-permute-start(bf16[256,256]{1,0:T(8,128)(2,1)S(1)} %get-tuple-element.59), channel_id=1, source_target_pairs={{0,8},{4,12},{8,0},{12,4},{16,24},{20,28},{24,16},{28,20},{1,9},{5... | collective-permute-start | bytes 393224 | tf_op jit(solution)/shard_map/ppermute | solution.py:554
  63.1 0.9 %collective-permute-done.16.second = f32[8,128]{1,0:T(8,128)S(1)} collective-permute-done((f32[8,128]{1,0:T(8,128)S(1)}, f32[8,128]{1,0:T(8,128)S(1)}, u32[]{:S(2)}, u32[]{:S(2)}) %collective-permute-start.16) | collective-permute-done | bytes 4128 | tf_op jit(solution)/shard_map/ppermute | solution.py:554
  64.0 2.7 %collective-permute-done.8.refs_3_ = bf16[256,256]{1,0:T(8,128)(2,1)S(1)} collective-permute-done((bf16[256,256]{1,0:T(8,128)(2,1)S(1)}, bf16[256,256]{1,0:T(8,128)(2,1)S(1)}, u32[]{:S(2)}, u32[]{:S(2)}) %collective-permute-start.8) | collective-permute-done | bytes 131104 | tf_op jit(solution)/shard_map/ppermute | solution.py:554
  66.7 0.5 collective-permute-done.7.refs_2_
  67.2 0.0 collective-permute-done.6.refs_1_
  67.2 0.0 collective-permute-done.11.refs_5_
  67.2 1.1 %shard_map.156 = (f32[256,256]{1,0:T(8,128)}, f32[256,256]{1,0:T(8,128)}, f32[128,256]{1,0:T(8,128)}) custom-call(f32[256,256]{1,0:T(8,128)S(1)} %get-tuple-element.58.refs_0_, bf16[256,256]{1,0:T(8,128)(2,1)S(1)} %collective-permute-done.6.refs_1_, bf16[256,256]{1,0:T(8,128)(2,1)S(1)} %collective-permute-done.7.refs_2_, ...), custom_call_target="tpu_custom_call" | custom-call | flops 2147483648 | tf_op jit(solution)/shard_map/pallas_call | solution.py:535
  (8 shorter events, 0.2 us)
Async XLA Ops:
  0.6 6.5 %collective-permute-start = (s32[1,3,128]{2,1,0:T(4,128)}, s32[1,3,128]{2,1,0:T(4,128)S(1)}, u32[]{:S(2)}, u32[]{:S(2)}) collective-permute-start(s32[1,3,128]{2,1,0:T(4,128)} %bitcast.16), channel_id=1, source_target_pairs={{0,1},{1,0},{2,3},{3,2},{4,5},{5,4},{6,7},{7,6},{8,9},{9,8},{10,11... | collective-permute-start | bytes 4616 | tf_op jit(solution)/shard_map/ppermute | solution.py:554
  3.8 9.9 %collective-permute-start.2 = (f32[1,128,256]{2,1,0:T(8,128)}, f32[1,128,256]{2,1,0:T(8,128)S(1)}, u32[]{:S(2)}, u32[]{:S(2)}) collective-permute-start(f32[1,128,256]{2,1,0:T(8,128)} %bitcast.14), channel_id=1, source_target_pairs={{0,1},{1,0},{2,3},{3,2},{4,5},{5,4},{6,7},{7,6},{8,9},{9,8},{10,11... | collective-permute-start | bytes 393224 | tf_op jit(solution)/shard_map/ppermute | solution.py:554
  7.1 6.7 %collective-permute-start.1 = (f32[2,8,128]{2,1,0:T(8,128)S(1)}, f32[2,8,128]{2,1,0:T(8,128)S(1)}, u32[]{:S(2)}, u32[]{:S(2)}) collective-permute-start(f32[2,8,128]{2,1,0:T(8,128)S(1)} %shard_map.138.kvecs.refs_7_), channel_id=1, source_target_pairs={{0,2},{1,3},{2,0},{3,1},{4,6},{5,7},{6,4},{7,5},{8,10},{9,11},{10,... | collective-permute-start | bytes 24584 | tf_op jit(solution)/shard_map/ppermute | solution.py:554
  13.7 8.2 %collective-permute-start.3 = (f32[2,128,128]{2,1,0:T(8,128)S(1)}, f32[2,128,128]{2,1,0:T(8,128)S(1)}, u32[]{:S(2)}, u32[]{:S(2)}) collective-permute-start(f32[2,128,128]{2,1,0:T(8,128)S(1)} %shard_map.142), channel_id=1, source_target_pairs={{0,2},{1,3},{2,0},{3,1},{4,6},{5,7},{6,4},{7,5},{8,10},{9,11},{10,... | collective-permute-start | bytes 393224 | tf_op jit(solution)/shard_map/ppermute | solution.py:554
  21.9 3.3 %collective-permute-start.4 = (f32[2,128,128]{2,1,0:T(8,128)S(1)}, f32[2,128,128]{2,1,0:T(8,128)S(1)}, u32[]{:S(2)}, u32[]{:S(2)}) collective-permute-start(f32[2,128,128]{2,1,0:T(8,128)S(1)} %collective-permute-done.3.refs_12_.refs_9_), channel_id=1, source_target_pairs={{0,4},{4,0},{8,12},{12,8},{16,20},{20,16},{24,28},{28,24},{1,5},{5... | collective-permute-start | bytes 393224 | tf_op jit(solution)/shard_map/ppermute | solution.py:554
  21.9 3.3 %copy-start = (bf16[2048,256]{1,0:T(8,128)(2,1)S(1)}, bf16[2048,256]{1,0:T(8,128)(2,1)}, u32[]{:S(2)}) copy-start(bf16[2048,256]{1,0:T(8,128)(2,1)} %refs_12_.1) | copy-start | bytes 3145732
  21.9 3.3 %copy-start.1 = (bf16[256,256]{1,0:T(8,128)(2,1)S(1)}, bf16[256,256]{1,0:T(8,128)(2,1)}, u32[]{:S(2)}) copy-start(bf16[256,256]{1,0:T(8,128)(2,1)} %refs_14_.1) | copy-start | bytes 393220
  21.9 3.3 %copy-start.2 = (f32[256]{0:T(256)S(1)}, f32[256]{0:T(256)}, u32[]{:S(2)}) copy-start(f32[256]{0:T(256)} %param.18) | copy-start | bytes 3076
  36.2 12.6 %collective-permute-start.13 = (bf16[128,256]{1,0:T(8,128)(2,1)S(1)}, bf16[128,256]{1,0:T(8,128)(2,1)S(1)}, u32[]{:S(2)}, u32[]{:S(2)}) collective-permute-start(bf16[128,256]{1,0:T(8,128)(2,1)S(1)} %get-tuple-element.62.filter_half), channel_id=1, source_target_pairs={{0,24},{4,28},{8,16},{12,20},{16,8},{20,12},{24,0},{28,4},{1,25},{... | collective-permute-start | bytes 196616 | tf_op jit(solution)/shard_map/ppermute | solution.py:554
  39.1 9.7 %collective-permute-start.12 = (bf16[128,256]{1,0:T(8,128)(2,1)S(1)}, bf16[128,256]{1,0:T(8,128)(2,1)S(1)}, u32[]{:S(2)}, u32[]{:S(2)}) collective-permute-start(bf16[128,256]{1,0:T(8,128)(2,1)S(1)} %get-tuple-element.62.filter_half), channel_id=1, source_target_pairs={{0,8},{4,12},{8,0},{12,4},{16,24},{20,28},{24,16},{28,20},{1,9},{5... | collective-permute-start | bytes 196616 | tf_op jit(solution)/shard_map/ppermute | solution.py:554
  39.3 7.6 %collective-permute-start.9 = (bf16[256,256]{1,0:T(8,128)(2,1)S(1)}, bf16[256,256]{1,0:T(8,128)(2,1)S(1)}, u32[]{:S(2)}, u32[]{:S(2)}) collective-permute-start(bf16[256,256]{1,0:T(8,128)(2,1)S(1)} %get-tuple-element.61), channel_id=1, source_target_pairs={{0,8},{4,12},{8,0},{12,4},{16,24},{20,28},{24,16},{28,20},{1,9},{5... | collective-permute-start | bytes 393224 | tf_op jit(solution)/shard_map/ppermute | solution.py:554
  46.8 12.7 %collective-permute-start.5 = (f32[256,256]{1,0:T(8,128)S(1)}, f32[256,256]{1,0:T(8,128)S(1)}, u32[]{:S(2)}, u32[]{:S(2)}) collective-permute-start(f32[256,256]{1,0:T(8,128)S(1)} %shard_map.148.raw_in_t), channel_id=1, source_target_pairs={{0,4},{4,0},{8,12},{12,8},{16,20},{20,16},{24,28},{28,24},{1,5},{5... | collective-permute-start | bytes 786440 | tf_op jit(solution)/shard_map/ppermute | solution.py:554
  46.9 7.4 %collective-permute-start.10 = (bf16[384,256]{1,0:T(8,128)(2,1)S(1)}, bf16[384,256]{1,0:T(8,128)(2,1)S(1)}, u32[]{:S(2)}, u32[]{:S(2)}) collective-permute-start(bf16[384,256]{1,0:T(8,128)(2,1)S(1)} %get-tuple-element.64), channel_id=1, source_target_pairs={{0,16},{4,20},{8,24},{12,28},{16,0},{20,4},{24,8},{28,12},{1,17},{... | collective-permute-start | bytes 589832 | tf_op jit(solution)/shard_map/ppermute | solution.py:554
  54.3 1.4 %collective-permute-start.14 = (f32[128,256]{1,0:T(8,128)S(1)}, f32[128,256]{1,0:T(8,128)S(1)}, u32[]{:S(2)}, u32[]{:S(2)}) collective-permute-start(f32[128,256]{1,0:T(8,128)S(1)} %shard_map.152.filt), channel_id=1, source_target_pairs={{0,4},{4,0},{8,12},{12,8},{16,20},{20,16},{24,28},{28,24},{1,5},{5... | collective-permute-start | bytes 393224 | tf_op jit(solution)/shard_map/ppermute | solution.py:554
  55.9 3.6 %collective-permute-start.15 = (f32[8,128]{1,0:T(8,128)S(1)}, f32[8,128]{1,0:T(8,128)S(1)}, u32[]{:S(2)}, u32[]{:S(2)}) collective-permute-start(f32[8,128]{1,0:T(8,128)S(1)} %get-tuple-element.67.first), channel_id=1, source_target_pairs={{0,1},{1,0},{2,3},{3,2},{4,5},{5,4},{6,7},{7,6},{8,9},{9,8},{10,11... | collective-permute-start | bytes 12296 | tf_op jit(solution)/shard_map/ppermute | solution.py:554
  55.9 11.3 %collective-permute-start.11 = (f32[256,256]{1,0:T(8,128)S(1)}, f32[256,256]{1,0:T(8,128)S(1)}, u32[]{:S(2)}, u32[]{:S(2)}) collective-permute-start(f32[256,256]{1,0:T(8,128)S(1)} %shard_map.151.refs_4_), channel_id=1, source_target_pairs={{0,4},{4,0},{8,12},{12,8},{16,20},{20,16},{24,28},{28,24},{1,5},{5... | collective-permute-start | bytes 786440 | tf_op jit(solution)/shard_map/ppermute | solution.py:554
  59.5 4.5 %collective-permute-start.16 = (f32[8,128]{1,0:T(8,128)S(1)}, f32[8,128]{1,0:T(8,128)S(1)}, u32[]{:S(2)}, u32[]{:S(2)}) collective-permute-start(f32[8,128]{1,0:T(8,128)S(1)} %shard_map.154.first), channel_id=1, source_target_pairs={{0,2},{1,3},{2,0},{3,1},{4,6},{5,7},{6,4},{7,5},{8,10},{9,11},{10,... | collective-permute-start | bytes 12296 | tf_op jit(solution)/shard_map/ppermute | solution.py:554
  59.5 7.2 %collective-permute-start.8 = (bf16[256,256]{1,0:T(8,128)(2,1)S(1)}, bf16[256,256]{1,0:T(8,128)(2,1)S(1)}, u32[]{:S(2)}, u32[]{:S(2)}) collective-permute-start(bf16[256,256]{1,0:T(8,128)(2,1)S(1)} %get-tuple-element.59), channel_id=1, source_target_pairs={{0,24},{4,28},{8,16},{12,20},{16,8},{20,12},{24,0},{28,4},{1,25},{... | collective-permute-start | bytes 393224 | tf_op jit(solution)/shard_map/ppermute | solution.py:554
  59.9 7.4 %collective-permute-start.7 = (bf16[256,256]{1,0:T(8,128)(2,1)S(1)}, bf16[256,256]{1,0:T(8,128)(2,1)S(1)}, u32[]{:S(2)}, u32[]{:S(2)}) collective-permute-start(bf16[256,256]{1,0:T(8,128)(2,1)S(1)} %get-tuple-element.59), channel_id=1, source_target_pairs={{0,16},{4,20},{8,24},{12,28},{16,0},{20,4},{24,8},{28,12},{1,17},{... | collective-permute-start | bytes 393224 | tf_op jit(solution)/shard_map/ppermute | solution.py:554
  61.4 5.9 %collective-permute-start.6 = (bf16[256,256]{1,0:T(8,128)(2,1)S(1)}, bf16[256,256]{1,0:T(8,128)(2,1)S(1)}, u32[]{:S(2)}, u32[]{:S(2)}) collective-permute-start(bf16[256,256]{1,0:T(8,128)(2,1)S(1)} %get-tuple-element.59), channel_id=1, source_target_pairs={{0,8},{4,12},{8,0},{12,4},{16,24},{20,28},{24,16},{28,20},{1,9},{5... | collective-permute-start | bytes 393224 | tf_op jit(solution)/shard_map/ppermute | solution.py:554

commit v8 on v6

--- a/solution.py
+++ b/solution.py
@@ -34,6 +34,7 @@
     41.34288235413569,
     -12.471243534350362,
 )
+CODES = 32767.0
 ROUNDER = 12582912.0
 
 
@@ -218,10 +219,23 @@
             kvecs[at] = rows
 
 
+def code_kernel(near, far, out):
+    chan = near.shape[2]
+    for j, ref in enumerate((near, far)):
+        values = ref[0].T
+        largest = jnp.max(jnp.abs(values), axis=0, keepdims=True)
+        power = jnp.ceil(jnp.log2(jnp.maximum(largest, 1e-30)) + 1e-3)
+        coded = values * (CODES * jnp.exp2(-power))
+        coded = (coded + ROUNDER) - ROUNDER
+        out[j, :chan, :] = coded.astype(jnp.int32).astype(jnp.int16)
+        powers = jnp.broadcast_to(power, (16, power.shape[1]))
+        out[j, chan:, :] = powers.astype(jnp.int32).astype(jnp.int16)
+
+
 def stack_kernel(near, far, out):
     count = near.shape[0]
-    out[:count] = near[...].astype(out.dtype)
-    out[count:] = far[...].astype(out.dtype)
+    out[:count] = near[...]
+    out[count:] = far[...]
 
 
 def project_kernel(coords, kvecs, feats_hbm, w_in_hbm, waves, proj_t, feats, w_in, kcols, sems):
@@ -277,15 +291,13 @@
             for j in range(2, n_ka):
                 for row in rows_of_share(cell, cells, own):
                     fill_slice(waves, 2 * own * j, own, kcols, (j - 2) * own, row, coords)
-            for row in rows_of_share(cell, cells, 2 * own):
-                from_rows = pl.ds(pl.multiple_of(row, 16), 16)
-                waves[from_rows, :] = first[from_rows, :]
-                waves[pl.ds(pl.multiple_of(2 * own + row, 16), 16), :] = second[from_rows, :]
 
         by_steps(steps, most, action)
         return carry
 
     lax.fori_loop(0, cells, early, 0)
+    waves[: 2 * own, :] = first[...]
+    waves[2 * own : 4 * own, :] = second[...]
 
     def late(cell, carry):
         start, steps, _ = span_of(bounds, cell)
@@ -301,12 +313,18 @@
     lax.fori_loop(0, cells, late, 0)
 
 
-def filters_first(filt_t, kfilts):
+def filters_first(filt_t, refs):
+    chan = filt_t.shape[0]
     chunk = 0
-    for ref in kfilts:
-        own = ref.shape[1]
+    for ref in refs:
         for j in range(ref.shape[0]):
-            filt_t[:, chunk * own : (chunk + 1) * own] = ref[j].astype(F32).T
+            if ref.dtype == F32:
+                own = ref.shape[1]
+                values = ref[j].T
+            else:
+                coded = ref[j].astype(jnp.int32).astype(F32)
+                values = coded[:chan, :] * (jnp.exp2(coded[chan : chan + 1, :]) * (1.0 / CODES))
+            filt_t[:, chunk * own : (chunk + 1) * own] = values
             chunk += 1
     return own
 
@@ -580,7 +598,12 @@
     )
     kfilts = kfilt
     for s in ka_steps:
-        (kfilts,) = call(stack_kernel, (kfilts, far_kfilts[-1]), 0, [((s, own, chan), F32)])
+        (kfilts,) = call(
+            code_kernel if s == 2 else stack_kernel,
+            (kfilts, far_kfilts[-1]),
+            0,
+            [((s, chan + 16, own), jnp.int16)],
+        )
         far_kfilts.append(send(kfilts, "ka", s))
     waves, factors, quad = call(
         functools.partial(waves_kernel, n_ka),
@@ -644,6 +667,7 @@
     (raw_in_t,) = call(gradient_kernel, (update_t, feats), 0, [((chan, chan), F32)])
     near = send(raw_in_t, "dp", 1)
     (out_sum,) = call(last_out_kernel, (raw_out, out_part), 0, [((chan, chan), F32)])
+    near_out = send(out_sum, "dp", 1)
     f_sum, squares = call(
         squares_kernel, (filt_sum, filt_near), 0, [((own, chan), F32), ((8, LANES), F32)]
     )
@@ -658,7 +682,6 @@
         (squares,) = call(add_kernel, (squares, square_part), 0, [((8, LANES), F32)])
         if s:
             square_part = send(squares, "ka", s)
-    near_out = send(out_sum, "dp", 1)
     mixed = residual(False, feats, act_t, w_out)
     grads = call(
         functools.partial(final_kernel, len(in_parts), n_ka),

time: 70.9 us -> 67.7 us (0.955)
  waiting for transfers between devices: 18.5 us -> 11.9 us
  starting transfers between devices: 15.9 us -> 19.5 us
    ppermute x16, waiting for transfers between devices: 18.5 us -> 11.9 us  [send(): return lax.ppermute(value, axis, routes(step, lax.axis_size(axis)))]
    ppermute x16, starting transfers between devices: 15.9 us -> 19.5 us  [send(): return lax.ppermute(value, axis, routes(step, lax.axis_size(axis)))]
  transfers between devices with their start and end apart: 16 -> 16, of which waited for: 6 -> 5; matrix products, arithmetic and copies ran while one was open for 0% -> 0% of each run, Pallas kernels for 33% -> 34%
where the time goes in v8:
time: 67.7 us; the launch traced here: 67.6 us
  Pallas kernels  35.3 us (52%)
  starting transfers between devices  19.5 us (29%)
  waiting for transfers between devices  11.9 us (18%)
  between operations  0.84 us (1%)
    pallas_call x17, Pallas kernels, call(): pl.pallas_call(kernel, out_shape=tuple((jax.ShapeDtypeStruct(*o) for o in...  32.6 us
    ppermute x16, starting transfers between devices, send(): return lax.ppermute(value, axis, routes(step, lax.axis_size(axis)))  19.5 us
    ppermute x16, waiting for transfers between devices, send(): return lax.ppermute(value, axis, routes(step, lax.axis_size(axis)))  11.9 us
    pallas_call x2, Pallas kernels, residual(): pl.pallas_call(functools.partial(residual_kernel, transposed), out_shape=...  2.69 us
  transfers between devices with their start and end apart: 16, of which 5 were waited for; matrix products, arithmetic and copies ran while one was open for 0% of the time, Pallas kernels for 34%

profile of v8, /device:TPU:0, one launch (start us, length us, event | category | flops | bytes accessed | tf_op | source)
XLA Modules:
  0.0 67.6 jit_solution(7496000538890446904)
XLA Ops:
  0.6 3.1 %collective-permute-start = (s32[1,3,128]{2,1,0:T(4,128)}, s32[1,3,128]{2,1,0:T(4,128)S(1)}, u32[]{:S(2)}, u32[]{:S(2)}) collective-permute-start(s32[1,3,128]{2,1,0:T(4,128)} %bitcast.15), channel_id=1, source_target_pairs={{0,1},{1,0},{2,3},{3,2},{4,5},{5,4},{6,7},{7,6},{8,9},{9,8},{10,11... | collective-permute-start | bytes 4616 | tf_op jit(solution)/shard_map/ppermute | solution.py:541
  3.8 0.1 collective-permute-start.2
  3.8 3.3 %shard_map.137 = (bf16[256,2176]{1,0:T(8,128)(2,1)S(1)}, s32[1,2176]{1,0:T(1,128)S(1)}, f32[3,2048]{1,0:T(4,128)S(1)}, f32[8,9]{1,0:T(8,128)S(1)}, s32[3,128]{1,...) custom-call(f32[3,2048]{1,0:T(4,128)} %coords_hbm.1, s32[1,2048]{1,0:T(1,128)} %ids_hbm.1, f32[8,9]{1,0:T(8,128)} %bitcast.14, ...), custom_call_target="tpu_custom_call" | custom-call | flops 3221225472 | tf_op jit(solution)/shard_map/pallas_call | solution.py:522
  7.1 0.0 collective-permute-done.other_kvec
  7.1 3.0 %collective-permute-start.1 = (f32[2,8,128]{2,1,0:T(8,128)S(1)}, f32[2,8,128]{2,1,0:T(8,128)S(1)}, u32[]{:S(2)}, u32[]{:S(2)}) collective-permute-start(f32[2,8,128]{2,1,0:T(8,128)S(1)} %shard_map.138.kvecs.refs_7_), channel_id=1, source_target_pairs={{0,2},{1,3},{2,0},{3,1},{4,6},{5,7},{6,4},{7,5},{8,10},{9,11},{10,... | collective-permute-start | bytes 24584 | tf_op jit(solution)/shard_map/ppermute | solution.py:541
  10.1 3.5 %shard_map.139 = (bf16[256,2176]{1,0:T(8,128)(2,1)S(1)}, bf16[256,2176]{1,0:T(8,128)(2,1)S(1)}) custom-call(f32[3,2048]{1,0:T(4,128)S(1)} %get-tuple-element.41.coords.refs_5_, f32[2,8,128]{2,1,0:T(8,128)S(1)} %shard_map.138.kvecs.refs_7_, bf16[2048,256]{1,0:T(8,128)(2,1)} %refs_9_.1, bf16[256,256]{1,0:T(8,128)(2,1)} %refs_11_.1), custom_call_target="tpu_custom_call" | custom-call | flops 3221225472 | tf_op jit(solution)/shard_map/pallas_call | solution.py:522
  13.7 0.0 collective-permute-done.2.far.refs_9_.refs_7_
  13.7 0.2 shard_map.141
  13.9 0.1 collective-permute-start.3
  14.0 0.0 collective-permute-done.1.refs_8_
  14.0 0.0 copy-start
  14.0 0.0 copy-start.1
  14.0 0.0 copy-start.2
  14.0 7.7 %shard_map.140 = (bf16[1024,2176]{1,0:T(8,128)(2,1)S(1)}, f32[8,256,1024]{2,1,0:T(8,128)S(1)}, f32[8,512]{1,0:T(8,128)S(1)}) custom-call(s32[2,8]{1,0:T(2,128)S(1)} %get-tuple-element.38.refs_0_, bf16[256,2176]{1,0:T(8,128)(2,1)S(1)} %get-tuple-element.40.refs_1_, bf16[256,2176]{1,0:T(8,128)(2,1)S(1)} %get-tuple-element.43.refs_2_, ...), custom_call_target="tpu_custom_call" | custom-call | flops 8589934592 | tf_op jit(solution)/shard_map/pallas_call | solution.py:522
  21.8 0.7 collective-permute-done.3.refs_10_.refs_8_
  22.4 0.0 copy-done
  22.4 0.0 copy-done.1
  22.4 0.0 copy-done.2
  22.4 6.3 %shard_map.142 = (bf16[256,2048]{1,0:T(8,128)(2,1)S(1)}, bf16[256,2176]{1,0:T(8,128)(2,1)S(1)}, f32[256,256]{1,0:T(8,128)S(1)}, bf16[256,256]{1,0:T(8,128)(2,1)S(1)}) custom-call(s32[2,8]{1,0:T(2,128)S(1)} %get-tuple-element.38.refs_0_, s32[1,2176]{1,0:T(1,128)S(1)} %get-tuple-element.39.refs_4_.refs_1_, f32[8,512]{1,0:T(8,128)S(1)} %get-tuple-element.46.refs_2_, ...), custom_call_target="tpu_custom_call" | custom-call | flops 8589934592 | tf_op jit(solution)/shard_map/pallas_call | solution.py:522
  28.8 4.6 %shard_map.143 = (f32[8,256,1024]{2,1,0:T(8,128)S(1)}, f32[128,256]{1,0:T(8,128)S(1)}, bf16[128,256]{1,0:T(8,128)(2,1)S(1)}) custom-call(s32[2,8]{1,0:T(2,128)S(1)} %get-tuple-element.38.refs_0_, s32[1,2176]{1,0:T(1,128)S(1)} %get-tuple-element.39.refs_4_.refs_1_, f32[8,512]{1,0:T(8,128)S(1)} %get-tuple-element.46.refs_2_, ...), custom_call_target="tpu_custom_call" | custom-call | flops 6442450944 | tf_op jit(solution)/shard_map/pallas_call | solution.py:522
  33.4 2.8 %collective-permute-start.12 = (bf16[128,256]{1,0:T(8,128)(2,1)S(1)}, bf16[128,256]{1,0:T(8,128)(2,1)S(1)}, u32[]{:S(2)}, u32[]{:S(2)}) collective-permute-start(bf16[128,256]{1,0:T(8,128)(2,1)S(1)} %get-tuple-element.62.filter_half), channel_id=1, source_target_pairs={{0,24},{4,28},{8,16},{12,20},{16,8},{20,12},{24,0},{28,4},{1,25},{... | collective-permute-start | bytes 196616 | tf_op jit(solution)/shard_map/ppermute | solution.py:541
  36.2 0.2 collective-permute-start.11
  36.4 1.8 %collective-permute-start.8 = (bf16[256,256]{1,0:T(8,128)(2,1)S(1)}, bf16[256,256]{1,0:T(8,128)(2,1)S(1)}, u32[]{:S(2)}, u32[]{:S(2)}) collective-permute-start(bf16[256,256]{1,0:T(8,128)(2,1)S(1)} %get-tuple-element.61), channel_id=1, source_target_pairs={{0,8},{4,12},{8,0},{12,4},{16,24},{20,28},{24,16},{28,20},{1,9},{5... | collective-permute-start | bytes 393224 | tf_op jit(solution)/shard_map/ppermute | solution.py:541
  38.3 5.2 %shard_map.144 = (bf16[256,2048]{1,0:T(8,128)(2,1)S(1)}, bf16[2048,256]{1,0:T(8,128)(2,1)S(1)}, bf16[2048,256]{1,0:T(8,128)(2,1)S(1)}, bf16[256,256]{1,0:T(8,128)(2,1)S(1)}, bf16[256,256]{1,0:T(8,128)(2,1)S(1)}) custom-call(s32[2,8]{1,0:T(2,128)S(1)} %get-tuple-element.38.refs_0_, s32[1,2176]{1,0:T(1,128)S(1)} %get-tuple-element.39.refs_4_.refs_1_, ...), custom_call_target="tpu_custom_call" | custom-call | flops 8589934592 | tf_op jit(solution)/shard_map/pallas_call | solution.py:522
  43.4 0.5 shard_map.147.raw_in_t
  43.9 0.1 collective-permute-start.4
  44.0 0.0 collective-permute-done.8.other_out
  44.0 0.6 collective-permute-start.9
  44.6 1.3 %shard_map.145 = bf16[2048,256]{1,0:T(8,128)(2,1)} custom-call(bf16[2048,256]{1,0:T(8,128)(2,1)S(1)} %get-tuple-element.52.base.feats, bf16[256,2048]{1,0:T(8,128)(2,1)S(1)} %get-tuple-element.53.values_t, bf16[256,256]{1,0:T(8,128)(2,1)S(1)} %get-tuple-element.54.weight), custom_call_target="tpu_custom_call" | custom-call | flops 2147483648 | tf_op jit(solution)/shard_map/pallas_call | solution.py:438
  45.9 0.0 collective-permute-done.12.refs_3_
  46.0 0.0 collective-permute-done.11.refs_1_
  46.0 5.4 %collective-permute-done.9.other_out.refs_2_ = bf16[384,256]{1,0:T(8,128)(2,1)S(1)} collective-permute-done((bf16[384,256]{1,0:T(8,128)(2,1)S(1)}, bf16[384,256]{1,0:T(8,128)(2,1)S(1)}, u32[]{:S(2)}, u32[]{:S(2)}) %collective-permute-start.9) | collective-permute-done | bytes 196640 | tf_op jit(solution)/shard_map/ppermute | solution.py:541
  51.4 0.1 collective-permute-start.13
  51.5 1.4 %shard_map.146 = bf16[2048,256]{1,0:T(8,128)(2,1)} custom-call(bf16[2048,256]{1,0:T(8,128)(2,1)S(1)} %get-tuple-element.55.base, bf16[256,2048]{1,0:T(8,128)(2,1)S(1)} %get-tuple-element.56.values_t.update_t, bf16[256,256]{1,0:T(8,128)(2,1)S(1)} %get-tuple-element.57.weight), custom_call_target="tpu_custom_call" | custom-call | flops 2147483648 | tf_op jit(solution)/shard_map/pallas_call | solution.py:438
  52.9 0.0 collective-permute-done.13.near
  52.9 0.1 shard_map.152
  53.0 1.4 %collective-permute-start.14 = (f32[8,128]{1,0:T(8,128)S(1)}, f32[8,128]{1,0:T(8,128)S(1)}, u32[]{:S(2)}, u32[]{:S(2)}) collective-permute-start(f32[8,128]{1,0:T(8,128)S(1)} %get-tuple-element.67.first), channel_id=1, source_target_pairs={{0,1},{1,0},{2,3},{3,2},{4,5},{5,4},{6,7},{7,6},{8,9},{9,8},{10,11... | collective-permute-start | bytes 12296 | tf_op jit(solution)/shard_map/ppermute | solution.py:541
  54.4 0.3 collective-permute-start.10
  54.7 1.9 %collective-permute-done.14.second = f32[8,128]{1,0:T(8,128)S(1)} collective-permute-done((f32[8,128]{1,0:T(8,128)S(1)}, f32[8,128]{1,0:T(8,128)S(1)}, u32[]{:S(2)}, u32[]{:S(2)}) %collective-permute-start.14) | collective-permute-done | bytes 4128 | tf_op jit(solution)/shard_map/ppermute | solution.py:541
  56.6 2.4 %collective-permute-start.15 = (f32[8,128]{1,0:T(8,128)S(1)}, f32[8,128]{1,0:T(8,128)S(1)}, u32[]{:S(2)}, u32[]{:S(2)}) collective-permute-start(f32[8,128]{1,0:T(8,128)S(1)} %shard_map.153.first), channel_id=1, source_target_pairs={{0,2},{1,3},{2,0},{3,1},{4,6},{5,7},{6,4},{7,5},{8,10},{9,11},{10,... | collective-permute-start | bytes 12296 | tf_op jit(solution)/shard_map/ppermute | solution.py:541
  59.0 0.0 collective-permute-done.4.near
  59.1 0.3 collective-permute-start.7
  59.4 1.4 %collective-permute-start.6 = (bf16[256,256]{1,0:T(8,128)(2,1)S(1)}, bf16[256,256]{1,0:T(8,128)(2,1)S(1)}, u32[]{:S(2)}, u32[]{:S(2)}) collective-permute-start(bf16[256,256]{1,0:T(8,128)(2,1)S(1)} %get-tuple-element.59), channel_id=1, source_target_pairs={{0,16},{4,20},{8,24},{12,28},{16,0},{20,4},{24,8},{28,12},{1,17},{... | collective-permute-start | bytes 393224 | tf_op jit(solution)/shard_map/ppermute | solution.py:541
  60.8 1.8 %collective-permute-start.5 = (bf16[256,256]{1,0:T(8,128)(2,1)S(1)}, bf16[256,256]{1,0:T(8,128)(2,1)S(1)}, u32[]{:S(2)}, u32[]{:S(2)}) collective-permute-start(bf16[256,256]{1,0:T(8,128)(2,1)S(1)} %get-tuple-element.59), channel_id=1, source_target_pairs={{0,8},{4,12},{8,0},{12,4},{16,24},{20,28},{24,16},{28,20},{1,9},{5... | collective-permute-start | bytes 393224 | tf_op jit(solution)/shard_map/ppermute | solution.py:541
  62.6 0.0 collective-permute-done.15.second
  62.6 3.3 %collective-permute-done.7.refs_3_ = bf16[256,256]{1,0:T(8,128)(2,1)S(1)} collective-permute-done((bf16[256,256]{1,0:T(8,128)(2,1)S(1)}, bf16[256,256]{1,0:T(8,128)(2,1)S(1)}, u32[]{:S(2)}, u32[]{:S(2)}) %collective-permute-start.7) | collective-permute-done | bytes 131104 | tf_op jit(solution)/shard_map/ppermute | solution.py:541
  66.0 0.5 collective-permute-done.6.refs_2_
  66.5 0.0 collective-permute-done.5.refs_1_
  66.5 0.0 collective-permute-done.10.refs_5_
  66.5 1.1 %shard_map.155 = (f32[256,256]{1,0:T(8,128)}, f32[256,256]{1,0:T(8,128)}, f32[128,256]{1,0:T(8,128)}) custom-call(f32[256,256]{1,0:T(8,128)S(1)} %get-tuple-element.58.refs_0_, bf16[256,256]{1,0:T(8,128)(2,1)S(1)} %collective-permute-done.5.refs_1_, bf16[256,256]{1,0:T(8,128)(2,1)S(1)} %collective-permute-done.6.refs_2_, ...), custom_call_target="tpu_custom_call" | custom-call | flops 2147483648 | tf_op jit(solution)/shard_map/pallas_call | solution.py:522
  (7 shorter events, 0.1 us)
Async XLA Ops:
  0.6 6.5 %collective-permute-start = (s32[1,3,128]{2,1,0:T(4,128)}, s32[1,3,128]{2,1,0:T(4,128)S(1)}, u32[]{:S(2)}, u32[]{:S(2)}) collective-permute-start(s32[1,3,128]{2,1,0:T(4,128)} %bitcast.15), channel_id=1, source_target_pairs={{0,1},{1,0},{2,3},{3,2},{4,5},{5,4},{6,7},{7,6},{8,9},{9,8},{10,11... | collective-permute-start | bytes 4616 | tf_op jit(solution)/shard_map/ppermute | solution.py:541
  3.8 9.9 %collective-permute-start.2 = (f32[1,128,256]{2,1,0:T(8,128)}, f32[1,128,256]{2,1,0:T(8,128)S(1)}, u32[]{:S(2)}, u32[]{:S(2)}) collective-permute-start(f32[1,128,256]{2,1,0:T(8,128)} %bitcast.13), channel_id=1, source_target_pairs={{0,1},{1,0},{2,3},{3,2},{4,5},{5,4},{6,7},{7,6},{8,9},{9,8},{10,11... | collective-permute-start | bytes 393224 | tf_op jit(solution)/shard_map/ppermute | solution.py:541
  7.1 6.9 %collective-permute-start.1 = (f32[2,8,128]{2,1,0:T(8,128)S(1)}, f32[2,8,128]{2,1,0:T(8,128)S(1)}, u32[]{:S(2)}, u32[]{:S(2)}) collective-permute-start(f32[2,8,128]{2,1,0:T(8,128)S(1)} %shard_map.138.kvecs.refs_7_), channel_id=1, source_target_pairs={{0,2},{1,3},{2,0},{3,1},{4,6},{5,7},{6,4},{7,5},{8,10},{9,11},{10,... | collective-permute-start | bytes 24584 | tf_op jit(solution)/shard_map/ppermute | solution.py:541
  13.9 8.5 %collective-permute-start.3 = (s16[2,272,128]{2,1,0:T(8,128)(2,1)S(1)}, s16[2,272,128]{2,1,0:T(8,128)(2,1)S(1)}, u32[]{:S(2)}, u32[]{:S(2)}) collective-permute-start(s16[2,272,128]{2,1,0:T(8,128)(2,1)S(1)} %shard_map.141), channel_id=1, source_target_pairs={{0,2},{1,3},{2,0},{3,1},{4,6},{5,7},{6,4},{7,5},{8,10},{9,11},{10,... | collective-permute-start | bytes 417800 | tf_op jit(solution)/shard_map/ppermute | solution.py:541
  14.0 8.4 %copy-start = (bf16[2048,256]{1,0:T(8,128)(2,1)S(1)}, bf16[2048,256]{1,0:T(8,128)(2,1)}, u32[]{:S(2)}) copy-start(bf16[2048,256]{1,0:T(8,128)(2,1)} %refs_10_.1) | copy-start | bytes 3145732
  14.0 8.4 %copy-start.1 = (bf16[256,256]{1,0:T(8,128)(2,1)S(1)}, bf16[256,256]{1,0:T(8,128)(2,1)}, u32[]{:S(2)}) copy-start(bf16[256,256]{1,0:T(8,128)(2,1)} %refs_12_.1) | copy-start | bytes 393220
  14.0 8.4 %copy-start.2 = (f32[256]{0:T(256)S(1)}, f32[256]{0:T(256)}, u32[]{:S(2)}) copy-start(f32[256]{0:T(256)} %param.18) | copy-start | bytes 3076
  33.4 12.5 %collective-permute-start.12 = (bf16[128,256]{1,0:T(8,128)(2,1)S(1)}, bf16[128,256]{1,0:T(8,128)(2,1)S(1)}, u32[]{:S(2)}, u32[]{:S(2)}) collective-permute-start(bf16[128,256]{1,0:T(8,128)(2,1)S(1)} %get-tuple-element.62.filter_half), channel_id=1, source_target_pairs={{0,24},{4,28},{8,16},{12,20},{16,8},{20,12},{24,0},{28,4},{1,25},{... | collective-permute-start | bytes 196616 | tf_op jit(solution)/shard_map/ppermute | solution.py:541
  36.2 9.7 %collective-permute-start.11 = (bf16[128,256]{1,0:T(8,128)(2,1)S(1)}, bf16[128,256]{1,0:T(8,128)(2,1)S(1)}, u32[]{:S(2)}, u32[]{:S(2)}) collective-permute-start(bf16[128,256]{1,0:T(8,128)(2,1)S(1)} %get-tuple-element.62.filter_half), channel_id=1, source_target_pairs={{0,8},{4,12},{8,0},{12,4},{16,24},{20,28},{24,16},{28,20},{1,9},{5... | collective-permute-start | bytes 196616 | tf_op jit(solution)/shard_map/ppermute | solution.py:541
  36.4 7.5 %collective-permute-start.8 = (bf16[256,256]{1,0:T(8,128)(2,1)S(1)}, bf16[256,256]{1,0:T(8,128)(2,1)S(1)}, u32[]{:S(2)}, u32[]{:S(2)}) collective-permute-start(bf16[256,256]{1,0:T(8,128)(2,1)S(1)} %get-tuple-element.61), channel_id=1, source_target_pairs={{0,8},{4,12},{8,0},{12,4},{16,24},{20,28},{24,16},{28,20},{1,9},{5... | collective-permute-start | bytes 393224 | tf_op jit(solution)/shard_map/ppermute | solution.py:541
  43.9 15.1 %collective-permute-start.4 = (f32[256,256]{1,0:T(8,128)S(1)}, f32[256,256]{1,0:T(8,128)S(1)}, u32[]{:S(2)}, u32[]{:S(2)}) collective-permute-start(f32[256,256]{1,0:T(8,128)S(1)} %shard_map.147.raw_in_t), channel_id=1, source_target_pairs={{0,4},{4,0},{8,12},{12,8},{16,20},{20,16},{24,28},{28,24},{1,5},{5... | collective-permute-start | bytes 786440 | tf_op jit(solution)/shard_map/ppermute | solution.py:541
  44.0 7.4 %collective-permute-start.9 = (bf16[384,256]{1,0:T(8,128)(2,1)S(1)}, bf16[384,256]{1,0:T(8,128)(2,1)S(1)}, u32[]{:S(2)}, u32[]{:S(2)}) collective-permute-start(bf16[384,256]{1,0:T(8,128)(2,1)S(1)} %get-tuple-element.64), channel_id=1, source_target_pairs={{0,16},{4,20},{8,24},{12,28},{16,0},{20,4},{24,8},{28,12},{1,17},{... | collective-permute-start | bytes 589832 | tf_op jit(solution)/shard_map/ppermute | solution.py:541
  51.4 1.5 %collective-permute-start.13 = (f32[128,256]{1,0:T(8,128)S(1)}, f32[128,256]{1,0:T(8,128)S(1)}, u32[]{:S(2)}, u32[]{:S(2)}) collective-permute-start(f32[128,256]{1,0:T(8,128)S(1)} %shard_map.151.filt), channel_id=1, source_target_pairs={{0,4},{4,0},{8,12},{12,8},{16,20},{20,16},{24,28},{28,24},{1,5},{5... | collective-permute-start | bytes 393224 | tf_op jit(solution)/shard_map/ppermute | solution.py:541
  53.0 3.6 %collective-permute-start.14 = (f32[8,128]{1,0:T(8,128)S(1)}, f32[8,128]{1,0:T(8,128)S(1)}, u32[]{:S(2)}, u32[]{:S(2)}) collective-permute-start(f32[8,128]{1,0:T(8,128)S(1)} %get-tuple-element.67.first), channel_id=1, source_target_pairs={{0,1},{1,0},{2,3},{3,2},{4,5},{5,4},{6,7},{7,6},{8,9},{9,8},{10,11... | collective-permute-start | bytes 12296 | tf_op jit(solution)/shard_map/ppermute | solution.py:541
  54.4 12.1 %collective-permute-start.10 = (f32[256,256]{1,0:T(8,128)S(1)}, f32[256,256]{1,0:T(8,128)S(1)}, u32[]{:S(2)}, u32[]{:S(2)}) collective-permute-start(f32[256,256]{1,0:T(8,128)S(1)} %shard_map.150.refs_4_), channel_id=1, source_target_pairs={{0,4},{4,0},{8,12},{12,8},{16,20},{20,16},{24,28},{28,24},{1,5},{5... | collective-permute-start | bytes 786440 | tf_op jit(solution)/shard_map/ppermute | solution.py:541
  56.6 6.0 %collective-permute-start.15 = (f32[8,128]{1,0:T(8,128)S(1)}, f32[8,128]{1,0:T(8,128)S(1)}, u32[]{:S(2)}, u32[]{:S(2)}) collective-permute-start(f32[8,128]{1,0:T(8,128)S(1)} %shard_map.153.first), channel_id=1, source_target_pairs={{0,2},{1,3},{2,0},{3,1},{4,6},{5,7},{6,4},{7,5},{8,10},{9,11},{10,... | collective-permute-start | bytes 12296 | tf_op jit(solution)/shard_map/ppermute | solution.py:541
  59.1 6.9 %collective-permute-start.7 = (bf16[256,256]{1,0:T(8,128)(2,1)S(1)}, bf16[256,256]{1,0:T(8,128)(2,1)S(1)}, u32[]{:S(2)}, u32[]{:S(2)}) collective-permute-start(bf16[256,256]{1,0:T(8,128)(2,1)S(1)} %get-tuple-element.59), channel_id=1, source_target_pairs={{0,24},{4,28},{8,16},{12,20},{16,8},{20,12},{24,0},{28,4},{1,25},{... | collective-permute-start | bytes 393224 | tf_op jit(solution)/shard_map/ppermute | solution.py:541
  59.4 7.1 %collective-permute-start.6 = (bf16[256,256]{1,0:T(8,128)(2,1)S(1)}, bf16[256,256]{1,0:T(8,128)(2,1)S(1)}, u32[]{:S(2)}, u32[]{:S(2)}) collective-permute-start(bf16[256,256]{1,0:T(8,128)(2,1)S(1)} %get-tuple-element.59), channel_id=1, source_target_pairs={{0,16},{4,20},{8,24},{12,28},{16,0},{20,4},{24,8},{28,12},{1,17},{... | collective-permute-start | bytes 393224 | tf_op jit(solution)/shard_map/ppermute | solution.py:541
  60.8 5.7 %collective-permute-start.5 = (bf16[256,256]{1,0:T(8,128)(2,1)S(1)}, bf16[256,256]{1,0:T(8,128)(2,1)S(1)}, u32[]{:S(2)}, u32[]{:S(2)}) collective-permute-start(bf16[256,256]{1,0:T(8,128)(2,1)S(1)} %get-tuple-element.59), channel_id=1, source_target_pairs={{0,8},{4,12},{8,0},{12,4},{16,24},{20,28},{24,16},{28,20},{1,9},{5... | collective-permute-start | bytes 393224 | tf_op jit(solution)/shard_map/ppermute | solution.py:541

commit v9 on v8

--- a/solution.py
+++ b/solution.py
@@ -224,8 +224,8 @@
     for j, ref in enumerate((near, far)):
         values = ref[0].T
         largest = jnp.max(jnp.abs(values), axis=0, keepdims=True)
-        power = jnp.ceil(jnp.log2(jnp.maximum(largest, 1e-30)) + 1e-3)
-        coded = values * (CODES * jnp.exp2(-power))
+        power = jnp.ceil(jnp.log2(jnp.maximum(largest, 1e-30)) + 0.02)
+        coded = values * (CODES / jnp.exp2(power))
         coded = (coded + ROUNDER) - ROUNDER
         out[j, :chan, :] = coded.astype(jnp.int32).astype(jnp.int16)
         powers = jnp.broadcast_to(power, (16, power.shape[1]))
@@ -323,7 +323,7 @@
                 values = ref[j].T
             else:
                 coded = ref[j].astype(jnp.int32).astype(F32)
-                values = coded[:chan, :] * (jnp.exp2(coded[chan : chan + 1, :]) * (1.0 / CODES))
+                values = coded[:chan, :] * (jnp.exp2(coded[chan : chan + 1, :]) / CODES)
             filt_t[:, chunk * own : (chunk + 1) * own] = values
             chunk += 1
     return own

time: 67.7 us -> 67.8 us (level)
  no operation moved by 1% of the time
where the time goes in v9:
time: 67.8 us; the launch traced here: 67.6 us
  Pallas kernels  35.3 us (52%)
  starting transfers between devices  19.6 us (29%)
  waiting for transfers between devices  11.8 us (17%)
  between operations  0.84 us (1%)
    pallas_call x17, Pallas kernels, call(): pl.pallas_call(kernel, out_shape=tuple((jax.ShapeDtypeStruct(*o) for o in...  32.6 us
    ppermute x16, starting transfers between devices, send(): return lax.ppermute(value, axis, routes(step, lax.axis_size(axis)))  19.6 us
    ppermute x16, waiting for transfers between devices, send(): return lax.ppermute(value, axis, routes(step, lax.axis_size(axis)))  11.8 us
    pallas_call x2, Pallas kernels, residual(): pl.pallas_call(functools.partial(residual_kernel, transposed), out_shape=...  2.69 us
  transfers between devices with their start and end apart: 16, of which 5 were waited for; matrix products, arithmetic and copies ran while one was open for 0% of the time, Pallas kernels for 34%

profile of v9, /device:TPU:0, one launch (start us, length us, event | category | flops | bytes accessed | tf_op | source)
XLA Modules:
  0.0 67.6 jit_solution(8915281846727643069)
XLA Ops:
  0.6 3.1 %collective-permute-start = (s32[1,3,128]{2,1,0:T(4,128)}, s32[1,3,128]{2,1,0:T(4,128)S(1)}, u32[]{:S(2)}, u32[]{:S(2)}) collective-permute-start(s32[1,3,128]{2,1,0:T(4,128)} %bitcast.15), channel_id=1, source_target_pairs={{0,1},{1,0},{2,3},{3,2},{4,5},{5,4},{6,7},{7,6},{8,9},{9,8},{10,11... | collective-permute-start | bytes 4616 | tf_op jit(solution)/shard_map/ppermute | solution.py:541
  3.8 0.1 collective-permute-start.2
  3.8 3.3 %shard_map.137 = (bf16[256,2176]{1,0:T(8,128)(2,1)S(1)}, s32[1,2176]{1,0:T(1,128)S(1)}, f32[3,2048]{1,0:T(4,128)S(1)}, f32[8,9]{1,0:T(8,128)S(1)}, s32[3,128]{1,...) custom-call(f32[3,2048]{1,0:T(4,128)} %coords_hbm.1, s32[1,2048]{1,0:T(1,128)} %ids_hbm.1, f32[8,9]{1,0:T(8,128)} %bitcast.14, ...), custom_call_target="tpu_custom_call" | custom-call | flops 3221225472 | tf_op jit(solution)/shard_map/pallas_call | solution.py:522
  7.1 0.0 collective-permute-done.other_kvec
  7.1 3.0 %collective-permute-start.1 = (f32[2,8,128]{2,1,0:T(8,128)S(1)}, f32[2,8,128]{2,1,0:T(8,128)S(1)}, u32[]{:S(2)}, u32[]{:S(2)}) collective-permute-start(f32[2,8,128]{2,1,0:T(8,128)S(1)} %shard_map.138.kvecs.refs_7_), channel_id=1, source_target_pairs={{0,2},{1,3},{2,0},{3,1},{4,6},{5,7},{6,4},{7,5},{8,10},{9,11},{10,... | collective-permute-start | bytes 24584 | tf_op jit(solution)/shard_map/ppermute | solution.py:541
  10.1 3.5 %shard_map.139 = (bf16[256,2176]{1,0:T(8,128)(2,1)S(1)}, bf16[256,2176]{1,0:T(8,128)(2,1)S(1)}) custom-call(f32[3,2048]{1,0:T(4,128)S(1)} %get-tuple-element.41.coords.refs_5_, f32[2,8,128]{2,1,0:T(8,128)S(1)} %shard_map.138.kvecs.refs_7_, bf16[2048,256]{1,0:T(8,128)(2,1)} %refs_9_.1, bf16[256,256]{1,0:T(8,128)(2,1)} %refs_11_.1), custom_call_target="tpu_custom_call" | custom-call | flops 3221225472 | tf_op jit(solution)/shard_map/pallas_call | solution.py:522
  13.7 0.0 collective-permute-done.2.far.refs_9_.refs_7_
  13.7 0.2 shard_map.141
  13.9 0.1 collective-permute-start.3
  14.0 0.0 collective-permute-done.1.refs_8_
  14.0 0.0 copy-start
  14.0 0.0 copy-start.1
  14.0 0.0 copy-start.2
  14.0 7.7 %shard_map.140 = (bf16[1024,2176]{1,0:T(8,128)(2,1)S(1)}, f32[8,256,1024]{2,1,0:T(8,128)S(1)}, f32[8,512]{1,0:T(8,128)S(1)}) custom-call(s32[2,8]{1,0:T(2,128)S(1)} %get-tuple-element.38.refs_0_, bf16[256,2176]{1,0:T(8,128)(2,1)S(1)} %get-tuple-element.40.refs_1_, bf16[256,2176]{1,0:T(8,128)(2,1)S(1)} %get-tuple-element.43.refs_2_, ...), custom_call_target="tpu_custom_call" | custom-call | flops 8589934592 | tf_op jit(solution)/shard_map/pallas_call | solution.py:522
  21.8 0.7 collective-permute-done.3.refs_10_.refs_8_
  22.4 0.0 copy-done
  22.4 0.0 copy-done.1
  22.4 0.0 copy-done.2
  22.4 6.3 %shard_map.142 = (bf16[256,2048]{1,0:T(8,128)(2,1)S(1)}, bf16[256,2176]{1,0:T(8,128)(2,1)S(1)}, f32[256,256]{1,0:T(8,128)S(1)}, bf16[256,256]{1,0:T(8,128)(2,1)S(1)}) custom-call(s32[2,8]{1,0:T(2,128)S(1)} %get-tuple-element.38.refs_0_, s32[1,2176]{1,0:T(1,128)S(1)} %get-tuple-element.39.refs_4_.refs_1_, f32[8,512]{1,0:T(8,128)S(1)} %get-tuple-element.46.refs_2_, ...), custom_call_target="tpu_custom_call" | custom-call | flops 8589934592 | tf_op jit(solution)/shard_map/pallas_call | solution.py:522
  28.8 4.6 %shard_map.143 = (f32[8,256,1024]{2,1,0:T(8,128)S(1)}, f32[128,256]{1,0:T(8,128)S(1)}, bf16[128,256]{1,0:T(8,128)(2,1)S(1)}) custom-call(s32[2,8]{1,0:T(2,128)S(1)} %get-tuple-element.38.refs_0_, s32[1,2176]{1,0:T(1,128)S(1)} %get-tuple-element.39.refs_4_.refs_1_, f32[8,512]{1,0:T(8,128)S(1)} %get-tuple-element.46.refs_2_, ...), custom_call_target="tpu_custom_call" | custom-call | flops 6442450944 | tf_op jit(solution)/shard_map/pallas_call | solution.py:522
  33.4 2.8 %collective-permute-start.12 = (bf16[128,256]{1,0:T(8,128)(2,1)S(1)}, bf16[128,256]{1,0:T(8,128)(2,1)S(1)}, u32[]{:S(2)}, u32[]{:S(2)}) collective-permute-start(bf16[128,256]{1,0:T(8,128)(2,1)S(1)} %get-tuple-element.62.filter_half), channel_id=1, source_target_pairs={{0,24},{4,28},{8,16},{12,20},{16,8},{20,12},{24,0},{28,4},{1,25},{... | collective-permute-start | bytes 196616 | tf_op jit(solution)/shard_map/ppermute | solution.py:541
  36.2 0.2 collective-permute-start.11
  36.4 1.8 %collective-permute-start.8 = (bf16[256,256]{1,0:T(8,128)(2,1)S(1)}, bf16[256,256]{1,0:T(8,128)(2,1)S(1)}, u32[]{:S(2)}, u32[]{:S(2)}) collective-permute-start(bf16[256,256]{1,0:T(8,128)(2,1)S(1)} %get-tuple-element.61), channel_id=1, source_target_pairs={{0,8},{4,12},{8,0},{12,4},{16,24},{20,28},{24,16},{28,20},{1,9},{5... | collective-permute-start | bytes 393224 | tf_op jit(solution)/shard_map/ppermute | solution.py:541
  38.3 5.2 %shard_map.144 = (bf16[256,2048]{1,0:T(8,128)(2,1)S(1)}, bf16[2048,256]{1,0:T(8,128)(2,1)S(1)}, bf16[2048,256]{1,0:T(8,128)(2,1)S(1)}, bf16[256,256]{1,0:T(8,128)(2,1)S(1)}, bf16[256,256]{1,0:T(8,128)(2,1)S(1)}) custom-call(s32[2,8]{1,0:T(2,128)S(1)} %get-tuple-element.38.refs_0_, s32[1,2176]{1,0:T(1,128)S(1)} %get-tuple-element.39.refs_4_.refs_1_, ...), custom_call_target="tpu_custom_call" | custom-call | flops 8589934592 | tf_op jit(solution)/shard_map/pallas_call | solution.py:522
  43.4 0.5 shard_map.147.raw_in_t
  43.9 0.1 collective-permute-start.4
  44.0 0.0 collective-permute-done.8.other_out
  44.0 0.6 collective-permute-start.9
  44.6 1.3 %shard_map.145 = bf16[2048,256]{1,0:T(8,128)(2,1)} custom-call(bf16[2048,256]{1,0:T(8,128)(2,1)S(1)} %get-tuple-element.52.base.feats, bf16[256,2048]{1,0:T(8,128)(2,1)S(1)} %get-tuple-element.53.values_t, bf16[256,256]{1,0:T(8,128)(2,1)S(1)} %get-tuple-element.54.weight), custom_call_target="tpu_custom_call" | custom-call | flops 2147483648 | tf_op jit(solution)/shard_map/pallas_call | solution.py:438
  46.0 0.0 collective-permute-done.12.refs_3_
  46.0 0.0 collective-permute-done.11.refs_1_
  46.0 5.4 %collective-permute-done.9.other_out.refs_2_ = bf16[384,256]{1,0:T(8,128)(2,1)S(1)} collective-permute-done((bf16[384,256]{1,0:T(8,128)(2,1)S(1)}, bf16[384,256]{1,0:T(8,128)(2,1)S(1)}, u32[]{:S(2)}, u32[]{:S(2)}) %collective-permute-start.9) | collective-permute-done | bytes 196640 | tf_op jit(solution)/shard_map/ppermute | solution.py:541
  51.4 0.1 collective-permute-start.13
  51.5 1.4 %shard_map.146 = bf16[2048,256]{1,0:T(8,128)(2,1)} custom-call(bf16[2048,256]{1,0:T(8,128)(2,1)S(1)} %get-tuple-element.55.base, bf16[256,2048]{1,0:T(8,128)(2,1)S(1)} %get-tuple-element.56.values_t.update_t, bf16[256,256]{1,0:T(8,128)(2,1)S(1)} %get-tuple-element.57.weight), custom_call_target="tpu_custom_call" | custom-call | flops 2147483648 | tf_op jit(solution)/shard_map/pallas_call | solution.py:438
  52.9 0.0 collective-permute-done.13.near
  52.9 0.1 shard_map.152
  53.0 1.4 %collective-permute-start.14 = (f32[8,128]{1,0:T(8,128)S(1)}, f32[8,128]{1,0:T(8,128)S(1)}, u32[]{:S(2)}, u32[]{:S(2)}) collective-permute-start(f32[8,128]{1,0:T(8,128)S(1)} %get-tuple-element.67.first), channel_id=1, source_target_pairs={{0,1},{1,0},{2,3},{3,2},{4,5},{5,4},{6,7},{7,6},{8,9},{9,8},{10,11... | collective-permute-start | bytes 12296 | tf_op jit(solution)/shard_map/ppermute | solution.py:541
  54.4 0.3 collective-permute-start.10
  54.7 1.9 %collective-permute-done.14.second = f32[8,128]{1,0:T(8,128)S(1)} collective-permute-done((f32[8,128]{1,0:T(8,128)S(1)}, f32[8,128]{1,0:T(8,128)S(1)}, u32[]{:S(2)}, u32[]{:S(2)}) %collective-permute-start.14) | collective-permute-done | bytes 4128 | tf_op jit(solution)/shard_map/ppermute | solution.py:541
  56.6 2.4 %collective-permute-start.15 = (f32[8,128]{1,0:T(8,128)S(1)}, f32[8,128]{1,0:T(8,128)S(1)}, u32[]{:S(2)}, u32[]{:S(2)}) collective-permute-start(f32[8,128]{1,0:T(8,128)S(1)} %shard_map.153.first), channel_id=1, source_target_pairs={{0,2},{1,3},{2,0},{3,1},{4,6},{5,7},{6,4},{7,5},{8,10},{9,11},{10,... | collective-permute-start | bytes 12296 | tf_op jit(solution)/shard_map/ppermute | solution.py:541
  59.0 0.0 collective-permute-done.4.near
  59.1 0.3 collective-permute-start.7
  59.4 1.4 %collective-permute-start.6 = (bf16[256,256]{1,0:T(8,128)(2,1)S(1)}, bf16[256,256]{1,0:T(8,128)(2,1)S(1)}, u32[]{:S(2)}, u32[]{:S(2)}) collective-permute-start(bf16[256,256]{1,0:T(8,128)(2,1)S(1)} %get-tuple-element.59), channel_id=1, source_target_pairs={{0,16},{4,20},{8,24},{12,28},{16,0},{20,4},{24,8},{28,12},{1,17},{... | collective-permute-start | bytes 393224 | tf_op jit(solution)/shard_map/ppermute | solution.py:541
  60.8 1.8 %collective-permute-start.5 = (bf16[256,256]{1,0:T(8,128)(2,1)S(1)}, bf16[256,256]{1,0:T(8,128)(2,1)S(1)}, u32[]{:S(2)}, u32[]{:S(2)}) collective-permute-start(bf16[256,256]{1,0:T(8,128)(2,1)S(1)} %get-tuple-element.59), channel_id=1, source_target_pairs={{0,8},{4,12},{8,0},{12,4},{16,24},{20,28},{24,16},{28,20},{1,9},{5... | collective-permute-start | bytes 393224 | tf_op jit(solution)/shard_map/ppermute | solution.py:541
  62.6 0.0 collective-permute-done.15.second
  62.6 3.3 %collective-permute-done.7.refs_3_ = bf16[256,256]{1,0:T(8,128)(2,1)S(1)} collective-permute-done((bf16[256,256]{1,0:T(8,128)(2,1)S(1)}, bf16[256,256]{1,0:T(8,128)(2,1)S(1)}, u32[]{:S(2)}, u32[]{:S(2)}) %collective-permute-start.7) | collective-permute-done | bytes 131104 | tf_op jit(solution)/shard_map/ppermute | solution.py:541
  66.0 0.5 collective-permute-done.6.refs_2_
  66.5 0.0 collective-permute-done.5.refs_1_
  66.5 0.0 collective-permute-done.10.refs_5_
  66.5 1.1 %shard_map.155 = (f32[256,256]{1,0:T(8,128)}, f32[256,256]{1,0:T(8,128)}, f32[128,256]{1,0:T(8,128)}) custom-call(f32[256,256]{1,0:T(8,128)S(1)} %get-tuple-element.58.refs_0_, bf16[256,256]{1,0:T(8,128)(2,1)S(1)} %collective-permute-done.5.refs_1_, bf16[256,256]{1,0:T(8,128)(2,1)S(1)} %collective-permute-done.6.refs_2_, ...), custom_call_target="tpu_custom_call" | custom-call | flops 2147483648 | tf_op jit(solution)/shard_map/pallas_call | solution.py:522
  (7 shorter events, 0.1 us)
Async XLA Ops:
  0.6 6.5 %collective-permute-start = (s32[1,3,128]{2,1,0:T(4,128)}, s32[1,3,128]{2,1,0:T(4,128)S(1)}, u32[]{:S(2)}, u32[]{:S(2)}) collective-permute-start(s32[1,3,128]{2,1,0:T(4,128)} %bitcast.15), channel_id=1, source_target_pairs={{0,1},{1,0},{2,3},{3,2},{4,5},{5,4},{6,7},{7,6},{8,9},{9,8},{10,11... | collective-permute-start | bytes 4616 | tf_op jit(solution)/shard_map/ppermute | solution.py:541
  3.8 9.9 %collective-permute-start.2 = (f32[1,128,256]{2,1,0:T(8,128)}, f32[1,128,256]{2,1,0:T(8,128)S(1)}, u32[]{:S(2)}, u32[]{:S(2)}) collective-permute-start(f32[1,128,256]{2,1,0:T(8,128)} %bitcast.13), channel_id=1, source_target_pairs={{0,1},{1,0},{2,3},{3,2},{4,5},{5,4},{6,7},{7,6},{8,9},{9,8},{10,11... | collective-permute-start | bytes 393224 | tf_op jit(solution)/shard_map/ppermute | solution.py:541
  7.1 6.9 %collective-permute-start.1 = (f32[2,8,128]{2,1,0:T(8,128)S(1)}, f32[2,8,128]{2,1,0:T(8,128)S(1)}, u32[]{:S(2)}, u32[]{:S(2)}) collective-permute-start(f32[2,8,128]{2,1,0:T(8,128)S(1)} %shard_map.138.kvecs.refs_7_), channel_id=1, source_target_pairs={{0,2},{1,3},{2,0},{3,1},{4,6},{5,7},{6,4},{7,5},{8,10},{9,11},{10,... | collective-permute-start | bytes 24584 | tf_op jit(solution)/shard_map/ppermute | solution.py:541
  13.9 8.5 %collective-permute-start.3 = (s16[2,272,128]{2,1,0:T(8,128)(2,1)S(1)}, s16[2,272,128]{2,1,0:T(8,128)(2,1)S(1)}, u32[]{:S(2)}, u32[]{:S(2)}) collective-permute-start(s16[2,272,128]{2,1,0:T(8,128)(2,1)S(1)} %shard_map.141), channel_id=1, source_target_pairs={{0,2},{1,3},{2,0},{3,1},{4,6},{5,7},{6,4},{7,5},{8,10},{9,11},{10,... | collective-permute-start | bytes 417800 | tf_op jit(solution)/shard_map/ppermute | solution.py:541
  14.0 8.4 %copy-start = (bf16[2048,256]{1,0:T(8,128)(2,1)S(1)}, bf16[2048,256]{1,0:T(8,128)(2,1)}, u32[]{:S(2)}) copy-start(bf16[2048,256]{1,0:T(8,128)(2,1)} %refs_10_.1) | copy-start | bytes 3145732
  14.0 8.4 %copy-start.1 = (bf16[256,256]{1,0:T(8,128)(2,1)S(1)}, bf16[256,256]{1,0:T(8,128)(2,1)}, u32[]{:S(2)}) copy-start(bf16[256,256]{1,0:T(8,128)(2,1)} %refs_12_.1) | copy-start | bytes 393220
  14.0 8.4 %copy-start.2 = (f32[256]{0:T(256)S(1)}, f32[256]{0:T(256)}, u32[]{:S(2)}) copy-start(f32[256]{0:T(256)} %param.18) | copy-start | bytes 3076
  33.4 12.6 %collective-permute-start.12 = (bf16[128,256]{1,0:T(8,128)(2,1)S(1)}, bf16[128,256]{1,0:T(8,128)(2,1)S(1)}, u32[]{:S(2)}, u32[]{:S(2)}) collective-permute-start(bf16[128,256]{1,0:T(8,128)(2,1)S(1)} %get-tuple-element.62.filter_half), channel_id=1, source_target_pairs={{0,24},{4,28},{8,16},{12,20},{16,8},{20,12},{24,0},{28,4},{1,25},{... | collective-permute-start | bytes 196616 | tf_op jit(solution)/shard_map/ppermute | solution.py:541
  36.2 9.8 %collective-permute-start.11 = (bf16[128,256]{1,0:T(8,128)(2,1)S(1)}, bf16[128,256]{1,0:T(8,128)(2,1)S(1)}, u32[]{:S(2)}, u32[]{:S(2)}) collective-permute-start(bf16[128,256]{1,0:T(8,128)(2,1)S(1)} %get-tuple-element.62.filter_half), channel_id=1, source_target_pairs={{0,8},{4,12},{8,0},{12,4},{16,24},{20,28},{24,16},{28,20},{1,9},{5... | collective-permute-start | bytes 196616 | tf_op jit(solution)/shard_map/ppermute | solution.py:541
  36.4 7.5 %collective-permute-start.8 = (bf16[256,256]{1,0:T(8,128)(2,1)S(1)}, bf16[256,256]{1,0:T(8,128)(2,1)S(1)}, u32[]{:S(2)}, u32[]{:S(2)}) collective-permute-start(bf16[256,256]{1,0:T(8,128)(2,1)S(1)} %get-tuple-element.61), channel_id=1, source_target_pairs={{0,8},{4,12},{8,0},{12,4},{16,24},{20,28},{24,16},{28,20},{1,9},{5... | collective-permute-start | bytes 393224 | tf_op jit(solution)/shard_map/ppermute | solution.py:541
  43.9 15.1 %collective-permute-start.4 = (f32[256,256]{1,0:T(8,128)S(1)}, f32[256,256]{1,0:T(8,128)S(1)}, u32[]{:S(2)}, u32[]{:S(2)}) collective-permute-start(f32[256,256]{1,0:T(8,128)S(1)} %shard_map.147.raw_in_t), channel_id=1, source_target_pairs={{0,4},{4,0},{8,12},{12,8},{16,20},{20,16},{24,28},{28,24},{1,5},{5... | collective-permute-start | bytes 786440 | tf_op jit(solution)/shard_map/ppermute | solution.py:541
  44.0 7.4 %collective-permute-start.9 = (bf16[384,256]{1,0:T(8,128)(2,1)S(1)}, bf16[384,256]{1,0:T(8,128)(2,1)S(1)}, u32[]{:S(2)}, u32[]{:S(2)}) collective-permute-start(bf16[384,256]{1,0:T(8,128)(2,1)S(1)} %get-tuple-element.64), channel_id=1, source_target_pairs={{0,16},{4,20},{8,24},{12,28},{16,0},{20,4},{24,8},{28,12},{1,17},{... | collective-permute-start | bytes 589832 | tf_op jit(solution)/shard_map/ppermute | solution.py:541
  51.4 1.5 %collective-permute-start.13 = (f32[128,256]{1,0:T(8,128)S(1)}, f32[128,256]{1,0:T(8,128)S(1)}, u32[]{:S(2)}, u32[]{:S(2)}) collective-permute-start(f32[128,256]{1,0:T(8,128)S(1)} %shard_map.151.filt), channel_id=1, source_target_pairs={{0,4},{4,0},{8,12},{12,8},{16,20},{20,16},{24,28},{28,24},{1,5},{5... | collective-permute-start | bytes 393224 | tf_op jit(solution)/shard_map/ppermute | solution.py:541
  53.0 3.6 %collective-permute-start.14 = (f32[8,128]{1,0:T(8,128)S(1)}, f32[8,128]{1,0:T(8,128)S(1)}, u32[]{:S(2)}, u32[]{:S(2)}) collective-permute-start(f32[8,128]{1,0:T(8,128)S(1)} %get-tuple-element.67.first), channel_id=1, source_target_pairs={{0,1},{1,0},{2,3},{3,2},{4,5},{5,4},{6,7},{7,6},{8,9},{9,8},{10,11... | collective-permute-start | bytes 12296 | tf_op jit(solution)/shard_map/ppermute | solution.py:541
  54.4 12.1 %collective-permute-start.10 = (f32[256,256]{1,0:T(8,128)S(1)}, f32[256,256]{1,0:T(8,128)S(1)}, u32[]{:S(2)}, u32[]{:S(2)}) collective-permute-start(f32[256,256]{1,0:T(8,128)S(1)} %shard_map.150.refs_4_), channel_id=1, source_target_pairs={{0,4},{4,0},{8,12},{12,8},{16,20},{20,16},{24,28},{28,24},{1,5},{5... | collective-permute-start | bytes 786440 | tf_op jit(solution)/shard_map/ppermute | solution.py:541
  56.6 6.0 %collective-permute-start.15 = (f32[8,128]{1,0:T(8,128)S(1)}, f32[8,128]{1,0:T(8,128)S(1)}, u32[]{:S(2)}, u32[]{:S(2)}) collective-permute-start(f32[8,128]{1,0:T(8,128)S(1)} %shard_map.153.first), channel_id=1, source_target_pairs={{0,2},{1,3},{2,0},{3,1},{4,6},{5,7},{6,4},{7,5},{8,10},{9,11},{10,... | collective-permute-start | bytes 12296 | tf_op jit(solution)/shard_map/ppermute | solution.py:541
  59.1 6.9 %collective-permute-start.7 = (bf16[256,256]{1,0:T(8,128)(2,1)S(1)}, bf16[256,256]{1,0:T(8,128)(2,1)S(1)}, u32[]{:S(2)}, u32[]{:S(2)}) collective-permute-start(bf16[256,256]{1,0:T(8,128)(2,1)S(1)} %get-tuple-element.59), channel_id=1, source_target_pairs={{0,24},{4,28},{8,16},{12,20},{16,8},{20,12},{24,0},{28,4},{1,25},{... | collective-permute-start | bytes 393224 | tf_op jit(solution)/shard_map/ppermute | solution.py:541
  59.4 7.1 %collective-permute-start.6 = (bf16[256,256]{1,0:T(8,128)(2,1)S(1)}, bf16[256,256]{1,0:T(8,128)(2,1)S(1)}, u32[]{:S(2)}, u32[]{:S(2)}) collective-permute-start(bf16[256,256]{1,0:T(8,128)(2,1)S(1)} %get-tuple-element.59), channel_id=1, source_target_pairs={{0,16},{4,20},{8,24},{12,28},{16,0},{20,4},{24,8},{28,12},{1,17},{... | collective-permute-start | bytes 393224 | tf_op jit(solution)/shard_map/ppermute | solution.py:541
  60.8 5.7 %collective-permute-start.5 = (bf16[256,256]{1,0:T(8,128)(2,1)S(1)}, bf16[256,256]{1,0:T(8,128)(2,1)S(1)}, u32[]{:S(2)}, u32[]{:S(2)}) collective-permute-start(bf16[256,256]{1,0:T(8,128)(2,1)S(1)} %get-tuple-element.59), channel_id=1, source_target_pairs={{0,8},{4,12},{8,0},{12,4},{16,24},{20,28},{24,16},{28,20},{1,9},{5... | collective-permute-start | bytes 393224 | tf_op jit(solution)/shard_map/ppermute | solution.py:541

commit v10 on v9

--- a/solution.py
+++ b/solution.py
@@ -93,7 +93,7 @@
         filt = filt_t[:, own * j : own * (j + 1)] * scaled
         for half in (2 * j, 2 * j + 1):
             at = slice(own * half, own * (half + 1))
-            weights[:, at] = (filt * sums[cell, :, at]).astype(BF16)
+            weights[half] = (filt * sums[cell, :, at]).astype(BF16)
 
 
 def spread_cells(n_ka, bounds, ids, quad, filt_t, width_cols, sums, waves, even, odd, out):
@@ -106,9 +106,10 @@
         def action(n):
             if after is not None:
                 weigh(after, n_ka, bounds, quad, filt_t, width_cols, sums, target)
+            lhs = jnp.concatenate([weights[h] for h in range(2 * n_ka)], axis=1)
             for t in range(n):
                 at = pl.ds(pl.multiple_of(start + t * TILE, LANES), TILE)
-                value = mm(weights[...], waves[:, at])
+                value = mm(lhs, waves[:, at])
                 out[:, at] = jnp.where(ids[:, at] == cell, value, out[:, at])
 
         by_steps(steps, most, action)
@@ -614,7 +615,7 @@
         LIMIT,
         8,
     )
-    halves = [vm((chan, 2 * k_all), BF16)] * 2
+    halves = [vm((2 * n_ka, chan, own), BF16)] * 2
     act_t, mgrad_t, raw_out, raw_half = call(
         functools.partial(message_kernel, n_ka),
         (bounds, ids, quad, waves, factors, spread, cotan, w_out, *far_kfilts),

time: 67.8 us -> 67.6 us (level)
  no operation moved by 1% of the time
where the time goes in v10:
time: 67.6 us; the launch traced here: 67.4 us
  Pallas kernels  35.2 us (52%)
  starting transfers between devices  19.5 us (29%)
  waiting for transfers between devices  11.9 us (18%)
  between operations  0.84 us (1%)
    pallas_call x17, Pallas kernels, call(): pl.pallas_call(kernel, out_shape=tuple((jax.ShapeDtypeStruct(*o) for o in...  32.5 us
    ppermute x16, starting transfers between devices, send(): return lax.ppermute(value, axis, routes(step, lax.axis_size(axis)))  19.5 us
    ppermute x16, waiting for transfers between devices, send(): return lax.ppermute(value, axis, routes(step, lax.axis_size(axis)))  11.9 us
    pallas_call x2, Pallas kernels, residual(): pl.pallas_call(functools.partial(residual_kernel, transposed), out_shape=...  2.69 us
  transfers between devices with their start and end apart: 16, of which 5 were waited for; matrix products, arithmetic and copies ran while one was open for 0% of the time, Pallas kernels for 34%

profile of v10, /device:TPU:0, one launch (start us, length us, event | category | flops | bytes accessed | tf_op | source)
XLA Modules:
  0.0 67.4 jit_solution(12197359833298956147)
XLA Ops:
  0.6 3.1 %collective-permute-start = (s32[1,3,128]{2,1,0:T(4,128)}, s32[1,3,128]{2,1,0:T(4,128)S(1)}, u32[]{:S(2)}, u32[]{:S(2)}) collective-permute-start(s32[1,3,128]{2,1,0:T(4,128)} %bitcast.15), channel_id=1, source_target_pairs={{0,1},{1,0},{2,3},{3,2},{4,5},{5,4},{6,7},{7,6},{8,9},{9,8},{10,11... | collective-permute-start | bytes 4616 | tf_op jit(solution)/shard_map/ppermute | solution.py:542
  3.8 0.1 collective-permute-start.2
  3.8 3.3 %shard_map.137 = (bf16[256,2176]{1,0:T(8,128)(2,1)S(1)}, s32[1,2176]{1,0:T(1,128)S(1)}, f32[3,2048]{1,0:T(4,128)S(1)}, f32[8,9]{1,0:T(8,128)S(1)}, s32[3,128]{1,...) custom-call(f32[3,2048]{1,0:T(4,128)} %coords_hbm.1, s32[1,2048]{1,0:T(1,128)} %ids_hbm.1, f32[8,9]{1,0:T(8,128)} %bitcast.14, ...), custom_call_target="tpu_custom_call" | custom-call | flops 3221225472 | tf_op jit(solution)/shard_map/pallas_call | solution.py:523
  7.1 0.0 collective-permute-done.other_kvec
  7.1 3.0 %collective-permute-start.1 = (f32[2,8,128]{2,1,0:T(8,128)S(1)}, f32[2,8,128]{2,1,0:T(8,128)S(1)}, u32[]{:S(2)}, u32[]{:S(2)}) collective-permute-start(f32[2,8,128]{2,1,0:T(8,128)S(1)} %shard_map.138.kvecs.refs_7_), channel_id=1, source_target_pairs={{0,2},{1,3},{2,0},{3,1},{4,6},{5,7},{6,4},{7,5},{8,10},{9,11},{10,... | collective-permute-start | bytes 24584 | tf_op jit(solution)/shard_map/ppermute | solution.py:542
  10.1 3.5 %shard_map.139 = (bf16[256,2176]{1,0:T(8,128)(2,1)S(1)}, bf16[256,2176]{1,0:T(8,128)(2,1)S(1)}) custom-call(f32[3,2048]{1,0:T(4,128)S(1)} %get-tuple-element.41.coords.refs_5_, f32[2,8,128]{2,1,0:T(8,128)S(1)} %shard_map.138.kvecs.refs_7_, bf16[2048,256]{1,0:T(8,128)(2,1)} %refs_9_.1, bf16[256,256]{1,0:T(8,128)(2,1)} %refs_11_.1), custom_call_target="tpu_custom_call" | custom-call | flops 3221225472 | tf_op jit(solution)/shard_map/pallas_call | solution.py:523
  13.7 0.0 collective-permute-done.2.far.refs_9_.refs_7_
  13.7 0.2 shard_map.141
  13.9 0.1 collective-permute-start.3
  14.0 0.0 collective-permute-done.1.refs_8_
  14.0 0.0 copy-start
  14.0 0.0 copy-start.1
  14.0 0.0 copy-start.2
  14.0 7.7 %shard_map.140 = (bf16[1024,2176]{1,0:T(8,128)(2,1)S(1)}, f32[8,256,1024]{2,1,0:T(8,128)S(1)}, f32[8,512]{1,0:T(8,128)S(1)}) custom-call(s32[2,8]{1,0:T(2,128)S(1)} %get-tuple-element.38.refs_0_, bf16[256,2176]{1,0:T(8,128)(2,1)S(1)} %get-tuple-element.40.refs_1_, bf16[256,2176]{1,0:T(8,128)(2,1)S(1)} %get-tuple-element.43.refs_2_, ...), custom_call_target="tpu_custom_call" | custom-call | flops 8589934592 | tf_op jit(solution)/shard_map/pallas_call | solution.py:523
  21.8 0.7 collective-permute-done.3.refs_10_.refs_8_
  22.4 0.0 copy-done
  22.4 0.0 copy-done.1
  22.4 0.0 copy-done.2
  22.4 6.3 %shard_map.142 = (bf16[256,2048]{1,0:T(8,128)(2,1)S(1)}, bf16[256,2176]{1,0:T(8,128)(2,1)S(1)}, f32[256,256]{1,0:T(8,128)S(1)}, bf16[256,256]{1,0:T(8,128)(2,1)S(1)}) custom-call(s32[2,8]{1,0:T(2,128)S(1)} %get-tuple-element.38.refs_0_, s32[1,2176]{1,0:T(1,128)S(1)} %get-tuple-element.39.refs_4_.refs_1_, f32[8,512]{1,0:T(8,128)S(1)} %get-tuple-element.46.refs_2_, ...), custom_call_target="tpu_custom_call" | custom-call | flops 8589934592 | tf_op jit(solution)/shard_map/pallas_call | solution.py:523
  28.7 4.6 %shard_map.143 = (f32[8,256,1024]{2,1,0:T(8,128)S(1)}, f32[128,256]{1,0:T(8,128)S(1)}, bf16[128,256]{1,0:T(8,128)(2,1)S(1)}) custom-call(s32[2,8]{1,0:T(2,128)S(1)} %get-tuple-element.38.refs_0_, s32[1,2176]{1,0:T(1,128)S(1)} %get-tuple-element.39.refs_4_.refs_1_, f32[8,512]{1,0:T(8,128)S(1)} %get-tuple-element.46.refs_2_, ...), custom_call_target="tpu_custom_call" | custom-call | flops 6442450944 | tf_op jit(solution)/shard_map/pallas_call | solution.py:523
  33.3 2.9 %collective-permute-start.12 = (bf16[128,256]{1,0:T(8,128)(2,1)S(1)}, bf16[128,256]{1,0:T(8,128)(2,1)S(1)}, u32[]{:S(2)}, u32[]{:S(2)}) collective-permute-start(bf16[128,256]{1,0:T(8,128)(2,1)S(1)} %get-tuple-element.62.filter_half), channel_id=1, source_target_pairs={{0,24},{4,28},{8,16},{12,20},{16,8},{20,12},{24,0},{28,4},{1,25},{... | collective-permute-start | bytes 196616 | tf_op jit(solution)/shard_map/ppermute | solution.py:542
  36.2 0.2 collective-permute-start.11
  36.4 1.8 %collective-permute-start.8 = (bf16[256,256]{1,0:T(8,128)(2,1)S(1)}, bf16[256,256]{1,0:T(8,128)(2,1)S(1)}, u32[]{:S(2)}, u32[]{:S(2)}) collective-permute-start(bf16[256,256]{1,0:T(8,128)(2,1)S(1)} %get-tuple-element.61), channel_id=1, source_target_pairs={{0,8},{4,12},{8,0},{12,4},{16,24},{20,28},{24,16},{28,20},{1,9},{5... | collective-permute-start | bytes 393224 | tf_op jit(solution)/shard_map/ppermute | solution.py:542
  38.2 5.1 %shard_map.144 = (bf16[256,2048]{1,0:T(8,128)(2,1)S(1)}, bf16[2048,256]{1,0:T(8,128)(2,1)S(1)}, bf16[2048,256]{1,0:T(8,128)(2,1)S(1)}, bf16[256,256]{1,0:T(8,128)(2,1)S(1)}, bf16[256,256]{1,0:T(8,128)(2,1)S(1)}) custom-call(s32[2,8]{1,0:T(2,128)S(1)} %get-tuple-element.38.refs_0_, s32[1,2176]{1,0:T(1,128)S(1)} %get-tuple-element.39.refs_4_.refs_1_, ...), custom_call_target="tpu_custom_call" | custom-call | flops 8589934592 | tf_op jit(solution)/shard_map/pallas_call | solution.py:523
  43.3 0.5 shard_map.147.raw_in_t
  43.8 0.1 collective-permute-start.4
  43.8 0.0 collective-permute-done.8.other_out
  43.9 0.5 collective-permute-start.9
  44.4 1.3 %shard_map.145 = bf16[2048,256]{1,0:T(8,128)(2,1)} custom-call(bf16[2048,256]{1,0:T(8,128)(2,1)S(1)} %get-tuple-element.52.base.feats, bf16[256,2048]{1,0:T(8,128)(2,1)S(1)} %get-tuple-element.53.values_t, bf16[256,256]{1,0:T(8,128)(2,1)S(1)} %get-tuple-element.54.weight), custom_call_target="tpu_custom_call" | custom-call | flops 2147483648 | tf_op jit(solution)/shard_map/pallas_call | solution.py:439
  45.8 0.0 collective-permute-done.12.refs_3_
  45.8 0.0 collective-permute-done.11.refs_1_
  45.8 5.5 %collective-permute-done.9.other_out.refs_2_ = bf16[384,256]{1,0:T(8,128)(2,1)S(1)} collective-permute-done((bf16[384,256]{1,0:T(8,128)(2,1)S(1)}, bf16[384,256]{1,0:T(8,128)(2,1)S(1)}, u32[]{:S(2)}, u32[]{:S(2)}) %collective-permute-start.9) | collective-permute-done | bytes 196640 | tf_op jit(solution)/shard_map/ppermute | solution.py:542
  51.3 0.1 collective-permute-start.13
  51.4 1.4 %shard_map.146 = bf16[2048,256]{1,0:T(8,128)(2,1)} custom-call(bf16[2048,256]{1,0:T(8,128)(2,1)S(1)} %get-tuple-element.55.base, bf16[256,2048]{1,0:T(8,128)(2,1)S(1)} %get-tuple-element.56.values_t.update_t, bf16[256,256]{1,0:T(8,128)(2,1)S(1)} %get-tuple-element.57.weight), custom_call_target="tpu_custom_call" | custom-call | flops 2147483648 | tf_op jit(solution)/shard_map/pallas_call | solution.py:439
  52.7 0.0 collective-permute-done.13.near
  52.8 0.1 shard_map.152
  52.9 1.4 %collective-permute-start.14 = (f32[8,128]{1,0:T(8,128)S(1)}, f32[8,128]{1,0:T(8,128)S(1)}, u32[]{:S(2)}, u32[]{:S(2)}) collective-permute-start(f32[8,128]{1,0:T(8,128)S(1)} %get-tuple-element.67.first), channel_id=1, source_target_pairs={{0,1},{1,0},{2,3},{3,2},{4,5},{5,4},{6,7},{7,6},{8,9},{9,8},{10,11... | collective-permute-start | bytes 12296 | tf_op jit(solution)/shard_map/ppermute | solution.py:542
  54.3 0.3 collective-permute-start.10
  54.6 1.9 %collective-permute-done.14.second = f32[8,128]{1,0:T(8,128)S(1)} collective-permute-done((f32[8,128]{1,0:T(8,128)S(1)}, f32[8,128]{1,0:T(8,128)S(1)}, u32[]{:S(2)}, u32[]{:S(2)}) %collective-permute-start.14) | collective-permute-done | bytes 4128 | tf_op jit(solution)/shard_map/ppermute | solution.py:542
  56.5 2.4 %collective-permute-start.15 = (f32[8,128]{1,0:T(8,128)S(1)}, f32[8,128]{1,0:T(8,128)S(1)}, u32[]{:S(2)}, u32[]{:S(2)}) collective-permute-start(f32[8,128]{1,0:T(8,128)S(1)} %shard_map.153.first), channel_id=1, source_target_pairs={{0,2},{1,3},{2,0},{3,1},{4,6},{5,7},{6,4},{7,5},{8,10},{9,11},{10,... | collective-permute-start | bytes 12296 | tf_op jit(solution)/shard_map/ppermute | solution.py:542
  58.9 0.0 collective-permute-done.4.near
  58.9 0.3 collective-permute-start.7
  59.3 1.4 %collective-permute-start.6 = (bf16[256,256]{1,0:T(8,128)(2,1)S(1)}, bf16[256,256]{1,0:T(8,128)(2,1)S(1)}, u32[]{:S(2)}, u32[]{:S(2)}) collective-permute-start(bf16[256,256]{1,0:T(8,128)(2,1)S(1)} %get-tuple-element.59), channel_id=1, source_target_pairs={{0,16},{4,20},{8,24},{12,28},{16,0},{20,4},{24,8},{28,12},{1,17},{... | collective-permute-start | bytes 393224 | tf_op jit(solution)/shard_map/ppermute | solution.py:542
  60.7 1.8 %collective-permute-start.5 = (bf16[256,256]{1,0:T(8,128)(2,1)S(1)}, bf16[256,256]{1,0:T(8,128)(2,1)S(1)}, u32[]{:S(2)}, u32[]{:S(2)}) collective-permute-start(bf16[256,256]{1,0:T(8,128)(2,1)S(1)} %get-tuple-element.59), channel_id=1, source_target_pairs={{0,8},{4,12},{8,0},{12,4},{16,24},{20,28},{24,16},{28,20},{1,9},{5... | collective-permute-start | bytes 393224 | tf_op jit(solution)/shard_map/ppermute | solution.py:542
  62.5 0.0 collective-permute-done.15.second
  62.5 3.3 %collective-permute-done.7.refs_3_ = bf16[256,256]{1,0:T(8,128)(2,1)S(1)} collective-permute-done((bf16[256,256]{1,0:T(8,128)(2,1)S(1)}, bf16[256,256]{1,0:T(8,128)(2,1)S(1)}, u32[]{:S(2)}, u32[]{:S(2)}) %collective-permute-start.7) | collective-permute-done | bytes 131104 | tf_op jit(solution)/shard_map/ppermute | solution.py:542
  65.8 0.5 collective-permute-done.6.refs_2_
  66.4 0.0 collective-permute-done.5.refs_1_
  66.4 0.0 collective-permute-done.10.refs_5_
  66.4 1.1 %shard_map.155 = (f32[256,256]{1,0:T(8,128)}, f32[256,256]{1,0:T(8,128)}, f32[128,256]{1,0:T(8,128)}) custom-call(f32[256,256]{1,0:T(8,128)S(1)} %get-tuple-element.58.refs_0_, bf16[256,256]{1,0:T(8,128)(2,1)S(1)} %collective-permute-done.5.refs_1_, bf16[256,256]{1,0:T(8,128)(2,1)S(1)} %collective-permute-done.6.refs_2_, ...), custom_call_target="tpu_custom_call" | custom-call | flops 2147483648 | tf_op jit(solution)/shard_map/pallas_call | solution.py:523
  (7 shorter events, 0.1 us)
Async XLA Ops:
  0.6 6.5 %collective-permute-start = (s32[1,3,128]{2,1,0:T(4,128)}, s32[1,3,128]{2,1,0:T(4,128)S(1)}, u32[]{:S(2)}, u32[]{:S(2)}) collective-permute-start(s32[1,3,128]{2,1,0:T(4,128)} %bitcast.15), channel_id=1, source_target_pairs={{0,1},{1,0},{2,3},{3,2},{4,5},{5,4},{6,7},{7,6},{8,9},{9,8},{10,11... | collective-permute-start | bytes 4616 | tf_op jit(solution)/shard_map/ppermute | solution.py:542
  3.8 9.9 %collective-permute-start.2 = (f32[1,128,256]{2,1,0:T(8,128)}, f32[1,128,256]{2,1,0:T(8,128)S(1)}, u32[]{:S(2)}, u32[]{:S(2)}) collective-permute-start(f32[1,128,256]{2,1,0:T(8,128)} %bitcast.13), channel_id=1, source_target_pairs={{0,1},{1,0},{2,3},{3,2},{4,5},{5,4},{6,7},{7,6},{8,9},{9,8},{10,11... | collective-permute-start | bytes 393224 | tf_op jit(solution)/shard_map/ppermute | solution.py:542
  7.1 6.9 %collective-permute-start.1 = (f32[2,8,128]{2,1,0:T(8,128)S(1)}, f32[2,8,128]{2,1,0:T(8,128)S(1)}, u32[]{:S(2)}, u32[]{:S(2)}) collective-permute-start(f32[2,8,128]{2,1,0:T(8,128)S(1)} %shard_map.138.kvecs.refs_7_), channel_id=1, source_target_pairs={{0,2},{1,3},{2,0},{3,1},{4,6},{5,7},{6,4},{7,5},{8,10},{9,11},{10,... | collective-permute-start | bytes 24584 | tf_op jit(solution)/shard_map/ppermute | solution.py:542
  13.9 8.5 %collective-permute-start.3 = (s16[2,272,128]{2,1,0:T(8,128)(2,1)S(1)}, s16[2,272,128]{2,1,0:T(8,128)(2,1)S(1)}, u32[]{:S(2)}, u32[]{:S(2)}) collective-permute-start(s16[2,272,128]{2,1,0:T(8,128)(2,1)S(1)} %shard_map.141), channel_id=1, source_target_pairs={{0,2},{1,3},{2,0},{3,1},{4,6},{5,7},{6,4},{7,5},{8,10},{9,11},{10,... | collective-permute-start | bytes 417800 | tf_op jit(solution)/shard_map/ppermute | solution.py:542
  14.0 8.4 %copy-start = (bf16[2048,256]{1,0:T(8,128)(2,1)S(1)}, bf16[2048,256]{1,0:T(8,128)(2,1)}, u32[]{:S(2)}) copy-start(bf16[2048,256]{1,0:T(8,128)(2,1)} %refs_10_.1) | copy-start | bytes 3145732
  14.0 8.4 %copy-start.1 = (bf16[256,256]{1,0:T(8,128)(2,1)S(1)}, bf16[256,256]{1,0:T(8,128)(2,1)}, u32[]{:S(2)}) copy-start(bf16[256,256]{1,0:T(8,128)(2,1)} %refs_12_.1) | copy-start | bytes 393220
  14.0 8.4 %copy-start.2 = (f32[256]{0:T(256)S(1)}, f32[256]{0:T(256)}, u32[]{:S(2)}) copy-start(f32[256]{0:T(256)} %param.18) | copy-start | bytes 3076
  33.3 12.4 %collective-permute-start.12 = (bf16[128,256]{1,0:T(8,128)(2,1)S(1)}, bf16[128,256]{1,0:T(8,128)(2,1)S(1)}, u32[]{:S(2)}, u32[]{:S(2)}) collective-permute-start(bf16[128,256]{1,0:T(8,128)(2,1)S(1)} %get-tuple-element.62.filter_half), channel_id=1, source_target_pairs={{0,24},{4,28},{8,16},{12,20},{16,8},{20,12},{24,0},{28,4},{1,25},{... | collective-permute-start | bytes 196616 | tf_op jit(solution)/shard_map/ppermute | solution.py:542
  36.2 9.6 %collective-permute-start.11 = (bf16[128,256]{1,0:T(8,128)(2,1)S(1)}, bf16[128,256]{1,0:T(8,128)(2,1)S(1)}, u32[]{:S(2)}, u32[]{:S(2)}) collective-permute-start(bf16[128,256]{1,0:T(8,128)(2,1)S(1)} %get-tuple-element.62.filter_half), channel_id=1, source_target_pairs={{0,8},{4,12},{8,0},{12,4},{16,24},{20,28},{24,16},{28,20},{1,9},{5... | collective-permute-start | bytes 196616 | tf_op jit(solution)/shard_map/ppermute | solution.py:542
  36.4 7.4 %collective-permute-start.8 = (bf16[256,256]{1,0:T(8,128)(2,1)S(1)}, bf16[256,256]{1,0:T(8,128)(2,1)S(1)}, u32[]{:S(2)}, u32[]{:S(2)}) collective-permute-start(bf16[256,256]{1,0:T(8,128)(2,1)S(1)} %get-tuple-element.61), channel_id=1, source_target_pairs={{0,8},{4,12},{8,0},{12,4},{16,24},{20,28},{24,16},{28,20},{1,9},{5... | collective-permute-start | bytes 393224 | tf_op jit(solution)/shard_map/ppermute | solution.py:542
  43.8 15.1 %collective-permute-start.4 = (f32[256,256]{1,0:T(8,128)S(1)}, f32[256,256]{1,0:T(8,128)S(1)}, u32[]{:S(2)}, u32[]{:S(2)}) collective-permute-start(f32[256,256]{1,0:T(8,128)S(1)} %shard_map.147.raw_in_t), channel_id=1, source_target_pairs={{0,4},{4,0},{8,12},{12,8},{16,20},{20,16},{24,28},{28,24},{1,5},{5... | collective-permute-start | bytes 786440 | tf_op jit(solution)/shard_map/ppermute | solution.py:542
  43.9 7.4 %collective-permute-start.9 = (bf16[384,256]{1,0:T(8,128)(2,1)S(1)}, bf16[384,256]{1,0:T(8,128)(2,1)S(1)}, u32[]{:S(2)}, u32[]{:S(2)}) collective-permute-start(bf16[384,256]{1,0:T(8,128)(2,1)S(1)} %get-tuple-element.64), channel_id=1, source_target_pairs={{0,16},{4,20},{8,24},{12,28},{16,0},{20,4},{24,8},{28,12},{1,17},{... | collective-permute-start | bytes 589832 | tf_op jit(solution)/shard_map/ppermute | solution.py:542
  51.3 1.5 %collective-permute-start.13 = (f32[128,256]{1,0:T(8,128)S(1)}, f32[128,256]{1,0:T(8,128)S(1)}, u32[]{:S(2)}, u32[]{:S(2)}) collective-permute-start(f32[128,256]{1,0:T(8,128)S(1)} %shard_map.151.filt), channel_id=1, source_target_pairs={{0,4},{4,0},{8,12},{12,8},{16,20},{20,16},{24,28},{28,24},{1,5},{5... | collective-permute-start | bytes 393224 | tf_op jit(solution)/shard_map/ppermute | solution.py:542
  52.9 3.6 %collective-permute-start.14 = (f32[8,128]{1,0:T(8,128)S(1)}, f32[8,128]{1,0:T(8,128)S(1)}, u32[]{:S(2)}, u32[]{:S(2)}) collective-permute-start(f32[8,128]{1,0:T(8,128)S(1)} %get-tuple-element.67.first), channel_id=1, source_target_pairs={{0,1},{1,0},{2,3},{3,2},{4,5},{5,4},{6,7},{7,6},{8,9},{9,8},{10,11... | collective-permute-start | bytes 12296 | tf_op jit(solution)/shard_map/ppermute | solution.py:542
  54.3 12.1 %collective-permute-start.10 = (f32[256,256]{1,0:T(8,128)S(1)}, f32[256,256]{1,0:T(8,128)S(1)}, u32[]{:S(2)}, u32[]{:S(2)}) collective-permute-start(f32[256,256]{1,0:T(8,128)S(1)} %shard_map.150.refs_4_), channel_id=1, source_target_pairs={{0,4},{4,0},{8,12},{12,8},{16,20},{20,16},{24,28},{28,24},{1,5},{5... | collective-permute-start | bytes 786440 | tf_op jit(solution)/shard_map/ppermute | solution.py:542
  56.5 6.0 %collective-permute-start.15 = (f32[8,128]{1,0:T(8,128)S(1)}, f32[8,128]{1,0:T(8,128)S(1)}, u32[]{:S(2)}, u32[]{:S(2)}) collective-permute-start(f32[8,128]{1,0:T(8,128)S(1)} %shard_map.153.first), channel_id=1, source_target_pairs={{0,2},{1,3},{2,0},{3,1},{4,6},{5,7},{6,4},{7,5},{8,10},{9,11},{10,... | collective-permute-start | bytes 12296 | tf_op jit(solution)/shard_map/ppermute | solution.py:542
  58.9 6.9 %collective-permute-start.7 = (bf16[256,256]{1,0:T(8,128)(2,1)S(1)}, bf16[256,256]{1,0:T(8,128)(2,1)S(1)}, u32[]{:S(2)}, u32[]{:S(2)}) collective-permute-start(bf16[256,256]{1,0:T(8,128)(2,1)S(1)} %get-tuple-element.59), channel_id=1, source_target_pairs={{0,24},{4,28},{8,16},{12,20},{16,8},{20,12},{24,0},{28,4},{1,25},{... | collective-permute-start | bytes 393224 | tf_op jit(solution)/shard_map/ppermute | solution.py:542
  59.3 7.1 %collective-permute-start.6 = (bf16[256,256]{1,0:T(8,128)(2,1)S(1)}, bf16[256,256]{1,0:T(8,128)(2,1)S(1)}, u32[]{:S(2)}, u32[]{:S(2)}) collective-permute-start(bf16[256,256]{1,0:T(8,128)(2,1)S(1)} %get-tuple-element.59), channel_id=1, source_target_pairs={{0,16},{4,20},{8,24},{12,28},{16,0},{20,4},{24,8},{28,12},{1,17},{... | collective-permute-start | bytes 393224 | tf_op jit(solution)/shard_map/ppermute | solution.py:542
  60.7 5.7 %collective-permute-start.5 = (bf16[256,256]{1,0:T(8,128)(2,1)S(1)}, bf16[256,256]{1,0:T(8,128)(2,1)S(1)}, u32[]{:S(2)}, u32[]{:S(2)}) collective-permute-start(bf16[256,256]{1,0:T(8,128)(2,1)S(1)} %get-tuple-element.59), channel_id=1, source_target_pairs={{0,8},{4,12},{8,0},{12,4},{16,24},{20,28},{24,16},{28,20},{1,9},{5... | collective-permute-start | bytes 393224 | tf_op jit(solution)/shard_map/ppermute | solution.py:542
